TPU v7x, 32 devices: a whole 2x2x4 slice. The times are simulated.
32 devices in a mesh: dp: 8 (over y, x, core), tensor: 4 (over z).
Axes of the slice: x: 2, y: 2, z: 4, core: 2. Of those that a mesh axis runs over, the one named last changes fastest.
Arguments:
- tokens: bfloat16 [8192, 2048], P(('dp', 'tensor')), may hold values from -6 to 6
- lengths: int32 [8], P('dp'), may hold values from 256 to 1024, as said below
- ln1_gain: bfloat16 [2048], P('dp'), may hold values from 0.5 to 1.5
- ln1_bias: bfloat16 [2048], P('dp'), may hold values from -4 to 4
- qkv_weight: bfloat16 [2048, 3, 2048], P('dp', None, 'tensor'), may hold values from -0.125 to 0.125
- qv_bias: bfloat16 [2, 16, 128], P(None, 'tensor', 'dp'), may hold values from -4 to 4
- out_weight: bfloat16 [2048, 2048], P('tensor', 'dp'), may hold values from -0.75 to 0.75
- out_bias: bfloat16 [2048], P('dp'), may hold values from -4 to 4
- ln2_gain: bfloat16 [2048], P('dp'), may hold values from 0.5 to 1.5
- ln2_bias: bfloat16 [2048], P('dp'), may hold values from -4 to 4
- up_weight: bfloat16 [2048, 8192], P('dp', 'tensor'), may hold values from -0.125 to 0.125
- up_bias: bfloat16 [512, 16], P('tensor', 'dp'), may hold values from -4 to 4
- down_weight: bfloat16 [8192, 2048], P('tensor', 'dp'), may hold values from -0.0625 to 0.0625
- down_bias: bfloat16 [2048], P('dp'), may hold values from -4 to 4
- cotangent: bfloat16 [8192, 2048], P(('dp', 'tensor')), may hold values from -6 to 6
Outputs:
- output: bfloat16 [8192, 2048], P(('dp', 'tensor'))
- tokens_grad: float32 [8192, 2048], P(('dp', 'tensor'))
- ln1_gain_grad: float32 [2048], P('dp')
- ln1_bias_grad: float32 [2048], P('dp')
- qkv_weight_grad: float32 [2048, 3, 2048], P('dp', None, 'tensor')
- qv_bias_grad: float32 [2, 16, 128], P(None, 'tensor', 'dp')
- out_weight_grad: float32 [2048, 2048], P('tensor', 'dp')
- out_bias_grad: float32 [2048], P('dp')
- ln2_gain_grad: float32 [2048], P('dp')
- ln2_bias_grad: float32 [2048], P('dp')
- up_weight_grad: float32 [2048, 8192], P('dp', 'tensor')
- up_bias_grad: float32 [512, 16], P('tensor', 'dp')
- down_weight_grad: float32 [8192, 2048], P('tensor', 'dp')
- down_bias_grad: float32 [2048], P('dp')
- stream_rms: float32 [5], replicated
Inputs may be any that keep to these rules, and one draw needn't show every extreme that they name: `lengths`: each sequence's true token count.
All inputs are finite; a program needn't handle non-finite values.
Results may differ from a plain program's by a relative error of at most 0.02.
Values may be sent and summed in bfloat16 or wider, within the bound.
A program may use at most 256 MiB of HBM per device.

v0:
```python
import jax
import jax.numpy as jnp
from jax import lax
from jax.sharding import PartitionSpec as P

D = 2048
HD = 128
LEN = 1024


EPS = 1e-05


def layer_norm(values, norm_gain, norm_shift):
    center = values - jnp.mean(values, axis=-1, keepdims=True)
    spread = lax.rsqrt(jnp.mean(center * center, axis=-1, keepdims=True) + EPS)
    normed = center * spread
    return (normed * norm_gain + norm_shift, normed, spread)


def norm_backward(upstream, normed, spread, norm_gain):
    scaled = upstream * norm_gain
    mean_part = jnp.mean(scaled, axis=-1, keepdims=True)
    across = jnp.mean(scaled * normed, axis=-1, keepdims=True)
    return spread * (scaled - mean_part - normed * across)


def gelu_tanh(values):
    return jax.nn.gelu(values, approximate=True)


def contract_rows(left, right):
    return lax.dot_general(
        left, right, (((0,), (0,)), ((), ())), preferred_element_type=jnp.float32
    )


def contract_cols(left, right):
    return lax.dot_general(
        left, right, (((1,), (1,)), ((), ())), preferred_element_type=jnp.float32
    )


def allowed_keys(first_row, block_size, positions, length):
    query_pos = first_row + jnp.arange(block_size, dtype=jnp.int32)
    return (positions[None, :] <= query_pos[:, None]) & (positions[None, :] < length)


def attend_forward(queries, key_rows, value_rows, length):
    block_size = min(512, LEN)
    positions = jnp.arange(LEN, dtype=jnp.int32)
    score_scale = HD ** (-0.5)

    def one_block(block_index):
        first_row = block_index * block_size
        query_block = lax.dynamic_slice_in_dim(queries, first_row, block_size, 0)
        scores = (
            jnp.einsum("qhd,khd->hqk", query_block, key_rows, preferred_element_type=jnp.float32)
            * score_scale
        )
        allowed = allowed_keys(first_row, block_size, positions, length)
        scores = jnp.where(allowed[None], scores, -1e30)
        row_max = jnp.max(scores, axis=-1, keepdims=True)
        powers = jnp.exp(scores - row_max)
        totals = jnp.sum(powers, axis=-1, keepdims=True)
        shares = (powers / totals).astype(jnp.bfloat16)
        mixed = jnp.einsum("hqk,khd->qhd", shares, value_rows, preferred_element_type=jnp.float32)
        return (mixed.astype(jnp.bfloat16), (row_max + jnp.log(totals))[..., 0])

    mixed, log_totals = lax.map(one_block, jnp.arange(LEN // block_size, dtype=jnp.int32))
    return (mixed.reshape(LEN, queries.shape[1], HD), log_totals)


def attend_backward(queries, key_rows, value_rows, grad_out, log_totals, length):
    block_size = min(512, LEN)
    positions = jnp.arange(LEN, dtype=jnp.int32)
    score_scale = HD ** (-0.5)

    def one_block(carry, block_index):
        key_grad, value_grad = carry
        first_row = block_index * block_size
        query_block = lax.dynamic_slice_in_dim(queries, first_row, block_size, 0)
        grad_block = lax.dynamic_slice_in_dim(grad_out, first_row, block_size, 0)
        scores = (
            jnp.einsum("qhd,khd->hqk", query_block, key_rows, preferred_element_type=jnp.float32)
            * score_scale
        )
        allowed = allowed_keys(first_row, block_size, positions, length)
        shares = jnp.where(allowed[None], jnp.exp(scores - log_totals[block_index][..., None]), 0.0)
        value_grad = value_grad + jnp.einsum(
            "hqk,qhd->khd",
            shares.astype(jnp.bfloat16),
            grad_block,
            preferred_element_type=jnp.float32,
        )
        share_grad = jnp.einsum(
            "qhd,khd->hqk", grad_block, value_rows, preferred_element_type=jnp.float32
        )
        centre = jnp.sum(shares * share_grad, axis=-1, keepdims=True)
        score_grad = (shares * (share_grad - centre)).astype(jnp.bfloat16)
        query_grad = (
            jnp.einsum("hqk,khd->qhd", score_grad, key_rows, preferred_element_type=jnp.float32)
            * score_scale
        )
        key_grad = (
            key_grad
            + jnp.einsum(
                "hqk,qhd->khd", score_grad, query_block, preferred_element_type=jnp.float32
            )
            * score_scale
        )
        return ((key_grad, value_grad), query_grad.astype(jnp.bfloat16))

    zeros_kv = jnp.zeros((LEN, queries.shape[1], HD), jnp.float32)
    (key_grad, value_grad), query_grads = lax.scan(
        one_block, (zeros_kv, zeros_kv), jnp.arange(LEN // block_size, dtype=jnp.int32)
    )
    return (
        query_grads.reshape(LEN, queries.shape[1], HD),
        key_grad.astype(jnp.bfloat16),
        value_grad.astype(jnp.bfloat16),
    )


def shards(
    tokens,
    lengths,
    ln1_gain,
    ln1_bias,
    qkv_weight,
    qv_bias,
    out_weight,
    out_bias,
    ln2_gain,
    ln2_bias,
    up_weight,
    up_bias,
    down_weight,
    down_bias,
    cotangent,
):
    (
        gain_one,
        shift_one,
        qkv_full,
        qv_full,
        out_full,
        out_shift,
        gain_two,
        shift_two,
        up_full,
        up_shift,
        down_full,
        down_shift,
    ) = (
        lax.all_gather(ln1_gain, "dp", axis=0, tiled=True),
        lax.all_gather(ln1_bias, "dp", axis=0, tiled=True),
        lax.all_gather(qkv_weight, "dp", axis=0, tiled=True),
        lax.all_gather(qv_bias, "dp", axis=2, tiled=True),
        lax.all_gather(out_weight, "dp", axis=1, tiled=True),
        lax.all_gather(out_bias, "dp", axis=0, tiled=True),
        lax.all_gather(ln2_gain, "dp", axis=0, tiled=True),
        lax.all_gather(ln2_bias, "dp", axis=0, tiled=True),
        lax.all_gather(up_weight, "dp", axis=0, tiled=True),
        lax.all_gather(up_bias, "dp", axis=1, tiled=True),
        lax.all_gather(down_weight, "dp", axis=1, tiled=True),
        lax.all_gather(down_bias, "dp", axis=0, tiled=True),
    )
    gain_one = gain_one.astype(jnp.float32)
    shift_one = shift_one.astype(jnp.float32)
    gain_two = gain_two.astype(jnp.float32)
    shift_two = shift_two.astype(jnp.float32)
    out_shift = out_shift.astype(jnp.float32)
    down_shift = down_shift.astype(jnp.float32)
    own_rows = tokens.shape[0]
    group_rows = own_rows * lax.axis_size("tensor")
    seq_count = lengths.shape[0]
    local_heads = qkv_full.shape[2] // HD
    local_width = qkv_full.shape[2]
    local_hidden = up_full.shape[1]
    own_first = lax.axis_index("tensor") * own_rows
    positions = jnp.arange(group_rows, dtype=jnp.int32)
    seq_ids = positions // LEN
    length_rows = jnp.sum(
        jnp.where(
            seq_ids[:, None] == jnp.arange(seq_count, dtype=jnp.int32)[None, :], lengths[None, :], 0
        ),
        axis=1,
    )
    valid_all = (positions % LEN < length_rows).astype(jnp.float32)[:, None]
    valid_own = lax.dynamic_slice_in_dim(valid_all, own_first, own_rows, 0)
    own_count = jnp.sum(valid_own)
    tokens_in, cotangent_in = (
        lax.all_gather(tokens, "tensor", axis=0, tiled=True),
        lax.all_gather(cotangent, "tensor", axis=0, tiled=True),
    )

    def own_part(values):
        return lax.dynamic_slice_in_dim(values, own_first, own_rows, 0)

    def branch_total(source, weight):
        return lax.psum(
            jnp.dot(source, weight, preferred_element_type=jnp.float32).astype(jnp.bfloat16),
            "tensor",
        ).astype(jnp.float32)

    def input_total(source, weight):
        return lax.psum(contract_cols(source, weight).astype(jnp.bfloat16), "tensor").astype(
            jnp.float32
        )

    recorded = []

    def record(values):
        mine = own_part(values)
        square_sum = jnp.sum(valid_own * mine * mine)
        recorded.append(lax.psum((square_sum, own_count), ("dp", "tensor")))

    x_values = tokens_in.astype(jnp.float32)
    record(x_values)
    ln1_out, normed_one, spread_one = layer_norm(x_values, gain_one, shift_one)
    normed_a = ln1_out.astype(jnp.bfloat16)
    qkv_flat = qkv_full.reshape(D, 3 * local_width)
    projected = jnp.dot(normed_a, qkv_flat, preferred_element_type=jnp.float32)
    qv_values = qv_full.astype(jnp.float32)
    bias_all = jnp.stack([qv_values[0], jnp.zeros_like(qv_values[0]), qv_values[1]]).reshape(
        3 * local_width
    )
    qkv_low = (projected + bias_all).astype(jnp.bfloat16)
    qkv_seq = qkv_low.reshape(seq_count, LEN, 3, local_heads, HD)

    def forward_sequence(pair):
        seq_qkv, seq_len = pair
        return attend_forward(seq_qkv[:, 0], seq_qkv[:, 1], seq_qkv[:, 2], seq_len)

    attended, log_totals = lax.map(forward_sequence, (qkv_seq, lengths))
    attended_rows = attended.reshape(group_rows, local_width)
    attn_out = branch_total(attended_rows, out_full) + out_shift
    record(attn_out)
    middle = x_values + attn_out
    record(middle)
    ln2_out, normed_two, spread_two = layer_norm(middle, gain_two, shift_two)
    normed_c = ln2_out.astype(jnp.bfloat16)
    hidden_pre = jnp.dot(normed_c, up_full, preferred_element_type=jnp.float32) + up_shift.astype(
        jnp.float32
    ).reshape(local_hidden)
    hidden_act = gelu_tanh(hidden_pre).astype(jnp.bfloat16)
    mlp_out = branch_total(hidden_act, down_full) + down_shift
    record(mlp_out)
    result = middle + mlp_out
    record(result)
    grad_y = cotangent_in.astype(jnp.float32) * valid_all
    down_bias_grad = jnp.sum(own_part(grad_y), axis=0)
    grad_m = grad_y.astype(jnp.bfloat16)
    down_weight_grad = contract_rows(hidden_act, grad_m)
    grad_act = contract_cols(grad_m, down_full)
    gelu_value, gelu_back = jax.vjp(gelu_tanh, hidden_pre)
    grad_u = gelu_back(grad_act)[0].astype(jnp.bfloat16)
    up_bias_grad = jnp.sum(grad_u, axis=0, dtype=jnp.float32).reshape(local_hidden // 16, 16)
    up_weight_grad = contract_rows(normed_c, grad_u)
    grad_c = input_total(grad_u, up_full)
    grad_mid = grad_y + norm_backward(grad_c, normed_two, spread_two, gain_two)
    ln2_gain_grad = jnp.sum(own_part(grad_c * normed_two), axis=0)
    ln2_bias_grad = jnp.sum(own_part(grad_c), axis=0)
    out_bias_grad = jnp.sum(own_part(grad_mid), axis=0)
    grad_z = grad_mid.astype(jnp.bfloat16)
    out_weight_grad = contract_rows(attended_rows, grad_z)
    grad_o = contract_cols(grad_z, out_full).astype(jnp.bfloat16)
    grad_o_seq = grad_o.reshape(seq_count, LEN, local_heads, HD)

    def backward_sequence(group):
        seq_qkv, seq_grad, seq_totals, seq_len = group
        return attend_backward(
            seq_qkv[:, 0], seq_qkv[:, 1], seq_qkv[:, 2], seq_grad, seq_totals, seq_len
        )

    grad_q, grad_k, grad_v = lax.map(backward_sequence, (qkv_seq, grad_o_seq, log_totals, lengths))
    grad_qkv = jnp.stack([grad_q, grad_k, grad_v], axis=2).reshape(group_rows, 3 * local_width)
    qv_bias_grad = jnp.stack(
        [
            jnp.sum(grad_q, axis=(0, 1), dtype=jnp.float32),
            jnp.sum(grad_v, axis=(0, 1), dtype=jnp.float32),
        ]
    )
    qkv_weight_grad = contract_rows(normed_a, grad_qkv).reshape(D, 3, local_width)
    grad_a = input_total(grad_qkv, qkv_flat)
    grad_x_all = grad_mid + norm_backward(grad_a, normed_one, spread_one, gain_one)
    tokens_grad = own_part(grad_x_all)
    ln1_gain_grad = jnp.sum(own_part(grad_a * normed_one), axis=0)
    ln1_bias_grad = jnp.sum(own_part(grad_a), axis=0)
    (
        qkv_weight_out,
        qv_bias_out,
        out_weight_out,
        up_weight_out,
        up_bias_out,
        down_weight_out,
        ln1_gain_part,
        ln1_bias_part,
        out_bias_part,
        ln2_gain_part,
        ln2_bias_part,
        down_bias_part,
    ) = (
        lax.psum_scatter(
            qkv_weight_grad.astype(jnp.bfloat16), "dp", scatter_dimension=0, tiled=True
        ).astype(jnp.float32),
        lax.psum_scatter(
            qv_bias_grad.astype(jnp.bfloat16), "dp", scatter_dimension=2, tiled=True
        ).astype(jnp.float32),
        lax.psum_scatter(
            out_weight_grad.astype(jnp.bfloat16), "dp", scatter_dimension=1, tiled=True
        ).astype(jnp.float32),
        lax.psum_scatter(
            up_weight_grad.astype(jnp.bfloat16), "dp", scatter_dimension=0, tiled=True
        ).astype(jnp.float32),
        lax.psum_scatter(
            up_bias_grad.astype(jnp.bfloat16), "dp", scatter_dimension=1, tiled=True
        ).astype(jnp.float32),
        lax.psum_scatter(
            down_weight_grad.astype(jnp.bfloat16), "dp", scatter_dimension=1, tiled=True
        ).astype(jnp.float32),
        lax.psum_scatter(
            ln1_gain_grad.astype(jnp.bfloat16), "dp", scatter_dimension=0, tiled=True
        ).astype(jnp.float32),
        lax.psum_scatter(
            ln1_bias_grad.astype(jnp.bfloat16), "dp", scatter_dimension=0, tiled=True
        ).astype(jnp.float32),
        lax.psum_scatter(
            out_bias_grad.astype(jnp.bfloat16), "dp", scatter_dimension=0, tiled=True
        ).astype(jnp.float32),
        lax.psum_scatter(
            ln2_gain_grad.astype(jnp.bfloat16), "dp", scatter_dimension=0, tiled=True
        ).astype(jnp.float32),
        lax.psum_scatter(
            ln2_bias_grad.astype(jnp.bfloat16), "dp", scatter_dimension=0, tiled=True
        ).astype(jnp.float32),
        lax.psum_scatter(
            down_bias_grad.astype(jnp.bfloat16), "dp", scatter_dimension=0, tiled=True
        ).astype(jnp.float32),
    )
    ln1_gain_out, ln1_bias_out, out_bias_out, ln2_gain_out, ln2_bias_out, down_bias_out = lax.psum(
        (ln1_gain_part, ln1_bias_part, out_bias_part, ln2_gain_part, ln2_bias_part, down_bias_part),
        "tensor",
    )
    totals = jnp.stack([entry[0] for entry in recorded])
    count = recorded[0][1]
    stream_rms = jnp.sqrt(totals / (count * D))
    return (
        own_part(result).astype(jnp.bfloat16),
        tokens_grad,
        ln1_gain_out,
        ln1_bias_out,
        qkv_weight_out,
        qv_bias_out,
        out_weight_out,
        out_bias_out,
        ln2_gain_out,
        ln2_bias_out,
        up_weight_out,
        up_bias_out,
        down_weight_out,
        down_bias_out,
        stream_rms,
    )


def solution(mesh):
    placed = (
        P(("dp", "tensor"), None),
        P("dp"),
        P("dp"),
        P("dp"),
        P("dp", None, "tensor"),
        P(None, "tensor", "dp"),
        P("tensor", "dp"),
        P("dp"),
        P("dp"),
        P("dp"),
        P("dp", "tensor"),
        P("tensor", "dp"),
        P("tensor", "dp"),
        P("dp"),
        P(("dp", "tensor"), None),
    )
    return jax.shard_map(
        shards,
        mesh=mesh,
        in_specs=placed,
        out_specs=(
            P(("dp", "tensor"), None),
            P(("dp", "tensor"), None),
            P("dp"),
            P("dp"),
            P("dp", None, "tensor"),
            P(None, "tensor", "dp"),
            P("tensor", "dp"),
            P("dp"),
            P("dp"),
            P("dp"),
            P("dp", "tensor"),
            P("tensor", "dp"),
            P("tensor", "dp"),
            P("dp"),
            P(),
        ),
        check_vma=False,
    )
```

profile of v0, /device:TPU:0, one launch (start us, length us, event | category | flops | bytes accessed | tf_op | source)
XLA Modules:
  0.0 1391.2 jit_solution(11187329936646952826)
XLA Ops:
  12.4 10.4 all-gather.1
  22.8 8.9 all-gather
  32.5 8.3 all_gather.46
  41.2 51.9 %all-gather.14.cloned.1.call-done = bf16[1024,2048]{1,0:T(8,128)(2,1)} async-done(((bf16[256,2048]{1,0:T(8,128)(2,1)}), bf16[1024,2048]{1,0:T(8,128)(2,1)}) %all-gather.14.cloned.1.call-update) | async-done | bytes 4194320 | tf_op jit(solution)/shard_map/all_gather | solution.py:194
  99.3 41.3 %all-gather.16.cloned.1.call-done = bf16[2048,3,512]{0,2,1:T(8,128)(2,1)} async-done(((bf16[256,3,512]{0,2,1:T(8,128)(2,1)}), bf16[2048,3,512]{0,2,1:T(8,128)(2,1)}) %all-gather.16.cloned.1.call-update) | async-done | bytes 6291472 | tf_op jit(solution)/shard_map/all_gather | solution.py:158
  140.6 12.6 add_convert_fusion.2
  153.2 6.3 squeeze.48
  163.1 22.7 %while.50 = (s32[]{:T(128)}, bf16[2,512,4,128]{3,2,1,0:T(4,128)(2,1)}, f32[2,4,512]{2,1,0:T(4,128)S(1)}, s32[2]{0:T(128)S(1)}, s32[]{:T(128)}, /*index=5*/bf16[1...) while((s32[]{:T(128)}, ...), condition=%wide.region_5.6_spmd.clone.clone, body=%wide.region_2.5_spmd.clone.clone.sunk | while | flops 1100217856 | bytes 39917828 | solution.py:70
  186.0 7.0 convolution_convert_fusion.6
  195.7 8.6 all-gather.4
  204.4 8.2 all-gather.3
  212.6 8.6 all-gather.2
  221.3 8.1 all-gather.5
  229.6 118.3 %all-reduce.15.cloned.1.call-done = bf16[1024,2048]{1,0:T(8,128)(2,1)} async-done(((bf16[1024,2048]{1,0:T(8,128)(2,1)}), bf16[1024,2048]{1,0:T(8,128)(2,1)}) %all-reduce.15.cloned.1.call-update) | async-done | bytes 4194320 | tf_op jit(solution)/shard_map/psum | solution.py:202
  347.9 11.2 fusion.84
  359.1 4.5 multiply_reduce_fusion.3
  368.9 34.0 %all-gather.20.cloned.1.call-done = bf16[2048,2048]{1,0:T(8,128)(2,1)} async-done(((bf16[256,2048]{1,0:T(8,128)(2,1)}), bf16[2048,2048]{1,0:T(8,128)(2,1)}) %all-gather.20.cloned.1.call-update) | async-done | bytes 8388624 | tf_op jit(solution)/shard_map/all_gather | solution.py:164
  402.9 15.8 %fusion.69 = f32[1024,2048]{1,0:T(8,128)} fusion(bf16[2048,2048]{1,0:T(8,128)(2,1)} %all-gather.20.cloned.1.call-done, f32[1024,2048]{1,0:T(8,128)} %subtract_multiply_fusion, f32[2048]{0:T(1024)S(1)} %bitcast.153, f32[2048]{0:T(1024)S(1)} %bitcast.140), kind=kOutput, calls=%fused_computation.120 | convolution fusion | flops 8596226048 | bytes 25182208 | tf_op jit(solution)/shard_map/dot_general | solution.py:244
  418.7 66.4 %all-gather.24.cloned.1.call-done = bf16[1024,2048]{1,0:T(8,128)(2,1)} async-done(((bf16[256,2048]{1,0:T(8,128)(2,1)}), bf16[1024,2048]{1,0:T(8,128)(2,1)}) %all-gather.24.cloned.1.call-update) | async-done | bytes 4194320 | tf_op jit(solution)/shard_map/all_gather | solution.py:195
  485.1 56.3 %all-gather.22.cloned.1.call-done = bf16[2048,2048]{1,0:T(8,128)(2,1)} async-done(((bf16[2048,256]{1,0:T(8,128)(2,1)}), bf16[2048,2048]{1,0:T(8,128)(2,1)}) %all-gather.22.cloned.1.call-update) | async-done | bytes 8388624 | tf_op jit(solution)/shard_map/all_gather | solution.py:166
  541.4 19.2 %fusion.87 = (bf16[2048]{0:T(1024)(128)(2,1)}, bf16[1024,2048]{1,0:T(8,128)(2,1)S(1)}) fusion(f32[1024,2048]{1,0:T(8,128)} %fusion.69, f32[2048]{0:T(1024)S(1)} %reshape.277, bf16[2048,2048]{1,0:T(8,128)(2,1)} %all-gather.22.cloned.1.call-done, f32[1024]{0:T(1024)S(1)} %fusion.82, bf16[1024,2048]{1,0:T(8,128)(2,1)} %all-gather.24.cloned.1.call-done), kind=kOutput, calls=%fused_computation.167 | convolution fusion | flops 8642361344 | bytes 25182208 | tf_op jit(solution)/shard_map/dot_general | solution.py:39
  562.6 12.9 convolution_convert_fusion.4
  575.6 155.1 %all-reduce.17.cloned.1.call-done = bf16[1024,2048]{1,0:T(8,128)(2,1)} async-done(((bf16[1024,2048]{1,0:T(8,128)(2,1)}), bf16[1024,2048]{1,0:T(8,128)(2,1)}) %all-reduce.17.cloned.1.call-update) | async-done | bytes 4194320 | tf_op jit(solution)/shard_map/psum | solution.py:208
  730.6 6.0 multiply_reduce_fusion.5
  737.7 8.4 convert_multiply_fusion
  746.1 6.5 fusion.66
  752.6 41.4 %while.51 = (s32[]{:T(128)}, f32[1024,4,128]{0,2,1:T(8,128)S(1)}, f32[1024,4,128]{0,2,1:T(8,128)}, bf16[2,512,4,128]{3,1,2,0:T(8,128)(2,1)}, s32[2]{0:T(128)S(1)...) while((s32[]{:T(128)}, f32[1024,4,128]{0,2,1:T(8,128)S(1)}, ...), condition=%wide.region_15.16_spmd.clone.clone, body=%wide.region_13.15_spmd.clone.clone.sunk | while | flops 2720005632 | bytes 100202928 | solution.py:115
  763.6 4.0 multiply_reduce_fusion.8
  779.6 5.1 bitcast_add_fusion.5
  784.7 4.0 multiply_reduce_fusion.8
  798.3 7.4 convolution_convert_fusion.7
  805.9 16.3 %convolution_convert_fusion.5 = bf16[1024,2048]{1,0:T(8,128)(2,1)} fusion(bf16[2048,2048]{1,0:T(8,128)(2,1)} %all-gather.22.cloned.1.call-done, f32[1024,2048]{1,0:T(8,128)} %fusion.69, f32[2048]{0:T(1024)S(1)} %copy-done.27), kind=kOutput, calls=%fused_computation.86 | convolution fusion | flops 8613003264 | bytes 20979712 | tf_op jit(solution)/shard_map/dot_general | solution.py:203
  828.1 4.7 copy.114
  832.8 11.2 convolution_convert_fusion.3
  844.7 20.0 %convolution_convert_fusion = bf16[2048,2048]{1,0:T(8,128)(2,1)} fusion(bf16[1024,2048]{1,0:T(8,128)(2,1)} %all-gather.24.cloned.1.call-done, f32[1024]{0:T(1024)S(1)} %copy-done.25, f32[1024,2048]{1,0:T(8,128)} %fusion.69, f32[2048]{0:T(1024)S(1)} %copy-done.27), kind=kOutput, calls=%fused_computation.77 | convolution fusion | flops 8621391872 | bytes 20983808 | tf_op jit(solution)/shard_map/dot_general | solution.py:33
  865.4 14.8 %convolution_convert_fusion.1 = bf16[2048,2048]{1,0:T(8,128)(2,1)} fusion(bf16[1024,2048]{1,0:T(8,128)(2,1)} %copy-done.39, f32[1024,2048]{1,0:T(8,128)} %subtract_multiply_fusion, f32[2048]{0:T(1024)S(1)} %bitcast.154, f32[2048]{0:T(1024)S(1)} %bitcast.143), kind=kOutput, calls=%fused_computation.78 | convolution fusion | flops 8600420352 | bytes 20987904 | tf_op jit(solution)/shard_map/dot_general | solution.py:33
  880.9 14.3 %convolution_convert_fusion.2 = bf16[2048,3,512]{2,0,1:T(8,128)(2,1)} fusion(bf16[3,512,1024]{2,1,0:T(8,128)(2,1)} %bitcast.135, f32[2048]{0:T(1024)S(1)} %bitcast.152, f32[2048]{0:T(1024)S(1)} %bitcast.145, bf16[1024,2048]{1,0:T(8,128)(2,1)} %all-gather.14.cloned.1.call-done, f32[1024]{0:T(1024)S(1)} %copy-done.23, f32[1024]{0:T(1024)S(1)} %copy-done.19), kind=kOutput, calls=%fused_computation.81 | convolution fusion | flops 6458179584 | bytes 13656064 | tf_op jit(solution)/shard_map/dot_general | solution.py:33
  897.2 9.1 all-gather.6
  907.1 6.5 convert_element_type.197
  923.8 243.3 %all-reduce.19.cloned.1.call-done = (bf16[1024,2048]{1,0:T(8,128)(2,1)}, bf16[1024,2048]{1,0:T(8,128)(2,1)}) async-done(((bf16[1024,2048]{1,0:T(8,128)(2,1)}, bf16[1024,2048]{1,0:T(8,128)(2,1)}), (bf16[1024,2048]{1,0:T(8,128)(2,1)}, bf16[1024,2048]{1,0:T(8,128)(2,1)})) %all-reduce.19.cloned.1.call-update) | async-done | bytes 8388624 | tf_op jit(solution)/shard_map/psum | solution.py:202
  1170.5 5.6 fusion.52
  1176.1 40.6 %all-reduce.7 = (f32[1]{0:T(128)}, f32[1]{0:T(128)}, f32[1]{0:T(128)}, f32[1]{0:T(128)}, f32[1]{0:T(128)}, /*index=5*/f32[]{:T(128)}) all-reduce(f32[1]{0:T(128)} %bitcast.25, f32[1]{0:T(128)} %bitcast.26, f32[1]{0:T(128)} %bitcast.27, f32[1]{0:T(128)} %bitcast.28, ...), channel_id=1, replica_groups=mesh['dp'=8,'tensor'=4] {'dp','tensor'}, use_global_device_ids=true, to_apply=%region_47.48 | all-reduce | flops 6 | bytes 48 | tf_op jit(solution)/shard_map/psum | solution.py:217
  1216.7 6.7 convert_element_type.225
  1226.4 4.7 dynamic-slice_reduce_fusion.3
  1231.2 24.8 %all-reduce.9 = (bf16[2048]{0:T(1024)(128)(2,1)S(1)}, bf16[2048]{0:T(1024)(128)(2,1)S(1)}, bf16[2048]{0:T(1024)(128)(2,1)S(1)}, bf16[2048]{0:T(1024)(128)(2,1)S(...) all-reduce(bf16[2048]{0:T(1024)(128)(2,1)S(1)} %get-tuple-element.5, ...), channel_id=2, replica_groups=mesh['dp'=8,'tensor'=4] {'dp'}, use_global_device_ids=true, to_apply=%region_20.21.clone | all-reduce | flops 14336 | bytes 57344
  1263.4 53.3 %reduce-scatter.13.cloned.1.call-done = bf16[256,2048]{1,0:T(8,128)(2,1)} async-done(((bf16[2048,2048]{1,0:T(8,128)(2,1)}), bf16[256,2048]{1,0:T(8,128)(2,1)}) %reduce-scatter.13.cloned.1.call-update) | async-done | bytes 1048592 | tf_op jit(solution)/shard_map/reduce_scatter | solution.py:314
  1320.0 12.5 all-reduce.8
  1333.0 48.7 %reduce-scatter.9.cloned.1.call-done = bf16[256,3,512]{2,0,1:T(8,128)(2,1)} async-done(((bf16[2048,3,512]{2,0,1:T(8,128)(2,1)}), bf16[256,3,512]{2,0,1:T(8,128)(2,1)}) %reduce-scatter.9.cloned.1.call-update) | async-done | bytes 786448 | tf_op jit(solution)/shard_map/reduce_scatter | solution.py:305
  (244 shorter events, 113.4 us)
Async XLA Ops:
  7.2 85.9 %all-gather.14.cloned.1.call-start = ((), (), s32[]{:S(2)}) async-start(), calls=%async_computation.5 | async-start | bytes 5242880 | tf_op jit(solution)/shard_map/all_gather | solution.py:194
  7.9 132.7 %all-gather.16.cloned.1.call-start = ((), (), s32[]{:S(2)}) async-start(), calls=%async_computation.6 | async-start | bytes 7077888 | tf_op jit(solution)/shard_map/all_gather | solution.py:158
  10.3 175.7 %all-gather.18.cloned.1.call-start = ((), (), s32[]{:S(2)}) async-start(), calls=%async_computation.7 | async-start | bytes 2359296 | tf_op jit(solution)/shard_map/all_gather | solution.py:160
  11.0 336.9 %all-reduce.15.cloned.1.call-start = ((), (), s32[]{:S(2)}) async-start(), calls=%async_computation.8 | async-start | bytes 8388608 | tf_op jit(solution)/shard_map/psum | solution.py:202
  22.8 130.4 %copy-start.28 = (f32[8,1,256]{2,1,0:T(1,128)}, f32[8,1,256]{2,1,0:T(1,128)S(1)}, u32[]{:S(2)}) copy-start(f32[8,1,256]{2,1,0:T(1,128)S(1)} %convert_element_type.259) | copy-start | bytes 24580
  31.7 121.5 %copy-start.20 = (f32[8,1,256]{2,1,0:T(1,128)}, f32[8,1,256]{2,1,0:T(1,128)S(1)}, u32[]{:S(2)}) copy-start(f32[8,1,256]{2,1,0:T(1,128)S(1)} %convert_element_type.258) | copy-start | bytes 24580
  95.9 57.4 %copy-start.18 = (f32[1024]{0:T(1024)}, f32[1024]{0:T(1024)S(1)}, u32[]{:S(2)}) copy-start(f32[1024]{0:T(1024)S(1)} %broadcast_multiply_fusion.6) | copy-start | bytes 12292
  99.3 53.9 %copy-start.22 = (f32[1024]{0:T(1024)}, f32[1024]{0:T(1024)S(1)}, u32[]{:S(2)}) copy-start(f32[1024]{0:T(1024)S(1)} %add_rsqrt_fusion.1) | copy-start | bytes 12292
  169.6 3.2 copy-start.14
  180.7 3.2 copy-start.14
  185.9 7.7 copy-start.2
  185.9 7.7 copy-start.6
  185.9 9.7 copy-start.34
  185.9 9.7 copy-start.35
  186.0 9.7 copy-start.36
  186.0 35.3 %copy-start.33 = (bf16[128,2]{0,1:T(2,128)(2,1)S(1)}, bf16[128,2]{0,1:T(2,128)(2,1)}, u32[]{:S(2)}) copy-start(bf16[128,2]{0,1:T(2,128)(2,1)} %param.30) | copy-start | bytes 1540
  193.0 209.9 %all-gather.20.cloned.1.call-start = ((), (), s32[]{:S(2)}) async-start(), calls=%async_computation.9 | async-start | bytes 9437184 | tf_op jit(solution)/shard_map/all_gather | solution.py:164
  193.6 291.5 %all-gather.24.cloned.1.call-start = ((), (), s32[]{:S(2)}) async-start(), calls=%async_computation.11 | async-start | bytes 5242880 | tf_op jit(solution)/shard_map/all_gather | solution.py:195
  194.2 347.2 %all-gather.22.cloned.1.call-start = ((), (), s32[]{:S(2)}) async-start(), calls=%async_computation.10 | async-start | bytes 9437184 | tf_op jit(solution)/shard_map/all_gather | solution.py:166
  195.0 535.7 %all-reduce.17.cloned.1.call-start = ((), (), s32[]{:S(2)}) async-start(), calls=%async_computation.12 | async-start | bytes 8388608 | tf_op jit(solution)/shard_map/psum | solution.py:208
  204.4 198.5 %copy-start.30 = (f32[8,1,256]{2,1,0:T(1,128)}, f32[8,1,256]{2,1,0:T(1,128)S(1)}, u32[]{:S(2)}) copy-start(f32[8,1,256]{2,1,0:T(1,128)S(1)} %convert_element_type.262) | copy-start | bytes 24580
  212.6 524.0 %copy-start.16 = (f32[8,1,256]{2,1,0:T(1,128)}, f32[8,1,256]{2,1,0:T(1,128)S(1)}, u32[]{:S(2)}) copy-start(f32[8,1,256]{2,1,0:T(1,128)S(1)} %convert_element_type.261) | copy-start | bytes 24580
  229.6 311.8 %copy-start.26 = (f32[2048]{0:T(1024)}, f32[2048]{0:T(1024)S(1)}, u32[]{:S(2)}) copy-start(f32[2048]{0:T(1024)S(1)} %reshape.277) | copy-start | bytes 24580
  229.6 507.1 %copy-start.24 = (f32[1024]{0:T(1024)}, f32[1024]{0:T(1024)S(1)}, u32[]{:S(2)}) copy-start(f32[1024]{0:T(1024)S(1)} %fusion.82) | copy-start | bytes 12292
  359.1 5.8 copy-start
  575.5 345.1 %reduce-scatter.17.cloned.1.call-start = ((), (), s32[]{:S(2)}) async-start(), calls=%async_computation.17 | async-start | bytes 36864
  730.6 6.0 copy-start.5
  730.6 7.1 copy-start.10
  746.1 6.5 copy-start.4
  756.2 3.5 copy-start.9
  759.7 3.8 copy-start.7
  767.6 2.5 copy-start.11
  767.6 3.9 copy-start.3
  776.1 3.5 copy-start.9
  779.6 5.1 copy-start.7
  788.7 3.9 copy-start.3
  795.8 10.0 copy-start.27
  798.3 123.7 %reduce-scatter.11.cloned.1.call-start = ((), (), s32[]{:S(2)}) async-start(), calls=%async_computation.14 | async-start | bytes 2359296 | tf_op jit(solution)/shard_map/reduce_scatter | solution.py:311
  805.8 361.3 %all-reduce.19.cloned.1.call-start = ((), (), s32[]{:S(2)}) async-start(), calls=%async_computation.18 | async-start | bytes 16777216 | tf_op jit(solution)/shard_map/psum | solution.py:202
  805.8 16.3 %copy-start.13 = (bf16[2,512,4,128]{3,1,2,0:T(8,128)(2,1)S(1)}, bf16[2,512,4,128]{3,1,2,0:T(8,128)(2,1)}, u32[]{:S(2)}) copy-start(bf16[2,512,4,128]{3,1,2,0:T(8,128)(2,1)} %get-tuple-element.174) | copy-start | bytes 3145732
  844.0 416.7 %reduce-scatter.15.cloned.1.call-start = ((), (), s32[]{:S(2)}) async-start(), calls=%async_computation.16 | async-start | bytes 9437184 | tf_op jit(solution)/shard_map/reduce_scatter | solution.py:320
  864.8 452.0 %reduce-scatter.13.cloned.1.call-start = ((), (), s32[]{:S(2)}) async-start(), calls=%async_computation.15 | async-start | bytes 9437184 | tf_op jit(solution)/shard_map/reduce_scatter | solution.py:314
  880.3 501.4 %reduce-scatter.9.cloned.1.call-start = ((), (), s32[]{:S(2)}) async-start(), calls=%async_computation.13 | async-start | bytes 7077888 | tf_op jit(solution)/shard_map/reduce_scatter | solution.py:305
  880.9 14.3 %copy-start.38 = (u32[32]{0:T(128)S(1)}, u32[32]{0:T(128)}, u32[]{:S(2)}) copy-start(u32[32]{0:T(128)} %constant.157) | copy-start | bytes 388
  880.9 16.2 %copy-start.37 = (bf16[256]{0:T(256)(128)(2,1)S(1)}, bf16[256]{0:T(256)(128)(2,1)}, u32[]{:S(2)}) copy-start(bf16[256]{0:T(256)(128)(2,1)} %param.32) | copy-start | bytes 1540
  895.2 18.3 %copy-start.32 = (bf16[2048]{0:T(1024)(128)(2,1)S(1)}, bf16[2048]{0:T(1024)(128)(2,1)}, u32[]{:S(2)}) copy-start(bf16[2048]{0:T(1024)(128)(2,1)} %get-tuple-element.519) | copy-start | bytes 12292
  1216.7 6.7 copy-start.1
  1216.7 6.7 copy-start.8
  (13 other events, 14.1 us)
Sparse Core Ops, SparseCore 0:
  9.6 83.4 all-gather.13
  95.5 45.0 all-gather.15
  142.5 28.0 all-gather.17
  193.2 154.7 all-reduce.14
  349.7 53.2 all-gather.19
  404.3 80.7 all-gather.23
  487.0 54.3 all-gather.21
  575.6 154.9 all-reduce.16
  798.4 30.2 reduce-scatter.16
  832.4 41.1 reduce-scatter.10
  876.2 290.8 all-reduce.18
  1170.4 71.3 reduce-scatter.14
  1245.2 71.4 reduce-scatter.12
  1320.0 61.6 reduce-scatter.8
where the time goes:
time: 1400 us; the launch traced here: 1390 us
  waiting for transfers between devices  872 us (62%)
  matrix products  195 us (14%)
  blocking collectives  148 us (11%)
  other arithmetic  108 us (8%)
  local copies, waits for them, and re-layouts  41.9 us (3%)
  between operations  17.6 us (1%)
    psum x2, waiting for transfers between devices, branch_total(): lax.psum(jnp.dot(source, weight, preferred_element_type=jnp.float32).asty...  362 us
    psum x1, waiting for transfers between devices, input_total(): lax.psum(contract_cols(source, weight).astype(jnp.bfloat16), 'tensor')  155 us
    all_gather x1, waiting for transfers between devices, shards(): lax.all_gather(cotangent, 'tensor', axis=0, tiled=True)  66.4 us
    dot_general x4, matrix products, contract_rows(): lax.dot_general(left, right, (((0,), (0,)), ((), ())), preferred_element_...  56.5 us
    all_gather x1, waiting for transfers between devices, shards(): lax.all_gather(down_weight, 'dp', axis=1, tiled=True)  56.3 us
    reduce_scatter x1, waiting for transfers between devices, shards(): lax.psum_scatter(up_weight_grad.astype(jnp.bfloat16), 'dp', scatter_dimen...  53.3 us
    all_gather x1, waiting for transfers between devices, shards(): lax.all_gather(tokens, 'tensor', axis=0, tiled=True)  51.9 us
    dot_general x4, matrix products, contract_cols(): lax.dot_general(left, right, (((1,), (1,)), ((), ())), preferred_element_...  49.8 us
  transfers between devices with their start and end apart: 14, of which 10 were waited for; matrix products, arithmetic and copies ran while one was open for 17% of the time, Pallas kernels for 0%

commit v1 on v0

v1 whole, which is shorter than its diff:
```python
import functools

import jax
import jax.numpy as jnp
from jax import lax
from jax.experimental import pallas as pl
from jax.experimental.pallas import tpu as pltpu
from jax.sharding import PartitionSpec as P

HD = 128
LEN = 1024
EPS = 1e-05
MESH = pl.DeviceIdType.MESH
F32 = jnp.float32
BF16 = jnp.bfloat16
VMEM_CAP = 60 * 1024 * 1024
SUBS = 2
WHOLE = pl.BlockSpec(memory_space=pltpu.VMEM)


class Line:
    def __init__(self, size, rows):
        self.size, self.rows, self.t = size, rows, lax.axis_index("tensor")
        self.sub = rows // SUBS

    def barrier(self):
        sem = pltpu.get_barrier_semaphore()

        @pl.when(self.t > 0)
        def _():
            pl.semaphore_signal(sem, device_id={"tensor": self.t - 1}, device_id_type=MESH)

        @pl.when(self.t < self.size - 1)
        def _():
            pl.semaphore_signal(sem, device_id={"tensor": self.t + 1}, device_id_type=MESH)

        more = jnp.where(self.t > 0, 1, 0) + jnp.where(self.t < self.size - 1, 1, 0)
        pl.semaphore_wait(sem, more)

    def _copy(self, src, dst, sems, way, shard, part):
        send, recv = sems
        target = self.t + 1 if way == 0 else self.t - 1
        return pltpu.make_async_remote_copy(
            src_ref=src,
            dst_ref=dst.at[shard, pl.ds(part * self.sub, self.sub)],
            send_sem=send.at[way, shard, part],
            recv_sem=recv.at[way, shard, part],
            device_id={"tensor": target},
            device_id_type=MESH,
        )

    def _rows(self, ref, shard, part):
        return ref.at[shard, pl.ds(part * self.sub, self.sub)]

    def _edge(self, way):
        return self.t < self.size - 1 if way == 0 else self.t > 0

    def gather_step(self, way, k, part, buf, sems, first):
        t, last = self.t, self.size - 1
        shard = t - k if way == 0 else t + k
        inside = (t >= k) if way == 0 else (t + k <= last)

        @pl.when(inside)
        def _():
            held = self._rows(buf, shard, part)
            if k > 0:
                self._copy(held, buf, sems, way, shard, part).wait_recv()

            @pl.when(self._edge(way))
            def _():
                src = held
                if k == 0 and first is not None:
                    src = first.at[pl.ds(part * self.sub, self.sub)]
                self._copy(src, buf, sems, way, shard, part).start()

    def scatter_step(self, way, j, part, terms, buf, sems):
        t, last = self.t, self.size - 1
        shard = last - j if way == 0 else j
        beyond = (shard > t) if way == 0 else (shard < t)
        starts = (t == 0) if way == 0 else (t == last)

        @pl.when(beyond & starts)
        def _():
            self._copy(self._rows(terms, shard, part), buf, sems, way, shard, part).start()

        @pl.when(beyond & jnp.logical_not(starts))
        def _():
            held = self._rows(buf, shard, part)
            self._copy(held, buf, sems, way, shard, part).wait_recv()
            step = min(32, self.sub)

            def add(i, carry):
                rows = pl.ds(part * self.sub + i * step, step)
                total = buf[shard, rows, :].astype(F32) + terms[shard, rows, :].astype(F32)
                buf[shard, rows, :] = total.astype(BF16)
                return carry

            lax.fori_loop(0, self.sub // step, add, 0)
            self._copy(held, buf, sems, way, shard, part).start()

    def phase(self, gather=None, scatter=None, on_slot=None):
        n = self.size
        for k in range(n):
            for part in range(SUBS):
                for way in (0, 1):
                    if gather is not None:
                        self.gather_step(way, k, part, gather[0], gather[1], gather[2])
                    if scatter is not None:
                        if gather is None:
                            if k < n - 1:
                                self.scatter_step(way, k, part, scatter[0], scatter[1][way], scatter[2])
                        else:
                            behind = self.t if way == 0 else n - 1 - self.t
                            for b in range(k):

                                @pl.when(behind == b)
                                def _(b=b, k=k, part=part, way=way):
                                    self.scatter_step(
                                        way, k - 1 - b, part, scatter[0], scatter[1][way], scatter[2]
                                    )
            if on_slot is not None:
                on_slot(k)

    def own_wait(self, bufs, sems):
        for way in (0, 1):
            arrives = self.t > 0 if way == 0 else self.t < self.size - 1

            @pl.when(arrives)
            def _(way=way):
                for part in range(SUBS):
                    held = self._rows(bufs[way], self.t, part)
                    self._copy(held, bufs[way], sems, way, self.t, part).wait_recv()

    def own_sum(self, terms, bufs, rows):
        t = self.t
        zero = jnp.zeros((), F32)
        right = jnp.where(t > 0, bufs[0][t, rows, :].astype(F32), zero)
        left = jnp.where(t < self.size - 1, bufs[1][t, rows, :].astype(F32), zero)
        return terms[t, rows, :].astype(F32) + right + left

    def drain_gather(self, buf, sems):
        for way in (0, 1):
            for k in range(self.size):
                shard = self.t - k if way == 0 else self.t + k
                inside = (self.t >= k) if way == 0 else (self.t + k <= self.size - 1)

                @pl.when(inside & self._edge(way))
                def _(way=way, shard=shard):
                    for part in range(SUBS):
                        held = self._rows(buf, shard, part)
                        self._copy(held, buf, sems, way, shard, part).wait_send()

    def drain_scatter(self, bufs, sems):
        for way in (0, 1):
            for j in range(self.size - 1):
                shard = self.size - 1 - j if way == 0 else j
                beyond = (shard > self.t) if way == 0 else (shard < self.t)

                @pl.when(beyond)
                def _(way=way, shard=shard):
                    for part in range(SUBS):
                        held = self._rows(bufs[way], shard, part)
                        self._copy(held, bufs[way], sems, way, shard, part).wait_send()


def line_sems(size):
    return [pltpu.SemaphoreType.DMA((2, size, SUBS)), pltpu.SemaphoreType.DMA((2, size, SUBS))]


def fold(x):
    rows, width = x.shape
    return jnp.sum(x.reshape(rows // 8, 8, width), axis=0)


def normal(x):
    centre = x - jnp.mean(x, axis=-1, keepdims=True)
    spread = lax.rsqrt(jnp.mean(centre * centre, axis=-1, keepdims=True) + EPS)
    return centre * spread, spread


def normal_back(upstream, normed, spread, gain):
    scaled = upstream * gain
    mean_part = jnp.mean(scaled, axis=-1, keepdims=True)
    across = jnp.mean(scaled * normed, axis=-1, keepdims=True)
    return spread * (scaled - mean_part - normed * across)


def row_loop(rows, step, body):
    def one(i, carry):
        body(pl.ds(pl.multiple_of(i * step, step), step))
        return carry

    lax.fori_loop(0, rows // step, one, 0)


def params(collective_id=None):
    if collective_id is None:
        return pltpu.CompilerParams(vmem_limit_bytes=VMEM_CAP)
    return pltpu.CompilerParams(
        collective_id=collective_id, has_side_effects=True, vmem_limit_bytes=VMEM_CAP
    )


def gather_small_kernel(n_dp, small, out, send, recv):
    me = lax.axis_index("dp")
    sem = pltpu.get_barrier_semaphore()
    for p in range(1, n_dp):
        pl.semaphore_signal(
            sem, device_id={"dp": lax.rem(me + p, n_dp)}, device_id_type=MESH
        )
    pl.semaphore_wait(sem, n_dp - 1)
    for p in range(1, n_dp):
        pltpu.make_async_remote_copy(
            src_ref=small,
            dst_ref=out.at[me],
            send_sem=send.at[p],
            recv_sem=recv.at[me],
            device_id={"dp": lax.rem(me + p, n_dp)},
            device_id_type=MESH,
        ).start()
    out[pl.ds(me, 1)] = small[...][None]
    for p in range(1, n_dp):
        source = lax.rem(me + p, n_dp)
        done = pltpu.make_async_remote_copy(
            src_ref=small,
            dst_ref=out.at[source],
            send_sem=send.at[p],
            recv_sem=recv.at[source],
            device_id={"dp": source},
            device_id_type=MESH,
        )
        done.wait_recv()
        done.wait_send()


def gather_small(small, n_dp, cid):
    return pl.pallas_call(
        functools.partial(gather_small_kernel, n_dp),
        out_shape=jax.ShapeDtypeStruct((n_dp,) + small.shape, small.dtype),
        in_specs=[WHOLE],
        out_specs=WHOLE,
        scratch_shapes=[pltpu.SemaphoreType.DMA((n_dp,)), pltpu.SemaphoreType.DMA((n_dp,))],
        compiler_params=params(cid),
    )(small)


def gather_rows_kernel(size, own, out, send, recv):
    line = Line(size, own.shape[0])
    line.barrier()
    sems = (send, recv)
    line.phase(
        gather=(out, sems, own),
    )
    out[pl.ds(line.t, 1)] = own[...][None]
    line.drain_gather(out, sems)


def gather_rows(own, size, cid):
    rows, width = own.shape
    return pl.pallas_call(
        functools.partial(gather_rows_kernel, size),
        out_shape=jax.ShapeDtypeStruct((size, rows, width), own.dtype),
        in_specs=[WHOLE],
        out_specs=WHOLE,
        scratch_shapes=line_sems(size),
        compiler_params=params(cid),
        name="gather_tokens",
    )(own)


def middle_kernel(
    size, terms, cot, tok, valid, vecs, c_out, gm_out, mid_out, stats,
    right, left, gs, gr, ss, sr, cs, cr,
):
    line = Line(size, tok.shape[0])
    rows = tok.shape[0]
    step = min(32, rows)
    line.barrier()
    line.phase(gather=(gm_out, (gs, gr), cot), scatter=(terms, (right, left), (ss, sr)))
    gm_out[pl.ds(line.t, 1)] = cot[...][None]
    line.own_wait((right, left), (ss, sr))
    stats[...] = jnp.zeros_like(stats)

    def body(at):
        attn = line.own_sum(terms, (right, left), at) + vecs[2:3, :]
        x = tok[at, :].astype(F32)
        mid = x + attn
        normed, _ = normal(mid)
        c_out[line.t, at, :] = (normed * vecs[3:4, :] + vecs[4:5, :]).astype(BF16)
        mid_out[at, :] = mid
        ok = valid[at, 0:1]
        stats[0:8, :] += fold(ok * x * x)
        stats[8:16, :] += fold(ok * attn * attn)
        stats[16:24, :] += fold(ok * mid * mid)

    row_loop(rows, step, body)
    line.phase(gather=(c_out, (cs, cr), None))
    line.drain_gather(gm_out, (gs, gr))
    line.drain_scatter((right, left), (ss, sr))
    line.drain_gather(c_out, (cs, cr))


def middle(terms, cot, tok, valid, vecs, size, cid):
    rows, width = tok.shape
    full = (size, rows, width)
    return pl.pallas_call(
        functools.partial(middle_kernel, size),
        out_shape=(
            jax.ShapeDtypeStruct(full, BF16),
            jax.ShapeDtypeStruct(full, BF16),
            jax.ShapeDtypeStruct((rows, width), F32),
            jax.ShapeDtypeStruct((24, width), F32),
        ),
        in_specs=[WHOLE] * 5,
        out_specs=(WHOLE,) * 4,
        scratch_shapes=[pltpu.VMEM(full, BF16), pltpu.VMEM(full, BF16)]
        + line_sems(size)
        + line_sems(size)
        + line_sems(size),
        compiler_params=params(cid),
        name="middle",
    )(terms, cot, tok, valid, vecs)


def back_middle_kernel(
    size, terms, mlp, gm, mid, valid, vecs, gz_out, gmid_out, y_out, stats,
    right, left, right2, left2, ss, sr, ms, mr, gs, gr,
):
    line = Line(size, mid.shape[0])
    rows = mid.shape[0]
    step = min(32, rows)
    line.barrier()
    line.phase(scatter=(terms, (right, left), (ss, sr)))
    line.own_wait((right, left), (ss, sr))
    stats[...] = jnp.zeros_like(stats)

    def body(at):
        e = line.own_sum(terms, (right, left), at)
        normed, spread = normal(mid[at, :])
        gy = gm[at, :].astype(F32)
        gmid = gy + normal_back(e, normed, spread, vecs[3:4, :])
        gz_out[line.t, at, :] = gmid.astype(BF16)
        gmid_out[at, :] = gmid
        stats[0:8, :] += fold(e * normed)
        stats[8:16, :] += fold(e)
        stats[16:24, :] += fold(gmid)
        stats[24:32, :] += fold(gy)

    row_loop(rows, step, body)
    line.phase(gather=(gz_out, (gs, gr), None), scatter=(mlp, (right2, left2), (ms, mr)))
    line.own_wait((right2, left2), (ms, mr))

    def tail(at):
        out = line.own_sum(mlp, (right2, left2), at) + vecs[5:6, :]
        y = mid[at, :] + out
        y_out[at, :] = y.astype(BF16)
        ok = valid[at, 0:1]
        stats[32:40, :] += fold(ok * out * out)
        stats[40:48, :] += fold(ok * y * y)

    row_loop(rows, step, tail)
    line.drain_scatter((right, left), (ss, sr))
    line.drain_scatter((right2, left2), (ms, mr))
    line.drain_gather(gz_out, (gs, gr))


def back_middle(terms, mlp, gm, mid, valid, vecs, size, cid):
    rows, width = mid.shape
    full = (size, rows, width)
    return pl.pallas_call(
        functools.partial(back_middle_kernel, size),
        out_shape=(
            jax.ShapeDtypeStruct(full, BF16),
            jax.ShapeDtypeStruct((rows, width), F32),
            jax.ShapeDtypeStruct((rows, width), BF16),
            jax.ShapeDtypeStruct((48, width), F32),
        ),
        in_specs=[WHOLE] * 6,
        out_specs=(WHOLE,) * 4,
        scratch_shapes=[pltpu.VMEM(full, BF16)] * 4
        + line_sems(size)
        + line_sems(size)
        + line_sems(size),
        compiler_params=params(cid),
        name="back_middle",
    )(terms, mlp, gm, mid, valid, vecs)


def finish_kernel(size, terms, tok, gmid, vecs, grad_out, stats, right, left, ss, sr):
    line = Line(size, tok.shape[0])
    rows = tok.shape[0]
    step = min(32, rows)
    line.barrier()
    line.phase(scatter=(terms, (right, left), (ss, sr)))
    line.own_wait((right, left), (ss, sr))
    stats[...] = jnp.zeros_like(stats)

    def body(at):
        e = line.own_sum(terms, (right, left), at)
        normed, spread = normal(tok[at, :].astype(F32))
        grad_out[at, :] = gmid[at, :] + normal_back(e, normed, spread, vecs[0:1, :])
        stats[0:8, :] += fold(e * normed)
        stats[8:16, :] += fold(e)

    row_loop(rows, step, body)
    line.drain_scatter((right, left), (ss, sr))


def finish(terms, tok, gmid, vecs, size, cid):
    rows, width = tok.shape
    full = (size, rows, width)
    return pl.pallas_call(
        functools.partial(finish_kernel, size),
        out_shape=(
            jax.ShapeDtypeStruct((rows, width), F32),
            jax.ShapeDtypeStruct((16, width), F32),
        ),
        in_specs=[WHOLE] * 4,
        out_specs=(WHOLE,) * 2,
        scratch_shapes=[pltpu.VMEM(full, BF16)] * 2 + line_sems(size),
        compiler_params=params(cid),
        name="finish",
    )(terms, tok, gmid, vecs)


def reduce_small_kernel(n_dp, n_t, shared, blocks, out, land, sums, land2, s1, r1, s2, r2):
    me, t = lax.axis_index("dp"), lax.axis_index("tensor")
    sem = pltpu.get_barrier_semaphore()
    for p in range(1, n_dp):
        pl.semaphore_signal(sem, device_id={"dp": lax.rem(me + p, n_dp)}, device_id_type=MESH)
    for p in range(1, n_t):
        pl.semaphore_signal(sem, device_id={"tensor": lax.rem(t + p, n_t)}, device_id_type=MESH)
    pl.semaphore_wait(sem, n_dp + n_t - 2)

    def one(p):
        other = lax.rem(me + p, n_dp)
        return pltpu.make_async_remote_copy(
            src_ref=blocks.at[other],
            dst_ref=land.at[p],
            send_sem=s1.at[p],
            recv_sem=r1.at[p],
            device_id={"dp": other},
            device_id_type=MESH,
        )

    for p in range(1, n_dp):
        one(p).start()
    total = blocks[me]
    for p in range(1, n_dp):
        one(p).wait_recv()
        total = total + land[p]
    sums[...] = total

    def two(p):
        return pltpu.make_async_remote_copy(
            src_ref=sums.at[pl.ds(0, shared)],
            dst_ref=land2.at[p],
            send_sem=s2.at[p],
            recv_sem=r2.at[p],
            device_id={"tensor": lax.rem(t + p, n_t)},
            device_id_type=MESH,
        )

    for p in range(1, n_t):
        two(p).start()
    out[...] = total
    top = sums[pl.ds(0, shared), :]
    for p in range(1, n_t):
        two(p).wait_recv()
        top = top + land2[p]
    out[pl.ds(0, shared), :] = top
    for p in range(1, n_dp):
        one(p).wait_send()
    for p in range(1, n_t):
        two(p).wait_send()


def reduce_small(blocks, shared, n_dp, n_t, cid):
    _, rows, width = blocks.shape
    return pl.pallas_call(
        functools.partial(reduce_small_kernel, n_dp, n_t, shared),
        out_shape=jax.ShapeDtypeStruct((rows, width), F32),
        in_specs=[WHOLE],
        out_specs=WHOLE,
        scratch_shapes=[
            pltpu.VMEM((n_dp, rows, width), F32),
            pltpu.VMEM((rows, width), F32),
            pltpu.VMEM((n_t, shared, width), F32),
            pltpu.SemaphoreType.DMA((n_dp,)),
            pltpu.SemaphoreType.DMA((n_dp,)),
            pltpu.SemaphoreType.DMA((n_t,)),
            pltpu.SemaphoreType.DMA((n_t,)),
        ],
        compiler_params=params(cid),
        name="reduce_small",
    )(blocks)


BLOCK = 256
NEG = -1e30
SCALE = HD**-0.5


def dot(a, b):
    return jnp.dot(a, b, preferred_element_type=F32)


def dot_t(a, b):
    return lax.dot_general(a, b, (((1,), (1,)), ((), ())), preferred_element_type=F32)


def masked_scores(q, k, keys, first, bar):
    scores = dot_t(k, q) * SCALE + bar
    key_pos = lax.broadcasted_iota(jnp.int32, (keys, BLOCK), 0)
    query_pos = first + lax.broadcasted_iota(jnp.int32, (keys, BLOCK), 1)
    return jnp.where(key_pos <= query_pos, scores, NEG)


def attend_kernel(q, k, v, bar, out, log_totals):
    value_cols = v[...].T
    for block in range(LEN // BLOCK):
        first, keys = block * BLOCK, (block + 1) * BLOCK
        scores = masked_scores(
            q[first : first + BLOCK, :], k[0:keys, :], keys, first, bar[0:keys, 0:1]
        )
        top = jnp.max(scores, axis=0, keepdims=True)
        powers = jnp.exp(scores - top)
        total = jnp.sum(powers, axis=0, keepdims=True)
        shares = (powers * (1.0 / total)).astype(BF16)
        mixed = dot(value_cols[:, 0:keys], shares)
        out[first : first + BLOCK, :] = mixed.T.astype(BF16)
        log_totals[0, :, first : first + BLOCK] = jnp.broadcast_to(top + jnp.log(total), (8, BLOCK))


def attend(qkv, bar, heads):
    def column(part):
        return pl.BlockSpec((LEN, HD), lambda h: (0, part * heads + h))

    return pl.pallas_call(
        attend_kernel,
        grid=(heads,),
        out_shape=(
            jax.ShapeDtypeStruct((LEN, heads * HD), BF16),
            jax.ShapeDtypeStruct((heads, 8, LEN), F32),
        ),
        in_specs=[column(0), column(1), column(2), pl.BlockSpec((LEN, 128), lambda h: (0, 0))],
        out_specs=(
            pl.BlockSpec((LEN, HD), lambda h: (0, h)),
            pl.BlockSpec((1, 8, LEN), lambda h: (h, 0, 0)),
        ),
        compiler_params=params(),
        name="attend",
    )(qkv, qkv, qkv, bar)


def attend_back_kernel(heads, q, k, v, go, bar, log_totals, out, sums, key_grad, value_grad):
    h = pl.program_id(0)
    key_cols = k[...].T
    query_sum = jnp.zeros((1, HD), F32)
    width = heads * HD
    at_q = pl.ds(pl.multiple_of(h * HD, HD), HD)
    at_k = pl.ds(pl.multiple_of(width + h * HD, HD), HD)
    at_v = pl.ds(pl.multiple_of(2 * width + h * HD, HD), HD)
    for block in range(LEN // BLOCK - 1, -1, -1):
        first, keys = block * BLOCK, (block + 1) * BLOCK
        here = slice(first, first + BLOCK)
        scores = masked_scores(q[here, :], k[0:keys, :], keys, first, bar[0:keys, 0:1])
        shares = jnp.exp(scores - log_totals[0, 0:1, here])
        share_grad = dot_t(v[0:keys, :], go[here, :])
        centre = jnp.sum(shares * share_grad, axis=0, keepdims=True)
        score_grad = (shares * (share_grad - centre)).astype(BF16)
        values = dot(shares.astype(BF16), go[here, :])
        keyed = dot(score_grad, q[here, :])
        if block == LEN // BLOCK - 1:
            value_grad[...] = values
            key_grad[...] = keyed
        else:
            value_grad[0:keys, :] += values
            key_grad[0:keys, :] += keyed
        query_grad = ((dot(key_cols[:, 0:keys], score_grad)) * SCALE).T.astype(BF16)
        out[here, at_q] = query_grad
        query_sum = query_sum + jnp.sum(query_grad.astype(F32), axis=0, keepdims=True)
    out[:, at_k] = (key_grad[...] * SCALE).astype(BF16)
    rounded = value_grad[...].astype(BF16)
    out[:, at_v] = rounded
    value_sum = jnp.sum(rounded.astype(F32), axis=0, keepdims=True)
    sums[0, 0:8, :] = jnp.broadcast_to(query_sum, (8, HD))
    sums[0, 8:16, :] = jnp.broadcast_to(value_sum, (8, HD))


def attend_back(qkv, go, bar, log_totals, heads):
    def column(part):
        return pl.BlockSpec((LEN, HD), lambda h: (0, part * heads + h))

    return pl.pallas_call(
        functools.partial(attend_back_kernel, heads),
        grid=(heads,),
        out_shape=(
            jax.ShapeDtypeStruct((LEN, 3 * heads * HD), BF16),
            jax.ShapeDtypeStruct((heads, 16, HD), F32),
        ),
        in_specs=[
            column(0), column(1), column(2), column(0),
            pl.BlockSpec((LEN, 128), lambda h: (0, 0)),
            pl.BlockSpec((1, 8, LEN), lambda h: (h, 0, 0)),
        ],
        out_specs=(
            pl.BlockSpec((LEN, 3 * heads * HD), lambda h: (0, 0)),
            pl.BlockSpec((1, 16, HD), lambda h: (h, 0, 0)),
        ),
        scratch_shapes=[pltpu.VMEM((LEN, HD), F32), pltpu.VMEM((LEN, HD), F32)],
        compiler_params=params(),
        name="attend_back",
    )(qkv, qkv, qkv, go, bar, log_totals)


def gelu_both(u):
    inner = 0.7978845608028654 * (u + 0.044715 * (u * u * u))
    th = jnp.tanh(inner)
    half = 0.5 * (1.0 + th)
    slope = half + 0.5 * u * (1.0 - th * th) * (
        0.7978845608028654 * (1.0 + 3 * 0.044715 * (u * u))
    )
    return u * half, slope


def hidden_kernel(n_dp, c, gm, up, down, bias, act_out, gu_out, sums):
    width = down.shape[2]
    rows = c.shape[0]
    step = min(256, rows)
    sums[...] = jnp.zeros_like(sums)

    def body(at):
        u = dot(c[at, :], up[...]) + bias[0:1, :]
        grad = dot_t(gm[at, 0:width], down[0])
        for d in range(1, n_dp):
            grad = grad + dot_t(gm[at, d * width : (d + 1) * width], down[d])
        act, slope = gelu_both(u)
        act_out[at, :] = act.astype(BF16)
        gu = (grad * slope).astype(BF16)
        gu_out[at, :] = gu
        sums[...] += fold(gu.astype(F32))

    row_loop(rows, step, body)


def hidden(c, gm, up, down, bias):
    rows, width = c.shape
    n_dp, units, part = down.shape
    block = min(512, units)
    return pl.pallas_call(
        functools.partial(hidden_kernel, n_dp),
        grid=(units // block,),
        out_shape=(
            jax.ShapeDtypeStruct((rows, units), BF16),
            jax.ShapeDtypeStruct((rows, units), BF16),
            jax.ShapeDtypeStruct((8, units), F32),
        ),
        in_specs=[
            pl.BlockSpec((rows, width), lambda i: (0, 0), pipeline_mode=pl.Buffered(1)),
            pl.BlockSpec((rows, width), lambda i: (0, 0), pipeline_mode=pl.Buffered(1)),
            pl.BlockSpec((width, block), lambda i: (0, i)),
            pl.BlockSpec((n_dp, block, part), lambda i: (0, i, 0)),
            pl.BlockSpec((8, block), lambda i: (0, i)),
        ],
        out_specs=(
            pl.BlockSpec((rows, block), lambda i: (0, i)),
            pl.BlockSpec((rows, block), lambda i: (0, i)),
            pl.BlockSpec((8, block), lambda i: (0, i)),
        ),
        compiler_params=params(),
        name="hidden",
    )(c, gm, up, down, bias)


def pad_to(x, count):
    return jnp.pad(x, ((0, 0), (0, count - x.shape[1])))


def shards(
    tokens, lengths, ln1_gain, ln1_bias, qkv_weight, qv_bias, out_weight, out_bias,
    ln2_gain, ln2_bias, up_weight, up_bias, down_weight, down_bias, cotangent,
):
    n_dp, n_t = lax.axis_size("dp"), lax.axis_size("tensor")
    rows, width = tokens.shape
    part = ln1_gain.shape[0]
    local = qkv_weight.shape[2]
    heads = local // HD
    units = up_weight.shape[1]
    hd_part = qv_bias.shape[2]
    t = lax.axis_index("tensor")
    length = lengths[0]

    pieces = [
        ln1_gain, ln1_bias, out_bias, ln2_gain, ln2_bias, down_bias,
        qv_bias.reshape(-1), up_bias.reshape(-1),
    ]
    packed = jnp.concatenate(pieces)
    count = packed.shape[0]
    lanes = -(-count // 2048) * 2048
    small = jnp.pad(packed, (0, lanes - count)).reshape(lanes // 128, 128)
    smalls = gather_small(small, n_dp, 0).reshape(n_dp, lanes)
    vecs = jnp.stack([smalls[:, i * part : (i + 1) * part].reshape(width) for i in range(6)])
    vecs = jnp.pad(vecs, ((0, 2), (0, 0))).astype(F32)
    at = 6 * part
    qv_all = smalls[:, at : at + 2 * heads * hd_part].reshape(n_dp, 2, heads, hd_part)
    qv_all = qv_all.transpose(1, 2, 0, 3).reshape(2, local).astype(F32)
    at += 2 * heads * hd_part
    up_all = smalls[:, at : at + units // n_dp].reshape(n_dp, units // 16, 16 // n_dp)
    up_shift = up_all.transpose(1, 0, 2).reshape(1, units).astype(F32)
    qkv_shift = jnp.concatenate([qv_all[0], jnp.zeros_like(qv_all[0]), qv_all[1]])

    qkv_full = lax.all_gather(qkv_weight, "dp", axis=0, tiled=True).reshape(width, 3 * local)
    out_full = lax.all_gather(out_weight, "dp", axis=1, tiled=True)
    up_full = lax.all_gather(up_weight, "dp", axis=0, tiled=True)
    down_blocks = lax.all_gather(down_weight, "dp", axis=0, tiled=False)

    own_pos = t * rows + jnp.arange(rows, dtype=jnp.int32)
    valid_own = (own_pos < length).astype(F32)
    valid = jnp.broadcast_to(valid_own[:, None], (rows, 128))
    positions = jnp.arange(LEN, dtype=jnp.int32)
    bar = jnp.broadcast_to(jnp.where(positions < length, 0.0, NEG)[:, None], (LEN, 128))
    gm_own = (cotangent.astype(F32) * valid_own[:, None]).astype(BF16)

    all_tokens = gather_rows(tokens, n_t, 1).reshape(n_t * rows, width)
    normed_one, _ = normal(all_tokens.astype(F32))
    a = (normed_one * vecs[0:1] + vecs[1:2]).astype(BF16)
    qkv = (dot(a, qkv_full) + qkv_shift).astype(BF16)
    attended, log_totals = attend(qkv, bar, heads)
    terms = dot(attended, out_full).astype(BF16).reshape(n_t, rows, width)
    c, gm, mid, stats_a = middle(terms, gm_own, tokens, valid, vecs, n_t, 2)
    c, gm = c.reshape(-1, width), gm.reshape(-1, width)
    act, gu, up_sums = hidden(
        c, gm, up_full, down_blocks, jnp.broadcast_to(up_shift, (8, units))
    )
    down_mat = down_blocks.transpose(1, 0, 2).reshape(units, width)

    def rows_dot(left, right):
        return lax.dot_general(
            left, right, (((0,), (0,)), ((), ())), preferred_element_type=F32
        ).astype(BF16)

    down_grad = rows_dot(act, gm)
    down_out = lax.psum_scatter(down_grad, "dp", scatter_dimension=1, tiled=True)
    up_grad = rows_dot(c, gu)
    up_out = lax.psum_scatter(up_grad, "dp", scatter_dimension=0, tiled=True)
    back_terms = dot_t(gu, up_full).astype(BF16).reshape(n_t, rows, width)
    mlp = dot(act, down_mat).astype(BF16).reshape(n_t, rows, width)
    gz, gmid, output, stats_b = back_middle(back_terms, mlp, gm_own, mid, valid, vecs, n_t, 3)
    gz = gz.reshape(-1, width)
    go = dot_t(gz, out_full).astype(BF16)
    out_grad = rows_dot(attended, gz)
    out_out = lax.psum_scatter(out_grad, "dp", scatter_dimension=1, tiled=True)
    gqkv, head_sums = attend_back(qkv, go, bar, log_totals, heads)
    qkv_grad = rows_dot(a, gqkv).reshape(width, 3, local)
    qkv_out = lax.psum_scatter(qkv_grad, "dp", scatter_dimension=0, tiled=True)
    last_terms = dot_t(gqkv, qkv_full).astype(BF16).reshape(n_t, rows, width)
    tokens_grad, stats_c = finish(last_terms, tokens, gmid, vecs, n_t, 4)

    def vec_sum(stats, i):
        return jnp.sum(stats[8 * i : 8 * i + 8], axis=0)

    vectors = jnp.stack(
        [
            vec_sum(stats_c, 0), vec_sum(stats_c, 1), vec_sum(stats_b, 2),
            vec_sum(stats_b, 0), vec_sum(stats_b, 1), vec_sum(stats_b, 3),
        ]
    )
    squares = jnp.stack(
        [
            jnp.sum(stats_a[0:8]), jnp.sum(stats_a[8:16]), jnp.sum(stats_a[16:24]),
            jnp.sum(stats_b[32:40]), jnp.sum(stats_b[40:48]), jnp.sum(valid_own),
        ]
    )
    vector_blocks = vectors.reshape(6, n_dp, part).transpose(1, 0, 2).reshape(n_dp, 6 * part)
    scalar_blocks = jnp.broadcast_to(squares[None], (n_dp, 6))
    top = jnp.concatenate([vector_blocks, scalar_blocks], axis=1)
    top_len = -(-top.shape[1] // 1024) * 1024
    up_blocks = jnp.sum(up_sums, axis=0).reshape(units // 16, n_dp, 16 // n_dp)
    up_blocks = up_blocks.transpose(1, 0, 2).reshape(n_dp, units // n_dp)
    qv_sums = jnp.stack([head_sums[:, 0], head_sums[:, 8]])
    qv_blocks = qv_sums.reshape(2, heads, n_dp, hd_part).transpose(2, 0, 1, 3)
    qv_blocks = qv_blocks.reshape(n_dp, 2 * heads * hd_part)
    low = jnp.concatenate([up_blocks, qv_blocks], axis=1)
    low_len = -(-low.shape[1] // 1024) * 1024
    blocks = jnp.concatenate([pad_to(top, top_len), pad_to(low, low_len)], axis=1)
    blocks = blocks.reshape(n_dp, (top_len + low_len) // 128, 128)
    reduced = reduce_small(blocks, top_len // 128, n_dp, n_t, 5).reshape(-1)
    outs = [reduced[i * part : (i + 1) * part] for i in range(6)]
    totals = reduced[6 * part : 6 * part + 6]
    stream_rms = jnp.sqrt(totals[:5] / (totals[5] * width))
    at = top_len
    up_bias_out = reduced[at : at + units // n_dp].reshape(up_bias.shape)
    at += units // n_dp
    qv_bias_out = reduced[at : at + 2 * heads * hd_part].reshape(qv_bias.shape)

    return (
        output, tokens_grad, outs[0], outs[1],
        qkv_out.astype(F32), qv_bias_out, out_out.astype(F32), outs[2],
        outs[3], outs[4], up_out.astype(F32), up_bias_out,
        down_out.astype(F32), outs[5], stream_rms,
    )


def solution(mesh):
    vector = P("dp")
    rows = P(("dp", "tensor"), None)
    return jax.shard_map(
        shards,
        mesh=mesh,
        in_specs=(
            rows, vector, vector, vector, P("dp", None, "tensor"), P(None, "tensor", "dp"),
            P("tensor", "dp"), vector, vector, vector, P("dp", "tensor"), P("tensor", "dp"),
            P("tensor", "dp"), vector, rows,
        ),
        out_specs=(
            rows, rows, vector, vector, P("dp", None, "tensor"), P(None, "tensor", "dp"),
            P("tensor", "dp"), vector, vector, vector, P("dp", "tensor"), P("tensor", "dp"),
            P("tensor", "dp"), vector, P(),
        ),
        check_vma=False,
    )
```

time: 1400 us -> 833 us (0.59)
  waiting for transfers between devices: 872 us -> 62.7 us
  Pallas kernels: 0 us -> 566 us
  blocking collectives: 148 us -> 0 us
  matrix products: 195 us -> 102 us
  other arithmetic: 108 us -> 29.7 us
    pallas_call x0 -> x9, Pallas kernels: none -> 566 us  [the longest x1 173 us: middle(): pl.pallas_call(functools.partial(middle_kernel, size), out_shape=(jax.Sha...]
    psum x3 -> x0, waiting for transfers between devices: 517 us -> none  [the longest x2 362 us: branch_total(): lax.psum(jnp.dot(source, weight, preferred_element_type=jnp.float32).asty...]
    all_gather x5 -> x3, waiting for transfers between devices: 209 us -> 0.04 us  [the longest x1 0.02 us: shards(): down_blocks = lax.all_gather(down_weight, 'dp', axis=0, tiled=False)]
    dot_general x26 -> x10, matrix products: 195 us -> 102 us  [the longest x4 45.8 us: rows_dot(): lax.dot_general(left, right, (((0,), (0,)), ((), ())), preferred_element_...]
    all_gather x8 -> x0, blocking collectives: 70.3 us -> none  [the longest x1 10.4 us: shards(): lax.all_gather(ln1_bias, 'dp', axis=0, tiled=True)]
    psum x2 -> x0, blocking collectives: 53.1 us -> none  [the longest x1 40.6 us: record(): recorded.append(lax.psum((square_sum, own_count), ('dp', 'tensor')))]
    reduce_sum x15 -> x7, other arithmetic: 51.8 us -> 7.28 us  [the longest x1 3.28 us: normal(): centre = x - jnp.mean(x, axis=-1, keepdims=True)]
    reduce_scatter x4, waiting for transfers between devices: 102 us -> 60.7 us  [the longest x1 60.7 us: shards(): lax.psum_scatter(down_grad, 'dp', scatter_dimension=1, tiled=True)]
  transfers between devices with their start and end apart: 14 -> 8, of which waited for: 10 -> 1; matrix products, arithmetic and copies ran while one was open for 17% -> 17% of each run, Pallas kernels for 0% -> 45%
where the time goes in v1:
time: 833 us; the launch traced here: 823 us
  Pallas kernels  566 us (68%)
  matrix products  102 us (12%)
  waiting for transfers between devices  62.7 us (8%)
  local copies, waits for them, and re-layouts  45.9 us (6%)
  other arithmetic  29.7 us (4%)
  between operations  16.5 us (2%)
    pallas_call x1, Pallas kernels, middle(): pl.pallas_call(functools.partial(middle_kernel, size), out_shape=(jax.Sha...  173 us
    pallas_call x1, Pallas kernels, back_middle(): pl.pallas_call(functools.partial(back_middle_kernel, size), out_shape=(ja...  171 us
    pallas_call x1, Pallas kernels, gather_rows(): pl.pallas_call(functools.partial(gather_rows_kernel, size), out_shape=jax...  76.1 us
    pallas_call x1, Pallas kernels, finish(): pl.pallas_call(functools.partial(finish_kernel, size), out_shape=(jax.Sha...  71.1 us
    reduce_scatter x1, waiting for transfers between devices, shards(): lax.psum_scatter(down_grad, 'dp', scatter_dimension=1, tiled=True)  60.7 us
    dot_general x4, matrix products, rows_dot(): lax.dot_general(left, right, (((0,), (0,)), ((), ())), preferred_element_...  45.8 us
    dot_general x3, matrix products, dot(): return jnp.dot(a, b, preferred_element_type=F32)  31.6 us
    pallas_call x1, Pallas kernels, hidden(): pl.pallas_call(functools.partial(hidden_kernel, n_dp), grid=(units // blo...  26.4 us
  transfers between devices with their start and end apart: 8, of which 1 were waited for; matrix products, arithmetic and copies ran while one was open for 17% of the time, Pallas kernels for 45%

profile of v1, /device:TPU:0, one launch (start us, length us, event | category | flops | bytes accessed | tf_op | source)
XLA Modules:
  0.0 823.2 jit_solution(9233257744096134224)
XLA Ops:
  7.2 2.3 copy.56
  9.6 0.7 all-gather.8.cloned.1.call-update
  11.7 76.1 %gather_tokens.1 = bf16[4,256,2048]{2,1,0:T(8,128)(2,1)} custom-call(bf16[256,2048]{1,0:T(8,128)(2,1)} %tok.3), custom_call_target="tpu_custom_call" | custom-call | tf_op jit(solution)/shard_map/gather_tokens/pallas_call | solution.py:260
  90.6 6.1 shard_map.262
  96.7 0.8 copy.82
  98.7 0.8 copy.60
  99.8 3.3 convert_reduce_fusion
  103.6 1.2 multiply_reduce_fusion
  105.0 1.2 multiply_convert_fusion.cot.gm
  106.2 4.6 add_convert_fusion
  110.9 11.3 %add_convert_fusion.1.q.k.v = bf16[1024,1536]{1,0:T(8,128)(2,1)} fusion(bf16[1024,2048]{1,0:T(8,128)(2,1)} %bitcast.132, bf16[2048,1536]{0,1:T(8,128)(2,1)} %bitcast.164, f32[1536]{0:T(1024)S(1)} %pad_maximum_fusion.1), kind=kOutput, calls=%fused_computation.11 | convolution fusion | flops 6445596672 | bytes 13637632 | tf_op jit(solution)/shard_map/dot_general | solution.py:505
  122.2 1.0 broadcast_in_dim.21.bar
  123.2 11.2 %attend.1 = (bf16[1024,512]{1,0:T(8,128)(2,1)}, f32[4,8,1024]{2,1,0:T(8,128)}) custom-call(bf16[1024,1536]{1,0:T(8,128)(2,1)} %add_convert_fusion.1.q.k.v, bf16[1024,1536]{1,0:T(8,128)(2,1)} %add_convert_fusion.1.q.k.v, bf16[1024,1536]{1,0:T(8,128)(2,1)} %add_convert_fusion.1.q.k.v, f32[1024,128]{1,0:T(8,128)} %broadcast_in_dim.21.bar), custom_call_target="tpu_custom_call" | custom-call | tf_op jit(solution)/shard_map/attend/pallas_call | solution.py:539
  134.4 6.3 convolution_convert_fusion.6
  140.7 0.8 broadcast_in_dim.22.valid
  141.5 172.8 %middle.1 = (bf16[4,256,2048]{2,1,0:T(8,128)(2,1)}, bf16[4,256,2048]{2,1,0:T(8,128)(2,1)}, f32[256,2048]{1,0:T(8,128)}, f32[24,2048]{1,0:T(8,128)}) custom-call(bf16[4,256,2048]{2,1,0:T(8,128)(2,1)} %bitcast.134, bf16[256,2048]{1,0:T(8,128)(2,1)} %multiply_convert_fusion.cot.gm, bf16[256,2048]{1,0:T(8,128)(2,1)} %tok.3, f32[256,128]{1,0:T(8,128)} %broadcast_in_dim.22.valid, ...), custom_call_target="tpu_custom_call" | custom-call | tf_op jit(solution)/shard_map/middle/pallas_call | solution.py:306
  314.3 11.5 %copy.61 = bf16[2048,8,256]{0,2,1:T(8,128)(2,1)} copy(bf16[2048,8,256]{2,0,1:T(8,128)(2,1)} %bitcast.128) | data formatting | bytes 16777216 | tf_op jit(solution)/shard_map/transpose | solution.py:736
  326.4 26.4 %hidden.1 = (bf16[1024,2048]{1,0:T(8,128)(2,1)}, bf16[1024,2048]{1,0:T(8,128)(2,1)}, f32[8,2048]{1,0:T(8,128)}) custom-call(bf16[1024,2048]{1,0:T(8,128)(2,1)} %bitcast.137, bf16[1024,2048]{1,0:T(8,128)(2,1)} %bitcast.135, bf16[2048,2048]{1,0:T(8,128)(2,1)} %all-gather.10.cloned.1.call-done.up, bf16[8,2048,256]{2,1,0:T(8,128)(2,1)} %bitcast.129, ...), custom_call_target="tpu_custom_call" | custom-call | tf_op jit(solution)/shard_map/hidden/pallas_call | solution.py:651
  352.9 14.0 %convolution_convert_fusion.4 = bf16[1024,2048]{1,0:T(8,128)(2,1)} fusion(bf16[1024,2048]{1,0:T(8,128)(2,1)} %get-tuple-element.36, bf16[2048,2048]{0,1:T(8,128)(2,1)} %bitcast.130), kind=kOutput, calls=%fused_computation.13 | convolution fusion | flops 8592031744 | bytes 16777216 | tf_op jit(solution)/shard_map/dot_general | solution.py:505
  366.9 10.5 %convolution_convert_fusion.5 = bf16[1024,2048]{1,0:T(8,128)(2,1)} fusion(bf16[1024,2048]{1,0:T(8,128)(2,1)S(1)} %copy-done.17, bf16[2048,2048]{1,0:T(8,128)(2,1)S(1)} %copy-done.1), kind=kOutput, calls=%fused_computation.14 | convolution fusion | flops 8592031744 | bytes 16777216 | tf_op jit(solution)/shard_map/dot_general | solution.py:509
  377.4 171.2 %back_middle.1 = (bf16[4,256,2048]{2,1,0:T(8,128)(2,1)}, f32[256,2048]{1,0:T(8,128)}, bf16[256,2048]{1,0:T(8,128)(2,1)}, f32[48,2048]{1,0:T(8,128)}) custom-call(bf16[4,256,2048]{2,1,0:T(8,128)(2,1)} %bitcast.140, bf16[4,256,2048]{2,1,0:T(8,128)(2,1)} %bitcast.139, bf16[256,2048]{1,0:T(8,128)(2,1)} %multiply_convert_fusion.cot.gm, ...), custom_call_target="tpu_custom_call" | custom-call | tf_op jit(solution)/shard_map/back_middle/pallas_call | solution.py:370
  548.5 5.9 convolution_convert_fusion.7
  554.5 4.9 fusion.3
  559.9 3.3 convolution_convert_fusion.8.go
  563.2 14.4 %attend_back.1 = (bf16[1024,1536]{1,0:T(8,128)(2,1)}, f32[4,16,128]{2,1,0:T(8,128)}) custom-call(bf16[1024,1536]{1,0:T(8,128)(2,1)} %add_convert_fusion.1.q.k.v, bf16[1024,1536]{1,0:T(8,128)(2,1)} %add_convert_fusion.1.q.k.v, bf16[1024,1536]{1,0:T(8,128)(2,1)} %add_convert_fusion.1.q.k.v, bf16[1024,512]{1,0:T(8,128)(2,1)} %convolution_convert_fusion.8.go, ...), custom_call_target="tpu_custom_call" | custom-call | tf_op jit(solution)/shard_map/attend_back/pallas_call | solution.py:595
  577.6 11.4 %convolution_convert_fusion.2 = bf16[2048,1536]{0,1:T(8,128)(2,1)} fusion(bf16[1024,2048]{1,0:T(8,128)(2,1)} %fusion.3, bf16[1024,1536]{1,0:T(8,128)(2,1)} %get-tuple-element.41), kind=kOutput, calls=%fused_computation.10 | convolution fusion | flops 6445596672 | bytes 13631488 | tf_op jit(solution)/shard_map/dot_general | solution.py:739
  588.9 8.7 %copy.65 = bf16[2048,3,512]{2,0,1:T(8,128)(2,1)} copy(bf16[2048,3,512]{0,2,1:T(8,128)(2,1)} %bitcast.131) | data formatting | bytes 12582912 | tf_op jit(solution)/shard_map/reshape | solution.py:755
  597.7 14.3 %convolution_convert_fusion.1 = bf16[2048,2048]{1,0:T(8,128)(2,1)} fusion(bf16[1024,2048]{1,0:T(8,128)(2,1)} %bitcast.138, bf16[1024,2048]{1,0:T(8,128)(2,1)} %get-tuple-element.35), kind=kOutput, calls=%fused_computation.9 | convolution fusion | flops 8594128896 | bytes 16777216 | tf_op jit(solution)/shard_map/dot_general | solution.py:739
  612.0 14.3 %convolution_convert_fusion = bf16[2048,2048]{1,0:T(8,128)(2,1)} fusion(bf16[1024,2048]{1,0:T(8,128)(2,1)} %get-tuple-element.36, bf16[1024,2048]{1,0:T(8,128)(2,1)} %bitcast.136), kind=kOutput, calls=%fused_computation.8 | convolution fusion | flops 8594128896 | bytes 16777216 | tf_op jit(solution)/shard_map/dot_general | solution.py:739
  628.3 11.1 %convolution_convert_fusion.3 = bf16[1024,2048]{1,0:T(8,128)(2,1)} fusion(bf16[1024,1536]{1,0:T(8,128)(2,1)S(1)} %copy-done.19, bf16[2048,1536]{0,1:T(8,128)(2,1)} %bitcast.165), kind=kOutput, calls=%fused_computation.12 | convolution fusion | flops 6444548096 | bytes 13631488 | tf_op jit(solution)/shard_map/dot_general | solution.py:509
  639.4 71.1 %finish.1 = (f32[256,2048]{1,0:T(8,128)}, f32[16,2048]{1,0:T(8,128)}) custom-call(bf16[4,256,2048]{2,1,0:T(8,128)(2,1)} %bitcast.133, bf16[256,2048]{1,0:T(8,128)(2,1)} %tok.3, f32[256,2048]{1,0:T(8,128)} %get-tuple-element.42.gmid, f32[8,2048]{1,0:T(8,128)} %copy-done.3), custom_call_target="tpu_custom_call" | custom-call | tf_op jit(solution)/shard_map/finish/pallas_call | solution.py:412
  710.5 0.9 slice_reduce_fusion.9
  712.1 0.8 slice_reduce_fusion.12
  713.6 0.8 copy.62
  714.6 4.0 stack.66
  719.3 16.5 %reduce_small.1 = f32[24,128]{1,0:T(8,128)} custom-call(f32[8,24,128]{2,1,0:T(8,128)} %bitcast.144), custom_call_target="tpu_custom_call" | custom-call | tf_op jit(solution)/shard_map/reduce_small/pallas_call | solution.py:480
  735.8 0.7 slice_reduce_fusion.13
  736.5 0.7 reshape.236
  737.2 1.4 slice_bitcast_fusion.6
  739.4 1.3 slice.184
  741.3 1.2 fusion.6
  742.5 1.8 convert_element_type.138
  744.3 2.8 convert_element_type.136
  747.1 3.2 convert_element_type.140
  750.3 60.7 %reduce-scatter.11.cloned.1.call-done = bf16[2048,256]{1,0:T(8,128)(2,1)} async-done(((bf16[2048,2048]{1,0:T(8,128)(2,1)}), bf16[2048,256]{1,0:T(8,128)(2,1)}) %reduce-scatter.11.cloned.1.call-update) | async-done | bytes 1048592 | tf_op jit(solution)/shard_map/reduce_scatter | solution.py:744
  810.9 2.7 convert_element_type.142
  813.6 1.0 copy.99
  814.6 1.3 copy.100
  (137 shorter events, 11.8 us)
Async XLA Ops:
  7.2 103.7 %all-gather.6.cloned.1.call-start = ((), (), s32[]{:S(2)}) async-start(), calls=%async_computation.4 | async-start | bytes 7077888 | tf_op jit(solution)/shard_map/all_gather | solution.py:713
  9.5 78.4 %copy-start.9 = (bf16[2,4,16]{2,1,0:T(4,128)(2,1)S(1)}, bf16[2,4,16]{2,1,0:T(4,128)(2,1)}, u32[]{:S(2)}) copy-start(bf16[2,4,16]{2,1,0:T(4,128)(2,1)} %param.20) | copy-start | bytes 772
  9.5 78.5 %copy-start.10 = (bf16[128,2]{0,1:T(2,128)(2,1)S(1)}, bf16[128,2]{0,1:T(2,128)(2,1)}, u32[]{:S(2)}) copy-start(bf16[128,2]{0,1:T(2,128)(2,1)} %param.26) | copy-start | bytes 1540
  9.5 78.8 %copy-start.11 = (bf16[256]{0:T(256)(128)(2,1)S(1)}, bf16[256]{0:T(256)(128)(2,1)}, u32[]{:S(2)}) copy-start(bf16[256]{0:T(256)(128)(2,1)} %param.17) | copy-start | bytes 1540
  9.5 79.0 %copy-start.12 = (bf16[256]{0:T(256)(128)(2,1)S(1)}, bf16[256]{0:T(256)(128)(2,1)}, u32[]{:S(2)}) copy-start(bf16[256]{0:T(256)(128)(2,1)} %param.18) | copy-start | bytes 1540
  9.5 79.2 %copy-start.13 = (bf16[256]{0:T(256)(128)(2,1)S(1)}, bf16[256]{0:T(256)(128)(2,1)}, u32[]{:S(2)}) copy-start(bf16[256]{0:T(256)(128)(2,1)} %param.22) | copy-start | bytes 1540
  9.5 79.4 %copy-start.14 = (bf16[256]{0:T(256)(128)(2,1)S(1)}, bf16[256]{0:T(256)(128)(2,1)}, u32[]{:S(2)}) copy-start(bf16[256]{0:T(256)(128)(2,1)} %param.23) | copy-start | bytes 1540
  9.5 79.6 %copy-start.15 = (bf16[256]{0:T(256)(128)(2,1)S(1)}, bf16[256]{0:T(256)(128)(2,1)}, u32[]{:S(2)}) copy-start(bf16[256]{0:T(256)(128)(2,1)} %param.24) | copy-start | bytes 1540
  9.6 79.8 %copy-start.16 = (bf16[256]{0:T(256)(128)(2,1)S(1)}, bf16[256]{0:T(256)(128)(2,1)}, u32[]{:S(2)}) copy-start(bf16[256]{0:T(256)(128)(2,1)} %param.28) | copy-start | bytes 1540
  9.6 124.8 %all-gather.8.cloned.1.call-start = ((), (), s32[]{:S(2)}) async-start(), calls=%async_computation.5 | async-start | bytes 2359296 | tf_op jit(solution)/shard_map/all_gather | solution.py:714
  10.3 303.9 %all-gather.12.cloned.1.call-start = ((), (), s32[]{:S(2)}) async-start(), calls=%async_computation.11 | async-start | bytes 9437184 | tf_op jit(solution)/shard_map/all_gather | solution.py:716
  11.1 314.7 %all-gather.10.cloned.1.call-start = ((), (), s32[]{:S(2)}) async-start(), calls=%async_computation.6 | async-start | bytes 9437184 | tf_op jit(solution)/shard_map/all_gather | solution.py:715
  11.7 730.8 %reduce-scatter.7.cloned.1.call-start = ((), (), s32[]{:S(2)}) async-start(), calls=%async_computation.8 | async-start | bytes 2359296 | tf_op jit(solution)/shard_map/reduce_scatter | solution.py:753
  99.8 3.8 copy-start
  99.8 5.3 copy-start.5
  105.0 5.9 copy-start.3
  352.8 14.0 %copy-start.1 = (bf16[2048,2048]{1,0:T(8,128)(2,1)S(1)}, bf16[2048,2048]{1,0:T(8,128)(2,1)}, u32[]{:S(2)}) copy-start(bf16[2048,2048]{1,0:T(8,128)(2,1)} %all-gather.10.cloned.1.call-done.up) | copy-start | bytes 25165828
  352.9 14.0 %copy-start.17 = (bf16[1024,2048]{1,0:T(8,128)(2,1)S(1)}, bf16[1024,2048]{1,0:T(8,128)(2,1)}, u32[]{:S(2)}) copy-start(bf16[1024,2048]{1,0:T(8,128)(2,1)} %get-tuple-element.35) | copy-start | bytes 12582916
  377.4 171.2 %copy-start.21 = (bf16[1024,512]{1,0:T(8,128)(2,1)S(1)}, bf16[1024,512]{1,0:T(8,128)(2,1)}, u32[]{:S(2)}) copy-start(bf16[1024,512]{1,0:T(8,128)(2,1)} %get-tuple-element.32) | copy-start | bytes 3145732
  554.4 189.9 %reduce-scatter.5.cloned.1.call-start = ((), (), s32[]{:S(2)}) async-start(), calls=%async_computation.7 | async-start | bytes 7077888 | tf_op jit(solution)/shard_map/reduce_scatter | solution.py:756
  554.5 4.9 copy-start.18
  554.5 5.4 copy-start.20
  597.6 149.5 %reduce-scatter.9.cloned.1.call-start = ((), (), s32[]{:S(2)}) async-start(), calls=%async_computation.9 | async-start | bytes 9437184 | tf_op jit(solution)/shard_map/reduce_scatter | solution.py:746
  612.0 199.0 %reduce-scatter.11.cloned.1.call-start = ((), (), s32[]{:S(2)}) async-start(), calls=%async_computation.10 | async-start | bytes 9437184 | tf_op jit(solution)/shard_map/reduce_scatter | solution.py:744
  626.3 0.9 copy-start.7
  626.3 2.0 copy-start.19
  639.4 72.1 %copy-start.6 = (f32[48,2048]{1,0:T(8,128)S(1)}, f32[48,2048]{1,0:T(8,128)}, u32[]{:S(2)}) copy-start(f32[48,2048]{1,0:T(8,128)} %get-tuple-element.45) | copy-start | bytes 1179652
  639.4 73.8 %copy-start.8 = (f32[8,2048]{1,0:T(8,128)S(1)}, f32[8,2048]{1,0:T(8,128)}, u32[]{:S(2)}) copy-start(f32[8,2048]{1,0:T(8,128)} %get-tuple-element.47) | copy-start | bytes 196612
  744.3 69.4 %copy-start.4 = (bf16[256,2048]{1,0:T(8,128)(2,1)S(1)}, bf16[256,2048]{1,0:T(8,128)(2,1)}, u32[]{:S(2)}) copy-start(bf16[256,2048]{1,0:T(8,128)(2,1)} %get-tuple-element.159) | copy-start | bytes 3145732
  747.1 67.5 %copy-start.2 = (f32[256,2048]{1,0:T(8,128)S(1)}, f32[256,2048]{1,0:T(8,128)}, u32[]{:S(2)}) copy-start(f32[256,2048]{1,0:T(8,128)} %get-tuple-element.160) | copy-start | bytes 6291460
Sparse Core Ops, SparseCore 0:
  10.4 49.2 all-gather.5
  61.6 28.1 all-gather.7
  91.7 54.2 all-gather.11
  147.8 54.2 all-gather.9
  554.5 40.5 reduce-scatter.6
  598.4 61.6 reduce-scatter.4
  663.6 72.5 reduce-scatter.8
  739.6 71.2 reduce-scatter.10

commit v2 on v1

--- a/solution.py
+++ b/solution.py
@@ -25,7 +25,9 @@
 
     def barrier(self):
         sem = pltpu.get_barrier_semaphore()
-
+        pl.semaphore_wait(sem, self.greet(sem))
+
+    def greet(self, sem):
         @pl.when(self.t > 0)
         def _():
             pl.semaphore_signal(sem, device_id={"tensor": self.t - 1}, device_id_type=MESH)
@@ -34,8 +36,7 @@
         def _():
             pl.semaphore_signal(sem, device_id={"tensor": self.t + 1}, device_id_type=MESH)
 
-        more = jnp.where(self.t > 0, 1, 0) + jnp.where(self.t < self.size - 1, 1, 0)
-        pl.semaphore_wait(sem, more)
+        return jnp.where(self.t > 0, 1, 0) + jnp.where(self.t < self.size - 1, 1, 0)
 
     def _copy(self, src, dst, sems, way, shard, part):
         send, recv = sems
@@ -201,71 +202,90 @@
     )
 
 
-def gather_small_kernel(n_dp, small, out, send, recv):
+def first_kernel(n_dp, size, part, small, own, smalls, a_out, tok, send, recv, gs, gr):
+    line = Line(size, own.shape[0])
     me = lax.axis_index("dp")
+    rows, width = own.shape
     sem = pltpu.get_barrier_semaphore()
     for p in range(1, n_dp):
-        pl.semaphore_signal(
-            sem, device_id={"dp": lax.rem(me + p, n_dp)}, device_id_type=MESH
-        )
-    pl.semaphore_wait(sem, n_dp - 1)
-    for p in range(1, n_dp):
-        pltpu.make_async_remote_copy(
+        pl.semaphore_signal(sem, device_id={"dp": lax.rem(me + p, n_dp)}, device_id_type=MESH)
+    ends = line.greet(sem)
+    pl.semaphore_wait(sem, ends + n_dp - 1)
+    sems = (gs, gr)
+
+    def small_copy(p, slot):
+        return pltpu.make_async_remote_copy(
             src_ref=small,
-            dst_ref=out.at[me],
+            dst_ref=smalls.at[slot],
             send_sem=send.at[p],
-            recv_sem=recv.at[me],
+            recv_sem=recv.at[slot],
             device_id={"dp": lax.rem(me + p, n_dp)},
             device_id_type=MESH,
-        ).start()
-    out[pl.ds(me, 1)] = small[...][None]
+        )
+
     for p in range(1, n_dp):
-        source = lax.rem(me + p, n_dp)
-        done = pltpu.make_async_remote_copy(
-            src_ref=small,
-            dst_ref=out.at[source],
-            send_sem=send.at[p],
-            recv_sem=recv.at[source],
-            device_id={"dp": source},
-            device_id_type=MESH,
-        )
-        done.wait_recv()
-        done.wait_send()
-
-
-def gather_small(small, n_dp, cid):
-    return pl.pallas_call(
-        functools.partial(gather_small_kernel, n_dp),
-        out_shape=jax.ShapeDtypeStruct((n_dp,) + small.shape, small.dtype),
-        in_specs=[WHOLE],
-        out_specs=WHOLE,
-        scratch_shapes=[pltpu.SemaphoreType.DMA((n_dp,)), pltpu.SemaphoreType.DMA((n_dp,))],
-        compiler_params=params(cid),
-    )(small)
-
-
-def gather_rows_kernel(size, own, out, send, recv):
-    line = Line(size, own.shape[0])
-    line.barrier()
-    sems = (send, recv)
-    line.phase(
-        gather=(out, sems, own),
-    )
-    out[pl.ds(line.t, 1)] = own[...][None]
-    line.drain_gather(out, sems)
-
-
-def gather_rows(own, size, cid):
+        small_copy(p, me).start()
+    smalls[pl.ds(me, 1)] = small[...][None]
+    step = min(32, rows)
+    vec_rows = part // 128
+
+    def normalise(source, shard):
+        gain = jnp.concatenate(
+            [smalls[d, r : r + 1, :] for d in range(n_dp) for r in range(vec_rows)], axis=1
+        ).astype(F32)
+        shift = jnp.concatenate(
+            [smalls[d, r : r + 1, :] for d in range(n_dp) for r in range(vec_rows, 2 * vec_rows)],
+            axis=1,
+        ).astype(F32)
+
+        def body(at):
+            x = source[at, :] if shard is None else source[shard, at, :]
+            normed, _ = normal(x.astype(F32))
+            to = line.t if shard is None else shard
+            a_out[to, at, :] = (normed * gain + shift).astype(BF16)
+
+        row_loop(rows, step, body)
+
+    def on_slot(k):
+        if k == 0:
+            for p in range(1, n_dp):
+                small_copy(p, lax.rem(me + p, n_dp)).wait_recv()
+            normalise(own, None)
+        else:
+
+            @pl.when(line.t >= k)
+            def _():
+                normalise(tok, line.t - k)
+
+            @pl.when(line.t + k <= size - 1)
+            def _():
+                normalise(tok, line.t + k)
+
+    line.phase(gather=(tok, sems, own), on_slot=on_slot)
+    line.drain_gather(tok, sems)
+    for p in range(1, n_dp):
+        small_copy(p, me).wait_send()
+
+
+def first(small, own, part, n_dp, size, cid):
     rows, width = own.shape
     return pl.pallas_call(
-        functools.partial(gather_rows_kernel, size),
-        out_shape=jax.ShapeDtypeStruct((size, rows, width), own.dtype),
-        in_specs=[WHOLE],
-        out_specs=WHOLE,
-        scratch_shapes=line_sems(size),
+        functools.partial(first_kernel, n_dp, size, part),
+        out_shape=(
+            jax.ShapeDtypeStruct((n_dp,) + small.shape, small.dtype),
+            jax.ShapeDtypeStruct((size, rows, width), BF16),
+        ),
+        in_specs=[WHOLE, WHOLE],
+        out_specs=(WHOLE, WHOLE),
+        scratch_shapes=[
+            pltpu.VMEM((size, rows, width), BF16),
+            pltpu.SemaphoreType.DMA((n_dp,)),
+            pltpu.SemaphoreType.DMA((n_dp,)),
+        ]
+        + line_sems(size),
         compiler_params=params(cid),
-        name="gather_tokens",
-    )(own)
+        name="first",
+    )(small, own)
 
 
 def middle_kernel(
@@ -673,6 +693,27 @@
     )(c, gm, up, down, bias)
 
 
+def project_kernel(act, down, out):
+    out[...] = dot(act[...], down[0]).astype(BF16)
+
+
+def project(act, down):
+    rows, units = act.shape
+    n_dp, _, part = down.shape
+    return pl.pallas_call(
+        project_kernel,
+        grid=(n_dp,),
+        out_shape=jax.ShapeDtypeStruct((rows, n_dp * part), BF16),
+        in_specs=[
+            pl.BlockSpec((rows, units), lambda i: (0, 0), pipeline_mode=pl.Buffered(1)),
+            pl.BlockSpec((1, units, part), lambda i: (i, 0, 0)),
+        ],
+        out_specs=pl.BlockSpec((rows, part), lambda i: (0, i)),
+        compiler_params=params(),
+        name="project",
+    )(act, down)
+
+
 def pad_to(x, count):
     return jnp.pad(x, ((0, 0), (0, count - x.shape[1])))
 
@@ -699,7 +740,8 @@
     count = packed.shape[0]
     lanes = -(-count // 2048) * 2048
     small = jnp.pad(packed, (0, lanes - count)).reshape(lanes // 128, 128)
-    smalls = gather_small(small, n_dp, 0).reshape(n_dp, lanes)
+    smalls, a = first(small, tokens, part, n_dp, n_t, 0)
+    smalls, a = smalls.reshape(n_dp, lanes), a.reshape(n_t * rows, width)
     vecs = jnp.stack([smalls[:, i * part : (i + 1) * part].reshape(width) for i in range(6)])
     vecs = jnp.pad(vecs, ((0, 2), (0, 0))).astype(F32)
     at = 6 * part
@@ -722,9 +764,6 @@
     bar = jnp.broadcast_to(jnp.where(positions < length, 0.0, NEG)[:, None], (LEN, 128))
     gm_own = (cotangent.astype(F32) * valid_own[:, None]).astype(BF16)
 
-    all_tokens = gather_rows(tokens, n_t, 1).reshape(n_t * rows, width)
-    normed_one, _ = normal(all_tokens.astype(F32))
-    a = (normed_one * vecs[0:1] + vecs[1:2]).astype(BF16)
     qkv = (dot(a, qkv_full) + qkv_shift).astype(BF16)
     attended, log_totals = attend(qkv, bar, heads)
     terms = dot(attended, out_full).astype(BF16).reshape(n_t, rows, width)
@@ -733,7 +772,6 @@
     act, gu, up_sums = hidden(
         c, gm, up_full, down_blocks, jnp.broadcast_to(up_shift, (8, units))
     )
-    down_mat = down_blocks.transpose(1, 0, 2).reshape(units, width)
 
     def rows_dot(left, right):
         return lax.dot_general(
@@ -741,12 +779,16 @@
         ).astype(BF16)
 
     down_grad = rows_dot(act, gm)
+    up_grad = rows_dot(c, gu)
+    back_terms = dot_t(gu, up_full).astype(BF16).reshape(n_t, rows, width)
+    mlp = project(act, down_blocks).reshape(n_t, rows, width)
+    back_terms, mlp, down_grad, up_grad = lax.optimization_barrier(
+        (back_terms, mlp, down_grad, up_grad)
+    )
     down_out = lax.psum_scatter(down_grad, "dp", scatter_dimension=1, tiled=True)
-    up_grad = rows_dot(c, gu)
     up_out = lax.psum_scatter(up_grad, "dp", scatter_dimension=0, tiled=True)
-    back_terms = dot_t(gu, up_full).astype(BF16).reshape(n_t, rows, width)
-    mlp = dot(act, down_mat).astype(BF16).reshape(n_t, rows, width)
     gz, gmid, output, stats_b = back_middle(back_terms, mlp, gm_own, mid, valid, vecs, n_t, 3)
+    gz, down_out, up_out = lax.optimization_barrier((gz, down_out, up_out))
     gz = gz.reshape(-1, width)
     go = dot_t(gz, out_full).astype(BF16)
     out_grad = rows_dot(attended, gz)

time: 833 us -> 746 us (0.90)
  waiting for transfers between devices: 62.7 us -> 2.57 us
  other arithmetic: 29.7 us -> 13.2 us
  local copies, waits for them, and re-layouts: 45.9 us -> 34.2 us
  Pallas kernels: 566 us -> 575 us
    reduce_scatter x1, waiting for transfers between devices: 60.7 us -> 0.02 us  [shards(): lax.psum_scatter(down_grad, 'dp', scatter_dimension=1, tiled=True)]
    dot_general x3 -> x2, matrix products: 31.6 us -> 18 us  [dot(): return jnp.dot(a, b, preferred_element_type=F32)]
    transpose x1 -> x0, local copies, waits for them, and re-layouts: 11.5 us -> none  [shards(): down_mat = down_blocks.transpose(1, 0, 2).reshape(units, width)]
    pallas_call x2, Pallas kernels: 82.3 us -> 93.4 us  [the longest x1 79.5 us: first(): pl.pallas_call(functools.partial(first_kernel, n_dp, size, part), out_sha...]
    convert_element_type x2 -> x0, other arithmetic: 9.47 us -> none  [shards(): a = (normed_one * vecs[0:1] + vecs[1:2]).astype(BF16)]
  transfers between devices with their start and end apart: 8 -> 8, of which waited for: 1 -> 0; matrix products, arithmetic and copies ran while one was open for 17% -> 11% of each run, Pallas kernels for 45% -> 73%
where the time goes in v2:
time: 746 us; the launch traced here: 736 us
  Pallas kernels  575 us (77%)
  matrix products  94.9 us (13%)
  local copies, waits for them, and re-layouts  34.2 us (5%)
  between operations  16.1 us (2%)
  other arithmetic  13.2 us (2%)
    pallas_call x1, Pallas kernels, middle(): pl.pallas_call(functools.partial(middle_kernel, size), out_shape=(jax.Sha...  172 us
    pallas_call x1, Pallas kernels, back_middle(): pl.pallas_call(functools.partial(back_middle_kernel, size), out_shape=(ja...  169 us
    pallas_call x1, Pallas kernels, first(): pl.pallas_call(functools.partial(first_kernel, n_dp, size, part), out_sha...  79.5 us
    pallas_call x1, Pallas kernels, finish(): pl.pallas_call(functools.partial(finish_kernel, size), out_shape=(jax.Sha...  73.5 us
    dot_general x4, matrix products, rows_dot(): lax.dot_general(left, right, (((0,), (0,)), ((), ())), preferred_element_...  45.4 us
    dot_general x3, matrix products, dot_t(): lax.dot_general(a, b, (((1,), (1,)), ((), ())), preferred_element_type=F32)  31.5 us
    pallas_call x1, Pallas kernels, hidden(): pl.pallas_call(functools.partial(hidden_kernel, n_dp), grid=(units // blo...  26.3 us
    dot_general x2, matrix products, dot(): return jnp.dot(a, b, preferred_element_type=F32)  18 us
  transfers between devices with their start and end apart: 8, of which 0 were waited for; matrix products, arithmetic and copies ran while one was open for 11% of the time, Pallas kernels for 73%

profile of v2, /device:TPU:0, one launch (start us, length us, event | category | flops | bytes accessed | tf_op | source)
XLA Modules:
  0.0 736.4 jit_solution(1928731919563035882)
XLA Ops:
  7.3 2.4 copy.54
  9.8 0.7 all-gather.8.cloned.1.call-update
  10.5 0.7 all-gather.10.cloned.1.call-update
  15.2 79.5 %first.1 = (bf16[8,16,128]{2,1,0:T(8,128)(2,1)}, bf16[4,256,2048]{2,1,0:T(8,128)(2,1)}) custom-call(bf16[16,128]{1,0:T(8,128)(2,1)} %pad_bitcast_fusion.small, bf16[256,2048]{1,0:T(8,128)(2,1)} %tok.3), custom_call_target="tpu_custom_call" | custom-call | tf_op jit(solution)/shard_map/first/pallas_call | solution.py:272
  94.7 0.8 copy.77
  96.0 0.8 copy.58
  97.2 0.6 pad_convert_fusion.vecs
  97.8 1.2 multiply_convert_fusion.cot.gm
  99.0 11.8 %add_convert_fusion.q.k.v = bf16[1024,1536]{1,0:T(8,128)(2,1)} fusion(bf16[1024,2048]{1,0:T(8,128)(2,1)} %bitcast.135, bf16[2048,1536]{0,1:T(8,128)(2,1)} %bitcast.133, f32[1536]{0:T(1024)S(1)} %pad_maximum_fusion.1), kind=kOutput, calls=%fused_computation.3 | convolution fusion | flops 6445596672 | bytes 13637632 | tf_op jit(solution)/shard_map/dot_general | solution.py:525
  110.8 1.0 broadcast_in_dim.21.bar
  111.8 10.9 %attend.1 = (bf16[1024,512]{1,0:T(8,128)(2,1)}, f32[4,8,1024]{2,1,0:T(8,128)}) custom-call(bf16[1024,1536]{1,0:T(8,128)(2,1)} %add_convert_fusion.q.k.v, bf16[1024,1536]{1,0:T(8,128)(2,1)} %add_convert_fusion.q.k.v, bf16[1024,1536]{1,0:T(8,128)(2,1)} %add_convert_fusion.q.k.v, f32[1024,128]{1,0:T(8,128)} %broadcast_in_dim.21.bar), custom_call_target="tpu_custom_call" | custom-call | tf_op jit(solution)/shard_map/attend/pallas_call | solution.py:559
  122.7 6.2 convolution_convert_fusion.5
  129.0 0.8 broadcast_in_dim.40.valid
  129.7 171.6 %middle.1 = (bf16[4,256,2048]{2,1,0:T(8,128)(2,1)}, bf16[4,256,2048]{2,1,0:T(8,128)(2,1)}, f32[256,2048]{1,0:T(8,128)}, f32[24,2048]{1,0:T(8,128)}) custom-call(bf16[4,256,2048]{2,1,0:T(8,128)(2,1)} %bitcast.110, bf16[256,2048]{1,0:T(8,128)(2,1)} %multiply_convert_fusion.cot.gm, bf16[256,2048]{1,0:T(8,128)(2,1)} %tok.3, f32[256,128]{1,0:T(8,128)} %broadcast_in_dim.40.valid, ...), custom_call_target="tpu_custom_call" | custom-call | tf_op jit(solution)/shard_map/middle/pallas_call | solution.py:326
  301.4 0.6 broadcast_in_dim.41.bias
  302.0 26.3 %hidden.1 = (bf16[1024,2048]{1,0:T(8,128)(2,1)}, bf16[1024,2048]{1,0:T(8,128)(2,1)}, f32[8,2048]{1,0:T(8,128)}) custom-call(bf16[1024,2048]{1,0:T(8,128)(2,1)} %bitcast.112, bf16[1024,2048]{1,0:T(8,128)(2,1)} %bitcast.114, bf16[2048,2048]{1,0:T(8,128)(2,1)} %all-gather.10.cloned.1.call-done.up, bf16[8,2048,256]{2,1,0:T(8,128)(2,1)} %bitcast.105, ...), custom_call_target="tpu_custom_call" | custom-call | tf_op jit(solution)/shard_map/hidden/pallas_call | solution.py:671
  328.4 14.0 %project.1 = bf16[1024,2048]{1,0:T(8,128)(2,1)} custom-call(bf16[1024,2048]{1,0:T(8,128)(2,1)} %get-tuple-element.47.act, bf16[8,2048,256]{2,1,0:T(8,128)(2,1)} %bitcast.106), custom_call_target="tpu_custom_call" | custom-call | tf_op jit(solution)/shard_map/project/pallas_call | solution.py:703
  342.3 14.0 %convolution_convert_fusion.2 = bf16[2048,2048]{1,0:T(8,128)(2,1)} fusion(bf16[1024,2048]{1,0:T(8,128)(2,1)} %get-tuple-element.47.act, bf16[1024,2048]{1,0:T(8,128)(2,1)} %bitcast.115), kind=kOutput, calls=%fused_computation.2 | convolution fusion | flops 8594128896 | bytes 16777216 | tf_op jit(solution)/shard_map/dot_general | solution.py:777
  356.4 14.1 %convolution_convert_fusion.1 = bf16[2048,2048]{1,0:T(8,128)(2,1)} fusion(bf16[1024,2048]{1,0:T(8,128)(2,1)} %bitcast.113, bf16[1024,2048]{1,0:T(8,128)(2,1)} %get-tuple-element.46), kind=kOutput, calls=%fused_computation.1 | convolution fusion | flops 8594128896 | bytes 16777216 | tf_op jit(solution)/shard_map/dot_general | solution.py:777
  370.4 14.4 %convolution_convert_fusion.4 = bf16[1024,2048]{1,0:T(8,128)(2,1)} fusion(bf16[1024,2048]{1,0:T(8,128)(2,1)} %get-tuple-element.46, bf16[2048,2048]{1,0:T(8,128)(2,1)} %all-gather.10.cloned.1.call-done.up), kind=kOutput, calls=%fused_computation.5 | convolution fusion | flops 8592031744 | bytes 16777216 | tf_op jit(solution)/shard_map/dot_general | solution.py:529
  385.4 169.0 %back_middle.1 = (bf16[4,256,2048]{2,1,0:T(8,128)(2,1)}, f32[256,2048]{1,0:T(8,128)}, bf16[256,2048]{1,0:T(8,128)(2,1)}, f32[48,2048]{1,0:T(8,128)}) custom-call(bf16[4,256,2048]{2,1,0:T(8,128)(2,1)} %bitcast.111, bf16[4,256,2048]{2,1,0:T(8,128)(2,1)} %bitcast.107, bf16[256,2048]{1,0:T(8,128)(2,1)} %multiply_convert_fusion.cot.gm, ...), custom_call_target="tpu_custom_call" | custom-call | tf_op jit(solution)/shard_map/back_middle/pallas_call | solution.py:390
  554.5 6.0 convolution_convert_fusion.6
  560.6 5.5 convolution_convert_fusion.7.go
  566.1 14.5 %attend_back.1 = (bf16[1024,1536]{1,0:T(8,128)(2,1)}, f32[4,16,128]{2,1,0:T(8,128)}) custom-call(bf16[1024,1536]{1,0:T(8,128)(2,1)} %add_convert_fusion.q.k.v, bf16[1024,1536]{1,0:T(8,128)(2,1)} %add_convert_fusion.q.k.v, bf16[1024,1536]{1,0:T(8,128)(2,1)} %add_convert_fusion.q.k.v, bf16[1024,512]{1,0:T(8,128)(2,1)} %convolution_convert_fusion.7.go, ...), custom_call_target="tpu_custom_call" | custom-call | tf_op jit(solution)/shard_map/attend_back/pallas_call | solution.py:615
  580.6 11.3 %convolution_convert_fusion = bf16[2048,1536]{0,1:T(8,128)(2,1)} fusion(bf16[1024,2048]{1,0:T(8,128)(2,1)} %bitcast.136, bf16[1024,1536]{1,0:T(8,128)(2,1)} %get-tuple-element.57), kind=kOutput, calls=%fused_computation | convolution fusion | flops 6445596672 | bytes 13631488 | tf_op jit(solution)/shard_map/dot_general | solution.py:777
  591.9 8.6 %copy.62 = bf16[2048,3,512]{2,0,1:T(8,128)(2,1)} copy(bf16[2048,3,512]{0,2,1:T(8,128)(2,1)} %bitcast.108) | data formatting | bytes 12582912 | tf_op jit(solution)/shard_map/reshape | solution.py:797
  601.5 0.6 slice_reduce_fusion.2
  602.6 0.8 copy.59
  603.5 0.6 slice_reduce_fusion
  604.1 4.0 stack.66
  608.1 11.6 %convolution_convert_fusion.3 = bf16[1024,2048]{1,0:T(8,128)(2,1)} fusion(bf16[1024,1536]{1,0:T(8,128)(2,1)} %get-tuple-element.57, bf16[2048,1536]{0,1:T(8,128)(2,1)} %bitcast.134), kind=kOutput, calls=%fused_computation.4 | convolution fusion | flops 6444548096 | bytes 13631488 | tf_op jit(solution)/shard_map/dot_general | solution.py:529
  619.8 73.5 %finish.1 = (f32[256,2048]{1,0:T(8,128)}, f32[16,2048]{1,0:T(8,128)}) custom-call(bf16[4,256,2048]{2,1,0:T(8,128)(2,1)} %bitcast.109, bf16[256,2048]{1,0:T(8,128)(2,1)} %tok.3, f32[256,2048]{1,0:T(8,128)} %get-tuple-element.58.gmid, f32[8,2048]{1,0:T(8,128)} %pad_convert_fusion.vecs), custom_call_target="tpu_custom_call" | custom-call | tf_op jit(solution)/shard_map/finish/pallas_call | solution.py:432
  693.3 0.8 slice_reduce_fusion.12
  694.3 0.9 slice_reduce_fusion.9
  695.3 0.7 copy.76
  696.0 15.8 %reduce_small.1 = f32[24,128]{1,0:T(8,128)} custom-call(f32[8,24,128]{2,1,0:T(8,128)} %bitcast.119), custom_call_target="tpu_custom_call" | custom-call | tf_op jit(solution)/shard_map/reduce_small/pallas_call | solution.py:500
  711.8 1.3 slice.174
  713.0 0.7 slice_reduce_fusion.13
  713.7 0.7 reshape.180
  714.4 1.4 slice_bitcast_fusion.6
  716.0 0.6 copy.63
  716.6 1.6 convert_element_type.112
  718.2 1.5 convert_element_type.113
  720.3 1.2 fusion.2
  721.5 1.8 convert_element_type.111
  723.3 2.5 convert_element_type.109
  725.8 2.3 copy.94
  728.1 1.3 copy.95
  (116 shorter events, 7.0 us)
Async XLA Ops:
  7.2 5.3 copy-start.7
  7.2 5.4 copy-start.8
  7.2 5.7 copy-start.9
  7.2 5.9 copy-start.10
  7.2 6.1 copy-start.11
  7.2 6.3 copy-start.12
  7.2 6.6 copy-start.13
  7.3 6.8 copy-start.14
  7.3 90.5 %copy-start.3 = (bf16[256,2048]{1,0:T(8,128)(2,1)S(1)}, bf16[256,2048]{1,0:T(8,128)(2,1)}, u32[]{:S(2)}) copy-start(bf16[256,2048]{1,0:T(8,128)(2,1)} %param.29) | copy-start | bytes 3145732
  7.3 91.7 %all-gather.6.cloned.1.call-start = ((), (), s32[]{:S(2)}) async-start(), calls=%async_computation.4 | async-start | bytes 7077888 | tf_op jit(solution)/shard_map/all_gather | solution.py:755
  9.7 113.0 %all-gather.8.cloned.1.call-start = ((), (), s32[]{:S(2)}) async-start(), calls=%async_computation.5 | async-start | bytes 2359296 | tf_op jit(solution)/shard_map/all_gather | solution.py:756
  10.5 290.9 %all-gather.10.cloned.1.call-start = ((), (), s32[]{:S(2)}) async-start(), calls=%async_computation.6 | async-start | bytes 9437184 | tf_op jit(solution)/shard_map/all_gather | solution.py:757
  11.2 290.2 %all-gather.12.cloned.1.call-start = ((), (), s32[]{:S(2)}) async-start(), calls=%async_computation.11 | async-start | bytes 9437184 | tf_op jit(solution)/shard_map/all_gather | solution.py:758
  11.8 542.7 %reduce-scatter.5.cloned.1.call-start = ((), (), s32[]{:S(2)}) async-start(), calls=%async_computation.7 | async-start | bytes 9437184 | tf_op jit(solution)/shard_map/reduce_scatter | solution.py:788
  384.8 169.7 %reduce-scatter.7.cloned.1.call-start = ((), (), s32[]{:S(2)}) async-start(), calls=%async_computation.8 | async-start | bytes 9437184 | tf_op jit(solution)/shard_map/reduce_scatter | solution.py:789
  385.4 336.1 %reduce-scatter.11.cloned.1.call-start = ((), (), s32[]{:S(2)}) async-start(), calls=%async_computation.10 | async-start | bytes 2359296 | tf_op jit(solution)/shard_map/reduce_scatter | solution.py:795
  385.4 169.0 %copy-start.16 = (bf16[1024,512]{1,0:T(8,128)(2,1)S(1)}, bf16[1024,512]{1,0:T(8,128)(2,1)}, u32[]{:S(2)}) copy-start(bf16[1024,512]{1,0:T(8,128)(2,1)} %get-tuple-element.43) | copy-start | bytes 3145732
  554.5 6.1 copy-start.15
  560.6 162.7 %reduce-scatter.9.cloned.1.call-start = ((), (), s32[]{:S(2)}) async-start(), calls=%async_computation.9 | async-start | bytes 7077888 | tf_op jit(solution)/shard_map/reduce_scatter | solution.py:798
  600.5 0.9 copy-start.5
  600.5 1.6 copy-start.6
  600.5 3.0 copy-start.4
  619.7 96.8 %copy-start.2 = (bf16[256,2048]{1,0:T(8,128)(2,1)S(1)}, bf16[256,2048]{1,0:T(8,128)(2,1)}, u32[]{:S(2)}) copy-start(bf16[256,2048]{1,0:T(8,128)(2,1)} %reduce-scatter.7.cloned.1.call-done) | copy-start | bytes 3145732
  619.8 98.4 %copy-start.1 = (bf16[2048,256]{1,0:T(8,128)(2,1)S(1)}, bf16[2048,256]{1,0:T(8,128)(2,1)}, u32[]{:S(2)}) copy-start(bf16[2048,256]{1,0:T(8,128)(2,1)} %reduce-scatter.5.cloned.1.call-done) | copy-start | bytes 3145732
  718.2 9.9 %copy-start = (f32[256,2048]{1,0:T(8,128)S(1)}, f32[256,2048]{1,0:T(8,128)}, u32[]{:S(2)}) copy-start(f32[256,2048]{1,0:T(8,128)} %get-tuple-element.172) | copy-start | bytes 6291460
Sparse Core Ops, SparseCore 0:
  10.5 49.2 all-gather.5
  61.7 28.0 all-gather.7
  91.8 54.2 all-gather.9
  147.8 54.2 all-gather.11
  384.9 68.7 reduce-scatter.4
  457.0 71.4 reduce-scatter.6
  560.7 40.1 reduce-scatter.10
  604.3 61.6 reduce-scatter.8

commit v3 on v2

--- a/solution.py
+++ b/solution.py
@@ -73,6 +73,49 @@
                 if k == 0 and first is not None:
                     src = first.at[pl.ds(part * self.sub, self.sub)]
                 self._copy(src, buf, sems, way, shard, part).start()
+
+    def relay(self, k, part, buf, sems):
+        for way in (0, 1):
+            shard = self.t - k if way == 0 else self.t + k
+            inside = (self.t >= k) if way == 0 else (self.t + k <= self.size - 1)
+
+            @pl.when(inside)
+            def _(way=way, shard=shard):
+                held = self._rows(buf, shard, part)
+                self._copy(held, buf, sems, way, shard, part).wait_recv()
+
+                @pl.when(self._edge(way))
+                def _():
+                    self._copy(held, buf, sems, way, shard, part).start()
+
+    def walk(self, buf, sems, work):
+        last_part = SUBS - 1
+
+        def visit(m, carry):
+            k = (m + 1) // 2
+            shard = jnp.where(m % 2 == 1, self.t - k, self.t + k)
+
+            @pl.when((shard >= 0) & (shard < self.size))
+            def _():
+                work(shard)
+
+            @pl.when(m == 0)
+            def _():
+                for part in range(last_part):
+                    self.relay(1, part, buf, sems)
+
+            @pl.when(m % 2 == 0)
+            def _():
+                self.relay(k + 1, last_part, buf, sems)
+
+            @pl.when(m % 2 == 1)
+            def _():
+                for part in range(last_part):
+                    self.relay(k + 1, part, buf, sems)
+
+            return carry
+
+        lax.fori_loop(0, 2 * self.size - 1, visit, 0)
 
     def scatter_step(self, way, j, part, terms, buf, sems):
         t, last = self.t, self.size - 1
@@ -290,7 +333,7 @@
 
 def middle_kernel(
     size, terms, cot, tok, valid, vecs, c_out, gm_out, mid_out, stats,
-    right, left, gs, gr, ss, sr, cs, cr,
+    right, left, gs, gr, ss, sr,
 ):
     line = Line(size, tok.shape[0])
     rows = tok.shape[0]
@@ -306,7 +349,7 @@
         x = tok[at, :].astype(F32)
         mid = x + attn
         normed, _ = normal(mid)
-        c_out[line.t, at, :] = (normed * vecs[3:4, :] + vecs[4:5, :]).astype(BF16)
+        c_out[at, :] = (normed * vecs[3:4, :] + vecs[4:5, :]).astype(BF16)
         mid_out[at, :] = mid
         ok = valid[at, 0:1]
         stats[0:8, :] += fold(ok * x * x)
@@ -314,10 +357,8 @@
         stats[16:24, :] += fold(ok * mid * mid)
 
     row_loop(rows, step, body)
-    line.phase(gather=(c_out, (cs, cr), None))
     line.drain_gather(gm_out, (gs, gr))
     line.drain_scatter((right, left), (ss, sr))
-    line.drain_gather(c_out, (cs, cr))
 
 
 def middle(terms, cot, tok, valid, vecs, size, cid):
@@ -326,7 +367,7 @@
     return pl.pallas_call(
         functools.partial(middle_kernel, size),
         out_shape=(
-            jax.ShapeDtypeStruct(full, BF16),
+            jax.ShapeDtypeStruct((rows, width), BF16),
             jax.ShapeDtypeStruct(full, BF16),
             jax.ShapeDtypeStruct((rows, width), F32),
             jax.ShapeDtypeStruct((24, width), F32),
@@ -334,7 +375,6 @@
         in_specs=[WHOLE] * 5,
         out_specs=(WHOLE,) * 4,
         scratch_shapes=[pltpu.VMEM(full, BF16), pltpu.VMEM(full, BF16)]
-        + line_sems(size)
         + line_sems(size)
         + line_sems(size),
         compiler_params=params(cid),
@@ -343,8 +383,8 @@
 
 
 def back_middle_kernel(
-    size, terms, mlp, gm, mid, valid, vecs, gz_out, gmid_out, y_out, stats,
-    right, left, right2, left2, ss, sr, ms, mr, gs, gr,
+    size, terms, mlp, gm, mid, valid, vecs, out_w, o_t, gz_out, gmid_out, y_out, stats,
+    go_out, grad_out, right, left, right2, left2, grad, ss, sr, ms, mr, gs, gr,
 ):
     line = Line(size, mid.shape[0])
     rows = mid.shape[0]
@@ -367,7 +407,39 @@
         stats[24:32, :] += fold(gy)
 
     row_loop(rows, step, body)
-    line.phase(gather=(gz_out, (gs, gr), None), scatter=(mlp, (right2, left2), (ms, mr)))
+    width = mid.shape[1]
+    block = min(512, width)
+
+    def weigh(shard):
+        go_out[shard] = dot_t(gz_out[shard], out_w[...]).astype(BF16)
+        here = o_t[:, pl.ds(pl.multiple_of(shard * rows, rows), rows)]
+
+        def column(j, carry):
+            at = pl.ds(pl.multiple_of(j * block, block), block)
+            grad[:, at] += dot(here, gz_out[shard, :, at])
+            return carry
+
+        lax.fori_loop(0, width // block, column, 0)
+
+    def on_slot(k):
+        def side(i, carry):
+            shard = line.t + k * (2 * i - 1)
+
+            @pl.when((shard >= 0) & (shard < size))
+            def _():
+                weigh(shard)
+
+            return carry
+
+        lax.fori_loop(0, 1 if k == 0 else 2, side, 0)
+
+    grad[...] = jnp.zeros_like(grad)
+    line.phase(
+        gather=(gz_out, (gs, gr), None),
+        scatter=(mlp, (right2, left2), (ms, mr)),
+        on_slot=on_slot,
+    )
+    grad_out[...] = grad[...].astype(BF16)
     line.own_wait((right2, left2), (ms, mr))
 
     def tail(at):
@@ -384,8 +456,9 @@
     line.drain_gather(gz_out, (gs, gr))
 
 
-def back_middle(terms, mlp, gm, mid, valid, vecs, size, cid):
+def back_middle(terms, mlp, gm, mid, valid, vecs, out_w, o_t, size, cid):
     rows, width = mid.shape
+    local = out_w.shape[0]
     full = (size, rows, width)
     return pl.pallas_call(
         functools.partial(back_middle_kernel, size),
@@ -394,16 +467,19 @@
             jax.ShapeDtypeStruct((rows, width), F32),
             jax.ShapeDtypeStruct((rows, width), BF16),
             jax.ShapeDtypeStruct((48, width), F32),
-        ),
-        in_specs=[WHOLE] * 6,
-        out_specs=(WHOLE,) * 4,
+            jax.ShapeDtypeStruct((size, rows, local), BF16),
+            jax.ShapeDtypeStruct((local, width), BF16),
+        ),
+        in_specs=[WHOLE] * 8,
+        out_specs=(WHOLE,) * 6,
         scratch_shapes=[pltpu.VMEM(full, BF16)] * 4
+        + [pltpu.VMEM((local, width), F32)]
         + line_sems(size)
         + line_sems(size)
         + line_sems(size),
         compiler_params=params(cid),
         name="back_middle",
-    )(terms, mlp, gm, mid, valid, vecs)
+    )(terms, mlp, gm, mid, valid, vecs, out_w, o_t)
 
 
 def finish_kernel(size, terms, tok, gmid, vecs, grad_out, stats, right, left, ss, sr):
@@ -536,7 +612,7 @@
     return jnp.where(key_pos <= query_pos, scores, NEG)
 
 
-def attend_kernel(q, k, v, bar, out, log_totals):
+def attend_kernel(q, k, v, bar, out, out_t, log_totals):
     value_cols = v[...].T
     for block in range(LEN // BLOCK):
         first, keys = block * BLOCK, (block + 1) * BLOCK
@@ -549,6 +625,7 @@
         shares = (powers * (1.0 / total)).astype(BF16)
         mixed = dot(value_cols[:, 0:keys], shares)
         out[first : first + BLOCK, :] = mixed.T.astype(BF16)
+        out_t[:, first : first + BLOCK] = mixed.astype(BF16)
         log_totals[0, :, first : first + BLOCK] = jnp.broadcast_to(top + jnp.log(total), (8, BLOCK))
 
 
@@ -561,11 +638,13 @@
         grid=(heads,),
         out_shape=(
             jax.ShapeDtypeStruct((LEN, heads * HD), BF16),
+            jax.ShapeDtypeStruct((heads * HD, LEN), BF16),
             jax.ShapeDtypeStruct((heads, 8, LEN), F32),
         ),
         in_specs=[column(0), column(1), column(2), pl.BlockSpec((LEN, 128), lambda h: (0, 0))],
         out_specs=(
             pl.BlockSpec((LEN, HD), lambda h: (0, h)),
+            pl.BlockSpec((HD, LEN), lambda h: (h, 0)),
             pl.BlockSpec((1, 8, LEN), lambda h: (h, 0, 0)),
         ),
         compiler_params=params(),
@@ -644,74 +723,99 @@
     return u * half, slope
 
 
-def hidden_kernel(n_dp, c, gm, up, down, bias, act_out, gu_out, sums):
-    width = down.shape[2]
-    rows = c.shape[0]
-    step = min(256, rows)
+def hidden_kernel(
+    n_dp, size, c_own, gm, up_in, down_in, bias, c_out, act_out, gu_out, mlp_out, back_out, sums,
+    up, down, act, gu, mlp, back, gs, gr, in_sem, out_sem,
+):
+    line = Line(size, c_own.shape[0])
+    rows, width = c_own.shape
+    units, part = down.shape[1], down.shape[2]
+    block = min(512, units)
+    loads = [
+        pltpu.make_async_copy(up_in, up, in_sem.at[0]),
+        pltpu.make_async_copy(down_in, down, in_sem.at[1]),
+    ]
+    for load in loads:
+        load.start()
+    line.barrier()
+    for piece in range(SUBS):
+        for way in (0, 1):
+            line.gather_step(way, 0, piece, c_out, (gs, gr), c_own)
+    c_out[pl.ds(line.t, 1)] = c_own[...][None]
     sums[...] = jnp.zeros_like(sums)
-
-    def body(at):
-        u = dot(c[at, :], up[...]) + bias[0:1, :]
-        grad = dot_t(gm[at, 0:width], down[0])
-        for d in range(1, n_dp):
-            grad = grad + dot_t(gm[at, d * width : (d + 1) * width], down[d])
-        act, slope = gelu_both(u)
-        act_out[at, :] = act.astype(BF16)
-        gu = (grad * slope).astype(BF16)
-        gu_out[at, :] = gu
-        sums[...] += fold(gu.astype(F32))
-
-    row_loop(rows, step, body)
-
-
-def hidden(c, gm, up, down, bias):
-    rows, width = c.shape
+    for load in loads:
+        load.wait()
+
+    def stores(shard):
+        pairs = ((act, act_out), (gu, gu_out), (mlp, mlp_out), (back, back_out))
+        return [
+            pltpu.make_async_copy(src.at[shard], dst.at[shard], out_sem.at[i, shard])
+            for i, (src, dst) in enumerate(pairs)
+        ]
+
+    def work(shard):
+        def unit_block(j, carry):
+            at = pl.ds(pl.multiple_of(j * block, block), block)
+            u = dot(c_out[shard], up[:, at]) + bias[0:1, at]
+            grad = dot_t(gm[shard, :, 0:part], down[0, at, :])
+            for d in range(1, n_dp):
+                grad = grad + dot_t(gm[shard, :, d * part : (d + 1) * part], down[d, at, :])
+            value, slope = gelu_both(u)
+            act[shard, :, at] = value.astype(BF16)
+            rounded = (grad * slope).astype(BF16)
+            gu[shard, :, at] = rounded
+            sums[:, at] += fold(rounded.astype(F32))
+            return carry
+
+        lax.fori_loop(0, units // block, unit_block, 0)
+
+        def feature_block(d, carry):
+            at = pl.ds(pl.multiple_of(d * part, part), part)
+            mlp[shard, :, at] = dot(act[shard], down[d]).astype(BF16)
+            back[shard, :, at] = dot_t(gu[shard], up[at, :]).astype(BF16)
+            return carry
+
+        lax.fori_loop(0, n_dp, feature_block, 0)
+        for store in stores(shard):
+            store.start()
+
+    line.walk(c_out, (gs, gr), work)
+    line.drain_gather(c_out, (gs, gr))
+    for shard in range(size):
+        for store in stores(shard):
+            store.wait()
+
+
+def hidden(c_own, gm, up, down, bias, size, cid):
+    rows, width = c_own.shape
     n_dp, units, part = down.shape
-    block = min(512, units)
+    full, wide = (size, rows, width), (size, rows, units)
+    hbm = pl.BlockSpec(memory_space=pltpu.HBM)
     return pl.pallas_call(
-        functools.partial(hidden_kernel, n_dp),
-        grid=(units // block,),
+        functools.partial(hidden_kernel, n_dp, size),
         out_shape=(
-            jax.ShapeDtypeStruct((rows, units), BF16),
-            jax.ShapeDtypeStruct((rows, units), BF16),
+            jax.ShapeDtypeStruct(full, BF16),
+            jax.ShapeDtypeStruct(wide, BF16),
+            jax.ShapeDtypeStruct(wide, BF16),
+            jax.ShapeDtypeStruct(full, BF16),
+            jax.ShapeDtypeStruct(full, BF16),
             jax.ShapeDtypeStruct((8, units), F32),
         ),
-        in_specs=[
-            pl.BlockSpec((rows, width), lambda i: (0, 0), pipeline_mode=pl.Buffered(1)),
-            pl.BlockSpec((rows, width), lambda i: (0, 0), pipeline_mode=pl.Buffered(1)),
-            pl.BlockSpec((width, block), lambda i: (0, i)),
-            pl.BlockSpec((n_dp, block, part), lambda i: (0, i, 0)),
-            pl.BlockSpec((8, block), lambda i: (0, i)),
-        ],
-        out_specs=(
-            pl.BlockSpec((rows, block), lambda i: (0, i)),
-            pl.BlockSpec((rows, block), lambda i: (0, i)),
-            pl.BlockSpec((8, block), lambda i: (0, i)),
-        ),
-        compiler_params=params(),
+        in_specs=[WHOLE, WHOLE, hbm, hbm, WHOLE],
+        out_specs=(WHOLE, hbm, hbm, hbm, hbm, WHOLE),
+        scratch_shapes=[
+            pltpu.VMEM((width, units), BF16),
+            pltpu.VMEM((n_dp, units, part), BF16),
+            pltpu.VMEM(wide, BF16),
+            pltpu.VMEM(wide, BF16),
+            pltpu.VMEM(full, BF16),
+            pltpu.VMEM(full, BF16),
+        ]
+        + line_sems(size)
+        + [pltpu.SemaphoreType.DMA((2,)), pltpu.SemaphoreType.DMA((4, size))],
+        compiler_params=params(cid),
         name="hidden",
-    )(c, gm, up, down, bias)
-
-
-def project_kernel(act, down, out):
-    out[...] = dot(act[...], down[0]).astype(BF16)
-
-
-def project(act, down):
-    rows, units = act.shape
-    n_dp, _, part = down.shape
-    return pl.pallas_call(
-        project_kernel,
-        grid=(n_dp,),
-        out_shape=jax.ShapeDtypeStruct((rows, n_dp * part), BF16),
-        in_specs=[
-            pl.BlockSpec((rows, units), lambda i: (0, 0), pipeline_mode=pl.Buffered(1)),
-            pl.BlockSpec((1, units, part), lambda i: (i, 0, 0)),
-        ],
-        out_specs=pl.BlockSpec((rows, part), lambda i: (0, i)),
-        compiler_params=params(),
-        name="project",
-    )(act, down)
+    )(c_own, gm, up, down, bias)
 
 
 def pad_to(x, count):
@@ -752,7 +856,7 @@
     up_shift = up_all.transpose(1, 0, 2).reshape(1, units).astype(F32)
     qkv_shift = jnp.concatenate([qv_all[0], jnp.zeros_like(qv_all[0]), qv_all[1]])
 
-    qkv_full = lax.all_gather(qkv_weight, "dp", axis=0, tiled=True).reshape(width, 3 * local)
+    qkv_full = lax.all_gather(qkv_weight.reshape(part, 3 * local), "dp", axis=0, tiled=True)
     out_full = lax.all_gather(out_weight, "dp", axis=1, tiled=True)
     up_full = lax.all_gather(up_weight, "dp", axis=0, tiled=True)
     down_blocks = lax.all_gather(down_weight, "dp", axis=0, tiled=False)
@@ -765,13 +869,14 @@
     gm_own = (cotangent.astype(F32) * valid_own[:, None]).astype(BF16)
 
     qkv = (dot(a, qkv_full) + qkv_shift).astype(BF16)
-    attended, log_totals = attend(qkv, bar, heads)
+    attended, attended_t, log_totals = attend(qkv, bar, heads)
     terms = dot(attended, out_full).astype(BF16).reshape(n_t, rows, width)
-    c, gm, mid, stats_a = middle(terms, gm_own, tokens, valid, vecs, n_t, 2)
+    c_own, gm, mid, stats_a = middle(terms, gm_own, tokens, valid, vecs, n_t, 2)
+    c, act, gu, mlp, back_terms, up_sums = hidden(
+        c_own, gm, up_full, down_blocks, jnp.broadcast_to(up_shift, (8, units)), n_t, 6
+    )
     c, gm = c.reshape(-1, width), gm.reshape(-1, width)
-    act, gu, up_sums = hidden(
-        c, gm, up_full, down_blocks, jnp.broadcast_to(up_shift, (8, units))
-    )
+    act, gu = act.reshape(-1, units), gu.reshape(-1, units)
 
     def rows_dot(left, right):
         return lax.dot_general(
@@ -780,22 +885,20 @@
 
     down_grad = rows_dot(act, gm)
     up_grad = rows_dot(c, gu)
-    back_terms = dot_t(gu, up_full).astype(BF16).reshape(n_t, rows, width)
-    mlp = project(act, down_blocks).reshape(n_t, rows, width)
     back_terms, mlp, down_grad, up_grad = lax.optimization_barrier(
         (back_terms, mlp, down_grad, up_grad)
     )
     down_out = lax.psum_scatter(down_grad, "dp", scatter_dimension=1, tiled=True)
     up_out = lax.psum_scatter(up_grad, "dp", scatter_dimension=0, tiled=True)
-    gz, gmid, output, stats_b = back_middle(back_terms, mlp, gm_own, mid, valid, vecs, n_t, 3)
-    gz, down_out, up_out = lax.optimization_barrier((gz, down_out, up_out))
-    gz = gz.reshape(-1, width)
-    go = dot_t(gz, out_full).astype(BF16)
-    out_grad = rows_dot(attended, gz)
+    _, gmid, output, stats_b, go, out_grad = back_middle(
+        back_terms, mlp, gm_own, mid, valid, vecs, out_full, attended_t, n_t, 3
+    )
+    go, out_grad, down_out, up_out = lax.optimization_barrier((go, out_grad, down_out, up_out))
     out_out = lax.psum_scatter(out_grad, "dp", scatter_dimension=1, tiled=True)
-    gqkv, head_sums = attend_back(qkv, go, bar, log_totals, heads)
-    qkv_grad = rows_dot(a, gqkv).reshape(width, 3, local)
+    gqkv, head_sums = attend_back(qkv, go.reshape(-1, local), bar, log_totals, heads)
+    qkv_grad = rows_dot(a, gqkv)
     qkv_out = lax.psum_scatter(qkv_grad, "dp", scatter_dimension=0, tiled=True)
+    qkv_out = qkv_out.reshape(part, 3, local)
     last_terms = dot_t(gqkv, qkv_full).astype(BF16).reshape(n_t, rows, width)
     tokens_grad, stats_c = finish(last_terms, tokens, gmid, vecs, n_t, 4)
 

time: 746 us -> 700 us (0.938)
  matrix products: 94.9 us -> 68.9 us
  Pallas kernels: 575 us -> 562 us
    pallas_call x1, Pallas kernels: 172 us -> 102 us  [middle(): pl.pallas_call(functools.partial(middle_kernel, size), out_shape=(jax.Sha...]
    pallas_call x2 -> x1, Pallas kernels: 40.3 us -> 88.4 us  [hidden(): pl.pallas_call(functools.partial(hidden_kernel, n_dp, size), out_shape=(j...]
    dot_general x3 -> x1, matrix products: 31.5 us -> 11.1 us  [dot_t(): lax.dot_general(a, b, (((1,), (1,)), ((), ())), preferred_element_type=F32)]
    reshape x1 -> x0, local copies, waits for them, and re-layouts: 8.59 us -> none  [shards(): qkv_grad = rows_dot(a, gqkv).reshape(width, 3, local)]
    pallas_call x1, Pallas kernels: 73.5 us -> 81.6 us  [finish(): pl.pallas_call(functools.partial(finish_kernel, size), out_shape=(jax.Sha...]
    dot_general x4 -> x3, matrix products: 45.4 us -> 39.6 us  [rows_dot(): lax.dot_general(left, right, (((0,), (0,)), ((), ())), preferred_element_...]
  transfers between devices with their start and end apart: 8 -> 8, of which waited for: 0 -> 0; matrix products, arithmetic and copies ran while one was open for 11% -> 10% of each run, Pallas kernels for 73% -> 69%
where the time goes in v3:
time: 700 us; the launch traced here: 690 us
  Pallas kernels  562 us (80%)
  matrix products  68.9 us (10%)
  local copies, waits for them, and re-layouts  29.1 us (4%)
  between operations  16.1 us (2%)
  other arithmetic  10.7 us (2%)
    pallas_call x1, Pallas kernels, back_middle(): pl.pallas_call(functools.partial(back_middle_kernel, size), out_shape=(ja...  171 us
    pallas_call x1, Pallas kernels, middle(): pl.pallas_call(functools.partial(middle_kernel, size), out_shape=(jax.Sha...  102 us
    pallas_call x1, Pallas kernels, hidden(): pl.pallas_call(functools.partial(hidden_kernel, n_dp, size), out_shape=(j...  88.4 us
    pallas_call x1, Pallas kernels, finish(): pl.pallas_call(functools.partial(finish_kernel, size), out_shape=(jax.Sha...  81.6 us
    pallas_call x1, Pallas kernels, first(): pl.pallas_call(functools.partial(first_kernel, n_dp, size, part), out_sha...  79.5 us
    dot_general x3, matrix products, rows_dot(): lax.dot_general(left, right, (((0,), (0,)), ((), ())), preferred_element_...  39.6 us
    dot_general x2, matrix products, dot(): return jnp.dot(a, b, preferred_element_type=F32)  18.2 us
    pallas_call x1, Pallas kernels, reduce_small(): pl.pallas_call(functools.partial(reduce_small_kernel, n_dp, n_t, shared),...  15.2 us
  transfers between devices with their start and end apart: 8, of which 0 were waited for; matrix products, arithmetic and copies ran while one was open for 10% of the time, Pallas kernels for 69%

profile of v3, /device:TPU:0, one launch (start us, length us, event | category | flops | bytes accessed | tf_op | source)
XLA Modules:
  0.0 690.2 jit_solution(13810390658314547489)
XLA Ops:
  7.3 2.4 copy.62
  9.8 0.7 all-gather.8.cloned.1.call-update
  10.5 0.7 all-gather.10.cloned.1.call-update
  11.3 0.5 all-gather.12.cloned.1.call-update
  14.6 0.6 pad_bitcast_fusion.small
  15.2 79.5 %first.1 = (bf16[8,16,128]{2,1,0:T(8,128)(2,1)}, bf16[4,256,2048]{2,1,0:T(8,128)(2,1)}) custom-call(bf16[16,128]{1,0:T(8,128)(2,1)} %pad_bitcast_fusion.small, bf16[256,2048]{1,0:T(8,128)(2,1)} %tok.3), custom_call_target="tpu_custom_call" | custom-call | tf_op jit(solution)/shard_map/first/pallas_call | solution.py:315
  94.7 0.8 copy.90
  96.0 0.8 copy.66
  97.2 0.6 pad_convert_fusion.vecs
  97.9 1.2 multiply_convert_fusion.cot.gm
  99.1 11.8 %add_convert_fusion.q.k.v = bf16[1024,1536]{1,0:T(8,128)(2,1)} fusion(bf16[1024,2048]{1,0:T(8,128)(2,1)} %bitcast.122, bf16[2048,1536]{0,1:T(8,128)(2,1)} %all-gather.6.cloned.1.call-done, f32[1536]{0:T(1024)S(1)} %pad_maximum_fusion.1), kind=kOutput, calls=%fused_computation.3 | convolution fusion | flops 6445596672 | bytes 13637632 | tf_op jit(solution)/shard_map/dot_general | solution.py:601
  110.9 1.0 broadcast_in_dim.21.bar
  111.9 10.9 %attend.1 = (bf16[1024,512]{1,0:T(8,128)(2,1)}, bf16[512,1024]{1,0:T(8,128)(2,1)}, f32[4,8,1024]{2,1,0:T(8,128)}) custom-call(bf16[1024,1536]{1,0:T(8,128)(2,1)} %add_convert_fusion.q.k.v, bf16[1024,1536]{1,0:T(8,128)(2,1)} %add_convert_fusion.q.k.v, bf16[1024,1536]{1,0:T(8,128)(2,1)} %add_convert_fusion.q.k.v, f32[1024,128]{1,0:T(8,128)} %broadcast_in_dim.21.bar), custom_call_target="tpu_custom_call" | custom-call | tf_op jit(solution)/shard_map/attend/pallas_call | solution.py:636
  122.9 6.3 convolution_convert_fusion.2
  129.2 0.8 broadcast_in_dim.40.valid
  130.0 101.9 %middle.1 = (bf16[256,2048]{1,0:T(8,128)(2,1)}, bf16[4,256,2048]{2,1,0:T(8,128)(2,1)}, f32[256,2048]{1,0:T(8,128)}, f32[24,2048]{1,0:T(8,128)}) custom-call(bf16[4,256,2048]{2,1,0:T(8,128)(2,1)} %bitcast.102, bf16[256,2048]{1,0:T(8,128)(2,1)} %multiply_convert_fusion.cot.gm, bf16[256,2048]{1,0:T(8,128)(2,1)} %tok.3, f32[256,128]{1,0:T(8,128)} %broadcast_in_dim.40.valid, ...), custom_call_target="tpu_custom_call" | custom-call | tf_op jit(solution)/shard_map/middle/pallas_call | solution.py:367
  231.9 0.6 broadcast_in_dim.41.bias
  232.5 88.4 %hidden.1 = (bf16[4,256,2048]{2,1,0:T(8,128)(2,1)}, bf16[4,256,2048]{2,1,0:T(8,128)(2,1)}, bf16[4,256,2048]{2,1,0:T(8,128)(2,1)}, bf16[4,256,2048]{2,1,0:T(8,128...) custom-call(bf16[256,2048]{1,0:T(8,128)(2,1)} %get-tuple-element.50.c_own, ...), custom_call_target="tpu_custom_call" | custom-call | tf_op jit(solution)/shard_map/hidden/pallas_call | solution.py:794
  320.9 14.1 %bitcast_convert_fusion.1 = bf16[2048,2048]{1,0:T(8,128)(2,1)} fusion(bf16[4,256,2048]{2,1,0:T(8,128)(2,1)} %get-tuple-element.54, bf16[4,256,2048]{2,1,0:T(8,128)(2,1)} %get-tuple-element.51.gm), kind=kOutput, calls=%fused_computation.1 | convolution fusion | flops 8594128896 | bytes 16777216 | tf_op jit(solution)/shard_map/dot_general | solution.py:882
  335.0 14.0 %bitcast_convert_fusion = bf16[2048,2048]{1,0:T(8,128)(2,1)} fusion(bf16[4,256,2048]{2,1,0:T(8,128)(2,1)} %get-tuple-element.55, bf16[4,256,2048]{2,1,0:T(8,128)(2,1)} %get-tuple-element.56), kind=kOutput, calls=%fused_computation | convolution fusion | flops 8594128896 | bytes 16777216 | tf_op jit(solution)/shard_map/dot_general | solution.py:882
  349.1 0.5 reduce-scatter.7.cloned.1.call-update
  349.6 170.7 %back_middle.1 = (bf16[4,256,2048]{2,1,0:T(8,128)(2,1)}, f32[256,2048]{1,0:T(8,128)}, bf16[256,2048]{1,0:T(8,128)(2,1)}, f32[48,2048]{1,0:T(8,128)}, bf16[4,256,...) custom-call(bf16[4,256,2048]{2,1,0:T(8,128)(2,1)} %get-tuple-element.57.terms, bf16[4,256,2048]{2,1,0:T(8,128)(2,1)} %get-tuple-element.58.mlp, ...), custom_call_target="tpu_custom_call" | custom-call | tf_op jit(solution)/shard_map/back_middle/pallas_call | solution.py:463
  520.5 14.3 %attend_back.1 = (bf16[1024,1536]{1,0:T(8,128)(2,1)}, f32[4,16,128]{2,1,0:T(8,128)}) custom-call(bf16[1024,1536]{1,0:T(8,128)(2,1)} %add_convert_fusion.q.k.v, bf16[1024,1536]{1,0:T(8,128)(2,1)} %add_convert_fusion.q.k.v, bf16[1024,1536]{1,0:T(8,128)(2,1)} %add_convert_fusion.q.k.v, bf16[1024,512]{1,0:T(8,128)(2,1)} %bitcast.105, ...), custom_call_target="tpu_custom_call" | custom-call | tf_op jit(solution)/shard_map/attend_back/pallas_call | solution.py:694
  534.8 11.5 %convolution_convert_fusion = bf16[2048,1536]{1,0:T(8,128)(2,1)} fusion(bf16[1024,2048]{1,0:T(8,128)(2,1)} %bitcast.123, bf16[1024,1536]{1,0:T(8,128)(2,1)} %get-tuple-element.68), kind=kOutput, calls=%fused_computation.2 | convolution fusion | flops 6445596672 | bytes 13631488 | tf_op jit(solution)/shard_map/dot_general | solution.py:882
  546.3 0.6 fusion.3
  547.2 0.6 slice_reduce_fusion.2
  548.3 0.8 copy.69
  549.2 0.6 slice_reduce_fusion
  549.9 4.0 stack.66
  553.9 11.1 %convolution_convert_fusion.1 = bf16[1024,2048]{1,0:T(8,128)(2,1)} fusion(bf16[1024,1536]{1,0:T(8,128)(2,1)} %get-tuple-element.68, bf16[2048,1536]{0,1:T(8,128)(2,1)} %all-gather.6.cloned.1.call-done), kind=kOutput, calls=%fused_computation.4 | convolution fusion | flops 6444548096 | bytes 13631488 | tf_op jit(solution)/shard_map/dot_general | solution.py:605
  565.0 81.6 %finish.1 = (f32[256,2048]{1,0:T(8,128)}, f32[16,2048]{1,0:T(8,128)}) custom-call(bf16[4,256,2048]{2,1,0:T(8,128)(2,1)} %bitcast.101, bf16[256,2048]{1,0:T(8,128)(2,1)} %tok.3, f32[256,2048]{1,0:T(8,128)} %get-tuple-element.69.gmid, f32[8,2048]{1,0:T(8,128)} %pad_convert_fusion.vecs), custom_call_target="tpu_custom_call" | custom-call | tf_op jit(solution)/shard_map/finish/pallas_call | solution.py:508
  646.6 0.8 slice_reduce_fusion.12
  647.6 0.9 slice_reduce_fusion.9
  648.6 0.7 copy.89
  649.3 15.2 %reduce_small.1 = f32[24,128]{1,0:T(8,128)} custom-call(f32[8,24,128]{2,1,0:T(8,128)} %bitcast.108), custom_call_target="tpu_custom_call" | custom-call | tf_op jit(solution)/shard_map/reduce_small/pallas_call | solution.py:576
  664.5 1.3 slice.174
  665.8 0.7 slice_reduce_fusion.13
  666.5 0.7 reshape.167
  667.2 1.4 slice_bitcast_fusion.6
  668.7 0.6 copy.74
  669.4 1.6 convert_element_type.104
  670.9 1.5 convert_element_type.105
  673.0 1.2 fusion.2
  674.3 1.8 convert_element_type.103
  676.0 1.4 copy.72
  677.4 1.6 copy.73
  679.1 1.0 copy.107
  680.0 3.1 copy.108
  (108 shorter events, 4.7 us)
Async XLA Ops:
  7.2 5.3 copy-start.7
  7.2 5.4 copy-start.8
  7.2 5.7 copy-start.9
  7.2 5.9 copy-start.10
  7.2 6.1 copy-start.11
  7.2 6.3 copy-start.12
  7.2 6.6 copy-start.13
  7.3 6.8 copy-start.14
  7.3 90.6 %copy-start.3 = (bf16[256,2048]{1,0:T(8,128)(2,1)S(1)}, bf16[256,2048]{1,0:T(8,128)(2,1)}, u32[]{:S(2)}) copy-start(bf16[256,2048]{1,0:T(8,128)(2,1)} %param.29) | copy-start | bytes 3145732
  7.3 91.8 %all-gather.6.cloned.1.call-start = ((), (), s32[]{:S(2)}) async-start(), calls=%async_computation.4 | async-start | bytes 7077888 | tf_op jit(solution)/shard_map/all_gather | solution.py:859
  9.7 113.1 %all-gather.8.cloned.1.call-start = ((), (), s32[]{:S(2)}) async-start(), calls=%async_computation.5 | async-start | bytes 2359296 | tf_op jit(solution)/shard_map/all_gather | solution.py:860
  10.5 221.4 %all-gather.10.cloned.1.call-start = ((), (), s32[]{:S(2)}) async-start(), calls=%async_computation.6 | async-start | bytes 9437184 | tf_op jit(solution)/shard_map/all_gather | solution.py:861
  11.2 220.7 %all-gather.12.cloned.1.call-start = ((), (), s32[]{:S(2)}) async-start(), calls=%async_computation.11 | async-start | bytes 9437184 | tf_op jit(solution)/shard_map/all_gather | solution.py:862
  11.8 508.6 %reduce-scatter.5.cloned.1.call-start = ((), (), s32[]{:S(2)}) async-start(), calls=%async_computation.7 | async-start | bytes 9437184 | tf_op jit(solution)/shard_map/reduce_scatter | solution.py:891
  349.0 171.4 %reduce-scatter.7.cloned.1.call-start = ((), (), s32[]{:S(2)}) async-start(), calls=%async_computation.8 | async-start | bytes 9437184 | tf_op jit(solution)/shard_map/reduce_scatter | solution.py:892
  349.6 324.7 %reduce-scatter.11.cloned.1.call-start = ((), (), s32[]{:S(2)}) async-start(), calls=%async_computation.10 | async-start | bytes 2359296 | tf_op jit(solution)/shard_map/reduce_scatter | solution.py:897
  520.4 155.6 %reduce-scatter.9.cloned.1.call-start = ((), (), s32[]{:S(2)}) async-start(), calls=%async_computation.9 | async-start | bytes 7077888 | tf_op jit(solution)/shard_map/reduce_scatter | solution.py:900
  546.3 0.9 copy-start.5
  546.3 1.5 copy-start.6
  546.3 3.0 copy-start.4
  565.0 104.4 %copy-start.1 = (bf16[256,2048]{1,0:T(8,128)(2,1)S(1)}, bf16[256,2048]{1,0:T(8,128)(2,1)}, u32[]{:S(2)}) copy-start(bf16[256,2048]{1,0:T(8,128)(2,1)} %reduce-scatter.7.cloned.1.call-done) | copy-start | bytes 3145732
  565.0 105.9 %copy-start = (bf16[2048,256]{1,0:T(8,128)(2,1)S(1)}, bf16[2048,256]{1,0:T(8,128)(2,1)}, u32[]{:S(2)}) copy-start(bf16[2048,256]{1,0:T(8,128)(2,1)} %reduce-scatter.5.cloned.1.call-done) | copy-start | bytes 3145732
  670.9 8.1 %copy-start.2 = (bf16[256,2048]{1,0:T(8,128)(2,1)S(1)}, bf16[256,2048]{1,0:T(8,128)(2,1)}, u32[]{:S(2)}) copy-start(bf16[256,2048]{1,0:T(8,128)(2,1)} %get-tuple-element.183) | copy-start | bytes 3145732
Sparse Core Ops, SparseCore 0:
  10.5 49.2 all-gather.5
  61.7 28.0 all-gather.7
  91.8 54.2 all-gather.9
  147.8 54.2 all-gather.11
  349.1 67.7 reduce-scatter.4
  420.2 71.5 reduce-scatter.6
  520.5 43.4 reduce-scatter.10
  567.5 61.7 reduce-scatter.8

commit v4 on v3

--- a/solution.py
+++ b/solution.py
@@ -16,6 +16,7 @@
 VMEM_CAP = 60 * 1024 * 1024
 SUBS = 2
 WHOLE = pl.BlockSpec(memory_space=pltpu.VMEM)
+HBM = pl.BlockSpec(memory_space=pltpu.HBM)
 
 
 class Line:
@@ -56,7 +57,37 @@
     def _edge(self, way):
         return self.t < self.size - 1 if way == 0 else self.t > 0
 
-    def gather_step(self, way, k, part, buf, sems, first):
+    def hop(self, way, src, dst, sems):
+        return pltpu.make_async_remote_copy(
+            src_ref=src,
+            dst_ref=dst.at[way],
+            send_sem=sems[0].at[way],
+            recv_sem=sems[1].at[way],
+            device_id={"tensor": self.t + 1 if way == 0 else self.t - 1},
+            device_id_type=MESH,
+        )
+
+    def hop_start(self, srcs, dst, sems):
+        for way in (0, 1):
+
+            @pl.when(self._edge(way))
+            def _(way=way):
+                self.hop(way, srcs[way], dst, sems).start()
+
+    def hop_wait(self, srcs, dst, sems):
+        for way in (0, 1):
+
+            @pl.when(self._edge(1 - way))
+            def _(way=way):
+                self.hop(way, srcs[way], dst, sems).wait_recv()
+
+        for way in (0, 1):
+
+            @pl.when(self._edge(way))
+            def _(way=way):
+                self.hop(way, srcs[way], dst, sems).wait_send()
+
+    def gather_step(self, way, k, part, buf, sems, first, near=None):
         t, last = self.t, self.size - 1
         shard = t - k if way == 0 else t + k
         inside = (t >= k) if way == 0 else (t + k <= last)
@@ -64,7 +95,7 @@
         @pl.when(inside)
         def _():
             held = self._rows(buf, shard, part)
-            if k > 0:
+            if k > 1 or (k == 1 and near is None):
                 self._copy(held, buf, sems, way, shard, part).wait_recv()
 
             @pl.when(self._edge(way))
@@ -72,6 +103,8 @@
                 src = held
                 if k == 0 and first is not None:
                     src = first.at[pl.ds(part * self.sub, self.sub)]
+                if k == 1 and near is not None:
+                    src = near.at[way, pl.ds(part * self.sub, self.sub)]
                 self._copy(src, buf, sems, way, shard, part).start()
 
     def relay(self, k, part, buf, sems):
@@ -117,21 +150,26 @@
 
         lax.fori_loop(0, 2 * self.size - 1, visit, 0)
 
-    def scatter_step(self, way, j, part, terms, buf, sems):
+    def scatter_step(self, way, j, part, terms, buf, sems, ends=None):
         t, last = self.t, self.size - 1
         shard = last - j if way == 0 else j
         beyond = (shard > t) if way == 0 else (shard < t)
         starts = (t == 0) if way == 0 else (t == last)
-
-        @pl.when(beyond & starts)
+        step = min(32, self.sub)
+        if ends is None:
+            goes, stays = beyond, None
+        else:
+            goes = (shard > t + 1) if way == 0 else (shard < t - 1)
+            stays = (shard == t + 1) if way == 0 else (shard == t - 1)
+
+        @pl.when(goes & starts)
         def _():
             self._copy(self._rows(terms, shard, part), buf, sems, way, shard, part).start()
 
-        @pl.when(beyond & jnp.logical_not(starts))
+        @pl.when(goes & jnp.logical_not(starts))
         def _():
             held = self._rows(buf, shard, part)
             self._copy(held, buf, sems, way, shard, part).wait_recv()
-            step = min(32, self.sub)
 
             def add(i, carry):
                 rows = pl.ds(part * self.sub + i * step, step)
@@ -142,13 +180,34 @@
             lax.fori_loop(0, self.sub // step, add, 0)
             self._copy(held, buf, sems, way, shard, part).start()
 
-    def phase(self, gather=None, scatter=None, on_slot=None):
+        if stays is None:
+            return
+
+        @pl.when(stays & starts)
+        def _():
+            rows = pl.ds(part * self.sub, self.sub)
+            ends[way, rows, :] = terms[shard, rows, :]
+
+        @pl.when(stays & jnp.logical_not(starts))
+        def _():
+            held = self._rows(buf, shard, part)
+            self._copy(held, buf, sems, way, shard, part).wait_recv()
+
+            def add(i, carry):
+                rows = pl.ds(part * self.sub + i * step, step)
+                total = buf[shard, rows, :].astype(F32) + terms[shard, rows, :].astype(F32)
+                ends[way, rows, :] = total.astype(BF16)
+                return carry
+
+            lax.fori_loop(0, self.sub // step, add, 0)
+
+    def phase(self, gather=None, scatter=None, on_slot=None, near=None, ends=None):
         n = self.size
-        for k in range(n):
+        for k in range(0 if near is None else 1, n):
             for part in range(SUBS):
                 for way in (0, 1):
                     if gather is not None:
-                        self.gather_step(way, k, part, gather[0], gather[1], gather[2])
+                        self.gather_step(way, k, part, gather[0], gather[1], gather[2], near)
                     if scatter is not None:
                         if gather is None:
                             if k < n - 1:
@@ -160,7 +219,8 @@
                                 @pl.when(behind == b)
                                 def _(b=b, k=k, part=part, way=way):
                                     self.scatter_step(
-                                        way, k - 1 - b, part, scatter[0], scatter[1][way], scatter[2]
+                                        way, k - 1 - b, part, scatter[0], scatter[1][way],
+                                        scatter[2], ends,
                                     )
             if on_slot is not None:
                 on_slot(k)
@@ -182,9 +242,9 @@
         left = jnp.where(t < self.size - 1, bufs[1][t, rows, :].astype(F32), zero)
         return terms[t, rows, :].astype(F32) + right + left
 
-    def drain_gather(self, buf, sems):
+    def drain_gather(self, buf, sems, first=0):
         for way in (0, 1):
-            for k in range(self.size):
+            for k in range(first, self.size):
                 shard = self.t - k if way == 0 else self.t + k
                 inside = (self.t >= k) if way == 0 else (self.t + k <= self.size - 1)
 
@@ -194,11 +254,11 @@
                         held = self._rows(buf, shard, part)
                         self._copy(held, buf, sems, way, shard, part).wait_send()
 
-    def drain_scatter(self, bufs, sems):
+    def drain_scatter(self, bufs, sems, margin=0):
         for way in (0, 1):
             for j in range(self.size - 1):
                 shard = self.size - 1 - j if way == 0 else j
-                beyond = (shard > self.t) if way == 0 else (shard < self.t)
+                beyond = (shard > self.t + margin) if way == 0 else (shard < self.t - margin)
 
                 @pl.when(beyond)
                 def _(way=way, shard=shard):
@@ -332,15 +392,31 @@
 
 
 def middle_kernel(
-    size, terms, cot, tok, valid, vecs, c_out, gm_out, mid_out, stats,
-    right, left, gs, gr, ss, sr,
+    size, terms, cot, near, tok, valid, vecs, c_out, gm_out, mid_out, stats,
+    right, left, gs, gr, ss, sr, near_sem,
 ):
     line = Line(size, tok.shape[0])
     rows = tok.shape[0]
     step = min(32, rows)
     line.barrier()
-    line.phase(gather=(gm_out, (gs, gr), cot), scatter=(terms, (right, left), (ss, sr)))
+
+    def keep(way):
+        shard = line.t - 1 if way == 0 else line.t + 1
+        return pltpu.make_async_copy(near.at[way], gm_out.at[shard], near_sem.at[way])
+
+    def keep_all(act):
+        for way in (0, 1):
+
+            @pl.when(line._edge(1 - way))
+            def _(way=way):
+                act(keep(way))
+
+    keep_all(lambda copy: copy.start())
+    line.phase(
+        gather=(gm_out, (gs, gr), None), scatter=(terms, (right, left), (ss, sr)), near=near
+    )
     gm_out[pl.ds(line.t, 1)] = cot[...][None]
+    keep_all(lambda copy: copy.wait())
     line.own_wait((right, left), (ss, sr))
     stats[...] = jnp.zeros_like(stats)
 
@@ -357,11 +433,11 @@
         stats[16:24, :] += fold(ok * mid * mid)
 
     row_loop(rows, step, body)
-    line.drain_gather(gm_out, (gs, gr))
+    line.drain_gather(gm_out, (gs, gr), 1)
     line.drain_scatter((right, left), (ss, sr))
 
 
-def middle(terms, cot, tok, valid, vecs, size, cid):
+def middle(terms, cot, near, tok, valid, vecs, size, cid):
     rows, width = tok.shape
     full = (size, rows, width)
     return pl.pallas_call(
@@ -372,18 +448,19 @@
             jax.ShapeDtypeStruct((rows, width), F32),
             jax.ShapeDtypeStruct((24, width), F32),
         ),
-        in_specs=[WHOLE] * 5,
+        in_specs=[WHOLE, WHOLE, HBM, WHOLE, WHOLE, WHOLE],
         out_specs=(WHOLE,) * 4,
         scratch_shapes=[pltpu.VMEM(full, BF16), pltpu.VMEM(full, BF16)]
         + line_sems(size)
-        + line_sems(size),
+        + line_sems(size)
+        + [pltpu.SemaphoreType.DMA((2,))],
         compiler_params=params(cid),
         name="middle",
-    )(terms, cot, tok, valid, vecs)
+    )(terms, cot, near, tok, valid, vecs)
 
 
 def back_middle_kernel(
-    size, terms, mlp, gm, mid, valid, vecs, out_w, o_t, gz_out, gmid_out, y_out, stats,
+    size, terms, mlp, gm, mid, vecs, out_w, o_t, gz_out, gmid_out, ends, stats,
     go_out, grad_out, right, left, right2, left2, grad, ss, sr, ms, mr, gs, gr,
 ):
     line = Line(size, mid.shape[0])
@@ -438,25 +515,15 @@
         gather=(gz_out, (gs, gr), None),
         scatter=(mlp, (right2, left2), (ms, mr)),
         on_slot=on_slot,
+        ends=ends,
     )
     grad_out[...] = grad[...].astype(BF16)
-    line.own_wait((right2, left2), (ms, mr))
-
-    def tail(at):
-        out = line.own_sum(mlp, (right2, left2), at) + vecs[5:6, :]
-        y = mid[at, :] + out
-        y_out[at, :] = y.astype(BF16)
-        ok = valid[at, 0:1]
-        stats[32:40, :] += fold(ok * out * out)
-        stats[40:48, :] += fold(ok * y * y)
-
-    row_loop(rows, step, tail)
     line.drain_scatter((right, left), (ss, sr))
-    line.drain_scatter((right2, left2), (ms, mr))
+    line.drain_scatter((right2, left2), (ms, mr), 1)
     line.drain_gather(gz_out, (gs, gr))
 
 
-def back_middle(terms, mlp, gm, mid, valid, vecs, out_w, o_t, size, cid):
+def back_middle(terms, mlp, gm, mid, vecs, out_w, o_t, size, cid):
     rows, width = mid.shape
     local = out_w.shape[0]
     full = (size, rows, width)
@@ -465,12 +532,12 @@
         out_shape=(
             jax.ShapeDtypeStruct(full, BF16),
             jax.ShapeDtypeStruct((rows, width), F32),
-            jax.ShapeDtypeStruct((rows, width), BF16),
-            jax.ShapeDtypeStruct((48, width), F32),
+            jax.ShapeDtypeStruct((2, rows, width), BF16),
+            jax.ShapeDtypeStruct((32, width), F32),
             jax.ShapeDtypeStruct((size, rows, local), BF16),
             jax.ShapeDtypeStruct((local, width), BF16),
         ),
-        in_specs=[WHOLE] * 8,
+        in_specs=[WHOLE] * 7,
         out_specs=(WHOLE,) * 6,
         scratch_shapes=[pltpu.VMEM(full, BF16)] * 4
         + [pltpu.VMEM((local, width), F32)]
@@ -479,17 +546,45 @@
         + line_sems(size),
         compiler_params=params(cid),
         name="back_middle",
-    )(terms, mlp, gm, mid, valid, vecs, out_w, o_t)
-
-
-def finish_kernel(size, terms, tok, gmid, vecs, grad_out, stats, right, left, ss, sr):
+    )(terms, mlp, gm, mid, vecs, out_w, o_t)
+
+
+def finish_kernel(
+    size, terms, tok, gmid, mlp, landed, mid, valid, vecs, grad_out, y_out, stats,
+    right, left, own_mlp, ends, ss, sr, load_sem,
+):
     line = Line(size, tok.shape[0])
     rows = tok.shape[0]
     step = min(32, rows)
+    loads = [
+        pltpu.make_async_copy(mlp.at[line.t], own_mlp, load_sem.at[0]),
+        pltpu.make_async_copy(landed, ends, load_sem.at[1]),
+    ]
+    for load in loads:
+        load.start()
     line.barrier()
-    line.phase(scatter=(terms, (right, left), (ss, sr)))
+    stats[...] = jnp.zeros_like(stats)
+
+    def tail(at):
+        zero = jnp.zeros((), F32)
+        from_left = jnp.where(line.t > 0, ends[0, at, :].astype(F32), zero)
+        from_right = jnp.where(line.t < size - 1, ends[1, at, :].astype(F32), zero)
+        out = own_mlp[at, :].astype(F32) + from_left + from_right + vecs[5:6, :]
+        y = mid[at, :] + out
+        y_out[at, :] = y.astype(BF16)
+        ok = valid[at, 0:1]
+        stats[16:24, :] += fold(ok * out * out)
+        stats[24:32, :] += fold(ok * y * y)
+
+    for j in range(size - 1):
+        for piece in range(SUBS):
+            for way in (0, 1):
+                line.scatter_step(way, j, piece, terms, (right, left)[way], (ss, sr))
+        if j == 0:
+            for load in loads:
+                load.wait()
+            row_loop(rows, step, tail)
     line.own_wait((right, left), (ss, sr))
-    stats[...] = jnp.zeros_like(stats)
 
     def body(at):
         e = line.own_sum(terms, (right, left), at)
@@ -502,21 +597,25 @@
     line.drain_scatter((right, left), (ss, sr))
 
 
-def finish(terms, tok, gmid, vecs, size, cid):
+def finish(terms, tok, gmid, mlp, landed, mid, valid, vecs, size, cid):
     rows, width = tok.shape
     full = (size, rows, width)
     return pl.pallas_call(
         functools.partial(finish_kernel, size),
         out_shape=(
             jax.ShapeDtypeStruct((rows, width), F32),
-            jax.ShapeDtypeStruct((16, width), F32),
+            jax.ShapeDtypeStruct((rows, width), BF16),
+            jax.ShapeDtypeStruct((32, width), F32),
         ),
-        in_specs=[WHOLE] * 4,
-        out_specs=(WHOLE,) * 2,
-        scratch_shapes=[pltpu.VMEM(full, BF16)] * 2 + line_sems(size),
+        in_specs=[WHOLE, WHOLE, WHOLE, HBM, HBM, WHOLE, WHOLE, WHOLE],
+        out_specs=(WHOLE,) * 3,
+        scratch_shapes=[pltpu.VMEM(full, BF16)] * 2
+        + [pltpu.VMEM((rows, width), BF16), pltpu.VMEM((2, rows, width), BF16)]
+        + line_sems(size)
+        + [pltpu.SemaphoreType.DMA((2,))],
         compiler_params=params(cid),
         name="finish",
-    )(terms, tok, gmid, vecs)
+    )(terms, tok, gmid, mlp, landed, mid, valid, vecs)
 
 
 def reduce_small_kernel(n_dp, n_t, shared, blocks, out, land, sums, land2, s1, r1, s2, r2):
@@ -612,54 +711,114 @@
     return jnp.where(key_pos <= query_pos, scores, NEG)
 
 
-def attend_kernel(q, k, v, bar, out, out_t, log_totals):
-    value_cols = v[...].T
+def head_cols(part, h, heads):
+    return pl.ds(pl.multiple_of((part * heads + h) * HD, HD), HD)
+
+
+def front_kernel(
+    size, heads, a, weights, shift, bar, out_w, cot, qkv, out_t, log_totals, terms, near,
+    cols, mixed_all, gs, gr, load_sem,
+):
+    h = pl.program_id(0)
+    rows = cot.shape[0]
+    local = heads * HD
+    line = Line(size, rows)
+
+    def load(part):
+        at = pl.ds(part * local, local)
+        return pltpu.make_async_copy(weights.at[:, at], cols.at[:, at], load_sem.at[part])
+
+    @pl.when(h == 0)
+    def _():
+        for part in range(3):
+            load(part).start()
+        line.barrier()
+        line.hop_start((cot, cot), near, (gs, gr))
+        for part in range(3):
+            load(part).wait()
+            span = slice(part * local, (part + 1) * local)
+
+            def product(at, span=span):
+                qkv[at, span] = (dot(a[at, :], cols[:, span]) + shift[0:1, span]).astype(BF16)
+
+            row_loop(LEN, min(256, LEN), product)
+
+    at_q, at_k, at_v = (head_cols(part, h, heads) for part in range(3))
+    value_cols = qkv[:, at_v].T
     for block in range(LEN // BLOCK):
         first, keys = block * BLOCK, (block + 1) * BLOCK
-        scores = masked_scores(
-            q[first : first + BLOCK, :], k[0:keys, :], keys, first, bar[0:keys, 0:1]
-        )
+        here = slice(first, first + BLOCK)
+        scores = masked_scores(qkv[here, at_q], qkv[0:keys, at_k], keys, first, bar[0:keys, 0:1])
         top = jnp.max(scores, axis=0, keepdims=True)
         powers = jnp.exp(scores - top)
         total = jnp.sum(powers, axis=0, keepdims=True)
         shares = (powers * (1.0 / total)).astype(BF16)
         mixed = dot(value_cols[:, 0:keys], shares)
-        out[first : first + BLOCK, :] = mixed.T.astype(BF16)
-        out_t[:, first : first + BLOCK] = mixed.astype(BF16)
-        log_totals[0, :, first : first + BLOCK] = jnp.broadcast_to(top + jnp.log(total), (8, BLOCK))
-
-
-def attend(qkv, bar, heads):
-    def column(part):
-        return pl.BlockSpec((LEN, HD), lambda h: (0, part * heads + h))
-
+        mixed_all[here, head_cols(0, h, heads)] = mixed.T.astype(BF16)
+        out_t[:, here] = mixed.astype(BF16)
+        log_totals[0, :, here] = jnp.broadcast_to(top + jnp.log(total), (8, BLOCK))
+
+    @pl.when(h == heads - 1)
+    def _():
+        def project(at):
+            terms[at, :] = dot(mixed_all[at, :], out_w[...]).astype(BF16)
+
+        row_loop(LEN, min(256, LEN), project)
+        line.hop_wait((cot, cot), near, (gs, gr))
+
+
+def front(a, weights, shift, bar, out_w, cot, size, cid):
+    width, local3 = weights.shape
+    local = local3 // 3
+    heads = local // HD
     return pl.pallas_call(
-        attend_kernel,
+        functools.partial(front_kernel, size, heads),
         grid=(heads,),
         out_shape=(
-            jax.ShapeDtypeStruct((LEN, heads * HD), BF16),
-            jax.ShapeDtypeStruct((heads * HD, LEN), BF16),
+            jax.ShapeDtypeStruct((LEN, local3), BF16),
+            jax.ShapeDtypeStruct((local, LEN), BF16),
             jax.ShapeDtypeStruct((heads, 8, LEN), F32),
+            jax.ShapeDtypeStruct((LEN, width), BF16),
+            jax.ShapeDtypeStruct((2,) + cot.shape, BF16),
         ),
-        in_specs=[column(0), column(1), column(2), pl.BlockSpec((LEN, 128), lambda h: (0, 0))],
+        in_specs=[WHOLE, HBM, WHOLE, WHOLE, WHOLE, HBM],
         out_specs=(
-            pl.BlockSpec((LEN, HD), lambda h: (0, h)),
+            pl.BlockSpec((LEN, local3), lambda h: (0, 0)),
             pl.BlockSpec((HD, LEN), lambda h: (h, 0)),
             pl.BlockSpec((1, 8, LEN), lambda h: (h, 0, 0)),
+            pl.BlockSpec((LEN, width), lambda h: (0, 0)),
+            HBM,
         ),
-        compiler_params=params(),
-        name="attend",
-    )(qkv, qkv, qkv, bar)
-
-
-def attend_back_kernel(heads, q, k, v, go, bar, log_totals, out, sums, key_grad, value_grad):
+        scratch_shapes=[
+            pltpu.VMEM((width, local3), BF16),
+            pltpu.VMEM((LEN, local), BF16),
+            pltpu.SemaphoreType.DMA((2,)),
+            pltpu.SemaphoreType.DMA((2,)),
+            pltpu.SemaphoreType.DMA((3,)),
+        ],
+        compiler_params=params(cid),
+        name="front",
+    )(a, weights, shift, bar, out_w, cot)
+
+
+def attend_back_kernel(
+    size, heads, q, k, v, go, bar, log_totals, weights, ends, out, sums, terms, landed,
+    key_grad, value_grad, cols, gs, gr, load_sem,
+):
     h = pl.program_id(0)
+    line = Line(size, ends.shape[1])
+    srcs = (ends.at[0], ends.at[1])
+    load = pltpu.make_async_copy(weights, cols, load_sem.at[0])
+
+    @pl.when(h == 0)
+    def _():
+        load.start()
+        line.barrier()
+        line.hop_start(srcs, landed, (gs, gr))
+
     key_cols = k[...].T
     query_sum = jnp.zeros((1, HD), F32)
-    width = heads * HD
-    at_q = pl.ds(pl.multiple_of(h * HD, HD), HD)
-    at_k = pl.ds(pl.multiple_of(width + h * HD, HD), HD)
-    at_v = pl.ds(pl.multiple_of(2 * width + h * HD, HD), HD)
+    at_q, at_k, at_v = (head_cols(part, h, heads) for part in range(3))
     for block in range(LEN // BLOCK - 1, -1, -1):
         first, keys = block * BLOCK, (block + 1) * BLOCK
         here = slice(first, first + BLOCK)
@@ -686,31 +845,56 @@
     sums[0, 0:8, :] = jnp.broadcast_to(query_sum, (8, HD))
     sums[0, 8:16, :] = jnp.broadcast_to(value_sum, (8, HD))
 
-
-def attend_back(qkv, go, bar, log_totals, heads):
+    @pl.when(h == heads - 1)
+    def _():
+        load.wait()
+
+        def product(at):
+            terms[at, :] = dot_t(out[at, :], cols[...]).astype(BF16)
+
+        row_loop(LEN, min(256, LEN), product)
+        line.hop_wait(srcs, landed, (gs, gr))
+
+
+def attend_back(qkv, go, bar, log_totals, weights, ends, size, cid):
+    width, local3 = weights.shape
+    heads = local3 // 3 // HD
+
     def column(part):
         return pl.BlockSpec((LEN, HD), lambda h: (0, part * heads + h))
 
     return pl.pallas_call(
-        functools.partial(attend_back_kernel, heads),
+        functools.partial(attend_back_kernel, size, heads),
         grid=(heads,),
         out_shape=(
-            jax.ShapeDtypeStruct((LEN, 3 * heads * HD), BF16),
+            jax.ShapeDtypeStruct((LEN, local3), BF16),
             jax.ShapeDtypeStruct((heads, 16, HD), F32),
+            jax.ShapeDtypeStruct((LEN, width), BF16),
+            jax.ShapeDtypeStruct(ends.shape, BF16),
         ),
         in_specs=[
             column(0), column(1), column(2), column(0),
             pl.BlockSpec((LEN, 128), lambda h: (0, 0)),
             pl.BlockSpec((1, 8, LEN), lambda h: (h, 0, 0)),
+            HBM, HBM,
         ],
         out_specs=(
-            pl.BlockSpec((LEN, 3 * heads * HD), lambda h: (0, 0)),
+            pl.BlockSpec((LEN, local3), lambda h: (0, 0)),
             pl.BlockSpec((1, 16, HD), lambda h: (h, 0, 0)),
+            pl.BlockSpec((LEN, width), lambda h: (0, 0)),
+            HBM,
         ),
-        scratch_shapes=[pltpu.VMEM((LEN, HD), F32), pltpu.VMEM((LEN, HD), F32)],
-        compiler_params=params(),
+        scratch_shapes=[
+            pltpu.VMEM((LEN, HD), F32),
+            pltpu.VMEM((LEN, HD), F32),
+            pltpu.VMEM((width, local3), BF16),
+            pltpu.SemaphoreType.DMA((2,)),
+            pltpu.SemaphoreType.DMA((2,)),
+            pltpu.SemaphoreType.DMA((1,)),
+        ],
+        compiler_params=params(cid),
         name="attend_back",
-    )(qkv, qkv, qkv, go, bar, log_totals)
+    )(qkv, qkv, qkv, go, bar, log_totals, weights, ends)
 
 
 def gelu_both(u):
@@ -790,7 +974,6 @@
     rows, width = c_own.shape
     n_dp, units, part = down.shape
     full, wide = (size, rows, width), (size, rows, units)
-    hbm = pl.BlockSpec(memory_space=pltpu.HBM)
     return pl.pallas_call(
         functools.partial(hidden_kernel, n_dp, size),
         out_shape=(
@@ -801,8 +984,8 @@
             jax.ShapeDtypeStruct(full, BF16),
             jax.ShapeDtypeStruct((8, units), F32),
         ),
-        in_specs=[WHOLE, WHOLE, hbm, hbm, WHOLE],
-        out_specs=(WHOLE, hbm, hbm, hbm, hbm, WHOLE),
+        in_specs=[WHOLE, WHOLE, HBM, HBM, WHOLE],
+        out_specs=(WHOLE, HBM, HBM, HBM, HBM, WHOLE),
         scratch_shapes=[
             pltpu.VMEM((width, units), BF16),
             pltpu.VMEM((n_dp, units, part), BF16),
@@ -868,10 +1051,12 @@
     bar = jnp.broadcast_to(jnp.where(positions < length, 0.0, NEG)[:, None], (LEN, 128))
     gm_own = (cotangent.astype(F32) * valid_own[:, None]).astype(BF16)
 
-    qkv = (dot(a, qkv_full) + qkv_shift).astype(BF16)
-    attended, attended_t, log_totals = attend(qkv, bar, heads)
-    terms = dot(attended, out_full).astype(BF16).reshape(n_t, rows, width)
-    c_own, gm, mid, stats_a = middle(terms, gm_own, tokens, valid, vecs, n_t, 2)
+    shift = jnp.broadcast_to(qkv_shift, (8, 3 * local))
+    qkv, attended_t, log_totals, terms, near = front(
+        a, qkv_full, shift, bar, out_full, gm_own, n_t, 7
+    )
+    terms = terms.reshape(n_t, rows, width)
+    c_own, gm, mid, stats_a = middle(terms, gm_own, near, tokens, valid, vecs, n_t, 2)
     c, act, gu, mlp, back_terms, up_sums = hidden(
         c_own, gm, up_full, down_blocks, jnp.broadcast_to(up_shift, (8, units)), n_t, 6
     )
@@ -890,17 +1075,21 @@
     )
     down_out = lax.psum_scatter(down_grad, "dp", scatter_dimension=1, tiled=True)
     up_out = lax.psum_scatter(up_grad, "dp", scatter_dimension=0, tiled=True)
-    _, gmid, output, stats_b, go, out_grad = back_middle(
-        back_terms, mlp, gm_own, mid, valid, vecs, out_full, attended_t, n_t, 3
+    _, gmid, ends, stats_b, go, out_grad = back_middle(
+        back_terms, mlp, gm_own, mid, vecs, out_full, attended_t, n_t, 3
     )
     go, out_grad, down_out, up_out = lax.optimization_barrier((go, out_grad, down_out, up_out))
     out_out = lax.psum_scatter(out_grad, "dp", scatter_dimension=1, tiled=True)
-    gqkv, head_sums = attend_back(qkv, go.reshape(-1, local), bar, log_totals, heads)
+    gqkv, head_sums, last_terms, landed = attend_back(
+        qkv, go.reshape(-1, local), bar, log_totals, qkv_full, ends, n_t, 8
+    )
     qkv_grad = rows_dot(a, gqkv)
+    last_terms, qkv_grad = lax.optimization_barrier((last_terms, qkv_grad))
     qkv_out = lax.psum_scatter(qkv_grad, "dp", scatter_dimension=0, tiled=True)
     qkv_out = qkv_out.reshape(part, 3, local)
-    last_terms = dot_t(gqkv, qkv_full).astype(BF16).reshape(n_t, rows, width)
-    tokens_grad, stats_c = finish(last_terms, tokens, gmid, vecs, n_t, 4)
+    tokens_grad, output, stats_c = finish(
+        last_terms.reshape(n_t, rows, width), tokens, gmid, mlp, landed, mid, valid, vecs, n_t, 4
+    )
 
     def vec_sum(stats, i):
         return jnp.sum(stats[8 * i : 8 * i + 8], axis=0)
@@ -914,7 +1103,7 @@
     squares = jnp.stack(
         [
             jnp.sum(stats_a[0:8]), jnp.sum(stats_a[8:16]), jnp.sum(stats_a[16:24]),
-            jnp.sum(stats_b[32:40]), jnp.sum(stats_b[40:48]), jnp.sum(valid_own),
+            jnp.sum(stats_c[16:24]), jnp.sum(stats_c[24:32]), jnp.sum(valid_own),
         ]
     )
     vector_blocks = vectors.reshape(6, n_dp, part).transpose(1, 0, 2).reshape(n_dp, 6 * part)

time: 700 us -> 661 us (0.944)
  matrix products: 68.9 us -> 39.6 us
  Pallas kernels: 562 us -> 553 us
    pallas_call x2, Pallas kernels: 25.2 us -> 56.6 us  [the longest x1 31.3 us: front(): pl.pallas_call(functools.partial(front_kernel, size, heads), grid=(heads,...]
    dot_general x3 -> x0, matrix products: 29.3 us -> none  [the longest x2 18.2 us: dot(): return jnp.dot(a, b, preferred_element_type=F32)]
    pallas_call x1, Pallas kernels: 102 us -> 79.1 us  [middle(): pl.pallas_call(functools.partial(middle_kernel, size), out_shape=(jax.Sha...]
    pallas_call x1, Pallas kernels: 171 us -> 152 us  [back_middle(): pl.pallas_call(functools.partial(back_middle_kernel, size), out_shape=(ja...]
  transfers between devices with their start and end apart: 8 -> 8, of which waited for: 0 -> 0; matrix products, arithmetic and copies ran while one was open for 10% -> 7% of each run, Pallas kernels for 69% -> 71%
where the time goes in v4:
time: 661 us; the launch traced here: 653 us
  Pallas kernels  553 us (84%)
  matrix products  39.6 us (6%)
  local copies, waits for them, and re-layouts  30 us (5%)
  between operations  16.4 us (2%)
  other arithmetic  10.9 us (2%)
    pallas_call x1, Pallas kernels, back_middle(): pl.pallas_call(functools.partial(back_middle_kernel, size), out_shape=(ja...  152 us
    pallas_call x1, Pallas kernels, hidden(): pl.pallas_call(functools.partial(hidden_kernel, n_dp, size), out_shape=(j...  88.4 us
    pallas_call x1, Pallas kernels, first(): pl.pallas_call(functools.partial(first_kernel, n_dp, size, part), out_sha...  79.5 us
    pallas_call x1, Pallas kernels, finish(): pl.pallas_call(functools.partial(finish_kernel, size), out_shape=(jax.Sha...  79.5 us
    pallas_call x1, Pallas kernels, middle(): pl.pallas_call(functools.partial(middle_kernel, size), out_shape=(jax.Sha...  79.1 us
    dot_general x3, matrix products, rows_dot(): lax.dot_general(left, right, (((0,), (0,)), ((), ())), preferred_element_...  39.6 us
    pallas_call x1, Pallas kernels, front(): pl.pallas_call(functools.partial(front_kernel, size, heads), grid=(heads,...  31.3 us
    pallas_call x1, Pallas kernels, attend_back(): pl.pallas_call(functools.partial(attend_back_kernel, size, heads), grid=(...  25.3 us
  transfers between devices with their start and end apart: 8, of which 0 were waited for; matrix products, arithmetic and copies ran while one was open for 7% of the time, Pallas kernels for 71%

profile of v4, /device:TPU:0, one launch (start us, length us, event | category | flops | bytes accessed | tf_op | source)
XLA Modules:
  0.0 652.7 jit_solution(14874300714725384362)
XLA Ops:
  7.3 0.7 all-gather.8.cloned.1.call-update
  8.0 1.4 copy.65
  9.5 1.2 copy.66
  10.7 0.7 all-gather.10.cloned.1.call-update
  11.4 0.5 all-gather.12.cloned.1.call-update
  14.8 0.6 pad_bitcast_fusion.small
  15.4 79.5 %first.1 = (bf16[8,16,128]{2,1,0:T(8,128)(2,1)}, bf16[4,256,2048]{2,1,0:T(8,128)(2,1)}) custom-call(bf16[16,128]{1,0:T(8,128)(2,1)} %pad_bitcast_fusion.small, bf16[256,2048]{1,0:T(8,128)(2,1)} %tok.3), custom_call_target="tpu_custom_call" | custom-call | tf_op jit(solution)/shard_map/first/pallas_call | solution.py:375
  94.9 0.8 copy.94
  96.2 0.8 copy.70
  97.4 0.6 pad_convert_fusion.vecs
  98.1 1.2 multiply_convert_fusion.cot.gm
  99.3 1.0 broadcast_in_dim.42.bar
  100.3 0.6 broadcast_in_dim.21.shift
  100.9 31.3 %front.1 = (bf16[1024,1536]{1,0:T(8,128)(2,1)}, bf16[512,1024]{1,0:T(8,128)(2,1)}, f32[4,8,1024]{2,1,0:T(8,128)}, bf16[1024,2048]{1,0:T(8,128)(2,1)}, bf16[2,256,2048]{2,1,0:T(8,128)(2,1)}) custom-call(bf16[1024,2048]{1,0:T(8,128)(2,1)} %bitcast.96, bf16[2048,1536]{1,0:T(8,128)(2,1)} %all-gather.6.cloned.1.call-done.weights, ...), custom_call_target="tpu_custom_call" | custom-call | tf_op jit(solution)/shard_map/front/pallas_call | solution.py:774
  132.1 0.8 broadcast_in_dim.43.valid
  132.9 79.1 %middle.1 = (bf16[256,2048]{1,0:T(8,128)(2,1)}, bf16[4,256,2048]{2,1,0:T(8,128)(2,1)}, f32[256,2048]{1,0:T(8,128)}, f32[24,2048]{1,0:T(8,128)}) custom-call(bf16[4,256,2048]{2,1,0:T(8,128)(2,1)} %bitcast.95, bf16[256,2048]{1,0:T(8,128)(2,1)} %multiply_convert_fusion.cot.gm, bf16[2,256,2048]{2,1,0:T(8,128)(2,1)} %get-tuple-element.58.near, ...), custom_call_target="tpu_custom_call" | custom-call | tf_op jit(solution)/shard_map/middle/pallas_call | solution.py:443
  212.1 0.6 broadcast_in_dim.44.bias
  212.7 88.4 %hidden.1 = (bf16[4,256,2048]{2,1,0:T(8,128)(2,1)}, bf16[4,256,2048]{2,1,0:T(8,128)(2,1)}, bf16[4,256,2048]{2,1,0:T(8,128)(2,1)}, bf16[4,256,2048]{2,1,0:T(8,128...) custom-call(bf16[256,2048]{1,0:T(8,128)(2,1)} %get-tuple-element.59.c_own, ...), custom_call_target="tpu_custom_call" | custom-call | tf_op jit(solution)/shard_map/hidden/pallas_call | solution.py:977
  301.1 14.1 %bitcast_convert_fusion.1 = bf16[2048,2048]{1,0:T(8,128)(2,1)} fusion(bf16[4,256,2048]{2,1,0:T(8,128)(2,1)} %get-tuple-element.63, bf16[4,256,2048]{2,1,0:T(8,128)(2,1)} %get-tuple-element.60.gm), kind=kOutput, calls=%fused_computation.1 | convolution fusion | flops 8594128896 | bytes 16777216 | tf_op jit(solution)/shard_map/dot_general | solution.py:1067
  315.2 14.0 %bitcast_convert_fusion = bf16[2048,2048]{1,0:T(8,128)(2,1)} fusion(bf16[4,256,2048]{2,1,0:T(8,128)(2,1)} %get-tuple-element.64, bf16[4,256,2048]{2,1,0:T(8,128)(2,1)} %get-tuple-element.65), kind=kOutput, calls=%fused_computation | convolution fusion | flops 8594128896 | bytes 16777216 | tf_op jit(solution)/shard_map/dot_general | solution.py:1067
  329.2 0.5 reduce-scatter.7.cloned.1.call-update
  329.8 152.4 %back_middle.1 = (bf16[4,256,2048]{2,1,0:T(8,128)(2,1)}, f32[256,2048]{1,0:T(8,128)}, bf16[2,256,2048]{2,1,0:T(8,128)(2,1)}, f32[32,2048]{1,0:T(8,128)}, bf16[4,...) custom-call(bf16[4,256,2048]{2,1,0:T(8,128)(2,1)} %get-tuple-element.66.terms, ...), custom_call_target="tpu_custom_call" | custom-call | tf_op jit(solution)/shard_map/back_middle/pallas_call | solution.py:530
  482.6 25.3 %attend_back.1 = (bf16[1024,1536]{1,0:T(8,128)(2,1)}, f32[4,16,128]{2,1,0:T(8,128)}, bf16[1024,2048]{1,0:T(8,128)(2,1)}, bf16[2,256,2048]{2,1,0:T(8,128)(2,1)}) custom-call(bf16[1024,1536]{1,0:T(8,128)(2,1)} %get-tuple-element.56.q.k.v, bf16[1024,1536]{1,0:T(8,128)(2,1)} %get-tuple-element.56.q.k.v, bf16[1024,1536]{1,0:T(8,128)(2,1)} %get-tuple-element.56.q.k.v, ...), custom_call_target="tpu_custom_call" | custom-call | tf_op jit(solution)/shard_map/attend_back/pallas_call | solution.py:866
  508.0 11.5 %convolution_convert_fusion = bf16[2048,1536]{1,0:T(8,128)(2,1)} fusion(bf16[1024,2048]{1,0:T(8,128)(2,1)} %bitcast.97, bf16[1024,1536]{1,0:T(8,128)(2,1)} %get-tuple-element.78), kind=kOutput, calls=%fused_computation.2 | convolution fusion | flops 6445596672 | bytes 13631488 | tf_op jit(solution)/shard_map/dot_general | solution.py:1067
  519.5 0.6 fusion.3
  520.1 0.3 copy-done.5
  520.4 0.6 slice_reduce_fusion.2
  521.1 0.5 reshape.162
  521.6 0.8 copy.73
  522.6 0.8 slice_reduce_fusion.12
  523.6 79.5 %finish.1 = (f32[256,2048]{1,0:T(8,128)}, bf16[256,2048]{1,0:T(8,128)(2,1)}, f32[32,2048]{1,0:T(8,128)}) custom-call(bf16[4,256,2048]{2,1,0:T(8,128)(2,1)} %bitcast.98, bf16[256,2048]{1,0:T(8,128)(2,1)} %tok.3, f32[256,2048]{1,0:T(8,128)} %get-tuple-element.80.gmid, bf16[4,256,2048]{2,1,0:T(8,128)(2,1)} %get-tuple-element.67.mlp, ...), custom_call_target="tpu_custom_call" | custom-call | tf_op jit(solution)/shard_map/finish/pallas_call | solution.py:603
  603.1 1.7 slice_reduce_fusion
  604.8 4.0 stack.66
  608.9 0.7 copy.93
  609.5 17.2 %reduce_small.1 = f32[24,128]{1,0:T(8,128)} custom-call(f32[8,24,128]{2,1,0:T(8,128)} %bitcast.104), custom_call_target="tpu_custom_call" | custom-call | tf_op jit(solution)/shard_map/reduce_small/pallas_call | solution.py:675
  626.8 1.3 slice.174
  628.0 0.7 slice_reduce_fusion.13
  628.7 0.7 reshape.166
  629.4 1.4 slice_bitcast_fusion.6
  630.9 0.6 copy.78
  631.6 1.6 convert_element_type.92
  633.2 1.5 convert_element_type.93
  635.3 1.2 fusion.2
  636.5 1.8 convert_element_type.91
  638.3 1.4 copy.76
  639.7 1.6 copy.77
  641.3 1.0 copy.111
  642.3 3.1 copy.112
  (107 shorter events, 4.3 us)
Async XLA Ops:
  7.2 5.5 copy-start.7
  7.2 5.6 copy-start.8
  7.2 5.9 copy-start.9
  7.2 6.1 copy-start.10
  7.2 6.3 copy-start.11
  7.2 6.5 copy-start.12
  7.2 6.7 %copy-start.13 = (bf16[256]{0:T(256)(128)(2,1)S(1)}, bf16[256]{0:T(256)(128)(2,1)}, u32[]{:S(2)}) copy-start(bf16[256]{0:T(256)(128)(2,1)} %param.24) | copy-start | bytes 1540
  7.3 6.9 %copy-start.14 = (bf16[256]{0:T(256)(128)(2,1)S(1)}, bf16[256]{0:T(256)(128)(2,1)}, u32[]{:S(2)}) copy-start(bf16[256]{0:T(256)(128)(2,1)} %param.28) | copy-start | bytes 1540
  7.3 92.0 %all-gather.8.cloned.1.call-start = ((), (), s32[]{:S(2)}) async-start(), calls=%async_computation.5 | async-start | bytes 2359296 | tf_op jit(solution)/shard_map/all_gather | solution.py:1043
  8.0 91.3 %all-gather.6.cloned.1.call-start = ((), (), s32[]{:S(2)}) async-start(), calls=%async_computation.4 | async-start | bytes 7077888 | tf_op jit(solution)/shard_map/all_gather | solution.py:1042
  9.5 88.6 %copy-start.3 = (bf16[256,2048]{1,0:T(8,128)(2,1)S(1)}, bf16[256,2048]{1,0:T(8,128)(2,1)}, u32[]{:S(2)}) copy-start(bf16[256,2048]{1,0:T(8,128)(2,1)} %param.29) | copy-start | bytes 3145732
  10.6 201.4 %all-gather.10.cloned.1.call-start = ((), (), s32[]{:S(2)}) async-start(), calls=%async_computation.6 | async-start | bytes 9437184 | tf_op jit(solution)/shard_map/all_gather | solution.py:1044
  11.4 200.7 %all-gather.12.cloned.1.call-start = ((), (), s32[]{:S(2)}) async-start(), calls=%async_computation.11 | async-start | bytes 9437184 | tf_op jit(solution)/shard_map/all_gather | solution.py:1045
  12.0 470.3 %reduce-scatter.5.cloned.1.call-start = ((), (), s32[]{:S(2)}) async-start(), calls=%async_computation.7 | async-start | bytes 9437184 | tf_op jit(solution)/shard_map/reduce_scatter | solution.py:1076
  329.2 153.1 %reduce-scatter.7.cloned.1.call-start = ((), (), s32[]{:S(2)}) async-start(), calls=%async_computation.8 | async-start | bytes 9437184 | tf_op jit(solution)/shard_map/reduce_scatter | solution.py:1077
  329.8 306.7 %reduce-scatter.11.cloned.1.call-start = ((), (), s32[]{:S(2)}) async-start(), calls=%async_computation.10 | async-start | bytes 2359296 | tf_op jit(solution)/shard_map/reduce_scatter | solution.py:1082
  482.4 155.9 %reduce-scatter.9.cloned.1.call-start = ((), (), s32[]{:S(2)}) async-start(), calls=%async_computation.9 | async-start | bytes 7077888 | tf_op jit(solution)/shard_map/reduce_scatter | solution.py:1088
  519.5 0.9 copy-start.5
  519.5 1.6 copy-start.6
  519.5 3.0 copy-start.4
  523.6 107.9 %copy-start.1 = (bf16[256,2048]{1,0:T(8,128)(2,1)S(1)}, bf16[256,2048]{1,0:T(8,128)(2,1)}, u32[]{:S(2)}) copy-start(bf16[256,2048]{1,0:T(8,128)(2,1)} %reduce-scatter.7.cloned.1.call-done) | copy-start | bytes 3145732
  603.1 30.0 %copy-start = (bf16[2048,256]{1,0:T(8,128)(2,1)S(1)}, bf16[2048,256]{1,0:T(8,128)(2,1)}, u32[]{:S(2)}) copy-start(bf16[2048,256]{1,0:T(8,128)(2,1)} %reduce-scatter.5.cloned.1.call-done) | copy-start | bytes 3145732
  633.1 8.1 %copy-start.2 = (bf16[256,2048]{1,0:T(8,128)(2,1)S(1)}, bf16[256,2048]{1,0:T(8,128)(2,1)}, u32[]{:S(2)}) copy-start(bf16[256,2048]{1,0:T(8,128)(2,1)} %get-tuple-element.197) | copy-start | bytes 3145732
Sparse Core Ops, SparseCore 0:
  9.9 31.0 all-gather.7
  43.5 45.4 all-gather.5
  90.9 54.2 all-gather.9
  146.9 54.2 all-gather.11
  329.3 67.8 reduce-scatter.4
  400.5 71.4 reduce-scatter.6
  482.5 39.2 reduce-scatter.10
  525.1 61.7 reduce-scatter.8

commit v5 on v4

--- a/solution.py
+++ b/solution.py
@@ -150,7 +150,7 @@
 
         lax.fori_loop(0, 2 * self.size - 1, visit, 0)
 
-    def scatter_step(self, way, j, part, terms, buf, sems, ends=None):
+    def scatter_step(self, way, j, part, terms, buf, sems, ends=None, early=None):
         t, last = self.t, self.size - 1
         shard = last - j if way == 0 else j
         beyond = (shard > t) if way == 0 else (shard < t)
@@ -162,14 +162,32 @@
             goes = (shard > t + 1) if way == 0 else (shard < t - 1)
             stays = (shard == t + 1) if way == 0 else (shard == t - 1)
 
-        @pl.when(goes & starts)
-        def _():
-            self._copy(self._rows(terms, shard, part), buf, sems, way, shard, part).start()
+        second = (t == 1) if way == 0 else (t == last - 1)
+        done = early is not None and j == 0
+
+        if not done:
+
+            @pl.when(goes & starts)
+            def _():
+                self._copy(self._rows(terms, shard, part), buf, sems, way, shard, part).start()
 
         @pl.when(goes & jnp.logical_not(starts))
         def _():
             held = self._rows(buf, shard, part)
-            self._copy(held, buf, sems, way, shard, part).wait_recv()
+            arrival = self._copy(held, buf, sems, way, shard, part)
+            if not done:
+                arrival.wait_recv()
+            else:
+
+                @pl.when(jnp.logical_not(second))
+                def _():
+                    arrival.wait_recv()
+
+                if part == 0:
+
+                    @pl.when(second)
+                    def _():
+                        early[way].wait()
 
             def add(i, carry):
                 rows = pl.ds(part * self.sub + i * step, step)
@@ -254,11 +272,13 @@
                         held = self._rows(buf, shard, part)
                         self._copy(held, buf, sems, way, shard, part).wait_send()
 
-    def drain_scatter(self, bufs, sems, margin=0):
+    def drain_scatter(self, bufs, sems, margin=0, early=False):
         for way in (0, 1):
             for j in range(self.size - 1):
                 shard = self.size - 1 - j if way == 0 else j
                 beyond = (shard > self.t + margin) if way == 0 else (shard < self.t - margin)
+                if early and j == 0:
+                    beyond = beyond & self._edge(1 - way)
 
                 @pl.when(beyond)
                 def _(way=way, shard=shard):
@@ -460,14 +480,29 @@
 
 
 def back_middle_kernel(
-    size, terms, mlp, gm, mid, vecs, out_w, o_t, gz_out, gmid_out, ends, stats,
-    go_out, grad_out, right, left, right2, left2, grad, ss, sr, ms, mr, gs, gr,
+    size, terms, landed, mlp, gm, mid, vecs, out_w, o_t, gz_out, gmid_out, ends, stats,
+    go_out, grad_out, right, left, right2, left2, grad, ss, sr, ms, mr, gs, gr, early_sem,
 ):
     line = Line(size, mid.shape[0])
     rows = mid.shape[0]
     step = min(32, rows)
+    early = (
+        pltpu.make_async_copy(landed.at[0], right.at[size - 1], early_sem.at[0]),
+        pltpu.make_async_copy(landed.at[1], left.at[0], early_sem.at[1]),
+    )
+    for copy, holder in zip(early, (1, size - 2)):
+
+        @pl.when(line.t == holder)
+        def _(copy=copy):
+            copy.start()
+
     line.barrier()
-    line.phase(scatter=(terms, (right, left), (ss, sr)))
+    for j in range(size - 1):
+        for piece in range(SUBS):
+            for way in (0, 1):
+                line.scatter_step(
+                    way, j, piece, terms, (right, left)[way], (ss, sr), None, early
+                )
     line.own_wait((right, left), (ss, sr))
     stats[...] = jnp.zeros_like(stats)
 
@@ -518,12 +553,12 @@
         ends=ends,
     )
     grad_out[...] = grad[...].astype(BF16)
-    line.drain_scatter((right, left), (ss, sr))
+    line.drain_scatter((right, left), (ss, sr), 0, True)
     line.drain_scatter((right2, left2), (ms, mr), 1)
     line.drain_gather(gz_out, (gs, gr))
 
 
-def back_middle(terms, mlp, gm, mid, vecs, out_w, o_t, size, cid):
+def back_middle(terms, landed, mlp, gm, mid, vecs, out_w, o_t, size, cid):
     rows, width = mid.shape
     local = out_w.shape[0]
     full = (size, rows, width)
@@ -537,16 +572,17 @@
             jax.ShapeDtypeStruct((size, rows, local), BF16),
             jax.ShapeDtypeStruct((local, width), BF16),
         ),
-        in_specs=[WHOLE] * 7,
+        in_specs=[WHOLE, HBM] + [WHOLE] * 6,
         out_specs=(WHOLE,) * 6,
         scratch_shapes=[pltpu.VMEM(full, BF16)] * 4
         + [pltpu.VMEM((local, width), F32)]
         + line_sems(size)
         + line_sems(size)
-        + line_sems(size),
+        + line_sems(size)
+        + [pltpu.SemaphoreType.DMA((2,))],
         compiler_params=params(cid),
         name="back_middle",
-    )(terms, mlp, gm, mid, vecs, out_w, o_t)
+    )(terms, landed, mlp, gm, mid, vecs, out_w, o_t)
 
 
 def finish_kernel(
@@ -1001,6 +1037,92 @@
     )(c_own, gm, up, down, bias)
 
 
+def cross(left, right):
+    return lax.dot_general(left, right, (((0,), (0,)), ((), ())), preferred_element_type=F32)
+
+
+def products_kernel(
+    size, steps, act, gm, c, gu_in, terms, down_out, up_out, landed, gu, gs, gr, load_sem
+):
+    i = pl.program_id(0)
+    last = size - 1
+    line = Line(size, terms.shape[1])
+    load = pltpu.make_async_copy(gu_in, gu, load_sem.at[0])
+    hops = [
+        (line.t == sender, line.t == taker, line.hop(way, terms.at[shard], landed, (gs, gr)))
+        for way, sender, taker, shard in ((0, 0, 1, last), (1, last, last - 1, 0))
+    ]
+
+    @pl.when(i == 0)
+    def _():
+        load.start()
+        line.barrier()
+        for sends, _, copy in hops:
+
+            @pl.when(sends)
+            def _(copy=copy):
+                copy.start()
+
+    @pl.when(i < steps)
+    def _():
+        down_out[...] = cross(act[...], gm[...]).astype(BF16)
+
+    @pl.when(i == steps)
+    def _():
+        load.wait()
+
+    @pl.when(i >= steps)
+    def _():
+        up_out[...] = cross(c[...], gu[...]).astype(BF16)
+
+    @pl.when(i == pl.num_programs(0) - 1)
+    def _():
+        for sends, takes, copy in hops:
+
+            @pl.when(sends)
+            def _(copy=copy):
+                copy.wait_send()
+
+            @pl.when(takes)
+            def _(copy=copy):
+                copy.wait_recv()
+
+
+def products(act, gm, c, gu, terms, size, cid):
+    rows, units = act.shape
+    width = gm.shape[1]
+    steps, more = units // BLOCK, width // BLOCK
+    return pl.pallas_call(
+        functools.partial(products_kernel, size, steps),
+        grid=(steps + more,),
+        out_shape=(
+            jax.ShapeDtypeStruct((units, width), BF16),
+            jax.ShapeDtypeStruct((width, units), BF16),
+            jax.ShapeDtypeStruct((2,) + terms.shape[1:], BF16),
+        ),
+        in_specs=[
+            pl.BlockSpec((rows, BLOCK), lambda i: (0, jnp.minimum(i, steps - 1))),
+            WHOLE,
+            pl.BlockSpec((rows, BLOCK), lambda i: (0, jnp.maximum(i - steps, 0))),
+            HBM,
+            HBM,
+        ],
+        out_specs=(
+            pl.BlockSpec((BLOCK, width), lambda i: (jnp.minimum(i, steps - 1), 0)),
+            pl.BlockSpec((BLOCK, units), lambda i: (jnp.maximum(i - steps, 0), 0)),
+            HBM,
+        ),
+        scratch_shapes=[
+            pltpu.VMEM((rows, units), BF16),
+            pltpu.SemaphoreType.DMA((2,)),
+            pltpu.SemaphoreType.DMA((2,)),
+            pltpu.SemaphoreType.DMA((1,)),
+        ],
+        compiler_params=params(cid),
+        name="products",
+    )(act, gm, c, gu, terms)
+
+
 def pad_to(x, count):
     return jnp.pad(x, ((0, 0), (0, count - x.shape[1])))
 
@@ -1068,15 +1190,11 @@
             left, right, (((0,), (0,)), ((), ())), preferred_element_type=F32
         ).astype(BF16)
 
-    down_grad = rows_dot(act, gm)
-    up_grad = rows_dot(c, gu)
-    back_terms, mlp, down_grad, up_grad = lax.optimization_barrier(
-        (back_terms, mlp, down_grad, up_grad)
-    )
+    down_grad, up_grad, early = products(act, gm, c, gu, back_terms, n_t, 9)
     down_out = lax.psum_scatter(down_grad, "dp", scatter_dimension=1, tiled=True)
     up_out = lax.psum_scatter(up_grad, "dp", scatter_dimension=0, tiled=True)
     _, gmid, ends, stats_b, go, out_grad = back_middle(
-        back_terms, mlp, gm_own, mid, vecs, out_full, attended_t, n_t, 3
+        back_terms, early, mlp, gm_own, mid, vecs, out_full, attended_t, n_t, 3
     )
     go, out_grad, down_out, up_out = lax.optimization_barrier((go, out_grad, down_out, up_out))
     out_out = lax.psum_scatter(out_grad, "dp", scatter_dimension=1, tiled=True)
@@ -1100,15 +1218,21 @@
             vec_sum(stats_b, 0), vec_sum(stats_b, 1), vec_sum(stats_b, 3),
         ]
     )
-    squares = jnp.stack(
+    def squares(stats, i):
+        return jnp.sum(stats[8 * i : 8 * i + 8].reshape(8, n_dp, part), axis=(0, 1))
+
+    sums = jnp.concatenate(
         [
-            jnp.sum(stats_a[0:8]), jnp.sum(stats_a[8:16]), jnp.sum(stats_a[16:24]),
-            jnp.sum(stats_c[16:24]), jnp.sum(stats_c[24:32]), jnp.sum(valid_own),
+            squares(stats_a, 0), squares(stats_a, 1), squares(stats_a, 2),
+            squares(stats_c, 2), squares(stats_c, 3),
         ]
     )
+    count = jnp.clip(length - t * rows, 0, rows).astype(F32)
     vector_blocks = vectors.reshape(6, n_dp, part).transpose(1, 0, 2).reshape(n_dp, 6 * part)
-    scalar_blocks = jnp.broadcast_to(squares[None], (n_dp, 6))
-    top = jnp.concatenate([vector_blocks, scalar_blocks], axis=1)
+    top = jnp.concatenate(
+        [vector_blocks, jnp.broadcast_to(sums[None], (n_dp, 5 * part)), jnp.full((n_dp, 1), count)],
+        axis=1,
+    )
     top_len = -(-top.shape[1] // 1024) * 1024
     up_blocks = jnp.sum(up_sums, axis=0).reshape(units // 16, n_dp, 16 // n_dp)
     up_blocks = up_blocks.transpose(1, 0, 2).reshape(n_dp, units // n_dp)
@@ -1121,8 +1245,8 @@
     blocks = blocks.reshape(n_dp, (top_len + low_len) // 128, 128)
     reduced = reduce_small(blocks, top_len // 128, n_dp, n_t, 5).reshape(-1)
     outs = [reduced[i * part : (i + 1) * part] for i in range(6)]
-    totals = reduced[6 * part : 6 * part + 6]
-    stream_rms = jnp.sqrt(totals[:5] / (totals[5] * width))
+    totals = jnp.sum(reduced[6 * part : 11 * part].reshape(5, part), axis=1)
+    stream_rms = jnp.sqrt(totals / (reduced[11 * part] * width))
     at = top_len
     up_bias_out = reduced[at : at + units // n_dp].reshape(up_bias.shape)
     at += units // n_dp

time: 661 us -> 636 us (0.962); the launches traced: 653 us -> 635 us
  matrix products: 39.6 us -> 11.6 us
  waiting for transfers between devices: 2.56 us -> 12.8 us
    dot_general x3 -> x1, matrix products: 39.6 us -> 11.6 us  [rows_dot(): lax.dot_general(left, right, (((0,), (0,)), ((), ())), preferred_element_...]
    pallas_call x0 -> x1, Pallas kernels: none -> 25.9 us  [products(): pl.pallas_call(functools.partial(products_kernel, size, steps), grid=(ste...]
    pallas_call x1, Pallas kernels: 152 us -> 133 us  [back_middle(): pl.pallas_call(functools.partial(back_middle_kernel, size), out_shape=(ja...]
    reduce_scatter x1, waiting for transfers between devices: 0.02 us -> 10.3 us  [shards(): up_out = lax.psum_scatter(up_grad, 'dp', scatter_dimension=0, tiled=True)]
  transfers between devices with their start and end apart: 8 -> 8, of which waited for: 0 -> 1; matrix products, arithmetic and copies ran while one was open for 7% -> 6% of each run, Pallas kernels for 71% -> 70%
where the time goes in v5:
time: 636 us; the launch traced here: 635 us
  Pallas kernels  558 us (88%)
  local copies, waits for them, and re-layouts  25.8 us (4%)
  between operations  16.1 us (3%)
  waiting for transfers between devices  12.8 us (2%)
  matrix products  11.6 us (2%)
  other arithmetic  9.62 us (2%)
    pallas_call x1, Pallas kernels, back_middle(): pl.pallas_call(functools.partial(back_middle_kernel, size), out_shape=(ja...  133 us
    pallas_call x1, Pallas kernels, hidden(): pl.pallas_call(functools.partial(hidden_kernel, n_dp, size), out_shape=(j...  88.4 us
    pallas_call x1, Pallas kernels, first(): pl.pallas_call(functools.partial(first_kernel, n_dp, size, part), out_sha...  79.5 us
    pallas_call x1, Pallas kernels, middle(): pl.pallas_call(functools.partial(middle_kernel, size), out_shape=(jax.Sha...  79.1 us
    pallas_call x1, Pallas kernels, finish(): pl.pallas_call(functools.partial(finish_kernel, size), out_shape=(jax.Sha...  73.6 us
    pallas_call x1, Pallas kernels, front(): pl.pallas_call(functools.partial(front_kernel, size, heads), grid=(heads,...  31.3 us
    pallas_call x1, Pallas kernels, attend_back(): pl.pallas_call(functools.partial(attend_back_kernel, size, heads), grid=(...  30.9 us
    pallas_call x1, Pallas kernels, products(): pl.pallas_call(functools.partial(products_kernel, size, steps), grid=(ste...  25.9 us
  transfers between devices with their start and end apart: 8, of which 1 were waited for; matrix products, arithmetic and copies ran while one was open for 6% of the time, Pallas kernels for 70%

profile of v5, /device:TPU:0, one launch (start us, length us, event | category | flops | bytes accessed | tf_op | source)
XLA Modules:
  0.0 634.8 jit_solution(17745991780428381053)
XLA Ops:
  7.3 0.7 all-gather.8.cloned.1.call-update
  8.0 1.4 copy.72
  9.5 1.2 copy.73
  10.7 0.7 all-gather.10.cloned.1.call-update
  11.4 0.5 all-gather.12.cloned.1.call-update
  14.8 0.6 pad_bitcast_fusion.small
  15.4 79.5 %first.1 = (bf16[8,16,128]{2,1,0:T(8,128)(2,1)}, bf16[4,256,2048]{2,1,0:T(8,128)(2,1)}) custom-call(bf16[16,128]{1,0:T(8,128)(2,1)} %pad_bitcast_fusion.small, bf16[256,2048]{1,0:T(8,128)(2,1)} %tok.3), custom_call_target="tpu_custom_call" | custom-call | tf_op jit(solution)/shard_map/first/pallas_call | solution.py:395
  94.9 0.8 copy.97
  96.2 0.8 copy.77
  97.0 0.3 reshape.195
  97.4 0.6 pad_convert_fusion.vecs
  98.0 1.2 multiply_convert_fusion.cot.gm
  99.3 1.0 broadcast_in_dim.45.bar
  100.3 0.6 broadcast_in_dim.42.shift
  100.9 31.3 %front.1 = (bf16[1024,1536]{1,0:T(8,128)(2,1)}, bf16[512,1024]{1,0:T(8,128)(2,1)}, f32[4,8,1024]{2,1,0:T(8,128)}, bf16[1024,2048]{1,0:T(8,128)(2,1)}, bf16[2,256,2048]{2,1,0:T(8,128)(2,1)}) custom-call(bf16[1024,2048]{1,0:T(8,128)(2,1)} %bitcast.91, bf16[2048,1536]{1,0:T(8,128)(2,1)} %all-gather.6.cloned.1.call-done.weights, ...), custom_call_target="tpu_custom_call" | custom-call | tf_op jit(solution)/shard_map/front/pallas_call | solution.py:810
  132.1 0.8 broadcast_in_dim.46.valid
  132.9 79.1 %middle.1 = (bf16[256,2048]{1,0:T(8,128)(2,1)}, bf16[4,256,2048]{2,1,0:T(8,128)(2,1)}, f32[256,2048]{1,0:T(8,128)}, f32[24,2048]{1,0:T(8,128)}) custom-call(bf16[4,256,2048]{2,1,0:T(8,128)(2,1)} %bitcast.90, bf16[256,2048]{1,0:T(8,128)(2,1)} %multiply_convert_fusion.cot.gm, bf16[2,256,2048]{2,1,0:T(8,128)(2,1)} %get-tuple-element.57.near, ...), custom_call_target="tpu_custom_call" | custom-call | tf_op jit(solution)/shard_map/middle/pallas_call | solution.py:463
  212.0 0.6 broadcast_in_dim.47.bias
  212.7 88.4 %hidden.1 = (bf16[4,256,2048]{2,1,0:T(8,128)(2,1)}, bf16[4,256,2048]{2,1,0:T(8,128)(2,1)}, bf16[4,256,2048]{2,1,0:T(8,128)(2,1)}, bf16[4,256,2048]{2,1,0:T(8,128...) custom-call(bf16[256,2048]{1,0:T(8,128)(2,1)} %get-tuple-element.58.c_own, ...), custom_call_target="tpu_custom_call" | custom-call | tf_op jit(solution)/shard_map/hidden/pallas_call | solution.py:1013
  301.0 25.9 %products.1 = (bf16[2048,2048]{1,0:T(8,128)(2,1)}, bf16[2048,2048]{1,0:T(8,128)(2,1)}, bf16[2,256,2048]{2,1,0:T(8,128)(2,1)}) custom-call(bf16[1024,2048]{1,0:T(8,128)(2,1)} %bitcast.88, bf16[1024,2048]{1,0:T(8,128)(2,1)} %bitcast.84, bf16[1024,2048]{1,0:T(8,128)(2,1)} %bitcast.87, bf16[1024,2048]{1,0:T(8,128)(2,1)} %bitcast.89, ...), custom_call_target="tpu_custom_call" | custom-call | tf_op jit(solution)/shard_map/products/pallas_call | solution.py:1095
  327.0 0.5 reduce-scatter.7.cloned.1.call-update
  327.6 133.1 %back_middle.1 = (bf16[4,256,2048]{2,1,0:T(8,128)(2,1)}, f32[256,2048]{1,0:T(8,128)}, bf16[2,256,2048]{2,1,0:T(8,128)(2,1)}, f32[32,2048]{1,0:T(8,128)}, bf16[4,...) custom-call(bf16[4,256,2048]{2,1,0:T(8,128)(2,1)} %get-tuple-element.60.terms, ...), custom_call_target="tpu_custom_call" | custom-call | tf_op jit(solution)/shard_map/back_middle/pallas_call | solution.py:565
  460.8 10.3 %reduce-scatter.7.cloned.1.call-done = bf16[256,2048]{1,0:T(8,128)(2,1)} async-done(((bf16[2048,2048]{1,0:T(8,128)(2,1)}), bf16[256,2048]{1,0:T(8,128)(2,1)}) %reduce-scatter.7.cloned.1.call-update) | async-done | bytes 1048592 | tf_op jit(solution)/shard_map/reduce_scatter | solution.py:1195
  471.4 30.9 %attend_back.1 = (bf16[1024,1536]{1,0:T(8,128)(2,1)}, f32[4,16,128]{2,1,0:T(8,128)}, bf16[1024,2048]{1,0:T(8,128)(2,1)}, bf16[2,256,2048]{2,1,0:T(8,128)(2,1)}) custom-call(bf16[1024,1536]{1,0:T(8,128)(2,1)} %get-tuple-element.55.q.k.v, bf16[1024,1536]{1,0:T(8,128)(2,1)} %get-tuple-element.55.q.k.v, bf16[1024,1536]{1,0:T(8,128)(2,1)} %get-tuple-element.55.q.k.v, ...), custom_call_target="tpu_custom_call" | custom-call | tf_op jit(solution)/shard_map/attend_back/pallas_call | solution.py:902
  502.3 11.6 %convolution_convert_fusion = bf16[2048,1536]{1,0:T(8,128)(2,1)} fusion(bf16[1024,2048]{1,0:T(8,128)(2,1)} %bitcast.92, bf16[1024,1536]{1,0:T(8,128)(2,1)} %get-tuple-element.76), kind=kOutput, calls=%fused_computation | convolution fusion | flops 6445596672 | bytes 13631488 | tf_op jit(solution)/shard_map/dot_general | solution.py:1189
  513.9 0.9 copy-done.6
  515.0 0.5 reshape.188
  515.4 0.8 copy.78
  516.5 0.8 slice_reduce_fusion.13
  517.5 73.6 %finish.1 = (f32[256,2048]{1,0:T(8,128)}, bf16[256,2048]{1,0:T(8,128)(2,1)}, f32[32,2048]{1,0:T(8,128)}) custom-call(bf16[4,256,2048]{2,1,0:T(8,128)(2,1)} %bitcast.93, bf16[256,2048]{1,0:T(8,128)(2,1)} %tok.3, f32[256,2048]{1,0:T(8,128)} %get-tuple-element.78.gmid, bf16[4,256,2048]{2,1,0:T(8,128)(2,1)} %get-tuple-element.65.mlp, ...), custom_call_target="tpu_custom_call" | custom-call | tf_op jit(solution)/shard_map/finish/pallas_call | solution.py:639
  591.2 1.1 slice_reduce_fusion
  592.5 0.7 copy.96
  593.2 16.6 %reduce_small.1 = f32[32,128]{1,0:T(8,128)} custom-call(f32[8,32,128]{2,1,0:T(8,128)} %bitcast.99), custom_call_target="tpu_custom_call" | custom-call | tf_op jit(solution)/shard_map/reduce_small/pallas_call | solution.py:711
  609.8 1.2 slice.171
  611.0 0.8 slice_reduce_fusion.11
  612.0 0.7 slice_reduce_fusion.14
  612.7 0.7 reshape.192
  613.4 1.4 slice_bitcast_fusion.6
  614.9 0.6 copy.83
  615.6 1.6 convert_element_type.88
  617.1 1.5 convert_element_type.89
  619.3 0.5 divide_sqrt_fusion
  619.8 1.9 convert_element_type.87
  621.7 1.4 copy.81
  623.1 1.6 copy.82
  624.7 1.0 copy.119
  625.7 1.0 copy-done
  626.6 1.3 copy.120
  (126 shorter events, 4.4 us)
Async XLA Ops:
  7.2 5.5 copy-start.8
  7.2 5.6 copy-start.9
  7.2 5.8 copy-start.10
  7.2 6.1 copy-start.11
  7.2 6.3 copy-start.12
  7.2 6.5 %copy-start.13 = (bf16[256]{0:T(256)(128)(2,1)S(1)}, bf16[256]{0:T(256)(128)(2,1)}, u32[]{:S(2)}) copy-start(bf16[256]{0:T(256)(128)(2,1)} %param.23) | copy-start | bytes 1540
  7.2 6.7 %copy-start.14 = (bf16[256]{0:T(256)(128)(2,1)S(1)}, bf16[256]{0:T(256)(128)(2,1)}, u32[]{:S(2)}) copy-start(bf16[256]{0:T(256)(128)(2,1)} %param.24) | copy-start | bytes 1540
  7.3 6.9 %copy-start.15 = (bf16[256]{0:T(256)(128)(2,1)S(1)}, bf16[256]{0:T(256)(128)(2,1)}, u32[]{:S(2)}) copy-start(bf16[256]{0:T(256)(128)(2,1)} %param.28) | copy-start | bytes 1540
  7.3 92.0 %all-gather.8.cloned.1.call-start = ((), (), s32[]{:S(2)}) async-start(), calls=%async_computation.5 | async-start | bytes 2359296 | tf_op jit(solution)/shard_map/all_gather | solution.py:1165
  8.0 91.3 %all-gather.6.cloned.1.call-start = ((), (), s32[]{:S(2)}) async-start(), calls=%async_computation.4 | async-start | bytes 7077888 | tf_op jit(solution)/shard_map/all_gather | solution.py:1164
  10.6 87.4 %copy-start.4 = (bf16[256,2048]{1,0:T(8,128)(2,1)S(1)}, bf16[256,2048]{1,0:T(8,128)(2,1)}, u32[]{:S(2)}) copy-start(bf16[256,2048]{1,0:T(8,128)(2,1)} %param.29) | copy-start | bytes 3145732
  10.6 201.4 %all-gather.10.cloned.1.call-start = ((), (), s32[]{:S(2)}) async-start(), calls=%async_computation.6 | async-start | bytes 9437184 | tf_op jit(solution)/shard_map/all_gather | solution.py:1166
  11.4 200.7 %all-gather.12.cloned.1.call-start = ((), (), s32[]{:S(2)}) async-start(), calls=%async_computation.11 | async-start | bytes 9437184 | tf_op jit(solution)/shard_map/all_gather | solution.py:1167
  11.9 448.8 %reduce-scatter.5.cloned.1.call-start = ((), (), s32[]{:S(2)}) async-start(), calls=%async_computation.7 | async-start | bytes 9437184 | tf_op jit(solution)/shard_map/reduce_scatter | solution.py:1194
  327.0 144.1 %reduce-scatter.7.cloned.1.call-start = ((), (), s32[]{:S(2)}) async-start(), calls=%async_computation.8 | async-start | bytes 9437184 | tf_op jit(solution)/shard_map/reduce_scatter | solution.py:1195
  327.6 292.2 %reduce-scatter.11.cloned.1.call-start = ((), (), s32[]{:S(2)}) async-start(), calls=%async_computation.10 | async-start | bytes 2359296 | tf_op jit(solution)/shard_map/reduce_scatter | solution.py:1200
  471.1 150.5 %reduce-scatter.9.cloned.1.call-start = ((), (), s32[]{:S(2)}) async-start(), calls=%async_computation.9 | async-start | bytes 7077888 | tf_op jit(solution)/shard_map/reduce_scatter | solution.py:1206
  513.8 0.9 copy-start.6
  513.8 1.1 copy-start.7
  513.8 2.5 copy-start.5
  517.5 98.0 %copy-start.2 = (bf16[256,2048]{1,0:T(8,128)(2,1)S(1)}, bf16[256,2048]{1,0:T(8,128)(2,1)}, u32[]{:S(2)}) copy-start(bf16[256,2048]{1,0:T(8,128)(2,1)} %reduce-scatter.7.cloned.1.call-done) | copy-start | bytes 3145732
  591.2 26.0 %copy-start.1 = (bf16[2048,256]{1,0:T(8,128)(2,1)S(1)}, bf16[2048,256]{1,0:T(8,128)(2,1)}, u32[]{:S(2)}) copy-start(bf16[2048,256]{1,0:T(8,128)(2,1)} %reduce-scatter.5.cloned.1.call-done) | copy-start | bytes 3145732
  619.8 4.9 copy-start.3
  624.7 2.0 copy-start
Sparse Core Ops, SparseCore 0:
  9.9 31.0 all-gather.7
  43.5 45.4 all-gather.5
  90.9 54.2 all-gather.9
  146.9 54.2 all-gather.11
  327.1 69.0 reduce-scatter.4
  399.6 71.4 reduce-scatter.6
  474.4 41.0 reduce-scatter.10
  518.9 61.7 reduce-scatter.8

commit v6 on v5

--- a/solution.py
+++ b/solution.py
@@ -86,6 +86,45 @@
             @pl.when(self._edge(way))
             def _(way=way):
                 self.hop(way, srcs[way], dst, sems).wait_send()
+
+    def first_hops(self, terms, landed, sems):
+        last = self.size - 1
+        return [
+            (self.t == sender, self.t == taker, self.hop(way, terms.at[shard], landed, sems))
+            for way, sender, taker, shard in ((0, 0, 1, last), (1, last, last - 1, 0))
+        ]
+
+    def hops_start(self, hops):
+        for sends, _, copy in hops:
+
+            @pl.when(sends)
+            def _(copy=copy):
+                copy.start()
+
+    def hops_wait(self, hops):
+        for sends, takes, copy in hops:
+
+            @pl.when(sends)
+            def _(copy=copy):
+                copy.wait_send()
+
+            @pl.when(takes)
+            def _(copy=copy):
+                copy.wait_recv()
+
+    def early_start(self, landed, bufs, sem):
+        last = self.size - 1
+        early = (
+            pltpu.make_async_copy(landed.at[0], bufs[0].at[last], sem.at[0]),
+            pltpu.make_async_copy(landed.at[1], bufs[1].at[0], sem.at[1]),
+        )
+        for copy, holder in zip(early, (1, last - 1)):
+
+            @pl.when(self.t == holder)
+            def _(copy=copy):
+                copy.start()
+
+        return early
 
     def gather_step(self, way, k, part, buf, sems, first, near=None):
         t, last = self.t, self.size - 1
@@ -480,22 +519,13 @@
 
 
 def back_middle_kernel(
-    size, terms, landed, mlp, gm, mid, vecs, out_w, o_t, gz_out, gmid_out, ends, stats,
-    go_out, grad_out, right, left, right2, left2, grad, ss, sr, ms, mr, gs, gr, early_sem,
+    size, terms, landed, mlp, gm, mid, vecs, out_w, gz_out, gmid_out, ends, stats,
+    go_out, right, left, right2, left2, ss, sr, ms, mr, gs, gr, early_sem,
 ):
     line = Line(size, mid.shape[0])
     rows = mid.shape[0]
     step = min(32, rows)
-    early = (
-        pltpu.make_async_copy(landed.at[0], right.at[size - 1], early_sem.at[0]),
-        pltpu.make_async_copy(landed.at[1], left.at[0], early_sem.at[1]),
-    )
-    for copy, holder in zip(early, (1, size - 2)):
-
-        @pl.when(line.t == holder)
-        def _(copy=copy):
-            copy.start()
-
+    early = line.early_start(landed, (right, left), early_sem)
     line.barrier()
     for j in range(size - 1):
         for piece in range(SUBS):
@@ -519,19 +549,8 @@
         stats[24:32, :] += fold(gy)
 
     row_loop(rows, step, body)
-    width = mid.shape[1]
-    block = min(512, width)
-
     def weigh(shard):
         go_out[shard] = dot_t(gz_out[shard], out_w[...]).astype(BF16)
-        here = o_t[:, pl.ds(pl.multiple_of(shard * rows, rows), rows)]
-
-        def column(j, carry):
-            at = pl.ds(pl.multiple_of(j * block, block), block)
-            grad[:, at] += dot(here, gz_out[shard, :, at])
-            return carry
-
-        lax.fori_loop(0, width // block, column, 0)
 
     def on_slot(k):
         def side(i, carry):
@@ -545,20 +564,18 @@
 
         lax.fori_loop(0, 1 if k == 0 else 2, side, 0)
 
-    grad[...] = jnp.zeros_like(grad)
     line.phase(
         gather=(gz_out, (gs, gr), None),
         scatter=(mlp, (right2, left2), (ms, mr)),
         on_slot=on_slot,
         ends=ends,
     )
-    grad_out[...] = grad[...].astype(BF16)
     line.drain_scatter((right, left), (ss, sr), 0, True)
     line.drain_scatter((right2, left2), (ms, mr), 1)
     line.drain_gather(gz_out, (gs, gr))
 
 
-def back_middle(terms, landed, mlp, gm, mid, vecs, out_w, o_t, size, cid):
+def back_middle(terms, landed, mlp, gm, mid, vecs, out_w, size, cid):
     rows, width = mid.shape
     local = out_w.shape[0]
     full = (size, rows, width)
@@ -570,24 +587,22 @@
             jax.ShapeDtypeStruct((2, rows, width), BF16),
             jax.ShapeDtypeStruct((32, width), F32),
             jax.ShapeDtypeStruct((size, rows, local), BF16),
-            jax.ShapeDtypeStruct((local, width), BF16),
         ),
-        in_specs=[WHOLE, HBM] + [WHOLE] * 6,
-        out_specs=(WHOLE,) * 6,
+        in_specs=[WHOLE, HBM] + [WHOLE] * 5,
+        out_specs=(WHOLE,) * 5,
         scratch_shapes=[pltpu.VMEM(full, BF16)] * 4
-        + [pltpu.VMEM((local, width), F32)]
         + line_sems(size)
         + line_sems(size)
         + line_sems(size)
         + [pltpu.SemaphoreType.DMA((2,))],
         compiler_params=params(cid),
         name="back_middle",
-    )(terms, landed, mlp, gm, mid, vecs, out_w, o_t)
+    )(terms, landed, mlp, gm, mid, vecs, out_w)
 
 
 def finish_kernel(
-    size, terms, tok, gmid, mlp, landed, mid, valid, vecs, grad_out, y_out, stats,
-    right, left, own_mlp, ends, ss, sr, load_sem,
+    size, terms, first_landed, tok, gmid, mlp, landed, mid, valid, vecs, grad_out, y_out, stats,
+    right, left, own_mlp, ends, ss, sr, load_sem, early_sem,
 ):
     line = Line(size, tok.shape[0])
     rows = tok.shape[0]
@@ -596,6 +611,7 @@
         pltpu.make_async_copy(mlp.at[line.t], own_mlp, load_sem.at[0]),
         pltpu.make_async_copy(landed, ends, load_sem.at[1]),
     ]
+    early = line.early_start(first_landed, (right, left), early_sem)
     for load in loads:
         load.start()
     line.barrier()
@@ -615,7 +631,9 @@
     for j in range(size - 1):
         for piece in range(SUBS):
             for way in (0, 1):
-                line.scatter_step(way, j, piece, terms, (right, left)[way], (ss, sr))
+                line.scatter_step(
+                    way, j, piece, terms, (right, left)[way], (ss, sr), None, early
+                )
         if j == 0:
             for load in loads:
                 load.wait()
@@ -630,10 +648,10 @@
         stats[8:16, :] += fold(e)
 
     row_loop(rows, step, body)
-    line.drain_scatter((right, left), (ss, sr))
-
-
-def finish(terms, tok, gmid, mlp, landed, mid, valid, vecs, size, cid):
+    line.drain_scatter((right, left), (ss, sr), 0, True)
+
+
+def finish(terms, first_landed, tok, gmid, mlp, landed, mid, valid, vecs, size, cid):
     rows, width = tok.shape
     full = (size, rows, width)
     return pl.pallas_call(
@@ -643,15 +661,15 @@
             jax.ShapeDtypeStruct((rows, width), BF16),
             jax.ShapeDtypeStruct((32, width), F32),
         ),
-        in_specs=[WHOLE, WHOLE, WHOLE, HBM, HBM, WHOLE, WHOLE, WHOLE],
+        in_specs=[WHOLE, HBM, WHOLE, WHOLE, HBM, HBM, WHOLE, WHOLE, WHOLE],
         out_specs=(WHOLE,) * 3,
         scratch_shapes=[pltpu.VMEM(full, BF16)] * 2
         + [pltpu.VMEM((rows, width), BF16), pltpu.VMEM((2, rows, width), BF16)]
         + line_sems(size)
-        + [pltpu.SemaphoreType.DMA((2,))],
+        + [pltpu.SemaphoreType.DMA((2,)), pltpu.SemaphoreType.DMA((2,))],
         compiler_params=params(cid),
         name="finish",
-    )(terms, tok, gmid, mlp, landed, mid, valid, vecs)
+    )(terms, first_landed, tok, gmid, mlp, landed, mid, valid, vecs)
 
 
 def reduce_small_kernel(n_dp, n_t, shared, blocks, out, land, sums, land2, s1, r1, s2, r2):
@@ -752,8 +770,8 @@
 
 
 def front_kernel(
-    size, heads, a, weights, shift, bar, out_w, cot, qkv, out_t, log_totals, terms, near,
-    cols, mixed_all, gs, gr, load_sem,
+    size, heads, a, weights, shift, bar, out_w, cot, qkv, mixed_all, log_totals, terms, near,
+    cols, gs, gr, load_sem,
 ):
     h = pl.program_id(0)
     rows = cot.shape[0]
@@ -791,7 +809,6 @@
         shares = (powers * (1.0 / total)).astype(BF16)
         mixed = dot(value_cols[:, 0:keys], shares)
         mixed_all[here, head_cols(0, h, heads)] = mixed.T.astype(BF16)
-        out_t[:, here] = mixed.astype(BF16)
         log_totals[0, :, here] = jnp.broadcast_to(top + jnp.log(total), (8, BLOCK))
 
     @pl.when(h == heads - 1)
@@ -812,7 +829,7 @@
         grid=(heads,),
         out_shape=(
             jax.ShapeDtypeStruct((LEN, local3), BF16),
-            jax.ShapeDtypeStruct((local, LEN), BF16),
+            jax.ShapeDtypeStruct((LEN, local), BF16),
             jax.ShapeDtypeStruct((heads, 8, LEN), F32),
             jax.ShapeDtypeStruct((LEN, width), BF16),
             jax.ShapeDtypeStruct((2,) + cot.shape, BF16),
@@ -820,14 +837,13 @@
         in_specs=[WHOLE, HBM, WHOLE, WHOLE, WHOLE, HBM],
         out_specs=(
             pl.BlockSpec((LEN, local3), lambda h: (0, 0)),
-            pl.BlockSpec((HD, LEN), lambda h: (h, 0)),
+            pl.BlockSpec((LEN, local), lambda h: (0, 0)),
             pl.BlockSpec((1, 8, LEN), lambda h: (h, 0, 0)),
             pl.BlockSpec((LEN, width), lambda h: (0, 0)),
             HBM,
         ),
         scratch_shapes=[
             pltpu.VMEM((width, local3), BF16),
-            pltpu.VMEM((LEN, local), BF16),
             pltpu.SemaphoreType.DMA((2,)),
             pltpu.SemaphoreType.DMA((2,)),
             pltpu.SemaphoreType.DMA((3,)),
@@ -1045,23 +1061,15 @@
     size, steps, act, gm, c, gu_in, terms, down_out, up_out, landed, gu, gs, gr, load_sem
 ):
     i = pl.program_id(0)
-    last = size - 1
     line = Line(size, terms.shape[1])
     load = pltpu.make_async_copy(gu_in, gu, load_sem.at[0])
-    hops = [
-        (line.t == sender, line.t == taker, line.hop(way, terms.at[shard], landed, (gs, gr)))
-        for way, sender, taker, shard in ((0, 0, 1, last), (1, last, last - 1, 0))
-    ]
+    hops = line.first_hops(terms, landed, (gs, gr))
 
     @pl.when(i == 0)
     def _():
         load.start()
         line.barrier()
-        for sends, _, copy in hops:
-
-            @pl.when(sends)
-            def _(copy=copy):
-                copy.start()
+        line.hops_start(hops)
 
     @pl.when(i < steps)
     def _():
@@ -1077,15 +1085,7 @@
 
     @pl.when(i == pl.num_programs(0) - 1)
     def _():
-        for sends, takes, copy in hops:
-
-            @pl.when(sends)
-            def _(copy=copy):
-                copy.wait_send()
-
-            @pl.when(takes)
-            def _(copy=copy):
-                copy.wait_recv()
+        line.hops_wait(hops)
 
 
 def products(act, gm, c, gu, terms, size, cid):
@@ -1123,6 +1123,49 @@
     )(act, gm, c, gu, terms)
 
 
+def head_products_kernel(size, gz, a, o, gqkv, terms, out, landed, gs, gr):
+    i = pl.program_id(0)
+    line = Line(size, terms.shape[1])
+    hops = line.first_hops(terms, landed, (gs, gr))
+    local = o.shape[1]
+
+    @pl.when(i == 0)
+    def _():
+        line.barrier()
+        line.hops_start(hops)
+
+    out[:, 0:local] = cross(gz[...], o[...]).astype(BF16)
+    out[:, local:] = cross(a[...], gqkv[...]).astype(BF16)
+
+    @pl.when(i == pl.num_programs(0) - 1)
+    def _():
+        line.hops_wait(hops)
+
+
+def head_products(gz, a, o, gqkv, terms, size, cid):
+    rows, width = a.shape
+    columns = o.shape[1] + gqkv.shape[1]
+    return pl.pallas_call(
+        functools.partial(head_products_kernel, size),
+        grid=(width // BLOCK,),
+        out_shape=(
+            jax.ShapeDtypeStruct((width, columns), BF16),
+            jax.ShapeDtypeStruct((2,) + terms.shape[1:], BF16),
+        ),
+        in_specs=[
+            pl.BlockSpec((rows, BLOCK), lambda i: (0, i)),
+            pl.BlockSpec((rows, BLOCK), lambda i: (0, i)),
+            WHOLE,
+            WHOLE,
+            HBM,
+        ],
+        out_specs=(pl.BlockSpec((BLOCK, columns), lambda i: (i, 0)), HBM),
+        scratch_shapes=[pltpu.SemaphoreType.DMA((2,)), pltpu.SemaphoreType.DMA((2,))],
+        compiler_params=params(cid),
+        name="head_products",
+    )(gz, a, o, gqkv, terms)
+
+
 def pad_to(x, count):
     return jnp.pad(x, ((0, 0), (0, count - x.shape[1])))
 
@@ -1174,7 +1217,7 @@
     gm_own = (cotangent.astype(F32) * valid_own[:, None]).astype(BF16)
 
     shift = jnp.broadcast_to(qkv_shift, (8, 3 * local))
-    qkv, attended_t, log_totals, terms, near = front(
+    qkv, attended, log_totals, terms, near = front(
         a, qkv_full, shift, bar, out_full, gm_own, n_t, 7
     )
     terms = terms.reshape(n_t, rows, width)
@@ -1185,28 +1228,27 @@
     c, gm = c.reshape(-1, width), gm.reshape(-1, width)
     act, gu = act.reshape(-1, units), gu.reshape(-1, units)
 
-    def rows_dot(left, right):
-        return lax.dot_general(
-            left, right, (((0,), (0,)), ((), ())), preferred_element_type=F32
-        ).astype(BF16)
-
     down_grad, up_grad, early = products(act, gm, c, gu, back_terms, n_t, 9)
     down_out = lax.psum_scatter(down_grad, "dp", scatter_dimension=1, tiled=True)
     up_out = lax.psum_scatter(up_grad, "dp", scatter_dimension=0, tiled=True)
-    _, gmid, ends, stats_b, go, out_grad = back_middle(
-        back_terms, early, mlp, gm_own, mid, vecs, out_full, attended_t, n_t, 3
-    )
-    go, out_grad, down_out, up_out = lax.optimization_barrier((go, out_grad, down_out, up_out))
-    out_out = lax.psum_scatter(out_grad, "dp", scatter_dimension=1, tiled=True)
+    gz, gmid, ends, stats_b, go = back_middle(
+        back_terms, early, mlp, gm_own, mid, vecs, out_full, n_t, 3
+    )
     gqkv, head_sums, last_terms, landed = attend_back(
         qkv, go.reshape(-1, local), bar, log_totals, qkv_full, ends, n_t, 8
     )
-    qkv_grad = rows_dot(a, gqkv)
-    last_terms, qkv_grad = lax.optimization_barrier((last_terms, qkv_grad))
-    qkv_out = lax.psum_scatter(qkv_grad, "dp", scatter_dimension=0, tiled=True)
-    qkv_out = qkv_out.reshape(part, 3, local)
+    last_terms = last_terms.reshape(n_t, rows, width)
+    head_grad, last_early = head_products(
+        gz.reshape(-1, width), a, attended, gqkv, last_terms, n_t, 10
+    )
+    last_early, head_grad, down_out, up_out = lax.optimization_barrier(
+        (last_early, head_grad, down_out, up_out)
+    )
+    head_out = lax.psum_scatter(head_grad, "dp", scatter_dimension=0, tiled=True)
+    out_out = head_out[:, :local].T
+    qkv_out = head_out[:, local:].reshape(part, 3, local)
     tokens_grad, output, stats_c = finish(
-        last_terms.reshape(n_t, rows, width), tokens, gmid, mlp, landed, mid, valid, vecs, n_t, 4
+        last_terms, last_early, tokens, gmid, mlp, landed, mid, valid, vecs, n_t, 4
     )
 
     def vec_sum(stats, i):

time: 636 us -> 623 us (0.980)
  matrix products: 11.6 us -> 0 us
  waiting for transfers between devices: 12.8 us -> 2.54 us
  Pallas kernels: 558 us -> 567 us
    pallas_call x0 -> x1, Pallas kernels: none -> 22.3 us  [head_products(): pl.pallas_call(functools.partial(head_products_kernel, size), grid=(width...]
    dot_general x1 -> x0, matrix products: 11.6 us -> none  [rows_dot(): lax.dot_general(left, right, (((0,), (0,)), ((), ())), preferred_element_...]
    reduce_scatter x1, waiting for transfers between devices: 10.3 us -> 0.02 us  [shards(): up_out = lax.psum_scatter(up_grad, 'dp', scatter_dimension=0, tiled=True)]
    pallas_call x1, Pallas kernels: 73.6 us -> 64.7 us  [finish(): pl.pallas_call(functools.partial(finish_kernel, size), out_shape=(jax.Sha...]
  transfers between devices with their start and end apart: 8 -> 7, of which waited for: 1 -> 0; matrix products, arithmetic and copies ran while one was open for 6% -> 4% of each run, Pallas kernels for 70% -> 73%
where the time goes in v6:
time: 623 us; the launch traced here: 621 us
  Pallas kernels  567 us (91%)
  local copies, waits for them, and re-layouts  25.9 us (4%)
  between operations  16.1 us (3%)
  other arithmetic  8.99 us (1%)
    pallas_call x1, Pallas kernels, back_middle(): pl.pallas_call(functools.partial(back_middle_kernel, size), out_shape=(ja...  131 us
    pallas_call x1, Pallas kernels, hidden(): pl.pallas_call(functools.partial(hidden_kernel, n_dp, size), out_shape=(j...  88.4 us
    pallas_call x1, Pallas kernels, first(): pl.pallas_call(functools.partial(first_kernel, n_dp, size, part), out_sha...  79.4 us
    pallas_call x1, Pallas kernels, middle(): pl.pallas_call(functools.partial(middle_kernel, size), out_shape=(jax.Sha...  79.1 us
    pallas_call x1, Pallas kernels, finish(): pl.pallas_call(functools.partial(finish_kernel, size), out_shape=(jax.Sha...  64.7 us
    pallas_call x1, Pallas kernels, front(): pl.pallas_call(functools.partial(front_kernel, size, heads), grid=(heads,...  31.3 us
    pallas_call x1, Pallas kernels, attend_back(): pl.pallas_call(functools.partial(attend_back_kernel, size, heads), grid=(...  28.2 us
    pallas_call x1, Pallas kernels, products(): pl.pallas_call(functools.partial(products_kernel, size, steps), grid=(ste...  25.9 us
  transfers between devices with their start and end apart: 7, of which 0 were waited for; matrix products, arithmetic and copies ran while one was open for 4% of the time, Pallas kernels for 73%

profile of v6, /device:TPU:0, one launch (start us, length us, event | category | flops | bytes accessed | tf_op | source)
XLA Modules:
  0.0 621.2 jit_solution(4542001602957969648)
XLA Ops:
  7.2 0.7 all-gather.8.cloned.1.call-update
  8.0 1.4 copy.76
  9.5 1.2 copy.77
  10.7 0.7 all-gather.10.cloned.1.call-update
  11.4 0.5 all-gather.12.cloned.1.call-update
  14.8 0.6 pad_bitcast_fusion.small
  15.4 79.4 %first.1 = (bf16[8,16,128]{2,1,0:T(8,128)(2,1)}, bf16[4,256,2048]{2,1,0:T(8,128)(2,1)}) custom-call(bf16[16,128]{1,0:T(8,128)(2,1)} %pad_bitcast_fusion.small, bf16[256,2048]{1,0:T(8,128)(2,1)} %tok.3), custom_call_target="tpu_custom_call" | custom-call | tf_op jit(solution)/shard_map/first/pallas_call | solution.py:434
  94.8 0.8 copy.102
  96.1 0.8 copy.81
  97.0 0.3 reshape.199
  97.4 0.6 pad_convert_fusion.vecs
  98.0 1.2 multiply_convert_fusion.cot.gm
  99.2 1.0 broadcast_in_dim.45.bar
  100.2 0.6 broadcast_in_dim.42.shift
  100.8 31.3 %front.1 = (bf16[1024,1536]{1,0:T(8,128)(2,1)}, bf16[1024,512]{1,0:T(8,128)(2,1)}, f32[4,8,1024]{2,1,0:T(8,128)}, bf16[1024,2048]{1,0:T(8,128)(2,1)}, bf16[2,256,2048]{2,1,0:T(8,128)(2,1)}) custom-call(bf16[1024,2048]{1,0:T(8,128)(2,1)} %bitcast.88, bf16[2048,1536]{1,0:T(8,128)(2,1)} %all-gather.6.cloned.1.call-done.weights, ...), custom_call_target="tpu_custom_call" | custom-call | tf_op jit(solution)/shard_map/front/pallas_call | solution.py:827
  132.2 0.8 broadcast_in_dim.46.valid
  132.9 79.1 %middle.1 = (bf16[256,2048]{1,0:T(8,128)(2,1)}, bf16[4,256,2048]{2,1,0:T(8,128)(2,1)}, f32[256,2048]{1,0:T(8,128)}, f32[24,2048]{1,0:T(8,128)}) custom-call(bf16[4,256,2048]{2,1,0:T(8,128)(2,1)} %bitcast.95, bf16[256,2048]{1,0:T(8,128)(2,1)} %multiply_convert_fusion.cot.gm, bf16[2,256,2048]{2,1,0:T(8,128)(2,1)} %get-tuple-element.57.near, ...), custom_call_target="tpu_custom_call" | custom-call | tf_op jit(solution)/shard_map/middle/pallas_call | solution.py:502
  212.1 0.6 broadcast_in_dim.47.bias
  212.7 88.4 %hidden.1 = (bf16[4,256,2048]{2,1,0:T(8,128)(2,1)}, bf16[4,256,2048]{2,1,0:T(8,128)(2,1)}, bf16[4,256,2048]{2,1,0:T(8,128)(2,1)}, bf16[4,256,2048]{2,1,0:T(8,128...) custom-call(bf16[256,2048]{1,0:T(8,128)(2,1)} %get-tuple-element.58.c_own, ...), custom_call_target="tpu_custom_call" | custom-call | tf_op jit(solution)/shard_map/hidden/pallas_call | solution.py:1029
  301.1 25.9 %products.1 = (bf16[2048,2048]{1,0:T(8,128)(2,1)}, bf16[2048,2048]{1,0:T(8,128)(2,1)}, bf16[2,256,2048]{2,1,0:T(8,128)(2,1)}) custom-call(bf16[1024,2048]{1,0:T(8,128)(2,1)} %bitcast.93, bf16[1024,2048]{1,0:T(8,128)(2,1)} %bitcast.87, bf16[1024,2048]{1,0:T(8,128)(2,1)} %bitcast.92, bf16[1024,2048]{1,0:T(8,128)(2,1)} %bitcast.94, ...), custom_call_target="tpu_custom_call" | custom-call | tf_op jit(solution)/shard_map/products/pallas_call | solution.py:1095
  327.1 0.5 reduce-scatter.6.cloned.1.call-update
  327.7 130.9 %back_middle.1 = (bf16[4,256,2048]{2,1,0:T(8,128)(2,1)}, f32[256,2048]{1,0:T(8,128)}, bf16[2,256,2048]{2,1,0:T(8,128)(2,1)}, f32[32,2048]{1,0:T(8,128)}, bf16[4,256,512]{2,1,0:T(8,128)(2,1)}) custom-call(bf16[4,256,2048]{2,1,0:T(8,128)(2,1)} %get-tuple-element.60.terms, bf16[2,256,2048]{2,1,0:T(8,128)(2,1)} %get-tuple-element.64.landed, ...), custom_call_target="tpu_custom_call" | custom-call | tf_op jit(solution)/shard_map/back_middle/pallas_call | solution.py:582
  458.6 28.2 %attend_back.1 = (bf16[1024,1536]{1,0:T(8,128)(2,1)}, f32[4,16,128]{2,1,0:T(8,128)}, bf16[1024,2048]{1,0:T(8,128)(2,1)}, bf16[2,256,2048]{2,1,0:T(8,128)(2,1)}) custom-call(bf16[1024,1536]{1,0:T(8,128)(2,1)} %get-tuple-element.55.q.k.v, bf16[1024,1536]{1,0:T(8,128)(2,1)} %get-tuple-element.55.q.k.v, bf16[1024,1536]{1,0:T(8,128)(2,1)} %get-tuple-element.55.q.k.v, ...), custom_call_target="tpu_custom_call" | custom-call | tf_op jit(solution)/shard_map/attend_back/pallas_call | solution.py:918
  486.8 22.3 %head_products.1 = (bf16[2048,2048]{1,0:T(8,128)(2,1)}, bf16[2,256,2048]{2,1,0:T(8,128)(2,1)}) custom-call(bf16[1024,2048]{1,0:T(8,128)(2,1)} %bitcast.96, bf16[1024,2048]{1,0:T(8,128)(2,1)} %bitcast.89, bf16[1024,512]{1,0:T(8,128)(2,1)} %get-tuple-element.72.o, bf16[1024,1536]{1,0:T(8,128)(2,1)} %get-tuple-element.73.gqkv, bf16[4,256,2048]{2,1,0:T(8,128)(2,1)} %bitcast.85), custom_call_target="tpu_custom_call" | custom-call | tf_op jit(solution)/shard_map/head_products/pallas_call | solution.py:1148
  509.3 0.8 copy-done.7
  510.4 0.5 reshape.192
  510.8 0.8 copy.82
  511.7 0.8 slice_reduce_fusion.13
  512.9 64.7 %finish.1 = (f32[256,2048]{1,0:T(8,128)}, bf16[256,2048]{1,0:T(8,128)(2,1)}, f32[32,2048]{1,0:T(8,128)}) custom-call(bf16[4,256,2048]{2,1,0:T(8,128)(2,1)} %bitcast.86, bf16[2,256,2048]{2,1,0:T(8,128)(2,1)} %get-tuple-element.78.first_landed, bf16[256,2048]{1,0:T(8,128)(2,1)} %tok.3, f32[256,2048]{1,0:T(8,128)} %get-tuple-element.79.gmid, ...), custom_call_target="tpu_custom_call" | custom-call | tf_op jit(solution)/shard_map/finish/pallas_call | solution.py:657
  577.7 1.1 slice_reduce_fusion
  579.0 0.7 copy.101
  579.7 17.0 %reduce_small.1 = f32[32,128]{1,0:T(8,128)} custom-call(f32[8,32,128]{2,1,0:T(8,128)} %bitcast.102), custom_call_target="tpu_custom_call" | custom-call | tf_op jit(solution)/shard_map/reduce_small/pallas_call | solution.py:729
  596.7 1.2 slice.181
  597.9 0.8 slice_reduce_fusion.11
  598.9 0.7 slice_reduce_fusion.14
  599.6 0.7 reshape.196
  600.3 1.4 slice_bitcast_fusion.6
  601.9 0.6 copy.88
  602.5 1.6 convert_element_type.88
  604.1 1.5 convert_element_type.89
  606.2 0.5 divide_sqrt_fusion
  606.7 1.1 convert_bitcast_fusion
  607.8 1.0 copy.87
  609.0 0.5 copy.85
  609.5 1.6 copy.86
  611.1 1.0 copy.124
  612.1 1.0 copy-done
  613.1 1.3 copy.125
  (127 shorter events, 4.3 us)
Async XLA Ops:
  7.2 92.0 %all-gather.8.cloned.1.call-start = ((), (), s32[]{:S(2)}) async-start(), calls=%async_computation.4 | async-start | bytes 2359296 | tf_op jit(solution)/shard_map/all_gather | solution.py:1208
  7.9 91.3 %all-gather.6.cloned.1.call-start = ((), (), s32[]{:S(2)}) async-start(), calls=%async_computation.3 | async-start | bytes 7077888 | tf_op jit(solution)/shard_map/all_gather | solution.py:1207
  9.4 3.3 copy-start.9
  9.4 3.4 copy-start.10
  9.4 3.7 copy-start.11
  9.4 3.9 copy-start.12
  9.4 4.1 copy-start.13
  9.4 4.3 copy-start.14
  9.4 4.5 copy-start.15
  9.5 4.7 copy-start.16
  10.6 201.4 %all-gather.10.cloned.1.call-start = ((), (), s32[]{:S(2)}) async-start(), calls=%async_computation.5 | async-start | bytes 9437184 | tf_op jit(solution)/shard_map/all_gather | solution.py:1209
  11.4 86.6 %copy-start.5 = (bf16[256,2048]{1,0:T(8,128)(2,1)S(1)}, bf16[256,2048]{1,0:T(8,128)(2,1)}, u32[]{:S(2)}) copy-start(bf16[256,2048]{1,0:T(8,128)(2,1)} %param.29) | copy-start | bytes 3145732
  11.4 200.7 %all-gather.12.cloned.1.call-start = ((), (), s32[]{:S(2)}) async-start(), calls=%async_computation.9 | async-start | bytes 9437184 | tf_op jit(solution)/shard_map/all_gather | solution.py:1210
  12.0 497.2 %reduce-scatter.4.cloned.1.call-start = ((), (), s32[]{:S(2)}) async-start(), calls=%async_computation.6 | async-start | bytes 9437184 | tf_op jit(solution)/shard_map/reduce_scatter | solution.py:1232
  327.1 182.1 %reduce-scatter.6.cloned.1.call-start = ((), (), s32[]{:S(2)}) async-start(), calls=%async_computation.7 | async-start | bytes 9437184 | tf_op jit(solution)/shard_map/reduce_scatter | solution.py:1233
  327.7 279.1 %reduce-scatter.8.cloned.1.call-start = ((), (), s32[]{:S(2)}) async-start(), calls=%async_computation.8 | async-start | bytes 9437184 | tf_op jit(solution)/shard_map/reduce_scatter | solution.py:1247
  509.2 0.9 copy-start.7
  509.2 1.1 copy-start.8
  509.3 3.5 copy-start.6
  577.7 24.9 %copy-start.2 = (bf16[256,2048]{1,0:T(8,128)(2,1)S(1)}, bf16[256,2048]{1,0:T(8,128)(2,1)}, u32[]{:S(2)}) copy-start(bf16[256,2048]{1,0:T(8,128)(2,1)} %reduce-scatter.6.cloned.1.call-done) | copy-start | bytes 3145732
  578.9 25.1 %copy-start.1 = (bf16[2048,256]{1,0:T(8,128)(2,1)S(1)}, bf16[2048,256]{1,0:T(8,128)(2,1)}, u32[]{:S(2)}) copy-start(bf16[2048,256]{1,0:T(8,128)(2,1)} %reduce-scatter.4.cloned.1.call-done) | copy-start | bytes 3145732
  606.7 2.1 copy-start.3
  609.5 1.6 copy-start.4
  611.1 2.0 copy-start
Sparse Core Ops, SparseCore 0:
  9.9 31.0 all-gather.7
  43.4 45.4 all-gather.5
  90.9 54.1 all-gather.9
  146.8 54.2 all-gather.11
  327.2 69.0 reduce-scatter.3
  399.6 71.4 reduce-scatter.5
  509.4 69.7 reduce-scatter.7

commit v7 on v6

--- a/solution.py
+++ b/solution.py
@@ -189,7 +189,33 @@
 
         lax.fori_loop(0, 2 * self.size - 1, visit, 0)
 
-    def scatter_step(self, way, j, part, terms, buf, sems, ends=None, early=None):
+    def _second(self, way):
+        return self.t == (1 if way == 0 else self.size - 2)
+
+    def send_sum(self, way, shard, part, terms, buf, sems):
+        step = min(32, self.sub)
+
+        def add(i, carry):
+            rows = pl.ds(part * self.sub + i * step, step)
+            total = buf[shard, rows, :].astype(F32) + terms[shard, rows, :].astype(F32)
+            buf[shard, rows, :] = total.astype(BF16)
+            return carry
+
+        lax.fori_loop(0, self.sub // step, add, 0)
+        held = self._rows(buf, shard, part)
+        self._copy(held, buf, sems, way, shard, part).start()
+
+    def early_sends(self, terms, bufs, sems, early):
+        for way in (0, 1):
+
+            @pl.when(self._second(way))
+            def _(way=way):
+                early[way].wait()
+                for part in range(SUBS):
+                    shard = self.size - 1 if way == 0 else 0
+                    self.send_sum(way, shard, part, terms, bufs[way], sems)
+
+    def scatter_step(self, way, j, part, terms, buf, sems, ends=None, early=False):
         t, last = self.t, self.size - 1
         shard = last - j if way == 0 else j
         beyond = (shard > t) if way == 0 else (shard < t)
@@ -201,8 +227,7 @@
             goes = (shard > t + 1) if way == 0 else (shard < t - 1)
             stays = (shard == t + 1) if way == 0 else (shard == t - 1)
 
-        second = (t == 1) if way == 0 else (t == last - 1)
-        done = early is not None and j == 0
+        done = early and j == 0
 
         if not done:
 
@@ -210,32 +235,15 @@
             def _():
                 self._copy(self._rows(terms, shard, part), buf, sems, way, shard, part).start()
 
-        @pl.when(goes & jnp.logical_not(starts))
+        relays = goes & jnp.logical_not(starts)
+        if done:
+            relays = relays & jnp.logical_not(self._second(way))
+
+        @pl.when(relays)
         def _():
             held = self._rows(buf, shard, part)
-            arrival = self._copy(held, buf, sems, way, shard, part)
-            if not done:
-                arrival.wait_recv()
-            else:
-
-                @pl.when(jnp.logical_not(second))
-                def _():
-                    arrival.wait_recv()
-
-                if part == 0:
-
-                    @pl.when(second)
-                    def _():
-                        early[way].wait()
-
-            def add(i, carry):
-                rows = pl.ds(part * self.sub + i * step, step)
-                total = buf[shard, rows, :].astype(F32) + terms[shard, rows, :].astype(F32)
-                buf[shard, rows, :] = total.astype(BF16)
-                return carry
-
-            lax.fori_loop(0, self.sub // step, add, 0)
-            self._copy(held, buf, sems, way, shard, part).start()
+            self._copy(held, buf, sems, way, shard, part).wait_recv()
+            self.send_sum(way, shard, part, terms, buf, sems)
 
         if stays is None:
             return
@@ -258,9 +266,9 @@
 
             lax.fori_loop(0, self.sub // step, add, 0)
 
-    def phase(self, gather=None, scatter=None, on_slot=None, near=None, ends=None):
+    def phase(self, gather=None, scatter=None, on_slot=None, near=None, ends=None, start=0):
         n = self.size
-        for k in range(0 if near is None else 1, n):
+        for k in range(start, n):
             for part in range(SUBS):
                 for way in (0, 1):
                     if gather is not None:
@@ -282,15 +290,14 @@
             if on_slot is not None:
                 on_slot(k)
 
-    def own_wait(self, bufs, sems):
+    def own_wait(self, bufs, sems, part):
         for way in (0, 1):
             arrives = self.t > 0 if way == 0 else self.t < self.size - 1
 
             @pl.when(arrives)
             def _(way=way):
-                for part in range(SUBS):
-                    held = self._rows(bufs[way], self.t, part)
-                    self._copy(held, bufs[way], sems, way, self.t, part).wait_recv()
+                held = self._rows(bufs[way], self.t, part)
+                self._copy(held, bufs[way], sems, way, self.t, part).wait_recv()
 
     def own_sum(self, terms, bufs, rows):
         t = self.t
@@ -348,9 +355,9 @@
     return spread * (scaled - mean_part - normed * across)
 
 
-def row_loop(rows, step, body):
+def row_loop(rows, step, body, base=0):
     def one(i, carry):
-        body(pl.ds(pl.multiple_of(i * step, step), step))
+        body(pl.ds(pl.multiple_of(base + i * step, step), step))
         return carry
 
     lax.fori_loop(0, rows // step, one, 0)
@@ -456,7 +463,9 @@
 ):
     line = Line(size, tok.shape[0])
     rows = tok.shape[0]
-    step = min(32, rows)
+    step = min(32, line.sub)
+    own = pltpu.make_async_copy(cot, gm_out.at[line.t], near_sem.at[2])
+    own.start()
     line.barrier()
 
     def keep(way):
@@ -472,11 +481,11 @@
 
     keep_all(lambda copy: copy.start())
     line.phase(
-        gather=(gm_out, (gs, gr), None), scatter=(terms, (right, left), (ss, sr)), near=near
-    )
-    gm_out[pl.ds(line.t, 1)] = cot[...][None]
-    keep_all(lambda copy: copy.wait())
-    line.own_wait((right, left), (ss, sr))
+        gather=(gm_out, (gs, gr), None),
+        scatter=(terms, (right, left), (ss, sr)),
+        near=near,
+        start=1,
+    )
     stats[...] = jnp.zeros_like(stats)
 
     def body(at):
@@ -491,7 +500,11 @@
         stats[8:16, :] += fold(ok * attn * attn)
         stats[16:24, :] += fold(ok * mid * mid)
 
-    row_loop(rows, step, body)
+    for piece in range(SUBS):
+        line.own_wait((right, left), (ss, sr), piece)
+        row_loop(line.sub, step, body, piece * line.sub)
+    own.wait()
+    keep_all(lambda copy: copy.wait())
     line.drain_gather(gm_out, (gs, gr), 1)
     line.drain_scatter((right, left), (ss, sr))
 
@@ -507,33 +520,44 @@
             jax.ShapeDtypeStruct((rows, width), F32),
             jax.ShapeDtypeStruct((24, width), F32),
         ),
-        in_specs=[WHOLE, WHOLE, HBM, WHOLE, WHOLE, WHOLE],
+        in_specs=[WHOLE, HBM, HBM, WHOLE, WHOLE, WHOLE],
         out_specs=(WHOLE,) * 4,
         scratch_shapes=[pltpu.VMEM(full, BF16), pltpu.VMEM(full, BF16)]
         + line_sems(size)
         + line_sems(size)
-        + [pltpu.SemaphoreType.DMA((2,))],
+        + [pltpu.SemaphoreType.DMA((3,))],
         compiler_params=params(cid),
         name="middle",
     )(terms, cot, near, tok, valid, vecs)
 
 
 def back_middle_kernel(
-    size, terms, landed, mlp, gm, mid, vecs, out_w, gz_out, gmid_out, ends, stats,
-    go_out, right, left, right2, left2, ss, sr, ms, mr, gs, gr, early_sem,
+    size, terms, landed, mlp_in, gm_in, mid_in, vecs, out_in, gz_out, gmid_out, ends, stats,
+    go_out, right, left, right2, left2, mlp, gm, mid, out_w,
+    ss, sr, ms, mr, gs, gr, early_sem, load_sem,
 ):
-    line = Line(size, mid.shape[0])
     rows = mid.shape[0]
-    step = min(32, rows)
+    line = Line(size, rows)
+    step = min(32, line.sub)
     early = line.early_start(landed, (right, left), early_sem)
+    loads = [
+        pltpu.make_async_copy(src, dst, load_sem.at[i])
+        for i, (src, dst) in enumerate(
+            ((gm_in, gm), (mid_in, mid), (mlp_in, mlp), (out_in, out_w))
+        )
+    ]
+    for load in loads:
+        load.start()
     line.barrier()
+    line.early_sends(terms, (right, left), (ss, sr), early)
     for j in range(size - 1):
         for piece in range(SUBS):
             for way in (0, 1):
                 line.scatter_step(
-                    way, j, piece, terms, (right, left)[way], (ss, sr), None, early
+                    way, j, piece, terms, (right, left)[way], (ss, sr), None, True
                 )
-    line.own_wait((right, left), (ss, sr))
+    for load in loads:
+        load.wait()
     stats[...] = jnp.zeros_like(stats)
 
     def body(at):
@@ -548,7 +572,11 @@
         stats[16:24, :] += fold(gmid)
         stats[24:32, :] += fold(gy)
 
-    row_loop(rows, step, body)
+    for piece in range(SUBS):
+        line.own_wait((right, left), (ss, sr), piece)
+        row_loop(line.sub, step, body, piece * line.sub)
+        for way in (0, 1):
+            line.gather_step(way, 0, piece, gz_out, (gs, gr), None)
     def weigh(shard):
         go_out[shard] = dot_t(gz_out[shard], out_w[...]).astype(BF16)
 
@@ -564,11 +592,13 @@
 
         lax.fori_loop(0, 1 if k == 0 else 2, side, 0)
 
+    on_slot(0)
     line.phase(
         gather=(gz_out, (gs, gr), None),
         scatter=(mlp, (right2, left2), (ms, mr)),
         on_slot=on_slot,
         ends=ends,
+        start=1,
     )
     line.drain_scatter((right, left), (ss, sr), 0, True)
     line.drain_scatter((right2, left2), (ms, mr), 1)
@@ -588,33 +618,45 @@
             jax.ShapeDtypeStruct((32, width), F32),
             jax.ShapeDtypeStruct((size, rows, local), BF16),
         ),
-        in_specs=[WHOLE, HBM] + [WHOLE] * 5,
+        in_specs=[WHOLE, HBM, HBM, HBM, HBM, WHOLE, HBM],
         out_specs=(WHOLE,) * 5,
-        scratch_shapes=[pltpu.VMEM(full, BF16)] * 4
+        scratch_shapes=[pltpu.VMEM(full, BF16)] * 5
+        + [
+            pltpu.VMEM((rows, width), BF16),
+            pltpu.VMEM((rows, width), F32),
+            pltpu.VMEM((local, width), BF16),
+        ]
         + line_sems(size)
         + line_sems(size)
         + line_sems(size)
-        + [pltpu.SemaphoreType.DMA((2,))],
+        + [pltpu.SemaphoreType.DMA((2,)), pltpu.SemaphoreType.DMA((4,))],
         compiler_params=params(cid),
         name="back_middle",
     )(terms, landed, mlp, gm, mid, vecs, out_w)
 
 
 def finish_kernel(
-    size, terms, first_landed, tok, gmid, mlp, landed, mid, valid, vecs, grad_out, y_out, stats,
-    right, left, own_mlp, ends, ss, sr, load_sem, early_sem,
+    size, terms, first_landed, tok_in, gmid_in, mlp, landed, mid_in, valid, vecs,
+    grad_out, y_out, stats, right, left, own_mlp, tok, ends, gmid, mid,
+    ss, sr, load_sem, early_sem,
 ):
-    line = Line(size, tok.shape[0])
     rows = tok.shape[0]
-    step = min(32, rows)
+    line = Line(size, rows)
+    step = min(32, line.sub)
     loads = [
-        pltpu.make_async_copy(mlp.at[line.t], own_mlp, load_sem.at[0]),
-        pltpu.make_async_copy(landed, ends, load_sem.at[1]),
+        pltpu.make_async_copy(src, dst, load_sem.at[i])
+        for i, (src, dst) in enumerate(
+            (
+                (mlp.at[line.t], own_mlp), (landed, ends), (mid_in, mid),
+                (tok_in, tok), (gmid_in, gmid),
+            )
+        )
     ]
     early = line.early_start(first_landed, (right, left), early_sem)
     for load in loads:
         load.start()
     line.barrier()
+    line.early_sends(terms, (right, left), (ss, sr), early)
     stats[...] = jnp.zeros_like(stats)
 
     def tail(at):
@@ -632,13 +674,12 @@
         for piece in range(SUBS):
             for way in (0, 1):
                 line.scatter_step(
-                    way, j, piece, terms, (right, left)[way], (ss, sr), None, early
+                    way, j, piece, terms, (right, left)[way], (ss, sr), None, True
                 )
         if j == 0:
             for load in loads:
                 load.wait()
             row_loop(rows, step, tail)
-    line.own_wait((right, left), (ss, sr))
 
     def body(at):
         e = line.own_sum(terms, (right, left), at)
@@ -647,7 +688,9 @@
         stats[0:8, :] += fold(e * normed)
         stats[8:16, :] += fold(e)
 
-    row_loop(rows, step, body)
+    for piece in range(SUBS):
+        line.own_wait((right, left), (ss, sr), piece)
+        row_loop(line.sub, step, body, piece * line.sub)
     line.drain_scatter((right, left), (ss, sr), 0, True)
 
 
@@ -661,12 +704,14 @@
             jax.ShapeDtypeStruct((rows, width), BF16),
             jax.ShapeDtypeStruct((32, width), F32),
         ),
-        in_specs=[WHOLE, HBM, WHOLE, WHOLE, HBM, HBM, WHOLE, WHOLE, WHOLE],
+        in_specs=[WHOLE] + [HBM] * 6 + [WHOLE, WHOLE],
         out_specs=(WHOLE,) * 3,
         scratch_shapes=[pltpu.VMEM(full, BF16)] * 2
-        + [pltpu.VMEM((rows, width), BF16), pltpu.VMEM((2, rows, width), BF16)]
+        + [pltpu.VMEM((rows, width), BF16)] * 2
+        + [pltpu.VMEM((2, rows, width), BF16)]
+        + [pltpu.VMEM((rows, width), F32)] * 2
         + line_sems(size)
-        + [pltpu.SemaphoreType.DMA((2,)), pltpu.SemaphoreType.DMA((2,))],
+        + [pltpu.SemaphoreType.DMA((5,)), pltpu.SemaphoreType.DMA((2,))],
         compiler_params=params(cid),
         name="finish",
     )(terms, first_landed, tok, gmid, mlp, landed, mid, valid, vecs)
@@ -769,6 +814,18 @@
     return pl.ds(pl.multiple_of((part * heads + h) * HD, HD), HD)
 
 
+def weight_loads(weights, cols, sem, part):
+    n_dp, _, rows, local = weights.shape
+    return [
+        pltpu.make_async_copy(
+            weights.at[d, part],
+            cols.at[pl.ds(d * rows, rows), pl.ds(part * local, local)],
+            sem.at[part, d],
+        )
+        for d in range(n_dp)
+    ]
+
+
 def front_kernel(
     size, heads, a, weights, shift, bar, out_w, cot, qkv, mixed_all, log_totals, terms, near,
     cols, gs, gr, load_sem,
@@ -778,18 +835,16 @@
     local = heads * HD
     line = Line(size, rows)
 
-    def load(part):
-        at = pl.ds(part * local, local)
-        return pltpu.make_async_copy(weights.at[:, at], cols.at[:, at], load_sem.at[part])
-
     @pl.when(h == 0)
     def _():
         for part in range(3):
-            load(part).start()
+            for load in weight_loads(weights, cols, load_sem, part):
+                load.start()
         line.barrier()
         line.hop_start((cot, cot), near, (gs, gr))
         for part in range(3):
-            load(part).wait()
+            for load in weight_loads(weights, cols, load_sem, part):
+                load.wait()
             span = slice(part * local, (part + 1) * local)
 
             def product(at, span=span):
@@ -821,8 +876,8 @@
 
 
 def front(a, weights, shift, bar, out_w, cot, size, cid):
-    width, local3 = weights.shape
-    local = local3 // 3
+    n_dp, _, part, local = weights.shape
+    width, local3 = n_dp * part, 3 * local
     heads = local // HD
     return pl.pallas_call(
         functools.partial(front_kernel, size, heads),
@@ -846,7 +901,7 @@
             pltpu.VMEM((width, local3), BF16),
             pltpu.SemaphoreType.DMA((2,)),
             pltpu.SemaphoreType.DMA((2,)),
-            pltpu.SemaphoreType.DMA((3,)),
+            pltpu.SemaphoreType.DMA((3, n_dp)),
         ],
         compiler_params=params(cid),
         name="front",
@@ -860,11 +915,12 @@
     h = pl.program_id(0)
     line = Line(size, ends.shape[1])
     srcs = (ends.at[0], ends.at[1])
-    load = pltpu.make_async_copy(weights, cols, load_sem.at[0])
+    loads = [load for part in range(3) for load in weight_loads(weights, cols, load_sem, part)]
 
     @pl.when(h == 0)
     def _():
-        load.start()
+        for load in loads:
+            load.start()
         line.barrier()
         line.hop_start(srcs, landed, (gs, gr))
 
@@ -899,7 +955,8 @@
 
     @pl.when(h == heads - 1)
     def _():
-        load.wait()
+        for load in loads:
+            load.wait()
 
         def product(at):
             terms[at, :] = dot_t(out[at, :], cols[...]).astype(BF16)
@@ -909,11 +966,12 @@
 
 
 def attend_back(qkv, go, bar, log_totals, weights, ends, size, cid):
-    width, local3 = weights.shape
-    heads = local3 // 3 // HD
-
-    def column(part):
-        return pl.BlockSpec((LEN, HD), lambda h: (0, part * heads + h))
+    n_dp, _, part, local = weights.shape
+    width, local3 = n_dp * part, 3 * local
+    heads = local // HD
+
+    def column(place):
+        return pl.BlockSpec((LEN, HD), lambda h: (0, place * heads + h))
 
     return pl.pallas_call(
         functools.partial(attend_back_kernel, size, heads),
@@ -942,7 +1000,7 @@
             pltpu.VMEM((width, local3), BF16),
             pltpu.SemaphoreType.DMA((2,)),
             pltpu.SemaphoreType.DMA((2,)),
-            pltpu.SemaphoreType.DMA((1,)),
+            pltpu.SemaphoreType.DMA((3, n_dp)),
         ],
         compiler_params=params(cid),
         name="attend_back",
@@ -960,8 +1018,8 @@
 
 
 def hidden_kernel(
-    n_dp, size, c_own, gm, up_in, down_in, bias, c_out, act_out, gu_out, mlp_out, back_out, sums,
-    up, down, act, gu, mlp, back, gs, gr, in_sem, out_sem,
+    n_dp, size, c_own, gm_in, up_in, down_in, bias,
+    c_out, act_out, gu_out, mlp_out, back_out, sums, gm, up, down, act, gu, mlp, back, gs, gr, in_sem, out_sem,
 ):
     line = Line(size, c_own.shape[0])
     rows, width = c_own.shape
@@ -970,6 +1028,7 @@
     loads = [
         pltpu.make_async_copy(up_in, up, in_sem.at[0]),
         pltpu.make_async_copy(down_in, down, in_sem.at[1]),
+        pltpu.make_async_copy(gm_in, gm, in_sem.at[2]),
     ]
     for load in loads:
         load.start()
@@ -1036,9 +1095,10 @@
             jax.ShapeDtypeStruct(full, BF16),
             jax.ShapeDtypeStruct((8, units), F32),
         ),
-        in_specs=[WHOLE, WHOLE, HBM, HBM, WHOLE],
+        in_specs=[WHOLE, HBM, HBM, HBM, WHOLE],
         out_specs=(WHOLE, HBM, HBM, HBM, HBM, WHOLE),
         scratch_shapes=[
+            pltpu.VMEM(full, BF16),
             pltpu.VMEM((width, units), BF16),
             pltpu.VMEM((n_dp, units, part), BF16),
             pltpu.VMEM(wide, BF16),
@@ -1047,7 +1107,7 @@
             pltpu.VMEM(full, BF16),
         ]
         + line_sems(size)
-        + [pltpu.SemaphoreType.DMA((2,)), pltpu.SemaphoreType.DMA((4, size))],
+        + [pltpu.SemaphoreType.DMA((3,)), pltpu.SemaphoreType.DMA((4, size))],
         compiler_params=params(cid),
         name="hidden",
     )(c_own, gm, up, down, bias)
@@ -1204,7 +1264,9 @@
     up_shift = up_all.transpose(1, 0, 2).reshape(1, units).astype(F32)
     qkv_shift = jnp.concatenate([qv_all[0], jnp.zeros_like(qv_all[0]), qv_all[1]])
 
-    qkv_full = lax.all_gather(qkv_weight.reshape(part, 3 * local), "dp", axis=0, tiled=True)
+    qkv_full = lax.all_gather(
+        qkv_weight.transpose(1, 0, 2).reshape(3 * part, local), "dp", axis=0, tiled=False
+    ).reshape(n_dp, 3, part, local)
     out_full = lax.all_gather(out_weight, "dp", axis=1, tiled=True)
     up_full = lax.all_gather(up_weight, "dp", axis=0, tiled=True)
     down_blocks = lax.all_gather(down_weight, "dp", axis=0, tiled=False)

time: 623 us -> 588 us (0.944)
  Pallas kernels: 567 us -> 535 us
    pallas_call x1, Pallas kernels: 64.7 us -> 48.3 us  [finish(): pl.pallas_call(functools.partial(finish_kernel, size), out_shape=(jax.Sha...]
    pallas_call x1, Pallas kernels: 131 us -> 116 us  [back_middle(): pl.pallas_call(functools.partial(back_middle_kernel, size), out_shape=(ja...]
  transfers between devices with their start and end apart: 7 -> 7, of which waited for: 0 -> 0; matrix products, arithmetic and copies ran while one was open for 4% -> 4% of each run, Pallas kernels for 73% -> 72%
where the time goes in v7:
time: 588 us; the launch traced here: 587 us
  Pallas kernels  535 us (91%)
  local copies, waits for them, and re-layouts  23.3 us (4%)
  between operations  16.1 us (3%)
  other arithmetic  8.99 us (2%)
    pallas_call x1, Pallas kernels, back_middle(): pl.pallas_call(functools.partial(back_middle_kernel, size), out_shape=(ja...  116 us
    pallas_call x1, Pallas kernels, hidden(): pl.pallas_call(functools.partial(hidden_kernel, n_dp, size), out_shape=(j...  87.1 us
    pallas_call x1, Pallas kernels, first(): pl.pallas_call(functools.partial(first_kernel, n_dp, size, part), out_sha...  79.4 us
    pallas_call x1, Pallas kernels, middle(): pl.pallas_call(functools.partial(middle_kernel, size), out_shape=(jax.Sha...  77.4 us
    pallas_call x1, Pallas kernels, finish(): pl.pallas_call(functools.partial(finish_kernel, size), out_shape=(jax.Sha...  48.3 us
    pallas_call x1, Pallas kernels, front(): pl.pallas_call(functools.partial(front_kernel, size, heads), grid=(heads,...  31.9 us
    pallas_call x1, Pallas kernels, attend_back(): pl.pallas_call(functools.partial(attend_back_kernel, size, heads), grid=(...  29.4 us
    pallas_call x1, Pallas kernels, products(): pl.pallas_call(functools.partial(products_kernel, size, steps), grid=(ste...  25.9 us
  transfers between devices with their start and end apart: 7, of which 0 were waited for; matrix products, arithmetic and copies ran while one was open for 4% of the time, Pallas kernels for 72%

profile of v7, /device:TPU:0, one launch (start us, length us, event | category | flops | bytes accessed | tf_op | source)
XLA Modules:
  0.0 587.0 jit_solution(1325347066177890252)
XLA Ops:
  7.3 0.7 all-gather.8.cloned.1.call-update
  8.0 0.7 all-gather.6.cloned.1.call-update
  8.8 0.7 all-gather.10.cloned.1.call-update
  9.5 0.5 all-gather.12.cloned.1.call-update
  11.2 0.2 dynamic-update-slice.11
  12.9 0.6 pad_bitcast_fusion.small
  13.5 79.4 %first.1 = (bf16[8,16,128]{2,1,0:T(8,128)(2,1)}, bf16[4,256,2048]{2,1,0:T(8,128)(2,1)}) custom-call(bf16[16,128]{1,0:T(8,128)(2,1)} %pad_bitcast_fusion.small, bf16[256,2048]{1,0:T(8,128)(2,1)} %tok_in.1), custom_call_target="tpu_custom_call" | custom-call | tf_op jit(solution)/shard_map/first/pallas_call | solution.py:441
  92.9 0.8 copy.93
  94.2 0.8 copy.72
  95.1 0.3 reshape.199
  95.5 0.6 pad_convert_fusion.vecs
  96.1 1.2 multiply_convert_fusion.cot.gm_in
  97.3 1.0 broadcast_in_dim.45.bar
  98.3 0.6 broadcast_in_dim.42.shift
  98.9 31.9 %front.1 = (bf16[1024,1536]{1,0:T(8,128)(2,1)}, bf16[1024,512]{1,0:T(8,128)(2,1)}, f32[4,8,1024]{2,1,0:T(8,128)}, bf16[1024,2048]{1,0:T(8,128)(2,1)}, bf16[2,256,2048]{2,1,0:T(8,128)(2,1)}) custom-call(bf16[1024,2048]{1,0:T(8,128)(2,1)} %bitcast.93, bf16[8,3,256,512]{3,2,1,0:T(8,128)(2,1)} %bitcast.88, f32[8,1536]{1,0:T(8,128)} %broadcast_in_dim.42.shift, ...), custom_call_target="tpu_custom_call" | custom-call | tf_op jit(solution)/shard_map/front/pallas_call | solution.py:882
  130.8 0.8 broadcast_in_dim.46.valid
  131.6 77.4 %middle.1 = (bf16[256,2048]{1,0:T(8,128)(2,1)}, bf16[4,256,2048]{2,1,0:T(8,128)(2,1)}, f32[256,2048]{1,0:T(8,128)}, f32[24,2048]{1,0:T(8,128)}) custom-call(bf16[4,256,2048]{2,1,0:T(8,128)(2,1)} %bitcast.100, bf16[256,2048]{1,0:T(8,128)(2,1)} %multiply_convert_fusion.cot.gm_in, bf16[2,256,2048]{2,1,0:T(8,128)(2,1)} %get-tuple-element.57.near, ...), custom_call_target="tpu_custom_call" | custom-call | tf_op jit(solution)/shard_map/middle/pallas_call | solution.py:515
  209.1 0.6 broadcast_in_dim.47.bias
  209.7 87.1 %hidden.1 = (bf16[4,256,2048]{2,1,0:T(8,128)(2,1)}, bf16[4,256,2048]{2,1,0:T(8,128)(2,1)}, bf16[4,256,2048]{2,1,0:T(8,128)(2,1)}, bf16[4,256,2048]{2,1,0:T(8,128...) custom-call(bf16[256,2048]{1,0:T(8,128)(2,1)} %get-tuple-element.58.c_own, ...), custom_call_target="tpu_custom_call" | custom-call | tf_op jit(solution)/shard_map/hidden/pallas_call | solution.py:1088
  296.8 25.9 %products.1 = (bf16[2048,2048]{1,0:T(8,128)(2,1)}, bf16[2048,2048]{1,0:T(8,128)(2,1)}, bf16[2,256,2048]{2,1,0:T(8,128)(2,1)}) custom-call(bf16[1024,2048]{1,0:T(8,128)(2,1)} %bitcast.98, bf16[1024,2048]{1,0:T(8,128)(2,1)} %bitcast.92, bf16[1024,2048]{1,0:T(8,128)(2,1)} %bitcast.97, bf16[1024,2048]{1,0:T(8,128)(2,1)} %bitcast.99, ...), custom_call_target="tpu_custom_call" | custom-call | tf_op jit(solution)/shard_map/products/pallas_call | solution.py:1155
  322.8 0.5 reduce-scatter.6.cloned.1.call-update
  323.4 116.1 %back_middle.1 = (bf16[4,256,2048]{2,1,0:T(8,128)(2,1)}, f32[256,2048]{1,0:T(8,128)}, bf16[2,256,2048]{2,1,0:T(8,128)(2,1)}, f32[32,2048]{1,0:T(8,128)}, bf16[4,256,512]{2,1,0:T(8,128)(2,1)}) custom-call(bf16[4,256,2048]{2,1,0:T(8,128)(2,1)} %get-tuple-element.60.terms, bf16[2,256,2048]{2,1,0:T(8,128)(2,1)} %get-tuple-element.64.landed, ...), custom_call_target="tpu_custom_call" | custom-call | tf_op jit(solution)/shard_map/back_middle/pallas_call | solution.py:612
  439.6 29.4 %attend_back.1 = (bf16[1024,1536]{1,0:T(8,128)(2,1)}, f32[4,16,128]{2,1,0:T(8,128)}, bf16[1024,2048]{1,0:T(8,128)(2,1)}, bf16[2,256,2048]{2,1,0:T(8,128)(2,1)}) custom-call(bf16[1024,1536]{1,0:T(8,128)(2,1)} %get-tuple-element.55.q.k.v, bf16[1024,1536]{1,0:T(8,128)(2,1)} %get-tuple-element.55.q.k.v, bf16[1024,1536]{1,0:T(8,128)(2,1)} %get-tuple-element.55.q.k.v, ...), custom_call_target="tpu_custom_call" | custom-call | tf_op jit(solution)/shard_map/attend_back/pallas_call | solution.py:976
  469.0 22.5 %head_products.1 = (bf16[2048,2048]{1,0:T(8,128)(2,1)}, bf16[2,256,2048]{2,1,0:T(8,128)(2,1)}) custom-call(bf16[1024,2048]{1,0:T(8,128)(2,1)} %bitcast.101, bf16[1024,2048]{1,0:T(8,128)(2,1)} %bitcast.94, bf16[1024,512]{1,0:T(8,128)(2,1)} %get-tuple-element.72.o, bf16[1024,1536]{1,0:T(8,128)(2,1)} %get-tuple-element.73.gqkv, bf16[4,256,2048]{2,1,0:T(8,128)(2,1)} %bitcast.90), custom_call_target="tpu_custom_call" | custom-call | tf_op jit(solution)/shard_map/head_products/pallas_call | solution.py:1208
  491.6 0.8 copy-done.7
  492.7 0.5 reshape.192
  493.2 0.8 copy.73
  494.1 0.8 slice_reduce_fusion.13
  495.2 48.3 %finish.1 = (f32[256,2048]{1,0:T(8,128)}, bf16[256,2048]{1,0:T(8,128)(2,1)}, f32[32,2048]{1,0:T(8,128)}) custom-call(bf16[4,256,2048]{2,1,0:T(8,128)(2,1)} %bitcast.91, bf16[2,256,2048]{2,1,0:T(8,128)(2,1)} %get-tuple-element.78.first_landed, bf16[256,2048]{1,0:T(8,128)(2,1)} %tok_in.1, f32[256,2048]{1,0:T(8,128)} %get-tuple-element.79.gmid_in, ...), custom_call_target="tpu_custom_call" | custom-call | tf_op jit(solution)/shard_map/finish/pallas_call | solution.py:700
  543.5 1.1 slice_reduce_fusion
  544.9 0.7 copy.92
  545.5 17.0 %reduce_small.1 = f32[32,128]{1,0:T(8,128)} custom-call(f32[8,32,128]{2,1,0:T(8,128)} %bitcast.107), custom_call_target="tpu_custom_call" | custom-call | tf_op jit(solution)/shard_map/reduce_small/pallas_call | solution.py:774
  562.5 1.2 slice.181
  563.7 0.8 slice_reduce_fusion.11
  564.7 0.7 slice_reduce_fusion.14
  565.4 0.7 reshape.196
  566.1 1.4 slice_bitcast_fusion.6
  567.7 0.6 copy.79
  568.3 1.6 convert_element_type.88
  569.9 1.5 convert_element_type.89
  572.0 0.5 divide_sqrt_fusion
  572.5 1.1 convert_bitcast_fusion
  573.6 1.0 copy.78
  574.8 0.5 copy.76
  575.3 1.6 copy.77
  576.9 1.0 copy.115
  577.9 1.0 copy-done
  578.9 1.3 copy.116
  (125 shorter events, 4.0 us)
Async XLA Ops:
  7.2 3.6 copy-start.9
  7.2 3.7 copy-start.10
  7.2 4.0 copy-start.11
  7.2 4.2 copy-start.12
  7.2 4.4 copy-start.13
  7.2 4.6 copy-start.14
  7.2 4.8 copy-start.15
  7.3 5.0 copy-start.16
  7.3 90.1 %all-gather.8.cloned.1.call-start = ((), (), s32[]{:S(2)}) async-start(), calls=%async_computation.4 | async-start | bytes 2359296 | tf_op jit(solution)/shard_map/all_gather | solution.py:1270
  8.0 89.3 %all-gather.6.cloned.1.call-start = ((), (), s32[]{:S(2)}) async-start(), calls=%async_computation.3 | async-start | bytes 7077888 | tf_op jit(solution)/shard_map/all_gather | solution.py:1267
  8.7 200.3 %all-gather.10.cloned.1.call-start = ((), (), s32[]{:S(2)}) async-start(), calls=%async_computation.5 | async-start | bytes 9437184 | tf_op jit(solution)/shard_map/all_gather | solution.py:1271
  9.5 86.6 %copy-start.5 = (bf16[256,2048]{1,0:T(8,128)(2,1)S(1)}, bf16[256,2048]{1,0:T(8,128)(2,1)}, u32[]{:S(2)}) copy-start(bf16[256,2048]{1,0:T(8,128)(2,1)} %param.29) | copy-start | bytes 3145732
  9.5 199.6 %all-gather.12.cloned.1.call-start = ((), (), s32[]{:S(2)}) async-start(), calls=%async_computation.9 | async-start | bytes 9437184 | tf_op jit(solution)/shard_map/all_gather | solution.py:1272
  10.1 481.4 %reduce-scatter.4.cloned.1.call-start = ((), (), s32[]{:S(2)}) async-start(), calls=%async_computation.6 | async-start | bytes 9437184 | tf_op jit(solution)/shard_map/reduce_scatter | solution.py:1294
  322.8 168.7 %reduce-scatter.6.cloned.1.call-start = ((), (), s32[]{:S(2)}) async-start(), calls=%async_computation.7 | async-start | bytes 9437184 | tf_op jit(solution)/shard_map/reduce_scatter | solution.py:1295
  323.4 249.2 %reduce-scatter.8.cloned.1.call-start = ((), (), s32[]{:S(2)}) async-start(), calls=%async_computation.8 | async-start | bytes 9437184 | tf_op jit(solution)/shard_map/reduce_scatter | solution.py:1309
  491.5 0.9 copy-start.7
  491.5 1.1 copy-start.8
  491.6 3.5 copy-start.6
  543.5 24.8 %copy-start.2 = (bf16[256,2048]{1,0:T(8,128)(2,1)S(1)}, bf16[256,2048]{1,0:T(8,128)(2,1)}, u32[]{:S(2)}) copy-start(bf16[256,2048]{1,0:T(8,128)(2,1)} %reduce-scatter.6.cloned.1.call-done) | copy-start | bytes 3145732
  544.8 25.1 %copy-start.1 = (bf16[2048,256]{1,0:T(8,128)(2,1)S(1)}, bf16[2048,256]{1,0:T(8,128)(2,1)}, u32[]{:S(2)}) copy-start(bf16[2048,256]{1,0:T(8,128)(2,1)} %reduce-scatter.4.cloned.1.call-done) | copy-start | bytes 3145732
  572.5 2.1 copy-start.3
  575.3 1.6 copy-start.4
  576.9 2.0 copy-start
Sparse Core Ops, SparseCore 0:
  9.9 30.8 all-gather.7
  42.7 45.4 all-gather.5
  90.1 54.2 all-gather.9
  146.1 54.2 all-gather.11
  322.9 68.8 reduce-scatter.3
  395.1 71.5 reduce-scatter.5
  491.7 73.1 reduce-scatter.7

commit v8 on v7

--- a/solution.py
+++ b/solution.py
@@ -636,9 +636,9 @@
 
 
 def finish_kernel(
-    size, terms, first_landed, tok_in, gmid_in, mlp, landed, mid_in, valid, vecs,
-    grad_out, y_out, stats, right, left, own_mlp, tok, ends, gmid, mid,
-    ss, sr, load_sem, early_sem,
+    n_dp, size, shared, terms, first_landed, tok_in, gmid_in, mlp, landed, mid_in, valid, vecs, given,
+    grad_out, y_out, reduced, rms, right, left, own_mlp, tok, ends, gmid, mid,
+    stats, blocks, land, sums, land2, ss, sr, load_sem, early_sem, s1, r1, s2, r2,
 ):
     rows = tok.shape[0]
     line = Line(size, rows)
@@ -655,7 +655,15 @@
     early = line.early_start(first_landed, (right, left), early_sem)
     for load in loads:
         load.start()
-    line.barrier()
+    me = lax.axis_index("dp")
+    entry = pltpu.get_barrier_semaphore()
+    for p in range(1, n_dp):
+        pl.semaphore_signal(entry, device_id={"dp": lax.rem(me + p, n_dp)}, device_id_type=MESH)
+    for p in range(1, size):
+        pl.semaphore_signal(
+            entry, device_id={"tensor": lax.rem(line.t + p, size)}, device_id_type=MESH
+        )
+    pl.semaphore_wait(entry, n_dp + size - 2)
     line.early_sends(terms, (right, left), (ss, sr), early)
     stats[...] = jnp.zeros_like(stats)
 
@@ -691,40 +699,26 @@
     for piece in range(SUBS):
         line.own_wait((right, left), (ss, sr), piece)
         row_loop(line.sub, step, body, piece * line.sub)
-    line.drain_scatter((right, left), (ss, sr), 0, True)
-
-
-def finish(terms, first_landed, tok, gmid, mlp, landed, mid, valid, vecs, size, cid):
-    rows, width = tok.shape
-    full = (size, rows, width)
-    return pl.pallas_call(
-        functools.partial(finish_kernel, size),
-        out_shape=(
-            jax.ShapeDtypeStruct((rows, width), F32),
-            jax.ShapeDtypeStruct((rows, width), BF16),
-            jax.ShapeDtypeStruct((32, width), F32),
-        ),
-        in_specs=[WHOLE] + [HBM] * 6 + [WHOLE, WHOLE],
-        out_specs=(WHOLE,) * 3,
-        scratch_shapes=[pltpu.VMEM(full, BF16)] * 2
-        + [pltpu.VMEM((rows, width), BF16)] * 2
-        + [pltpu.VMEM((2, rows, width), BF16)]
-        + [pltpu.VMEM((rows, width), F32)] * 2
-        + line_sems(size)
-        + [pltpu.SemaphoreType.DMA((5,)), pltpu.SemaphoreType.DMA((2,))],
-        compiler_params=params(cid),
-        name="finish",
-    )(terms, first_landed, tok, gmid, mlp, landed, mid, valid, vecs)
-
-
-def reduce_small_kernel(n_dp, n_t, shared, blocks, out, land, sums, land2, s1, r1, s2, r2):
-    me, t = lax.axis_index("dp"), lax.axis_index("tensor")
-    sem = pltpu.get_barrier_semaphore()
-    for p in range(1, n_dp):
-        pl.semaphore_signal(sem, device_id={"dp": lax.rem(me + p, n_dp)}, device_id_type=MESH)
-    for p in range(1, n_t):
-        pl.semaphore_signal(sem, device_id={"tensor": lax.rem(t + p, n_t)}, device_id_type=MESH)
-    pl.semaphore_wait(sem, n_dp + n_t - 2)
+    per = tok.shape[1] // n_dp // 128
+    blocks[...] = given[...]
+
+    def lanes(total, chunk):
+        return total[:, chunk * 128 : (chunk + 1) * 128]
+
+    for place, group in ((0, 0), (1, 1)):
+        total = jnp.sum(stats[8 * group : 8 * group + 8, :], axis=0, keepdims=True)
+        for d in range(n_dp):
+            for r in range(per):
+                row = place * per + r
+                blocks[d, row : row + 1, :] = lanes(total, d * per + r)
+    for place, group in ((9, 2), (10, 3)):
+        total = jnp.sum(stats[8 * group : 8 * group + 8, :], axis=0, keepdims=True)
+        short = lanes(total, 0)
+        for chunk in range(1, n_dp * per):
+            short = short + lanes(total, chunk)
+        for d in range(n_dp):
+            row = place * per
+            blocks[d, row : row + 1, :] = short
 
     def one(p):
         other = lax.rem(me + p, n_dp)
@@ -751,43 +745,69 @@
             dst_ref=land2.at[p],
             send_sem=s2.at[p],
             recv_sem=r2.at[p],
-            device_id={"tensor": lax.rem(t + p, n_t)},
+            device_id={"tensor": lax.rem(line.t + p, size)},
             device_id_type=MESH,
         )
 
-    for p in range(1, n_t):
+    for p in range(1, size):
         two(p).start()
-    out[...] = total
+    reduced[...] = total
     top = sums[pl.ds(0, shared), :]
-    for p in range(1, n_t):
+    for p in range(1, size):
         two(p).wait_recv()
         top = top + land2[p]
-    out[pl.ds(0, shared), :] = top
+    reduced[pl.ds(0, shared), :] = top
+    count = reduced[11 * per : 11 * per + 1, :] * jnp.float32(tok.shape[1])
+    for i in range(5):
+        row = (6 + i) * per
+        square = jnp.sum(reduced[row : row + per, :], keepdims=True)
+        rms[i : i + 1, :] = jnp.sqrt(square / count)
+    line.drain_scatter((right, left), (ss, sr), 0, True)
     for p in range(1, n_dp):
         one(p).wait_send()
-    for p in range(1, n_t):
+    for p in range(1, size):
         two(p).wait_send()
 
 
-def reduce_small(blocks, shared, n_dp, n_t, cid):
-    _, rows, width = blocks.shape
+def finish(
+    terms, first_landed, tok, gmid, mlp, landed, mid, valid, vecs, given, shared, size, cid
+):
+    rows, width = tok.shape
+    n_dp, lines, _ = given.shape
+    full = (size, rows, width)
     return pl.pallas_call(
-        functools.partial(reduce_small_kernel, n_dp, n_t, shared),
-        out_shape=jax.ShapeDtypeStruct((rows, width), F32),
-        in_specs=[WHOLE],
-        out_specs=WHOLE,
-        scratch_shapes=[
-            pltpu.VMEM((n_dp, rows, width), F32),
-            pltpu.VMEM((rows, width), F32),
-            pltpu.VMEM((n_t, shared, width), F32),
+        functools.partial(finish_kernel, n_dp, size, shared),
+        out_shape=(
+            jax.ShapeDtypeStruct((rows, width), F32),
+            jax.ShapeDtypeStruct((rows, width), BF16),
+            jax.ShapeDtypeStruct((lines, 128), F32),
+            jax.ShapeDtypeStruct((8, 128), F32),
+        ),
+        in_specs=[WHOLE] + [HBM] * 6 + [WHOLE] * 3,
+        out_specs=(WHOLE,) * 4,
+        scratch_shapes=[pltpu.VMEM(full, BF16)] * 2
+        + [pltpu.VMEM((rows, width), BF16)] * 2
+        + [pltpu.VMEM((2, rows, width), BF16)]
+        + [pltpu.VMEM((rows, width), F32)] * 2
+        + [
+            pltpu.VMEM((32, width), F32),
+            pltpu.VMEM((n_dp, lines, 128), F32),
+            pltpu.VMEM((n_dp, lines, 128), F32),
+            pltpu.VMEM((lines, 128), F32),
+            pltpu.VMEM((size, shared, 128), F32),
+        ]
+        + line_sems(size)
+        + [
+            pltpu.SemaphoreType.DMA((5,)),
+            pltpu.SemaphoreType.DMA((2,)),
             pltpu.SemaphoreType.DMA((n_dp,)),
             pltpu.SemaphoreType.DMA((n_dp,)),
-            pltpu.SemaphoreType.DMA((n_t,)),
-            pltpu.SemaphoreType.DMA((n_t,)),
+            pltpu.SemaphoreType.DMA((size,)),
+            pltpu.SemaphoreType.DMA((size,)),
         ],
         compiler_params=params(cid),
-        name="reduce_small",
-    )(blocks)
+        name="finish",
+    )(terms, first_landed, tok, gmid, mlp, landed, mid, valid, vecs, given)
 
 
 BLOCK = 256
@@ -1309,32 +1329,24 @@
     head_out = lax.psum_scatter(head_grad, "dp", scatter_dimension=0, tiled=True)
     out_out = head_out[:, :local].T
     qkv_out = head_out[:, local:].reshape(part, 3, local)
-    tokens_grad, output, stats_c = finish(
-        last_terms, last_early, tokens, gmid, mlp, landed, mid, valid, vecs, n_t, 4
-    )
-
     def vec_sum(stats, i):
         return jnp.sum(stats[8 * i : 8 * i + 8], axis=0)
 
-    vectors = jnp.stack(
-        [
-            vec_sum(stats_c, 0), vec_sum(stats_c, 1), vec_sum(stats_b, 2),
-            vec_sum(stats_b, 0), vec_sum(stats_b, 1), vec_sum(stats_b, 3),
-        ]
-    )
     def squares(stats, i):
         return jnp.sum(stats[8 * i : 8 * i + 8].reshape(8, n_dp, part), axis=(0, 1))
 
-    sums = jnp.concatenate(
-        [
-            squares(stats_a, 0), squares(stats_a, 1), squares(stats_a, 2),
-            squares(stats_c, 2), squares(stats_c, 3),
-        ]
-    )
+    vectors = jnp.concatenate(
+        [jnp.zeros((2, width), F32), jnp.stack([vec_sum(stats_b, i) for i in (2, 0, 1, 3)])]
+    )
+    sums = jnp.concatenate([squares(stats_a, i) for i in range(3)] + [jnp.zeros((2 * part,), F32)])
     count = jnp.clip(length - t * rows, 0, rows).astype(F32)
     vector_blocks = vectors.reshape(6, n_dp, part).transpose(1, 0, 2).reshape(n_dp, 6 * part)
     top = jnp.concatenate(
-        [vector_blocks, jnp.broadcast_to(sums[None], (n_dp, 5 * part)), jnp.full((n_dp, 1), count)],
+        [
+            vector_blocks,
+            jnp.broadcast_to(sums[None], (n_dp, 5 * part)),
+            jnp.full((n_dp, 128), count),
+        ],
         axis=1,
     )
     top_len = -(-top.shape[1] // 1024) * 1024
@@ -1345,12 +1357,15 @@
     qv_blocks = qv_blocks.reshape(n_dp, 2 * heads * hd_part)
     low = jnp.concatenate([up_blocks, qv_blocks], axis=1)
     low_len = -(-low.shape[1] // 1024) * 1024
-    blocks = jnp.concatenate([pad_to(top, top_len), pad_to(low, low_len)], axis=1)
-    blocks = blocks.reshape(n_dp, (top_len + low_len) // 128, 128)
-    reduced = reduce_small(blocks, top_len // 128, n_dp, n_t, 5).reshape(-1)
+    given = jnp.concatenate([pad_to(top, top_len), pad_to(low, low_len)], axis=1)
+    given = given.reshape(n_dp, (top_len + low_len) // 128, 128)
+    tokens_grad, output, reduced, rms = finish(
+        last_terms, last_early, tokens, gmid, mlp, landed, mid, valid, vecs, given,
+        top_len // 128, n_t, 4,
+    )
+    reduced = reduced.reshape(-1)
     outs = [reduced[i * part : (i + 1) * part] for i in range(6)]
-    totals = jnp.sum(reduced[6 * part : 11 * part].reshape(5, part), axis=1)
-    stream_rms = jnp.sqrt(totals / (reduced[11 * part] * width))
+    stream_rms = rms[:5, 0]
     at = top_len
     up_bias_out = reduced[at : at + units // n_dp].reshape(up_bias.shape)
     at += units // n_dp

time: 588 us -> 587 us (level)
    pallas_call x2 -> x1, Pallas kernels: 65.2 us -> 67.9 us  [finish(): pl.pallas_call(functools.partial(finish_kernel, n_dp, size, shared), out_...]
  transfers between devices with their start and end apart: 7 -> 7, of which waited for: 0 -> 0; matrix products, arithmetic and copies ran while one was open for 4% -> 3% of each run, Pallas kernels for 72% -> 73%
where the time goes in v8:
time: 587 us; the launch traced here: 586 us
  Pallas kernels  538 us (92%)
  local copies, waits for them, and re-layouts  22.7 us (4%)
  between operations  15.4 us (3%)
  other arithmetic  6.41 us (1%)
    pallas_call x1, Pallas kernels, back_middle(): pl.pallas_call(functools.partial(back_middle_kernel, size), out_shape=(ja...  116 us
    pallas_call x1, Pallas kernels, hidden(): pl.pallas_call(functools.partial(hidden_kernel, n_dp, size), out_shape=(j...  87.1 us
    pallas_call x1, Pallas kernels, first(): pl.pallas_call(functools.partial(first_kernel, n_dp, size, part), out_sha...  79.4 us
    pallas_call x1, Pallas kernels, middle(): pl.pallas_call(functools.partial(middle_kernel, size), out_shape=(jax.Sha...  77.5 us
    pallas_call x1, Pallas kernels, finish(): pl.pallas_call(functools.partial(finish_kernel, n_dp, size, shared), out_...  67.9 us
    pallas_call x1, Pallas kernels, front(): pl.pallas_call(functools.partial(front_kernel, size, heads), grid=(heads,...  31.9 us
    pallas_call x1, Pallas kernels, attend_back(): pl.pallas_call(functools.partial(attend_back_kernel, size, heads), grid=(...  29.4 us
    pallas_call x1, Pallas kernels, products(): pl.pallas_call(functools.partial(products_kernel, size, steps), grid=(ste...  25.9 us
  transfers between devices with their start and end apart: 7, of which 0 were waited for; matrix products, arithmetic and copies ran while one was open for 3% of the time, Pallas kernels for 73%

profile of v8, /device:TPU:0, one launch (start us, length us, event | category | flops | bytes accessed | tf_op | source)
XLA Modules:
  0.0 585.8 jit_solution(13278783065476487259)
XLA Ops:
  7.3 0.7 all-gather.8.cloned.1.call-update
  8.0 0.7 all-gather.6.cloned.1.call-update
  8.8 0.7 all-gather.10.cloned.1.call-update
  9.5 0.5 all-gather.12.cloned.1.call-update
  11.2 0.2 dynamic-update-slice.5
  11.4 0.2 dynamic-update-slice.6
  11.6 0.2 dynamic-update-slice.7
  11.9 0.2 dynamic-update-slice.8
  12.1 0.2 dynamic-update-slice.9
  12.9 0.6 pad_bitcast_fusion.small
  13.5 79.4 %first.1 = (bf16[8,16,128]{2,1,0:T(8,128)(2,1)}, bf16[4,256,2048]{2,1,0:T(8,128)(2,1)}) custom-call(bf16[16,128]{1,0:T(8,128)(2,1)} %pad_bitcast_fusion.small, bf16[256,2048]{1,0:T(8,128)(2,1)} %tok_in.1), custom_call_target="tpu_custom_call" | custom-call | tf_op jit(solution)/shard_map/first/pallas_call | solution.py:441
  92.9 0.8 copy.93
  94.2 0.8 copy.72
  95.1 0.3 reshape.183
  95.5 0.6 pad_convert_fusion.vecs
  96.1 1.2 multiply_convert_fusion.cot.gm_in
  97.3 1.0 broadcast_in_dim.44.bar
  98.3 0.6 broadcast_in_dim.22.shift
  98.9 31.9 %front.1 = (bf16[1024,1536]{1,0:T(8,128)(2,1)}, bf16[1024,512]{1,0:T(8,128)(2,1)}, f32[4,8,1024]{2,1,0:T(8,128)}, bf16[1024,2048]{1,0:T(8,128)(2,1)}, bf16[2,256,2048]{2,1,0:T(8,128)(2,1)}) custom-call(bf16[1024,2048]{1,0:T(8,128)(2,1)} %bitcast.90, bf16[8,3,256,512]{3,2,1,0:T(8,128)(2,1)} %bitcast.85, f32[8,1536]{1,0:T(8,128)} %broadcast_in_dim.22.shift, ...), custom_call_target="tpu_custom_call" | custom-call | tf_op jit(solution)/shard_map/front/pallas_call | solution.py:902
  130.8 0.8 broadcast_in_dim.45.valid
  131.6 77.5 %middle.1 = (bf16[256,2048]{1,0:T(8,128)(2,1)}, bf16[4,256,2048]{2,1,0:T(8,128)(2,1)}, f32[256,2048]{1,0:T(8,128)}, f32[24,2048]{1,0:T(8,128)}) custom-call(bf16[4,256,2048]{2,1,0:T(8,128)(2,1)} %bitcast.97, bf16[256,2048]{1,0:T(8,128)(2,1)} %multiply_convert_fusion.cot.gm_in, bf16[2,256,2048]{2,1,0:T(8,128)(2,1)} %get-tuple-element.58.near, ...), custom_call_target="tpu_custom_call" | custom-call | tf_op jit(solution)/shard_map/middle/pallas_call | solution.py:515
  209.1 0.6 broadcast_in_dim.46.bias
  209.7 87.1 %hidden.1 = (bf16[4,256,2048]{2,1,0:T(8,128)(2,1)}, bf16[4,256,2048]{2,1,0:T(8,128)(2,1)}, bf16[4,256,2048]{2,1,0:T(8,128)(2,1)}, bf16[4,256,2048]{2,1,0:T(8,128...) custom-call(bf16[256,2048]{1,0:T(8,128)(2,1)} %get-tuple-element.59.c_own, ...), custom_call_target="tpu_custom_call" | custom-call | tf_op jit(solution)/shard_map/hidden/pallas_call | solution.py:1108
  296.8 25.9 %products.1 = (bf16[2048,2048]{1,0:T(8,128)(2,1)}, bf16[2048,2048]{1,0:T(8,128)(2,1)}, bf16[2,256,2048]{2,1,0:T(8,128)(2,1)}) custom-call(bf16[1024,2048]{1,0:T(8,128)(2,1)} %bitcast.95, bf16[1024,2048]{1,0:T(8,128)(2,1)} %bitcast.89, bf16[1024,2048]{1,0:T(8,128)(2,1)} %bitcast.94, bf16[1024,2048]{1,0:T(8,128)(2,1)} %bitcast.96, ...), custom_call_target="tpu_custom_call" | custom-call | tf_op jit(solution)/shard_map/products/pallas_call | solution.py:1175
  322.9 0.5 reduce-scatter.6.cloned.1.call-update
  323.4 116.1 %back_middle.1 = (bf16[4,256,2048]{2,1,0:T(8,128)(2,1)}, f32[256,2048]{1,0:T(8,128)}, bf16[2,256,2048]{2,1,0:T(8,128)(2,1)}, f32[32,2048]{1,0:T(8,128)}, bf16[4,256,512]{2,1,0:T(8,128)(2,1)}) custom-call(bf16[4,256,2048]{2,1,0:T(8,128)(2,1)} %get-tuple-element.61.terms, bf16[2,256,2048]{2,1,0:T(8,128)(2,1)} %get-tuple-element.65.landed, ...), custom_call_target="tpu_custom_call" | custom-call | tf_op jit(solution)/shard_map/back_middle/pallas_call | solution.py:612
  439.6 29.4 %attend_back.1 = (bf16[1024,1536]{1,0:T(8,128)(2,1)}, f32[4,16,128]{2,1,0:T(8,128)}, bf16[1024,2048]{1,0:T(8,128)(2,1)}, bf16[2,256,2048]{2,1,0:T(8,128)(2,1)}) custom-call(bf16[1024,1536]{1,0:T(8,128)(2,1)} %get-tuple-element.56.q.k.v, bf16[1024,1536]{1,0:T(8,128)(2,1)} %get-tuple-element.56.q.k.v, bf16[1024,1536]{1,0:T(8,128)(2,1)} %get-tuple-element.56.q.k.v, ...), custom_call_target="tpu_custom_call" | custom-call | tf_op jit(solution)/shard_map/attend_back/pallas_call | solution.py:996
  469.0 22.5 %head_products.1 = (bf16[2048,2048]{1,0:T(8,128)(2,1)}, bf16[2,256,2048]{2,1,0:T(8,128)(2,1)}) custom-call(bf16[1024,2048]{1,0:T(8,128)(2,1)} %bitcast.98, bf16[1024,2048]{1,0:T(8,128)(2,1)} %bitcast.91, bf16[1024,512]{1,0:T(8,128)(2,1)} %get-tuple-element.73.o, bf16[1024,1536]{1,0:T(8,128)(2,1)} %get-tuple-element.74.gqkv, bf16[4,256,2048]{2,1,0:T(8,128)(2,1)} %bitcast.87), custom_call_target="tpu_custom_call" | custom-call | tf_op jit(solution)/shard_map/head_products/pallas_call | solution.py:1228
  491.7 0.8 copy-done.7
  492.7 0.5 reshape.177
  493.2 0.8 copy.73
  494.1 0.8 slice_reduce_fusion.9
  495.4 0.7 copy.92
  496.0 67.9 %finish.1 = (f32[256,2048]{1,0:T(8,128)}, bf16[256,2048]{1,0:T(8,128)(2,1)}, f32[32,128]{1,0:T(8,128)}, f32[8,128]{1,0:T(8,128)}) custom-call(bf16[4,256,2048]{2,1,0:T(8,128)(2,1)} %bitcast.88, bf16[2,256,2048]{2,1,0:T(8,128)(2,1)} %get-tuple-element.79.first_landed, bf16[256,2048]{1,0:T(8,128)(2,1)} %tok_in.1, f32[256,2048]{1,0:T(8,128)} %get-tuple-element.80.gmid_in, ...), custom_call_target="tpu_custom_call" | custom-call | tf_op jit(solution)/shard_map/finish/pallas_call | solution.py:778
  564.0 0.8 slice_reduce_fusion.10
  564.8 0.7 reshape.181
  565.5 1.4 slice_bitcast_fusion.6
  567.0 0.6 copy.79
  567.7 1.6 convert_element_type.88
  569.2 1.5 convert_element_type.89
  570.7 0.6 slice_reduce_fusion.7
  571.3 1.1 convert_bitcast_fusion
  572.4 1.0 copy.78
  573.6 0.5 copy.76
  574.1 1.6 copy.77
  575.7 1.0 copy.109
  576.7 1.0 copy-done
  577.7 1.3 copy.110
  (109 shorter events, 2.9 us)
Async XLA Ops:
  7.2 3.6 copy-start.10
  7.2 3.7 copy-start.11
  7.2 4.0 copy-start.12
  7.2 4.2 copy-start.13
  7.2 4.4 copy-start.14
  7.2 4.6 copy-start.15
  7.2 4.8 copy-start.16
  7.3 5.0 copy-start.17
  7.3 90.0 %all-gather.8.cloned.1.call-start = ((), (), s32[]{:S(2)}) async-start(), calls=%async_computation.4 | async-start | bytes 2359296 | tf_op jit(solution)/shard_map/all_gather | solution.py:1290
  8.0 89.3 %all-gather.6.cloned.1.call-start = ((), (), s32[]{:S(2)}) async-start(), calls=%async_computation.3 | async-start | bytes 7077888 | tf_op jit(solution)/shard_map/all_gather | solution.py:1287
  8.7 200.3 %all-gather.10.cloned.1.call-start = ((), (), s32[]{:S(2)}) async-start(), calls=%async_computation.5 | async-start | bytes 9437184 | tf_op jit(solution)/shard_map/all_gather | solution.py:1291
  9.5 86.6 %copy-start.5 = (bf16[256,2048]{1,0:T(8,128)(2,1)S(1)}, bf16[256,2048]{1,0:T(8,128)(2,1)}, u32[]{:S(2)}) copy-start(bf16[256,2048]{1,0:T(8,128)(2,1)} %param.29) | copy-start | bytes 3145732
  9.5 199.6 %all-gather.12.cloned.1.call-start = ((), (), s32[]{:S(2)}) async-start(), calls=%async_computation.9 | async-start | bytes 9437184 | tf_op jit(solution)/shard_map/all_gather | solution.py:1292
  10.1 481.5 %reduce-scatter.4.cloned.1.call-start = ((), (), s32[]{:S(2)}) async-start(), calls=%async_computation.6 | async-start | bytes 9437184 | tf_op jit(solution)/shard_map/reduce_scatter | solution.py:1314
  322.8 168.8 %reduce-scatter.6.cloned.1.call-start = ((), (), s32[]{:S(2)}) async-start(), calls=%async_computation.7 | async-start | bytes 9437184 | tf_op jit(solution)/shard_map/reduce_scatter | solution.py:1315
  323.4 247.9 %reduce-scatter.8.cloned.1.call-start = ((), (), s32[]{:S(2)}) async-start(), calls=%async_computation.8 | async-start | bytes 9437184 | tf_op jit(solution)/shard_map/reduce_scatter | solution.py:1329
  491.6 0.9 copy-start.7
  491.6 1.1 copy-start.8
  491.6 3.5 copy-start.6
  496.0 71.6 %copy-start.2 = (bf16[256,2048]{1,0:T(8,128)(2,1)S(1)}, bf16[256,2048]{1,0:T(8,128)(2,1)}, u32[]{:S(2)}) copy-start(bf16[256,2048]{1,0:T(8,128)(2,1)} %reduce-scatter.6.cloned.1.call-done) | copy-start | bytes 3145732
  564.0 5.2 copy-start.1
  569.2 1.5 copy-start.9
  571.3 2.1 copy-start.3
  574.1 1.6 copy-start.4
  575.7 2.0 copy-start
Sparse Core Ops, SparseCore 0:
  9.9 30.8 all-gather.7
  42.7 45.4 all-gather.5
  90.1 54.3 all-gather.9
  146.2 54.2 all-gather.11
  322.9 68.8 reduce-scatter.3
  395.1 71.4 reduce-scatter.5
  491.8 72.9 reduce-scatter.7

commit v9 on v8

--- a/solution.py
+++ b/solution.py
@@ -266,7 +266,9 @@
 
             lax.fori_loop(0, self.sub // step, add, 0)
 
-    def phase(self, gather=None, scatter=None, on_slot=None, near=None, ends=None, start=0):
+    def phase(
+        self, gather=None, scatter=None, on_slot=None, near=None, ends=None, start=0, on_part=None
+    ):
         n = self.size
         for k in range(start, n):
             for part in range(SUBS):
@@ -287,6 +289,8 @@
                                         way, k - 1 - b, part, scatter[0], scatter[1][way],
                                         scatter[2], ends,
                                     )
+                if on_part is not None:
+                    on_part(k, part)
             if on_slot is not None:
                 on_slot(k)
 
@@ -395,10 +399,10 @@
     for p in range(1, n_dp):
         small_copy(p, me).start()
     smalls[pl.ds(me, 1)] = small[...][None]
-    step = min(32, rows)
+    step = min(32, line.sub)
     vec_rows = part // 128
 
-    def normalise(source, shard):
+    def normalise(source, shard, piece):
         gain = jnp.concatenate(
             [smalls[d, r : r + 1, :] for d in range(n_dp) for r in range(vec_rows)], axis=1
         ).astype(F32)
@@ -413,24 +417,28 @@
             to = line.t if shard is None else shard
             a_out[to, at, :] = (normed * gain + shift).astype(BF16)
 
-        row_loop(rows, step, body)
-
-    def on_slot(k):
+        row_loop(line.sub, step, body, piece * line.sub)
+
+    def on_part(k, piece):
         if k == 0:
-            for p in range(1, n_dp):
-                small_copy(p, lax.rem(me + p, n_dp)).wait_recv()
-            normalise(own, None)
+            if piece == 0:
+                for p in range(1, n_dp):
+                    small_copy(p, lax.rem(me + p, n_dp)).wait_recv()
+            normalise(own, None, piece)
         else:
 
-            @pl.when(line.t >= k)
-            def _():
-                normalise(tok, line.t - k)
-
-            @pl.when(line.t + k <= size - 1)
-            def _():
-                normalise(tok, line.t + k)
-
-    line.phase(gather=(tok, sems, own), on_slot=on_slot)
+            def side(i, carry):
+                shard = line.t + k * (2 * i - 1)
+
+                @pl.when((shard >= 0) & (shard < size))
+                def _():
+                    normalise(tok, shard, piece)
+
+                return carry
+
+            lax.fori_loop(0, 2, side, 0)
+
+    line.phase(gather=(tok, sems, own), on_part=on_part)
     line.drain_gather(tok, sems)
     for p in range(1, n_dp):
         small_copy(p, me).wait_send()
@@ -458,8 +466,8 @@
 
 
 def middle_kernel(
-    size, terms, cot, near, tok, valid, vecs, c_out, gm_out, mid_out, stats,
-    right, left, gs, gr, ss, sr, near_sem,
+    size, terms, cot, near, tok, valid, vecs, c_out, gm_done, mid_out, stats,
+    gm_out, right, left, gs, gr, ss, sr, near_sem, out_sem,
 ):
     line = Line(size, tok.shape[0])
     rows = tok.shape[0]
@@ -486,6 +494,14 @@
         near=near,
         start=1,
     )
+    own.wait()
+    keep_all(lambda copy: copy.wait())
+    stores = [
+        pltpu.make_async_copy(gm_out.at[shard], gm_done.at[shard], out_sem.at[shard])
+        for shard in range(size)
+    ]
+    for store in stores:
+        store.start()
     stats[...] = jnp.zeros_like(stats)
 
     def body(at):
@@ -503,8 +519,8 @@
     for piece in range(SUBS):
         line.own_wait((right, left), (ss, sr), piece)
         row_loop(line.sub, step, body, piece * line.sub)
-    own.wait()
-    keep_all(lambda copy: copy.wait())
+    for store in stores:
+        store.wait()
     line.drain_gather(gm_out, (gs, gr), 1)
     line.drain_scatter((right, left), (ss, sr))
 
@@ -521,20 +537,20 @@
             jax.ShapeDtypeStruct((24, width), F32),
         ),
         in_specs=[WHOLE, HBM, HBM, WHOLE, WHOLE, WHOLE],
-        out_specs=(WHOLE,) * 4,
-        scratch_shapes=[pltpu.VMEM(full, BF16), pltpu.VMEM(full, BF16)]
+        out_specs=(WHOLE, HBM, WHOLE, WHOLE),
+        scratch_shapes=[pltpu.VMEM(full, BF16)] * 3
         + line_sems(size)
         + line_sems(size)
-        + [pltpu.SemaphoreType.DMA((3,))],
+        + [pltpu.SemaphoreType.DMA((3,)), pltpu.SemaphoreType.DMA((size,))],
         compiler_params=params(cid),
         name="middle",
     )(terms, cot, near, tok, valid, vecs)
 
 
 def back_middle_kernel(
-    size, terms, landed, mlp_in, gm_in, mid_in, vecs, out_in, gz_out, gmid_out, ends, stats,
-    go_out, right, left, right2, left2, mlp, gm, mid, out_w,
-    ss, sr, ms, mr, gs, gr, early_sem, load_sem,
+    size, terms, landed, mlp_in, gm_in, mid_in, vecs, out_in, gz_done, gmid_out, ends, stats,
+    go_out, gz_out, right, left, right2, left2, mlp, gm, mid, out_w,
+    ss, sr, ms, mr, gs, gr, early_sem, load_sem, out_sem,
 ):
     rows = mid.shape[0]
     line = Line(size, rows)
@@ -577,7 +593,11 @@
         row_loop(line.sub, step, body, piece * line.sub)
         for way in (0, 1):
             line.gather_step(way, 0, piece, gz_out, (gs, gr), None)
+    def store(shard):
+        return pltpu.make_async_copy(gz_out.at[shard], gz_done.at[shard], out_sem.at[shard])
+
     def weigh(shard):
+        store(shard).start()
         go_out[shard] = dot_t(gz_out[shard], out_w[...]).astype(BF16)
 
     def on_slot(k):
@@ -600,6 +620,8 @@
         ends=ends,
         start=1,
     )
+    for shard in range(size):
+        store(shard).wait()
     line.drain_scatter((right, left), (ss, sr), 0, True)
     line.drain_scatter((right2, left2), (ms, mr), 1)
     line.drain_gather(gz_out, (gs, gr))
@@ -619,8 +641,8 @@
             jax.ShapeDtypeStruct((size, rows, local), BF16),
         ),
         in_specs=[WHOLE, HBM, HBM, HBM, HBM, WHOLE, HBM],
-        out_specs=(WHOLE,) * 5,
-        scratch_shapes=[pltpu.VMEM(full, BF16)] * 5
+        out_specs=(HBM, WHOLE, WHOLE, WHOLE, WHOLE),
+        scratch_shapes=[pltpu.VMEM(full, BF16)] * 6
         + [
             pltpu.VMEM((rows, width), BF16),
             pltpu.VMEM((rows, width), F32),
@@ -629,16 +651,21 @@
         + line_sems(size)
         + line_sems(size)
         + line_sems(size)
-        + [pltpu.SemaphoreType.DMA((2,)), pltpu.SemaphoreType.DMA((4,))],
+        + [
+            pltpu.SemaphoreType.DMA((2,)),
+            pltpu.SemaphoreType.DMA((4,)),
+            pltpu.SemaphoreType.DMA((size,)),
+        ],
         compiler_params=params(cid),
         name="back_middle",
     )(terms, landed, mlp, gm, mid, vecs, out_w)
 
 
 def finish_kernel(
-    n_dp, size, shared, terms, first_landed, tok_in, gmid_in, mlp, landed, mid_in, valid, vecs, given,
-    grad_out, y_out, reduced, rms, right, left, own_mlp, tok, ends, gmid, mid,
-    stats, blocks, land, sums, land2, ss, sr, load_sem, early_sem, s1, r1, s2, r2,
+    n_dp, size, shared, terms, first_landed, tok_in, gmid_in, mlp, landed, mid_in, valid, vecs,
+    stats_a, stats_b, given, grad_out, y_out, reduced, rms, right, left, own_mlp, tok, ends,
+    gmid, mid, stats, blocks, land, sums, land2, late, late_land,
+    ss, sr, load_sem, early_sem, s1, r1, s2, r2, s3, r3,
 ):
     rows = tok.shape[0]
     line = Line(size, rows)
@@ -657,13 +684,17 @@
         load.start()
     me = lax.axis_index("dp")
     entry = pltpu.get_barrier_semaphore()
-    for p in range(1, n_dp):
-        pl.semaphore_signal(entry, device_id={"dp": lax.rem(me + p, n_dp)}, device_id_type=MESH)
-    for p in range(1, size):
-        pl.semaphore_signal(
-            entry, device_id={"tensor": lax.rem(line.t + p, size)}, device_id_type=MESH
-        )
-    pl.semaphore_wait(entry, n_dp + size - 2)
+    everyone = n_dp * size
+
+    def place(q):
+        return {"dp": lax.rem(me + q // size, n_dp), "tensor": lax.rem(line.t + q % size, size)}
+
+    def greet(q, carry):
+        pl.semaphore_signal(entry, device_id=place(q), device_id_type=MESH)
+        return carry
+
+    lax.fori_loop(1, everyone, greet, 0)
+    pl.semaphore_wait(entry, everyone - 1)
     line.early_sends(terms, (right, left), (ss, sr), early)
     stats[...] = jnp.zeros_like(stats)
 
@@ -678,6 +709,58 @@
         stats[16:24, :] += fold(ok * out * out)
         stats[24:32, :] += fold(ok * y * y)
 
+    per = tok.shape[1] // n_dp // 128
+
+    def lanes(total, chunk):
+        return total[:, chunk * 128 : (chunk + 1) * 128]
+
+    def group_sum(source, group):
+        return jnp.sum(source[8 * group : 8 * group + 8, :], axis=0, keepdims=True)
+
+    def put_vector(dst, row, total):
+        for d in range(n_dp):
+            for r in range(per):
+                dst[d, row + r : row + r + 1, :] = lanes(total, d * per + r)
+
+    def put_square(dst, row, total):
+        short = lanes(total, 0)
+        for chunk in range(1, n_dp * per):
+            short = short + lanes(total, chunk)
+        for d in range(n_dp):
+            dst[d, row : row + 1, :] = short
+
+    def one(p):
+        other = lax.rem(me + p, n_dp)
+        return pltpu.make_async_remote_copy(
+            src_ref=blocks.at[other],
+            dst_ref=land.at[p],
+            send_sem=s1.at[p],
+            recv_sem=r1.at[p],
+            device_id={"dp": other},
+            device_id_type=MESH,
+        )
+
+    def two(p):
+        return pltpu.make_async_remote_copy(
+            src_ref=sums.at[pl.ds(0, shared)],
+            dst_ref=land2.at[p],
+            send_sem=s2.at[p],
+            recv_sem=r2.at[p],
+            device_id={"tensor": lax.rem(line.t + p, size)},
+            device_id_type=MESH,
+        )
+
+    def three(q):
+        target = place(q)
+        return pltpu.make_async_remote_copy(
+            src_ref=late.at[target["dp"]],
+            dst_ref=late_land.at[q],
+            send_sem=s3.at[q],
+            recv_sem=r3.at[q],
+            device_id=target,
+            device_id_type=MESH,
+        )
+
     for j in range(size - 1):
         for piece in range(SUBS):
             for way in (0, 1):
@@ -688,6 +771,24 @@
             for load in loads:
                 load.wait()
             row_loop(rows, step, tail)
+            blocks[:, 0:shared, :] = jnp.zeros((n_dp, shared, 128), F32)
+            blocks[:, shared:, :] = given[...]
+            for i, group in ((2, 2), (3, 0), (4, 1), (5, 3)):
+                put_vector(blocks, i * per, group_sum(stats_b, group))
+            for i in range(3):
+                put_square(blocks, (6 + i) * per, group_sum(stats_a, i))
+            count = jnp.sum(valid[...], axis=0, keepdims=True)
+            for d in range(n_dp):
+                blocks[d, 11 * per : 11 * per + 1, :] = count
+            for p in range(1, n_dp):
+                one(p).start()
+    total = blocks[me]
+    for p in range(1, n_dp):
+        one(p).wait_recv()
+        total = total + land[p]
+    sums[...] = total
+    for p in range(1, size):
+        two(p).start()
 
     def body(at):
         e = line.own_sum(terms, (right, left), at)
@@ -699,69 +800,44 @@
     for piece in range(SUBS):
         line.own_wait((right, left), (ss, sr), piece)
         row_loop(line.sub, step, body, piece * line.sub)
-    per = tok.shape[1] // n_dp // 128
-    blocks[...] = given[...]
-
-    def lanes(total, chunk):
-        return total[:, chunk * 128 : (chunk + 1) * 128]
-
-    for place, group in ((0, 0), (1, 1)):
-        total = jnp.sum(stats[8 * group : 8 * group + 8, :], axis=0, keepdims=True)
-        for d in range(n_dp):
-            for r in range(per):
-                row = place * per + r
-                blocks[d, row : row + 1, :] = lanes(total, d * per + r)
-    for place, group in ((9, 2), (10, 3)):
-        total = jnp.sum(stats[8 * group : 8 * group + 8, :], axis=0, keepdims=True)
-        short = lanes(total, 0)
-        for chunk in range(1, n_dp * per):
-            short = short + lanes(total, chunk)
-        for d in range(n_dp):
-            row = place * per
-            blocks[d, row : row + 1, :] = short
-
-    def one(p):
-        other = lax.rem(me + p, n_dp)
-        return pltpu.make_async_remote_copy(
-            src_ref=blocks.at[other],
-            dst_ref=land.at[p],
-            send_sem=s1.at[p],
-            recv_sem=r1.at[p],
-            device_id={"dp": other},
-            device_id_type=MESH,
-        )
-
-    for p in range(1, n_dp):
-        one(p).start()
-    total = blocks[me]
-    for p in range(1, n_dp):
-        one(p).wait_recv()
-        total = total + land[p]
-    sums[...] = total
-
-    def two(p):
-        return pltpu.make_async_remote_copy(
-            src_ref=sums.at[pl.ds(0, shared)],
-            dst_ref=land2.at[p],
-            send_sem=s2.at[p],
-            recv_sem=r2.at[p],
-            device_id={"tensor": lax.rem(line.t + p, size)},
-            device_id_type=MESH,
-        )
-
-    for p in range(1, size):
-        two(p).start()
+    late[...] = jnp.zeros_like(late)
+    put_vector(late, 0, group_sum(stats, 0))
+    put_vector(late, per, group_sum(stats, 1))
+    put_square(late, 2 * per, group_sum(stats, 2))
+    put_square(late, 2 * per + 1, group_sum(stats, 3))
+
+    def send_late(q, carry):
+        three(q).start()
+        return carry
+
+    lax.fori_loop(1, everyone, send_late, 0)
     reduced[...] = total
     top = sums[pl.ds(0, shared), :]
     for p in range(1, size):
         two(p).wait_recv()
         top = top + land2[p]
     reduced[pl.ds(0, shared), :] = top
+
+    def take_late(q, held):
+        three(q).wait_recv()
+        return held + late_land[q]
+
+    final = lax.fori_loop(1, everyone, take_late, late[me])
+    reduced[0 : 2 * per, :] = final[0 : 2 * per, :]
+    for i in (9, 10):
+        row = 2 * per + i - 9
+        reduced[i * per : i * per + 1, :] = final[row : row + 1, :]
     count = reduced[11 * per : 11 * per + 1, :] * jnp.float32(tok.shape[1])
     for i in range(5):
         row = (6 + i) * per
-        square = jnp.sum(reduced[row : row + per, :], keepdims=True)
+        square = jnp.sum(reduced[row : row + 1, :], keepdims=True)
         rms[i : i + 1, :] = jnp.sqrt(square / count)
+
+    def sent_late(q, carry):
+        three(q).wait_send()
+        return carry
+
+    lax.fori_loop(1, everyone, sent_late, 0)
     line.drain_scatter((right, left), (ss, sr), 0, True)
     for p in range(1, n_dp):
         one(p).wait_send()
@@ -770,10 +846,13 @@
 
 
 def finish(
-    terms, first_landed, tok, gmid, mlp, landed, mid, valid, vecs, given, shared, size, cid
+    terms, first_landed, tok, gmid, mlp, landed, mid, valid, vecs, stats_a, stats_b, given,
+    shared, size, cid,
 ):
     rows, width = tok.shape
-    n_dp, lines, _ = given.shape
+    n_dp = given.shape[0]
+    lines = shared + given.shape[1]
+    late = (-(-(2 * width // n_dp // 128 + 2) // 8) * 8, 128)
     full = (size, rows, width)
     return pl.pallas_call(
         functools.partial(finish_kernel, n_dp, size, shared),
@@ -783,7 +862,7 @@
             jax.ShapeDtypeStruct((lines, 128), F32),
             jax.ShapeDtypeStruct((8, 128), F32),
         ),
-        in_specs=[WHOLE] + [HBM] * 6 + [WHOLE] * 3,
+        in_specs=[WHOLE] + [HBM] * 6 + [WHOLE] * 5,
         out_specs=(WHOLE,) * 4,
         scratch_shapes=[pltpu.VMEM(full, BF16)] * 2
         + [pltpu.VMEM((rows, width), BF16)] * 2
@@ -795,6 +874,8 @@
             pltpu.VMEM((n_dp, lines, 128), F32),
             pltpu.VMEM((lines, 128), F32),
             pltpu.VMEM((size, shared, 128), F32),
+            pltpu.VMEM((n_dp,) + late, F32),
+            pltpu.VMEM((n_dp * size,) + late, F32),
         ]
         + line_sems(size)
         + [
@@ -804,10 +885,12 @@
             pltpu.SemaphoreType.DMA((n_dp,)),
             pltpu.SemaphoreType.DMA((size,)),
             pltpu.SemaphoreType.DMA((size,)),
+            pltpu.SemaphoreType.DMA((n_dp * size,)),
+            pltpu.SemaphoreType.DMA((n_dp * size,)),
         ],
         compiler_params=params(cid),
         name="finish",
-    )(terms, first_landed, tok, gmid, mlp, landed, mid, valid, vecs, given)
+    )(terms, first_landed, tok, gmid, mlp, landed, mid, valid, vecs, stats_a, stats_b, given)
 
 
 BLOCK = 256
@@ -1039,7 +1122,7 @@
 
 def hidden_kernel(
     n_dp, size, c_own, gm_in, up_in, down_in, bias,
-    c_out, act_out, gu_out, mlp_out, back_out, sums, gm, up, down, act, gu, mlp, back, gs, gr, in_sem, out_sem,
+    c_done, act_out, gu_out, mlp_out, back_out, sums, c_out, gm, up, down, act, gu, mlp, back, gs, gr, in_sem, out_sem,
 ):
     line = Line(size, c_own.shape[0])
     rows, width = c_own.shape
@@ -1062,7 +1145,9 @@
         load.wait()
 
     def stores(shard):
-        pairs = ((act, act_out), (gu, gu_out), (mlp, mlp_out), (back, back_out))
+        pairs = (
+            (c_out, c_done), (act, act_out), (gu, gu_out), (mlp, mlp_out), (back, back_out),
+        )
         return [
             pltpu.make_async_copy(src.at[shard], dst.at[shard], out_sem.at[i, shard])
             for i, (src, dst) in enumerate(pairs)
@@ -1116,8 +1201,9 @@
             jax.ShapeDtypeStruct((8, units), F32),
         ),
         in_specs=[WHOLE, HBM, HBM, HBM, WHOLE],
-        out_specs=(WHOLE, HBM, HBM, HBM, HBM, WHOLE),
+        out_specs=(HBM, HBM, HBM, HBM, HBM, WHOLE),
         scratch_shapes=[
+            pltpu.VMEM(full, BF16),
             pltpu.VMEM(full, BF16),
             pltpu.VMEM((width, units), BF16),
             pltpu.VMEM((n_dp, units, part), BF16),
@@ -1127,7 +1213,7 @@
             pltpu.VMEM(full, BF16),
         ]
         + line_sems(size)
-        + [pltpu.SemaphoreType.DMA((3,)), pltpu.SemaphoreType.DMA((4, size))],
+        + [pltpu.SemaphoreType.DMA((3,)), pltpu.SemaphoreType.DMA((5, size))],
         compiler_params=params(cid),
         name="hidden",
     )(c_own, gm, up, down, bias)
@@ -1329,27 +1415,6 @@
     head_out = lax.psum_scatter(head_grad, "dp", scatter_dimension=0, tiled=True)
     out_out = head_out[:, :local].T
     qkv_out = head_out[:, local:].reshape(part, 3, local)
-    def vec_sum(stats, i):
-        return jnp.sum(stats[8 * i : 8 * i + 8], axis=0)
-
-    def squares(stats, i):
-        return jnp.sum(stats[8 * i : 8 * i + 8].reshape(8, n_dp, part), axis=(0, 1))
-
-    vectors = jnp.concatenate(
-        [jnp.zeros((2, width), F32), jnp.stack([vec_sum(stats_b, i) for i in (2, 0, 1, 3)])]
-    )
-    sums = jnp.concatenate([squares(stats_a, i) for i in range(3)] + [jnp.zeros((2 * part,), F32)])
-    count = jnp.clip(length - t * rows, 0, rows).astype(F32)
-    vector_blocks = vectors.reshape(6, n_dp, part).transpose(1, 0, 2).reshape(n_dp, 6 * part)
-    top = jnp.concatenate(
-        [
-            vector_blocks,
-            jnp.broadcast_to(sums[None], (n_dp, 5 * part)),
-            jnp.full((n_dp, 128), count),
-        ],
-        axis=1,
-    )
-    top_len = -(-top.shape[1] // 1024) * 1024
     up_blocks = jnp.sum(up_sums, axis=0).reshape(units // 16, n_dp, 16 // n_dp)
     up_blocks = up_blocks.transpose(1, 0, 2).reshape(n_dp, units // n_dp)
     qv_sums = jnp.stack([head_sums[:, 0], head_sums[:, 8]])
@@ -1357,11 +1422,12 @@
     qv_blocks = qv_blocks.reshape(n_dp, 2 * heads * hd_part)
     low = jnp.concatenate([up_blocks, qv_blocks], axis=1)
     low_len = -(-low.shape[1] // 1024) * 1024
-    given = jnp.concatenate([pad_to(top, top_len), pad_to(low, low_len)], axis=1)
-    given = given.reshape(n_dp, (top_len + low_len) // 128, 128)
+    given = pad_to(low, low_len).reshape(n_dp, low_len // 128, 128)
+    shared = -(-(11 * part // 128 + 1) // 8) * 8
+    top_len = shared * 128
     tokens_grad, output, reduced, rms = finish(
-        last_terms, last_early, tokens, gmid, mlp, landed, mid, valid, vecs, given,
-        top_len // 128, n_t, 4,
+        last_terms, last_early, tokens, gmid, mlp, landed, mid, valid, vecs,
+        stats_a, stats_b, given, shared, n_t, 4,
     )
     reduced = reduced.reshape(-1)
     outs = [reduced[i * part : (i + 1) * part] for i in range(6)]

time: 587 us -> 584 us (level)
  no operation moved by 1% of the time
where the time goes in v9:
time: 584 us; the launch traced here: 583 us
  Pallas kernels  536 us (92%)
  local copies, waits for them, and re-layouts  22.6 us (4%)
  between operations  15.2 us (3%)
  other arithmetic  6.19 us (1%)
    pallas_call x1, Pallas kernels, back_middle(): pl.pallas_call(functools.partial(back_middle_kernel, size), out_shape=(ja...  114 us
    pallas_call x1, Pallas kernels, hidden(): pl.pallas_call(functools.partial(hidden_kernel, n_dp, size), out_shape=(j...  86.1 us
    pallas_call x1, Pallas kernels, first(): pl.pallas_call(functools.partial(first_kernel, n_dp, size, part), out_sha...  78.5 us
    pallas_call x1, Pallas kernels, middle(): pl.pallas_call(functools.partial(middle_kernel, size), out_shape=(jax.Sha...  75.8 us
    pallas_call x1, Pallas kernels, finish(): pl.pallas_call(functools.partial(finish_kernel, n_dp, size, shared), out_...  70.2 us
    pallas_call x1, Pallas kernels, front(): pl.pallas_call(functools.partial(front_kernel, size, heads), grid=(heads,...  32.1 us
    pallas_call x1, Pallas kernels, attend_back(): pl.pallas_call(functools.partial(attend_back_kernel, size, heads), grid=(...  29.6 us
    pallas_call x1, Pallas kernels, products(): pl.pallas_call(functools.partial(products_kernel, size, steps), grid=(ste...  25.9 us
  transfers between devices with their start and end apart: 7, of which 0 were waited for; matrix products, arithmetic and copies ran while one was open for 3% of the time, Pallas kernels for 73%

profile of v9, /device:TPU:0, one launch (start us, length us, event | category | flops | bytes accessed | tf_op | source)
XLA Modules:
  0.0 583.1 jit_solution(16646115810492303020)
XLA Ops:
  7.3 0.7 all-gather.8.cloned.1.call-update
  8.0 0.7 all-gather.6.cloned.1.call-update
  8.8 0.7 all-gather.10.cloned.1.call-update
  9.5 0.5 all-gather.12.cloned.1.call-update
  11.2 0.2 dynamic-update-slice
  11.4 0.2 dynamic-update-slice.1
  11.6 0.2 dynamic-update-slice.2
  11.9 0.2 dynamic-update-slice.3
  12.1 0.2 dynamic-update-slice.4
  12.9 0.6 pad_bitcast_fusion.small
  13.5 78.5 %first.1 = (bf16[8,16,128]{2,1,0:T(8,128)(2,1)}, bf16[4,256,2048]{2,1,0:T(8,128)(2,1)}) custom-call(bf16[16,128]{1,0:T(8,128)(2,1)} %pad_bitcast_fusion.small, bf16[256,2048]{1,0:T(8,128)(2,1)} %tok_in.1), custom_call_target="tpu_custom_call" | custom-call | tf_op jit(solution)/shard_map/first/pallas_call | solution.py:449
  92.0 0.8 copy.81
  93.3 0.8 copy.60
  94.1 0.3 reshape.162
  94.5 0.6 pad_convert_fusion.vecs
  95.2 1.2 multiply_convert_fusion.cot.gm_in
  96.4 1.0 broadcast_in_dim.36.bar
  97.4 0.6 broadcast_in_dim.33.shift
  98.0 32.1 %front.1 = (bf16[1024,1536]{1,0:T(8,128)(2,1)}, bf16[1024,512]{1,0:T(8,128)(2,1)}, f32[4,8,1024]{2,1,0:T(8,128)}, bf16[1024,2048]{1,0:T(8,128)(2,1)}, bf16[2,256,2048]{2,1,0:T(8,128)(2,1)}) custom-call(bf16[1024,2048]{1,0:T(8,128)(2,1)} %bitcast.84, bf16[8,3,256,512]{3,2,1,0:T(8,128)(2,1)} %bitcast.81, f32[8,1536]{1,0:T(8,128)} %broadcast_in_dim.33.shift, ...), custom_call_target="tpu_custom_call" | custom-call | tf_op jit(solution)/shard_map/front/pallas_call | solution.py:985
  130.2 0.8 broadcast_in_dim.37.valid
  130.9 75.8 %middle.1 = (bf16[256,2048]{1,0:T(8,128)(2,1)}, bf16[4,256,2048]{2,1,0:T(8,128)(2,1)}, f32[256,2048]{1,0:T(8,128)}, f32[24,2048]{1,0:T(8,128)}) custom-call(bf16[4,256,2048]{2,1,0:T(8,128)(2,1)} %bitcast.93, bf16[256,2048]{1,0:T(8,128)(2,1)} %multiply_convert_fusion.cot.gm_in, bf16[2,256,2048]{2,1,0:T(8,128)(2,1)} %get-tuple-element.58.near, ...), custom_call_target="tpu_custom_call" | custom-call | tf_op jit(solution)/shard_map/middle/pallas_call | solution.py:531
  206.8 0.6 broadcast_in_dim.38.bias
  207.4 86.1 %hidden.1 = (bf16[4,256,2048]{2,1,0:T(8,128)(2,1)}, bf16[4,256,2048]{2,1,0:T(8,128)(2,1)}, bf16[4,256,2048]{2,1,0:T(8,128)(2,1)}, bf16[4,256,2048]{2,1,0:T(8,128...) custom-call(bf16[256,2048]{1,0:T(8,128)(2,1)} %get-tuple-element.59.c_own, ...), custom_call_target="tpu_custom_call" | custom-call | tf_op jit(solution)/shard_map/hidden/pallas_call | solution.py:1193
  293.6 25.9 %products.1 = (bf16[2048,2048]{1,0:T(8,128)(2,1)}, bf16[2048,2048]{1,0:T(8,128)(2,1)}, bf16[2,256,2048]{2,1,0:T(8,128)(2,1)}) custom-call(bf16[1024,2048]{1,0:T(8,128)(2,1)} %bitcast.91, bf16[1024,2048]{1,0:T(8,128)(2,1)} %bitcast.83, bf16[1024,2048]{1,0:T(8,128)(2,1)} %bitcast.90, bf16[1024,2048]{1,0:T(8,128)(2,1)} %bitcast.92, ...), custom_call_target="tpu_custom_call" | custom-call | tf_op jit(solution)/shard_map/products/pallas_call | solution.py:1261
  319.6 0.5 reduce-scatter.6.cloned.1.call-update
  320.1 114.4 %back_middle.1 = (bf16[4,256,2048]{2,1,0:T(8,128)(2,1)}, f32[256,2048]{1,0:T(8,128)}, bf16[2,256,2048]{2,1,0:T(8,128)(2,1)}, f32[32,2048]{1,0:T(8,128)}, bf16[4,256,512]{2,1,0:T(8,128)(2,1)}) custom-call(bf16[4,256,2048]{2,1,0:T(8,128)(2,1)} %get-tuple-element.61.terms, bf16[2,256,2048]{2,1,0:T(8,128)(2,1)} %get-tuple-element.65.landed, ...), custom_call_target="tpu_custom_call" | custom-call | tf_op jit(solution)/shard_map/back_middle/pallas_call | solution.py:634
  434.5 29.6 %attend_back.1 = (bf16[1024,1536]{1,0:T(8,128)(2,1)}, f32[4,16,128]{2,1,0:T(8,128)}, bf16[1024,2048]{1,0:T(8,128)(2,1)}, bf16[2,256,2048]{2,1,0:T(8,128)(2,1)}) custom-call(bf16[1024,1536]{1,0:T(8,128)(2,1)} %get-tuple-element.56.q.k.v, bf16[1024,1536]{1,0:T(8,128)(2,1)} %get-tuple-element.56.q.k.v, bf16[1024,1536]{1,0:T(8,128)(2,1)} %get-tuple-element.56.q.k.v, ...), custom_call_target="tpu_custom_call" | custom-call | tf_op jit(solution)/shard_map/attend_back/pallas_call | solution.py:1079
  464.2 22.9 %head_products.1 = (bf16[2048,2048]{1,0:T(8,128)(2,1)}, bf16[2,256,2048]{2,1,0:T(8,128)(2,1)}) custom-call(bf16[1024,2048]{1,0:T(8,128)(2,1)} %bitcast.94, bf16[1024,2048]{1,0:T(8,128)(2,1)} %bitcast.85, bf16[1024,512]{1,0:T(8,128)(2,1)} %get-tuple-element.73.o, bf16[1024,1536]{1,0:T(8,128)(2,1)} %get-tuple-element.74.gqkv, bf16[4,256,2048]{2,1,0:T(8,128)(2,1)} %bitcast.86), custom_call_target="tpu_custom_call" | custom-call | tf_op jit(solution)/shard_map/head_products/pallas_call | solution.py:1314
  487.1 0.8 copy-done.6
  488.0 0.5 reshape.156
  488.4 0.8 copy.61
  489.3 0.8 slice_reduce_fusion.2
  490.4 0.6 copy.80
  491.0 70.2 %finish.1 = (f32[256,2048]{1,0:T(8,128)}, bf16[256,2048]{1,0:T(8,128)(2,1)}, f32[32,128]{1,0:T(8,128)}, f32[8,128]{1,0:T(8,128)}) custom-call(bf16[4,256,2048]{2,1,0:T(8,128)(2,1)} %bitcast.87, bf16[2,256,2048]{2,1,0:T(8,128)(2,1)} %get-tuple-element.79.first_landed, bf16[256,2048]{1,0:T(8,128)(2,1)} %tok_in.1, f32[256,2048]{1,0:T(8,128)} %get-tuple-element.80.gmid_in, ...), custom_call_target="tpu_custom_call" | custom-call | tf_op jit(solution)/shard_map/finish/pallas_call | solution.py:857
  561.2 0.8 slice_reduce_fusion.3
  562.0 0.7 reshape.160
  562.7 1.4 slice_bitcast_fusion.6
  564.3 0.6 copy.67
  564.9 1.6 convert_element_type.82
  566.5 1.5 convert_element_type.83
  567.9 0.6 slice_reduce_fusion
  568.6 1.1 convert_bitcast_fusion
  569.7 1.0 copy.66
  570.8 0.5 copy.64
  571.3 1.6 copy.65
  572.9 1.0 copy.93
  573.9 1.0 copy-done
  574.9 1.3 copy.94
  (83 shorter events, 2.6 us)
Async XLA Ops:
  7.2 3.6 copy-start.8
  7.2 3.7 copy-start.9
  7.2 4.0 copy-start.10
  7.2 4.2 copy-start.11
  7.2 4.4 copy-start.12
  7.2 4.6 copy-start.13
  7.2 4.8 copy-start.14
  7.3 5.0 copy-start.15
  7.3 89.1 %all-gather.8.cloned.1.call-start = ((), (), s32[]{:S(2)}) async-start(), calls=%async_computation.4 | async-start | bytes 2359296 | tf_op jit(solution)/shard_map/all_gather | solution.py:1376
  8.0 88.4 %all-gather.6.cloned.1.call-start = ((), (), s32[]{:S(2)}) async-start(), calls=%async_computation.3 | async-start | bytes 7077888 | tf_op jit(solution)/shard_map/all_gather | solution.py:1373
  8.7 198.0 %all-gather.10.cloned.1.call-start = ((), (), s32[]{:S(2)}) async-start(), calls=%async_computation.5 | async-start | bytes 9437184 | tf_op jit(solution)/shard_map/all_gather | solution.py:1377
  9.5 85.7 %copy-start.5 = (bf16[256,2048]{1,0:T(8,128)(2,1)S(1)}, bf16[256,2048]{1,0:T(8,128)(2,1)}, u32[]{:S(2)}) copy-start(bf16[256,2048]{1,0:T(8,128)(2,1)} %param.29) | copy-start | bytes 3145732
  9.5 197.3 %all-gather.12.cloned.1.call-start = ((), (), s32[]{:S(2)}) async-start(), calls=%async_computation.9 | async-start | bytes 9437184 | tf_op jit(solution)/shard_map/all_gather | solution.py:1378
  10.1 477.0 %reduce-scatter.4.cloned.1.call-start = ((), (), s32[]{:S(2)}) async-start(), calls=%async_computation.6 | async-start | bytes 9437184 | tf_op jit(solution)/shard_map/reduce_scatter | solution.py:1400
  319.5 167.6 %reduce-scatter.6.cloned.1.call-start = ((), (), s32[]{:S(2)}) async-start(), calls=%async_computation.7 | async-start | bytes 9437184 | tf_op jit(solution)/shard_map/reduce_scatter | solution.py:1401
  320.1 248.5 %reduce-scatter.8.cloned.1.call-start = ((), (), s32[]{:S(2)}) async-start(), calls=%async_computation.8 | async-start | bytes 9437184 | tf_op jit(solution)/shard_map/reduce_scatter | solution.py:1415
  487.1 0.8 copy-start.6
  491.0 73.9 %copy-start.2 = (bf16[256,2048]{1,0:T(8,128)(2,1)S(1)}, bf16[256,2048]{1,0:T(8,128)(2,1)}, u32[]{:S(2)}) copy-start(bf16[256,2048]{1,0:T(8,128)(2,1)} %reduce-scatter.6.cloned.1.call-done) | copy-start | bytes 3145732
  561.2 5.2 copy-start.1
  566.5 1.5 copy-start.7
  568.6 2.1 copy-start.3
  571.3 1.6 copy-start.4
  572.9 2.0 copy-start
Sparse Core Ops, SparseCore 0:
  9.9 30.8 all-gather.7
  42.7 45.4 all-gather.5
  90.1 54.3 all-gather.9
  146.2 54.2 all-gather.11
  319.6 68.9 reduce-scatter.3
  391.9 71.4 reduce-scatter.5
  487.2 73.3 reduce-scatter.7

commit v10 on v9

--- a/solution.py
+++ b/solution.py
@@ -548,9 +548,9 @@
 
 
 def back_middle_kernel(
-    size, terms, landed, mlp_in, gm_in, mid_in, vecs, out_in, gz_done, gmid_out, ends, stats,
-    go_out, gz_out, right, left, right2, left2, mlp, gm, mid, out_w,
-    ss, sr, ms, mr, gs, gr, early_sem, load_sem, out_sem,
+    size, terms, landed, mlp_in, gm_in, mid_in, vecs, out_in, o, gmid_out, ends, stats,
+    go_out, grad_out, gz_out, right, left, right2, left2, mlp, gm, mid, out_w, grad,
+    ss, sr, ms, mr, gs, gr, early_sem, load_sem,
 ):
     rows = mid.shape[0]
     line = Line(size, rows)
@@ -593,12 +593,19 @@
         row_loop(line.sub, step, body, piece * line.sub)
         for way in (0, 1):
             line.gather_step(way, 0, piece, gz_out, (gs, gr), None)
-    def store(shard):
-        return pltpu.make_async_copy(gz_out.at[shard], gz_done.at[shard], out_sem.at[shard])
+    width = mid.shape[1]
+    block = min(512, width)
 
     def weigh(shard):
-        store(shard).start()
         go_out[shard] = dot_t(gz_out[shard], out_w[...]).astype(BF16)
+        here = o[pl.ds(pl.multiple_of(shard * rows, rows), rows), :].T
+
+        def column(j, carry):
+            at = pl.ds(pl.multiple_of(j * block, block), block)
+            grad[:, at] += dot(here, gz_out[shard, :, at])
+            return carry
+
+        lax.fori_loop(0, width // block, column, 0)
 
     def on_slot(k):
         def side(i, carry):
@@ -612,6 +619,7 @@
 
         lax.fori_loop(0, 1 if k == 0 else 2, side, 0)
 
+    grad[...] = jnp.zeros_like(grad)
     on_slot(0)
     line.phase(
         gather=(gz_out, (gs, gr), None),
@@ -620,33 +628,33 @@
         ends=ends,
         start=1,
     )
-    for shard in range(size):
-        store(shard).wait()
+    grad_out[...] = grad[...].astype(BF16)
     line.drain_scatter((right, left), (ss, sr), 0, True)
     line.drain_scatter((right2, left2), (ms, mr), 1)
     line.drain_gather(gz_out, (gs, gr))
 
 
-def back_middle(terms, landed, mlp, gm, mid, vecs, out_w, size, cid):
+def back_middle(terms, landed, mlp, gm, mid, vecs, out_w, o, size, cid):
     rows, width = mid.shape
     local = out_w.shape[0]
     full = (size, rows, width)
     return pl.pallas_call(
         functools.partial(back_middle_kernel, size),
         out_shape=(
-            jax.ShapeDtypeStruct(full, BF16),
             jax.ShapeDtypeStruct((rows, width), F32),
             jax.ShapeDtypeStruct((2, rows, width), BF16),
             jax.ShapeDtypeStruct((32, width), F32),
             jax.ShapeDtypeStruct((size, rows, local), BF16),
+            jax.ShapeDtypeStruct((local, width), BF16),
         ),
-        in_specs=[WHOLE, HBM, HBM, HBM, HBM, WHOLE, HBM],
-        out_specs=(HBM, WHOLE, WHOLE, WHOLE, WHOLE),
+        in_specs=[WHOLE, HBM, HBM, HBM, HBM, WHOLE, HBM, WHOLE],
+        out_specs=(WHOLE,) * 5,
         scratch_shapes=[pltpu.VMEM(full, BF16)] * 6
         + [
             pltpu.VMEM((rows, width), BF16),
             pltpu.VMEM((rows, width), F32),
             pltpu.VMEM((local, width), BF16),
+            pltpu.VMEM((local, width), F32),
         ]
         + line_sems(size)
         + line_sems(size)
@@ -654,11 +662,10 @@
         + [
             pltpu.SemaphoreType.DMA((2,)),
             pltpu.SemaphoreType.DMA((4,)),
-            pltpu.SemaphoreType.DMA((size,)),
         ],
         compiler_params=params(cid),
         name="back_middle",
-    )(terms, landed, mlp, gm, mid, vecs, out_w)
+    )(terms, landed, mlp, gm, mid, vecs, out_w, o)
 
 
 def finish_kernel(
@@ -1223,9 +1230,7 @@
     return lax.dot_general(left, right, (((0,), (0,)), ((), ())), preferred_element_type=F32)
 
 
-def products_kernel(
-    size, steps, act, gm, c, gu_in, terms, down_out, up_out, landed, gu, gs, gr, load_sem
-):
+def products_kernel(size, steps, gm, act, c, gu_in, terms, out, landed, gu, gs, gr, load_sem):
     i = pl.program_id(0)
     line = Line(size, terms.shape[1])
     load = pltpu.make_async_copy(gu_in, gu, load_sem.at[0])
@@ -1239,7 +1244,7 @@
 
     @pl.when(i < steps)
     def _():
-        down_out[...] = cross(act[...], gm[...]).astype(BF16)
+        out[...] = cross(gm[...], act[...]).astype(BF16)
 
     @pl.when(i == steps)
     def _():
@@ -1247,7 +1252,7 @@
 
     @pl.when(i >= steps)
     def _():
-        up_out[...] = cross(c[...], gu[...]).astype(BF16)
+        out[...] = cross(c[...], gu[...]).astype(BF16)
 
     @pl.when(i == pl.num_programs(0) - 1)
     def _():
@@ -1257,13 +1262,12 @@
 def products(act, gm, c, gu, terms, size, cid):
     rows, units = act.shape
     width = gm.shape[1]
-    steps, more = units // BLOCK, width // BLOCK
+    steps = width // BLOCK
     return pl.pallas_call(
         functools.partial(products_kernel, size, steps),
-        grid=(steps + more,),
+        grid=(2 * steps,),
         out_shape=(
-            jax.ShapeDtypeStruct((units, width), BF16),
-            jax.ShapeDtypeStruct((width, units), BF16),
+            jax.ShapeDtypeStruct((width, 2 * units), BF16),
             jax.ShapeDtypeStruct((2,) + terms.shape[1:], BF16),
         ),
         in_specs=[
@@ -1273,11 +1277,7 @@
             HBM,
             HBM,
         ],
-        out_specs=(
-            pl.BlockSpec((BLOCK, width), lambda i: (jnp.minimum(i, steps - 1), 0)),
-            pl.BlockSpec((BLOCK, units), lambda i: (jnp.maximum(i - steps, 0), 0)),
-            HBM,
-        ),
+        out_specs=(pl.BlockSpec((BLOCK, units), lambda i: (i % steps, i // steps)), HBM),
         scratch_shapes=[
             pltpu.VMEM((rows, units), BF16),
             pltpu.SemaphoreType.DMA((2,)),
@@ -1286,31 +1286,29 @@
         ],
         compiler_params=params(cid),
         name="products",
-    )(act, gm, c, gu, terms)
-
-
-def head_products_kernel(size, gz, a, o, gqkv, terms, out, landed, gs, gr):
+    )(gm, act, c, gu, terms)
+
+
+def head_products_kernel(size, a, gqkv, terms, out, landed, gs, gr):
     i = pl.program_id(0)
     line = Line(size, terms.shape[1])
     hops = line.first_hops(terms, landed, (gs, gr))
-    local = o.shape[1]
 
     @pl.when(i == 0)
     def _():
         line.barrier()
         line.hops_start(hops)
 
-    out[:, 0:local] = cross(gz[...], o[...]).astype(BF16)
-    out[:, local:] = cross(a[...], gqkv[...]).astype(BF16)
+    out[...] = cross(a[...], gqkv[...]).astype(BF16)
 
     @pl.when(i == pl.num_programs(0) - 1)
     def _():
         line.hops_wait(hops)
 
 
-def head_products(gz, a, o, gqkv, terms, size, cid):
+def head_products(a, gqkv, terms, size, cid):
     rows, width = a.shape
-    columns = o.shape[1] + gqkv.shape[1]
+    columns = gqkv.shape[1]
     return pl.pallas_call(
         functools.partial(head_products_kernel, size),
         grid=(width // BLOCK,),
@@ -1320,8 +1318,6 @@
         ),
         in_specs=[
             pl.BlockSpec((rows, BLOCK), lambda i: (0, i)),
-            pl.BlockSpec((rows, BLOCK), lambda i: (0, i)),
-            WHOLE,
             WHOLE,
             HBM,
         ],
@@ -1329,7 +1325,7 @@
         scratch_shapes=[pltpu.SemaphoreType.DMA((2,)), pltpu.SemaphoreType.DMA((2,))],
         compiler_params=params(cid),
         name="head_products",
-    )(gz, a, o, gqkv, terms)
+    )(a, gqkv, terms)
 
 
 def pad_to(x, count):
@@ -1396,25 +1392,23 @@
     c, gm = c.reshape(-1, width), gm.reshape(-1, width)
     act, gu = act.reshape(-1, units), gu.reshape(-1, units)
 
-    down_grad, up_grad, early = products(act, gm, c, gu, back_terms, n_t, 9)
-    down_out = lax.psum_scatter(down_grad, "dp", scatter_dimension=1, tiled=True)
-    up_out = lax.psum_scatter(up_grad, "dp", scatter_dimension=0, tiled=True)
-    gz, gmid, ends, stats_b, go = back_middle(
-        back_terms, early, mlp, gm_own, mid, vecs, out_full, n_t, 3
+    both_grad, early = products(act, gm, c, gu, back_terms, n_t, 9)
+    both_out = lax.psum_scatter(both_grad, "dp", scatter_dimension=0, tiled=True)
+    gmid, ends, stats_b, go, out_grad = back_middle(
+        back_terms, early, mlp, gm_own, mid, vecs, out_full, attended, n_t, 3
     )
+    go, out_grad, both_out = lax.optimization_barrier((go, out_grad, both_out))
+    down_out, up_out = both_out[:, :units].T, both_out[:, units:]
+    out_out = lax.psum_scatter(out_grad, "dp", scatter_dimension=1, tiled=True)
     gqkv, head_sums, last_terms, landed = attend_back(
         qkv, go.reshape(-1, local), bar, log_totals, qkv_full, ends, n_t, 8
     )
     last_terms = last_terms.reshape(n_t, rows, width)
-    head_grad, last_early = head_products(
-        gz.reshape(-1, width), a, attended, gqkv, last_terms, n_t, 10
-    )
-    last_early, head_grad, down_out, up_out = lax.optimization_barrier(
-        (last_early, head_grad, down_out, up_out)
-    )
-    head_out = lax.psum_scatter(head_grad, "dp", scatter_dimension=0, tiled=True)
-    out_out = head_out[:, :local].T
-    qkv_out = head_out[:, local:].reshape(part, 3, local)
+    qkv_grad, last_early = head_products(a, gqkv, last_terms, n_t, 10)
+    last_early, qkv_grad = lax.optimization_barrier((last_early, qkv_grad))
+    qkv_out = lax.psum_scatter(qkv_grad, "dp", scatter_dimension=0, tiled=True)
+    qkv_out = qkv_out.reshape(part, 3, local)
+
     up_blocks = jnp.sum(up_sums, axis=0).reshape(units // 16, n_dp, 16 // n_dp)
     up_blocks = up_blocks.transpose(1, 0, 2).reshape(n_dp, units // n_dp)
     qv_sums = jnp.stack([head_sums[:, 0], head_sums[:, 8]])

time: 584 us -> 587 us (level)
  transfers between devices with their start and end apart: 7 -> 7, of which waited for: 0 -> 0; matrix products, arithmetic and copies ran while one was open for 3% -> 4% of each run, Pallas kernels for 73% -> 72%
where the time goes in v10:
time: 587 us; the launch traced here: 586 us
  Pallas kernels  537 us (91%)
  local copies, waits for them, and re-layouts  24.2 us (4%)
  between operations  15.2 us (3%)
  other arithmetic  7.06 us (1%)
    pallas_call x1, Pallas kernels, back_middle(): pl.pallas_call(functools.partial(back_middle_kernel, size), out_shape=(ja...  115 us
    pallas_call x1, Pallas kernels, hidden(): pl.pallas_call(functools.partial(hidden_kernel, n_dp, size), out_shape=(j...  86 us
    pallas_call x1, Pallas kernels, first(): pl.pallas_call(functools.partial(first_kernel, n_dp, size, part), out_sha...  78.6 us
    pallas_call x1, Pallas kernels, middle(): pl.pallas_call(functools.partial(middle_kernel, size), out_shape=(jax.Sha...  75.8 us
    pallas_call x1, Pallas kernels, finish(): pl.pallas_call(functools.partial(finish_kernel, n_dp, size, shared), out_...  70.4 us
    pallas_call x1, Pallas kernels, front(): pl.pallas_call(functools.partial(front_kernel, size, heads), grid=(heads,...  32.3 us
    pallas_call x1, Pallas kernels, attend_back(): pl.pallas_call(functools.partial(attend_back_kernel, size, heads), grid=(...  30.2 us
    pallas_call x1, Pallas kernels, products(): pl.pallas_call(functools.partial(products_kernel, size, steps), grid=(2 *...  25.7 us
  transfers between devices with their start and end apart: 7, of which 0 were waited for; matrix products, arithmetic and copies ran while one was open for 4% of the time, Pallas kernels for 72%

profile of v10, /device:TPU:0, one launch (start us, length us, event | category | flops | bytes accessed | tf_op | source)
XLA Modules:
  0.0 586.0 jit_solution(11740426958494079241)
XLA Ops:
  7.3 0.7 all-gather.8.cloned.1.call-update
  8.0 0.7 all-gather.6.cloned.1.call-update
  8.8 0.7 all-gather.10.cloned.1.call-update
  9.5 0.5 all-gather.12.cloned.1.call-update
  11.2 0.2 dynamic-update-slice
  11.4 0.2 dynamic-update-slice.1
  11.6 0.2 dynamic-update-slice.2
  11.9 0.2 dynamic-update-slice.3
  12.1 0.2 dynamic-update-slice.4
  12.3 0.2 dynamic-update-slice.5
  12.5 0.2 dynamic-update-slice.6
  12.9 0.6 pad_bitcast_fusion.small
  13.5 78.6 %first.1 = (bf16[8,16,128]{2,1,0:T(8,128)(2,1)}, bf16[4,256,2048]{2,1,0:T(8,128)(2,1)}) custom-call(bf16[16,128]{1,0:T(8,128)(2,1)} %pad_bitcast_fusion.small, bf16[256,2048]{1,0:T(8,128)(2,1)} %tok_in.1), custom_call_target="tpu_custom_call" | custom-call | tf_op jit(solution)/shard_map/first/pallas_call | solution.py:449
  92.1 0.8 copy.81
  93.4 0.8 copy.60
  94.2 0.3 reshape.158
  94.6 0.6 pad_convert_fusion.vecs
  95.3 1.2 multiply_convert_fusion.cot.gm_in
  96.5 1.0 broadcast_in_dim.36.bar
  97.5 0.6 broadcast_in_dim.33.shift
  98.1 32.3 %front.1 = (bf16[1024,1536]{1,0:T(8,128)(2,1)}, bf16[1024,512]{1,0:T(8,128)(2,1)}, f32[4,8,1024]{2,1,0:T(8,128)}, bf16[1024,2048]{1,0:T(8,128)(2,1)}, bf16[2,256,2048]{2,1,0:T(8,128)(2,1)}) custom-call(bf16[1024,2048]{1,0:T(8,128)(2,1)} %bitcast.83, bf16[8,3,256,512]{3,2,1,0:T(8,128)(2,1)} %bitcast.80, f32[8,1536]{1,0:T(8,128)} %broadcast_in_dim.33.shift, ...), custom_call_target="tpu_custom_call" | custom-call | tf_op jit(solution)/shard_map/front/pallas_call | solution.py:992
  130.4 0.8 broadcast_in_dim.37.valid
  131.1 75.8 %middle.1 = (bf16[256,2048]{1,0:T(8,128)(2,1)}, bf16[4,256,2048]{2,1,0:T(8,128)(2,1)}, f32[256,2048]{1,0:T(8,128)}, f32[24,2048]{1,0:T(8,128)}) custom-call(bf16[4,256,2048]{2,1,0:T(8,128)(2,1)} %bitcast.92, bf16[256,2048]{1,0:T(8,128)(2,1)} %multiply_convert_fusion.cot.gm_in, bf16[2,256,2048]{2,1,0:T(8,128)(2,1)} %get-tuple-element.58.near, ...), custom_call_target="tpu_custom_call" | custom-call | tf_op jit(solution)/shard_map/middle/pallas_call | solution.py:531
  206.9 0.6 broadcast_in_dim.38.bias
  207.6 86.0 %hidden.1 = (bf16[4,256,2048]{2,1,0:T(8,128)(2,1)}, bf16[4,256,2048]{2,1,0:T(8,128)(2,1)}, bf16[4,256,2048]{2,1,0:T(8,128)(2,1)}, bf16[4,256,2048]{2,1,0:T(8,128...) custom-call(bf16[256,2048]{1,0:T(8,128)(2,1)} %get-tuple-element.59.c_own, ...), custom_call_target="tpu_custom_call" | custom-call | tf_op jit(solution)/shard_map/hidden/pallas_call | solution.py:1200
  293.6 25.7 %products.1 = (bf16[2048,4096]{1,0:T(8,128)(2,1)}, bf16[2,256,2048]{2,1,0:T(8,128)(2,1)}) custom-call(bf16[1024,2048]{1,0:T(8,128)(2,1)} %bitcast.82, bf16[1024,2048]{1,0:T(8,128)(2,1)} %bitcast.90, bf16[1024,2048]{1,0:T(8,128)(2,1)} %bitcast.89, bf16[1024,2048]{1,0:T(8,128)(2,1)} %bitcast.91, bf16[4,256,2048]{2,1,0:T(8,128)(2,1)} %get-tuple-element.61.terms), custom_call_target="tpu_custom_call" | custom-call | tf_op jit(solution)/shard_map/products/pallas_call | solution.py:1266
  319.4 115.2 %back_middle.1 = (f32[256,2048]{1,0:T(8,128)}, bf16[2,256,2048]{2,1,0:T(8,128)(2,1)}, f32[32,2048]{1,0:T(8,128)}, bf16[4,256,512]{2,1,0:T(8,128)(2,1)}, bf16[512,2048]{1,0:T(8,128)(2,1)}) custom-call(bf16[4,256,2048]{2,1,0:T(8,128)(2,1)} %get-tuple-element.61.terms, bf16[2,256,2048]{2,1,0:T(8,128)(2,1)} %get-tuple-element.65.landed, ...), custom_call_target="tpu_custom_call" | custom-call | tf_op jit(solution)/shard_map/back_middle/pallas_call | solution.py:641
  434.7 30.2 %attend_back.1 = (bf16[1024,1536]{1,0:T(8,128)(2,1)}, f32[4,16,128]{2,1,0:T(8,128)}, bf16[1024,2048]{1,0:T(8,128)(2,1)}, bf16[2,256,2048]{2,1,0:T(8,128)(2,1)}) custom-call(bf16[1024,1536]{1,0:T(8,128)(2,1)} %get-tuple-element.56.q.k.v, bf16[1024,1536]{1,0:T(8,128)(2,1)} %get-tuple-element.56.q.k.v, bf16[1024,1536]{1,0:T(8,128)(2,1)} %get-tuple-element.56.q.k.v, ...), custom_call_target="tpu_custom_call" | custom-call | tf_op jit(solution)/shard_map/attend_back/pallas_call | solution.py:1086
  464.8 22.5 %head_products.1 = (bf16[2048,1536]{1,0:T(8,128)(2,1)}, bf16[2,256,2048]{2,1,0:T(8,128)(2,1)}) custom-call(bf16[1024,2048]{1,0:T(8,128)(2,1)} %bitcast.84, bf16[1024,1536]{1,0:T(8,128)(2,1)} %get-tuple-element.76.gqkv, bf16[4,256,2048]{2,1,0:T(8,128)(2,1)} %bitcast.85), custom_call_target="tpu_custom_call" | custom-call | tf_op jit(solution)/shard_map/head_products/pallas_call | solution.py:1312
  487.3 0.8 copy-done.3
  488.2 0.5 reshape.152
  488.6 0.8 copy.61
  489.6 0.8 slice_reduce_fusion.2
  490.6 0.6 copy.80
  491.2 70.4 %finish.1 = (f32[256,2048]{1,0:T(8,128)}, bf16[256,2048]{1,0:T(8,128)(2,1)}, f32[32,128]{1,0:T(8,128)}, f32[8,128]{1,0:T(8,128)}) custom-call(bf16[4,256,2048]{2,1,0:T(8,128)(2,1)} %bitcast.86, bf16[2,256,2048]{2,1,0:T(8,128)(2,1)} %get-tuple-element.79.first_landed, bf16[256,2048]{1,0:T(8,128)(2,1)} %tok_in.1, f32[256,2048]{1,0:T(8,128)} %get-tuple-element.80.gmid_in, ...), custom_call_target="tpu_custom_call" | custom-call | tf_op jit(solution)/shard_map/finish/pallas_call | solution.py:864
  561.6 0.7 slice_reduce_fusion.3
  562.3 0.7 reshape.156
  563.0 1.4 slice_bitcast_fusion.6
  564.6 0.6 copy.66
  565.2 3.4 convert_bitcast_fusion
  568.6 1.8 copy.67
  570.4 0.6 slice_reduce_fusion
  571.0 1.8 convert_element_type.80
  572.8 1.4 copy.64
  574.2 1.6 copy.65
  575.8 1.0 copy.93
  576.8 1.0 copy-done
  577.8 1.3 copy.94
  (75 shorter events, 2.0 us)
Async XLA Ops:
  7.2 3.6 copy-start.5
  7.2 3.7 copy-start.6
  7.2 4.0 copy-start.7
  7.2 4.2 copy-start.8
  7.2 4.4 copy-start.9
  7.2 4.6 copy-start.10
  7.2 4.8 copy-start.11
  7.3 5.0 copy-start.12
  7.3 89.2 %all-gather.8.cloned.1.call-start = ((), (), s32[]{:S(2)}) async-start(), calls=%async_computation.4 | async-start | bytes 2359296 | tf_op jit(solution)/shard_map/all_gather | solution.py:1372
  8.0 88.5 %all-gather.6.cloned.1.call-start = ((), (), s32[]{:S(2)}) async-start(), calls=%async_computation.3 | async-start | bytes 7077888 | tf_op jit(solution)/shard_map/all_gather | solution.py:1369
  8.7 198.2 %all-gather.10.cloned.1.call-start = ((), (), s32[]{:S(2)}) async-start(), calls=%async_computation.5 | async-start | bytes 9437184 | tf_op jit(solution)/shard_map/all_gather | solution.py:1373
  9.5 85.8 %copy-start.2 = (bf16[256,2048]{1,0:T(8,128)(2,1)S(1)}, bf16[256,2048]{1,0:T(8,128)(2,1)}, u32[]{:S(2)}) copy-start(bf16[256,2048]{1,0:T(8,128)(2,1)} %param.29) | copy-start | bytes 3145732
  9.5 197.5 %all-gather.12.cloned.1.call-start = ((), (), s32[]{:S(2)}) async-start(), calls=%async_computation.9 | async-start | bytes 9437184 | tf_op jit(solution)/shard_map/all_gather | solution.py:1374
  10.1 424.5 %reduce-scatter.4.cloned.1.call-start = ((), (), s32[]{:S(2)}) async-start(), calls=%async_computation.6 | async-start | bytes 18874368 | tf_op jit(solution)/shard_map/reduce_scatter | solution.py:1396
  319.3 251.7 %reduce-scatter.8.cloned.1.call-start = ((), (), s32[]{:S(2)}) async-start(), calls=%async_computation.8 | async-start | bytes 2359296 | tf_op jit(solution)/shard_map/reduce_scatter | solution.py:1402
  434.6 138.2 %reduce-scatter.6.cloned.1.call-start = ((), (), s32[]{:S(2)}) async-start(), calls=%async_computation.7 | async-start | bytes 7077888 | tf_op jit(solution)/shard_map/reduce_scatter | solution.py:1409
  487.3 0.8 copy-start.3
  568.6 1.8 copy-start.4
  574.2 1.6 copy-start.1
  575.8 2.0 copy-start
Sparse Core Ops, SparseCore 0:
  9.9 30.8 all-gather.7
  42.7 45.4 all-gather.5
  90.1 54.2 all-gather.9
  146.2 54.2 all-gather.11
  319.5 113.8 reduce-scatter.3
  436.5 41.9 reduce-scatter.7
  487.5 64.0 reduce-scatter.5

commit v11 on v10

--- a/solution.py
+++ b/solution.py
@@ -671,8 +671,8 @@
 def finish_kernel(
     n_dp, size, shared, terms, first_landed, tok_in, gmid_in, mlp, landed, mid_in, valid, vecs,
     stats_a, stats_b, given, grad_out, y_out, reduced, rms, right, left, own_mlp, tok, ends,
-    gmid, mid, stats, blocks, land, sums, land2, late, late_land,
-    ss, sr, load_sem, early_sem, s1, r1, s2, r2, s3, r3,
+    gmid, mid, stats, blocks, land, sums, land2, late, late_land, late_sums, late_land2,
+    ss, sr, load_sem, early_sem, s1, r1, s2, r2, s3, r3, s4, r4,
 ):
     rows = tok.shape[0]
     line = Line(size, rows)
@@ -691,17 +691,13 @@
         load.start()
     me = lax.axis_index("dp")
     entry = pltpu.get_barrier_semaphore()
-    everyone = n_dp * size
-
-    def place(q):
-        return {"dp": lax.rem(me + q // size, n_dp), "tensor": lax.rem(line.t + q % size, size)}
-
-    def greet(q, carry):
-        pl.semaphore_signal(entry, device_id=place(q), device_id_type=MESH)
-        return carry
-
-    lax.fori_loop(1, everyone, greet, 0)
-    pl.semaphore_wait(entry, everyone - 1)
+    for p in range(1, n_dp):
+        pl.semaphore_signal(entry, device_id={"dp": lax.rem(me + p, n_dp)}, device_id_type=MESH)
+    for p in range(1, size):
+        pl.semaphore_signal(
+            entry, device_id={"tensor": lax.rem(line.t + p, size)}, device_id_type=MESH
+        )
+    pl.semaphore_wait(entry, n_dp + size - 2)
     line.early_sends(terms, (right, left), (ss, sr), early)
     stats[...] = jnp.zeros_like(stats)
 
@@ -757,14 +753,24 @@
             device_id_type=MESH,
         )
 
-    def three(q):
-        target = place(q)
+    def three(p):
+        other = lax.rem(me + p, n_dp)
         return pltpu.make_async_remote_copy(
-            src_ref=late.at[target["dp"]],
-            dst_ref=late_land.at[q],
-            send_sem=s3.at[q],
-            recv_sem=r3.at[q],
-            device_id=target,
+            src_ref=late.at[other],
+            dst_ref=late_land.at[p],
+            send_sem=s3.at[p],
+            recv_sem=r3.at[p],
+            device_id={"dp": other},
+            device_id_type=MESH,
+        )
+
+    def four(p):
+        return pltpu.make_async_remote_copy(
+            src_ref=late_sums,
+            dst_ref=late_land2.at[p],
+            send_sem=s4.at[p],
+            recv_sem=r4.at[p],
+            device_id={"tensor": lax.rem(line.t + p, size)},
             device_id_type=MESH,
         )
 
@@ -813,11 +819,8 @@
     put_square(late, 2 * per, group_sum(stats, 2))
     put_square(late, 2 * per + 1, group_sum(stats, 3))
 
-    def send_late(q, carry):
-        three(q).start()
-        return carry
-
-    lax.fori_loop(1, everyone, send_late, 0)
+    for p in range(1, n_dp):
+        three(p).start()
     reduced[...] = total
     top = sums[pl.ds(0, shared), :]
     for p in range(1, size):
@@ -825,11 +828,16 @@
         top = top + land2[p]
     reduced[pl.ds(0, shared), :] = top
 
-    def take_late(q, held):
-        three(q).wait_recv()
-        return held + late_land[q]
-
-    final = lax.fori_loop(1, everyone, take_late, late[me])
+    final = late[me]
+    for p in range(1, n_dp):
+        three(p).wait_recv()
+        final = final + late_land[p]
+    late_sums[...] = final
+    for p in range(1, size):
+        four(p).start()
+    for p in range(1, size):
+        four(p).wait_recv()
+        final = final + late_land2[p]
     reduced[0 : 2 * per, :] = final[0 : 2 * per, :]
     for i in (9, 10):
         row = 2 * per + i - 9
@@ -840,11 +848,10 @@
         square = jnp.sum(reduced[row : row + 1, :], keepdims=True)
         rms[i : i + 1, :] = jnp.sqrt(square / count)
 
-    def sent_late(q, carry):
-        three(q).wait_send()
-        return carry
-
-    lax.fori_loop(1, everyone, sent_late, 0)
+    for p in range(1, n_dp):
+        three(p).wait_send()
+    for p in range(1, size):
+        four(p).wait_send()
     line.drain_scatter((right, left), (ss, sr), 0, True)
     for p in range(1, n_dp):
         one(p).wait_send()
@@ -882,7 +889,9 @@
             pltpu.VMEM((lines, 128), F32),
             pltpu.VMEM((size, shared, 128), F32),
             pltpu.VMEM((n_dp,) + late, F32),
-            pltpu.VMEM((n_dp * size,) + late, F32),
+            pltpu.VMEM((n_dp,) + late, F32),
+            pltpu.VMEM(late, F32),
+            pltpu.VMEM((size,) + late, F32),
         ]
         + line_sems(size)
         + [
@@ -892,8 +901,10 @@
             pltpu.SemaphoreType.DMA((n_dp,)),
             pltpu.SemaphoreType.DMA((size,)),
             pltpu.SemaphoreType.DMA((size,)),
-            pltpu.SemaphoreType.DMA((n_dp * size,)),
-            pltpu.SemaphoreType.DMA((n_dp * size,)),
+            pltpu.SemaphoreType.DMA((n_dp,)),
+            pltpu.SemaphoreType.DMA((n_dp,)),
+            pltpu.SemaphoreType.DMA((size,)),
+            pltpu.SemaphoreType.DMA((size,)),
         ],
         compiler_params=params(cid),
         name="finish",

time: 587 us -> 586 us (level)
  no operation moved by 1% of the time
where the time goes in v11:
time: 586 us; the launch traced here: 584 us
  Pallas kernels  535 us (91%)
  local copies, waits for them, and re-layouts  24.2 us (4%)
  between operations  15.2 us (3%)
  other arithmetic  7.06 us (1%)
    pallas_call x1, Pallas kernels, back_middle(): pl.pallas_call(functools.partial(back_middle_kernel, size), out_shape=(ja...  115 us
    pallas_call x1, Pallas kernels, hidden(): pl.pallas_call(functools.partial(hidden_kernel, n_dp, size), out_shape=(j...  86 us
    pallas_call x1, Pallas kernels, first(): pl.pallas_call(functools.partial(first_kernel, n_dp, size, part), out_sha...  78.6 us
    pallas_call x1, Pallas kernels, middle(): pl.pallas_call(functools.partial(middle_kernel, size), out_shape=(jax.Sha...  75.8 us
    pallas_call x1, Pallas kernels, finish(): pl.pallas_call(functools.partial(finish_kernel, n_dp, size, shared), out_...  68.8 us
    pallas_call x1, Pallas kernels, front(): pl.pallas_call(functools.partial(front_kernel, size, heads), grid=(heads,...  32.3 us
    pallas_call x1, Pallas kernels, attend_back(): pl.pallas_call(functools.partial(attend_back_kernel, size, heads), grid=(...  30.2 us
    pallas_call x1, Pallas kernels, products(): pl.pallas_call(functools.partial(products_kernel, size, steps), grid=(2 *...  25.7 us
  transfers between devices with their start and end apart: 7, of which 0 were waited for; matrix products, arithmetic and copies ran while one was open for 4% of the time, Pallas kernels for 72%

profile of v11, /device:TPU:0, one launch (start us, length us, event | category | flops | bytes accessed | tf_op | source)
XLA Modules:
  0.0 584.4 jit_solution(13976642912147967146)
XLA Ops:
  7.3 0.7 all-gather.8.cloned.1.call-update
  8.0 0.7 all-gather.6.cloned.1.call-update
  8.8 0.7 all-gather.10.cloned.1.call-update
  9.5 0.5 all-gather.12.cloned.1.call-update
  11.2 0.2 dynamic-update-slice
  11.4 0.2 dynamic-update-slice.1
  11.6 0.2 dynamic-update-slice.2
  11.9 0.2 dynamic-update-slice.3
  12.1 0.2 dynamic-update-slice.4
  12.3 0.2 dynamic-update-slice.5
  12.5 0.2 dynamic-update-slice.6
  12.9 0.6 pad_bitcast_fusion.small
  13.5 78.6 %first.1 = (bf16[8,16,128]{2,1,0:T(8,128)(2,1)}, bf16[4,256,2048]{2,1,0:T(8,128)(2,1)}) custom-call(bf16[16,128]{1,0:T(8,128)(2,1)} %pad_bitcast_fusion.small, bf16[256,2048]{1,0:T(8,128)(2,1)} %tok_in.1), custom_call_target="tpu_custom_call" | custom-call | tf_op jit(solution)/shard_map/first/pallas_call | solution.py:449
  92.1 0.8 copy.81
  93.4 0.8 copy.60
  94.2 0.3 reshape.158
  94.6 0.6 pad_convert_fusion.vecs
  95.3 1.2 multiply_convert_fusion.cot.gm_in
  96.5 1.0 broadcast_in_dim.36.bar
  97.5 0.6 broadcast_in_dim.33.shift
  98.1 32.3 %front.1 = (bf16[1024,1536]{1,0:T(8,128)(2,1)}, bf16[1024,512]{1,0:T(8,128)(2,1)}, f32[4,8,1024]{2,1,0:T(8,128)}, bf16[1024,2048]{1,0:T(8,128)(2,1)}, bf16[2,256,2048]{2,1,0:T(8,128)(2,1)}) custom-call(bf16[1024,2048]{1,0:T(8,128)(2,1)} %bitcast.83, bf16[8,3,256,512]{3,2,1,0:T(8,128)(2,1)} %bitcast.80, f32[8,1536]{1,0:T(8,128)} %broadcast_in_dim.33.shift, ...), custom_call_target="tpu_custom_call" | custom-call | tf_op jit(solution)/shard_map/front/pallas_call | solution.py:1003
  130.4 0.8 broadcast_in_dim.37.valid
  131.1 75.8 %middle.1 = (bf16[256,2048]{1,0:T(8,128)(2,1)}, bf16[4,256,2048]{2,1,0:T(8,128)(2,1)}, f32[256,2048]{1,0:T(8,128)}, f32[24,2048]{1,0:T(8,128)}) custom-call(bf16[4,256,2048]{2,1,0:T(8,128)(2,1)} %bitcast.92, bf16[256,2048]{1,0:T(8,128)(2,1)} %multiply_convert_fusion.cot.gm_in, bf16[2,256,2048]{2,1,0:T(8,128)(2,1)} %get-tuple-element.58.near, ...), custom_call_target="tpu_custom_call" | custom-call | tf_op jit(solution)/shard_map/middle/pallas_call | solution.py:531
  206.9 0.6 broadcast_in_dim.38.bias
  207.6 86.0 %hidden.1 = (bf16[4,256,2048]{2,1,0:T(8,128)(2,1)}, bf16[4,256,2048]{2,1,0:T(8,128)(2,1)}, bf16[4,256,2048]{2,1,0:T(8,128)(2,1)}, bf16[4,256,2048]{2,1,0:T(8,128...) custom-call(bf16[256,2048]{1,0:T(8,128)(2,1)} %get-tuple-element.59.c_own, ...), custom_call_target="tpu_custom_call" | custom-call | tf_op jit(solution)/shard_map/hidden/pallas_call | solution.py:1211
  293.6 25.7 %products.1 = (bf16[2048,4096]{1,0:T(8,128)(2,1)}, bf16[2,256,2048]{2,1,0:T(8,128)(2,1)}) custom-call(bf16[1024,2048]{1,0:T(8,128)(2,1)} %bitcast.82, bf16[1024,2048]{1,0:T(8,128)(2,1)} %bitcast.90, bf16[1024,2048]{1,0:T(8,128)(2,1)} %bitcast.89, bf16[1024,2048]{1,0:T(8,128)(2,1)} %bitcast.91, bf16[4,256,2048]{2,1,0:T(8,128)(2,1)} %get-tuple-element.61.terms), custom_call_target="tpu_custom_call" | custom-call | tf_op jit(solution)/shard_map/products/pallas_call | solution.py:1277
  319.4 115.2 %back_middle.1 = (f32[256,2048]{1,0:T(8,128)}, bf16[2,256,2048]{2,1,0:T(8,128)(2,1)}, f32[32,2048]{1,0:T(8,128)}, bf16[4,256,512]{2,1,0:T(8,128)(2,1)}, bf16[512,2048]{1,0:T(8,128)(2,1)}) custom-call(bf16[4,256,2048]{2,1,0:T(8,128)(2,1)} %get-tuple-element.61.terms, bf16[2,256,2048]{2,1,0:T(8,128)(2,1)} %get-tuple-element.65.landed, ...), custom_call_target="tpu_custom_call" | custom-call | tf_op jit(solution)/shard_map/back_middle/pallas_call | solution.py:641
  434.7 30.2 %attend_back.1 = (bf16[1024,1536]{1,0:T(8,128)(2,1)}, f32[4,16,128]{2,1,0:T(8,128)}, bf16[1024,2048]{1,0:T(8,128)(2,1)}, bf16[2,256,2048]{2,1,0:T(8,128)(2,1)}) custom-call(bf16[1024,1536]{1,0:T(8,128)(2,1)} %get-tuple-element.56.q.k.v, bf16[1024,1536]{1,0:T(8,128)(2,1)} %get-tuple-element.56.q.k.v, bf16[1024,1536]{1,0:T(8,128)(2,1)} %get-tuple-element.56.q.k.v, ...), custom_call_target="tpu_custom_call" | custom-call | tf_op jit(solution)/shard_map/attend_back/pallas_call | solution.py:1097
  464.8 22.5 %head_products.1 = (bf16[2048,1536]{1,0:T(8,128)(2,1)}, bf16[2,256,2048]{2,1,0:T(8,128)(2,1)}) custom-call(bf16[1024,2048]{1,0:T(8,128)(2,1)} %bitcast.84, bf16[1024,1536]{1,0:T(8,128)(2,1)} %get-tuple-element.76.gqkv, bf16[4,256,2048]{2,1,0:T(8,128)(2,1)} %bitcast.85), custom_call_target="tpu_custom_call" | custom-call | tf_op jit(solution)/shard_map/head_products/pallas_call | solution.py:1323
  487.3 0.8 copy-done.3
  488.2 0.5 reshape.152
  488.6 0.8 copy.61
  489.6 0.8 slice_reduce_fusion.2
  490.6 0.6 copy.80
  491.2 68.8 %finish.1 = (f32[256,2048]{1,0:T(8,128)}, bf16[256,2048]{1,0:T(8,128)(2,1)}, f32[32,128]{1,0:T(8,128)}, f32[8,128]{1,0:T(8,128)}) custom-call(bf16[4,256,2048]{2,1,0:T(8,128)(2,1)} %bitcast.86, bf16[2,256,2048]{2,1,0:T(8,128)(2,1)} %get-tuple-element.79.first_landed, bf16[256,2048]{1,0:T(8,128)(2,1)} %tok_in.1, f32[256,2048]{1,0:T(8,128)} %get-tuple-element.80.gmid_in, ...), custom_call_target="tpu_custom_call" | custom-call | tf_op jit(solution)/shard_map/finish/pallas_call | solution.py:871
  560.0 0.7 slice_reduce_fusion.3
  560.7 0.7 reshape.156
  561.4 1.4 slice_bitcast_fusion.6
  563.0 0.6 copy.66
  563.6 3.4 convert_bitcast_fusion
  567.0 1.8 copy.67
  568.8 0.6 slice_reduce_fusion
  569.4 1.8 convert_element_type.80
  571.2 1.4 copy.64
  572.6 1.6 copy.65
  574.2 1.0 copy.93
  575.2 1.0 copy-done
  576.2 1.3 copy.94
  (75 shorter events, 2.0 us)
Async XLA Ops:
  7.2 3.6 copy-start.5
  7.2 3.7 copy-start.6
  7.2 4.0 copy-start.7
  7.2 4.2 copy-start.8
  7.2 4.4 copy-start.9
  7.2 4.6 copy-start.10
  7.2 4.8 copy-start.11
  7.3 5.0 copy-start.12
  7.3 89.2 %all-gather.8.cloned.1.call-start = ((), (), s32[]{:S(2)}) async-start(), calls=%async_computation.4 | async-start | bytes 2359296 | tf_op jit(solution)/shard_map/all_gather | solution.py:1383
  8.0 88.5 %all-gather.6.cloned.1.call-start = ((), (), s32[]{:S(2)}) async-start(), calls=%async_computation.3 | async-start | bytes 7077888 | tf_op jit(solution)/shard_map/all_gather | solution.py:1380
  8.7 198.2 %all-gather.10.cloned.1.call-start = ((), (), s32[]{:S(2)}) async-start(), calls=%async_computation.5 | async-start | bytes 9437184 | tf_op jit(solution)/shard_map/all_gather | solution.py:1384
  9.5 85.8 %copy-start.2 = (bf16[256,2048]{1,0:T(8,128)(2,1)S(1)}, bf16[256,2048]{1,0:T(8,128)(2,1)}, u32[]{:S(2)}) copy-start(bf16[256,2048]{1,0:T(8,128)(2,1)} %param.29) | copy-start | bytes 3145732
  9.5 197.5 %all-gather.12.cloned.1.call-start = ((), (), s32[]{:S(2)}) async-start(), calls=%async_computation.9 | async-start | bytes 9437184 | tf_op jit(solution)/shard_map/all_gather | solution.py:1385
  10.1 424.5 %reduce-scatter.4.cloned.1.call-start = ((), (), s32[]{:S(2)}) async-start(), calls=%async_computation.6 | async-start | bytes 18874368 | tf_op jit(solution)/shard_map/reduce_scatter | solution.py:1407
  319.3 250.1 %reduce-scatter.8.cloned.1.call-start = ((), (), s32[]{:S(2)}) async-start(), calls=%async_computation.8 | async-start | bytes 2359296 | tf_op jit(solution)/shard_map/reduce_scatter | solution.py:1413
  434.6 136.6 %reduce-scatter.6.cloned.1.call-start = ((), (), s32[]{:S(2)}) async-start(), calls=%async_computation.7 | async-start | bytes 7077888 | tf_op jit(solution)/shard_map/reduce_scatter | solution.py:1420
  487.3 0.8 copy-start.3
  567.0 1.8 copy-start.4
  572.6 1.6 copy-start.1
  574.2 2.0 copy-start
Sparse Core Ops, SparseCore 0:
  9.9 30.8 all-gather.7
  42.7 45.4 all-gather.5
  90.1 54.2 all-gather.9
  146.2 54.2 all-gather.11
  319.5 113.8 reduce-scatter.3
  436.5 41.9 reduce-scatter.7
  487.5 63.9 reduce-scatter.5

commit v12 on v9

--- a/solution.py
+++ b/solution.py
@@ -664,8 +664,8 @@
 def finish_kernel(
     n_dp, size, shared, terms, first_landed, tok_in, gmid_in, mlp, landed, mid_in, valid, vecs,
     stats_a, stats_b, given, grad_out, y_out, reduced, rms, right, left, own_mlp, tok, ends,
-    gmid, mid, stats, blocks, land, sums, land2, late, late_land,
-    ss, sr, load_sem, early_sem, s1, r1, s2, r2, s3, r3,
+    gmid, mid, stats, blocks, land, sums, land2, late, late_land, late_sums, late_land2,
+    ss, sr, load_sem, early_sem, s1, r1, s2, r2, s3, r3, s4, r4,
 ):
     rows = tok.shape[0]
     line = Line(size, rows)
@@ -684,17 +684,13 @@
         load.start()
     me = lax.axis_index("dp")
     entry = pltpu.get_barrier_semaphore()
-    everyone = n_dp * size
-
-    def place(q):
-        return {"dp": lax.rem(me + q // size, n_dp), "tensor": lax.rem(line.t + q % size, size)}
-
-    def greet(q, carry):
-        pl.semaphore_signal(entry, device_id=place(q), device_id_type=MESH)
-        return carry
-
-    lax.fori_loop(1, everyone, greet, 0)
-    pl.semaphore_wait(entry, everyone - 1)
+    for p in range(1, n_dp):
+        pl.semaphore_signal(entry, device_id={"dp": lax.rem(me + p, n_dp)}, device_id_type=MESH)
+    for p in range(1, size):
+        pl.semaphore_signal(
+            entry, device_id={"tensor": lax.rem(line.t + p, size)}, device_id_type=MESH
+        )
+    pl.semaphore_wait(entry, n_dp + size - 2)
     line.early_sends(terms, (right, left), (ss, sr), early)
     stats[...] = jnp.zeros_like(stats)
 
@@ -750,14 +746,24 @@
             device_id_type=MESH,
         )
 
-    def three(q):
-        target = place(q)
+    def three(p):
+        other = lax.rem(me + p, n_dp)
         return pltpu.make_async_remote_copy(
-            src_ref=late.at[target["dp"]],
-            dst_ref=late_land.at[q],
-            send_sem=s3.at[q],
-            recv_sem=r3.at[q],
-            device_id=target,
+            src_ref=late.at[other],
+            dst_ref=late_land.at[p],
+            send_sem=s3.at[p],
+            recv_sem=r3.at[p],
+            device_id={"dp": other},
+            device_id_type=MESH,
+        )
+
+    def four(p):
+        return pltpu.make_async_remote_copy(
+            src_ref=late_sums,
+            dst_ref=late_land2.at[p],
+            send_sem=s4.at[p],
+            recv_sem=r4.at[p],
+            device_id={"tensor": lax.rem(line.t + p, size)},
             device_id_type=MESH,
         )
 
@@ -806,11 +812,8 @@
     put_square(late, 2 * per, group_sum(stats, 2))
     put_square(late, 2 * per + 1, group_sum(stats, 3))
 
-    def send_late(q, carry):
-        three(q).start()
-        return carry
-
-    lax.fori_loop(1, everyone, send_late, 0)
+    for p in range(1, n_dp):
+        three(p).start()
     reduced[...] = total
     top = sums[pl.ds(0, shared), :]
     for p in range(1, size):
@@ -818,11 +821,16 @@
         top = top + land2[p]
     reduced[pl.ds(0, shared), :] = top
 
-    def take_late(q, held):
-        three(q).wait_recv()
-        return held + late_land[q]
-
-    final = lax.fori_loop(1, everyone, take_late, late[me])
+    final = late[me]
+    for p in range(1, n_dp):
+        three(p).wait_recv()
+        final = final + late_land[p]
+    late_sums[...] = final
+    for p in range(1, size):
+        four(p).start()
+    for p in range(1, size):
+        four(p).wait_recv()
+        final = final + late_land2[p]
     reduced[0 : 2 * per, :] = final[0 : 2 * per, :]
     for i in (9, 10):
         row = 2 * per + i - 9
@@ -833,11 +841,10 @@
         square = jnp.sum(reduced[row : row + 1, :], keepdims=True)
         rms[i : i + 1, :] = jnp.sqrt(square / count)
 
-    def sent_late(q, carry):
-        three(q).wait_send()
-        return carry
-
-    lax.fori_loop(1, everyone, sent_late, 0)
+    for p in range(1, n_dp):
+        three(p).wait_send()
+    for p in range(1, size):
+        four(p).wait_send()
     line.drain_scatter((right, left), (ss, sr), 0, True)
     for p in range(1, n_dp):
         one(p).wait_send()
@@ -875,7 +882,9 @@
             pltpu.VMEM((lines, 128), F32),
             pltpu.VMEM((size, shared, 128), F32),
             pltpu.VMEM((n_dp,) + late, F32),
-            pltpu.VMEM((n_dp * size,) + late, F32),
+            pltpu.VMEM((n_dp,) + late, F32),
+            pltpu.VMEM(late, F32),
+            pltpu.VMEM((size,) + late, F32),
         ]
         + line_sems(size)
         + [
@@ -885,8 +894,10 @@
             pltpu.SemaphoreType.DMA((n_dp,)),
             pltpu.SemaphoreType.DMA((size,)),
             pltpu.SemaphoreType.DMA((size,)),
-            pltpu.SemaphoreType.DMA((n_dp * size,)),
-            pltpu.SemaphoreType.DMA((n_dp * size,)),
+            pltpu.SemaphoreType.DMA((n_dp,)),
+            pltpu.SemaphoreType.DMA((n_dp,)),
+            pltpu.SemaphoreType.DMA((size,)),
+            pltpu.SemaphoreType.DMA((size,)),
         ],
         compiler_params=params(cid),
         name="finish",

time: 584 us -> 583 us (level)
  no operation moved by 1% of the time
where the time goes in v12:
time: 583 us; the launch traced here: 582 us
  Pallas kernels  534 us (92%)
  local copies, waits for them, and re-layouts  22.6 us (4%)
  between operations  15.2 us (3%)
  other arithmetic  6.19 us (1%)
    pallas_call x1, Pallas kernels, back_middle(): pl.pallas_call(functools.partial(back_middle_kernel, size), out_shape=(ja...  114 us
    pallas_call x1, Pallas kernels, hidden(): pl.pallas_call(functools.partial(hidden_kernel, n_dp, size), out_shape=(j...  86.1 us
    pallas_call x1, Pallas kernels, first(): pl.pallas_call(functools.partial(first_kernel, n_dp, size, part), out_sha...  78.5 us
    pallas_call x1, Pallas kernels, middle(): pl.pallas_call(functools.partial(middle_kernel, size), out_shape=(jax.Sha...  75.8 us
    pallas_call x1, Pallas kernels, finish(): pl.pallas_call(functools.partial(finish_kernel, n_dp, size, shared), out_...  68.7 us
    pallas_call x1, Pallas kernels, front(): pl.pallas_call(functools.partial(front_kernel, size, heads), grid=(heads,...  32.1 us
    pallas_call x1, Pallas kernels, attend_back(): pl.pallas_call(functools.partial(attend_back_kernel, size, heads), grid=(...  29.6 us
    pallas_call x1, Pallas kernels, products(): pl.pallas_call(functools.partial(products_kernel, size, steps), grid=(ste...  25.9 us
  transfers between devices with their start and end apart: 7, of which 0 were waited for; matrix products, arithmetic and copies ran while one was open for 3% of the time, Pallas kernels for 73%

profile of v12, /device:TPU:0, one launch (start us, length us, event | category | flops | bytes accessed | tf_op | source)
XLA Modules:
  0.0 581.6 jit_solution(1971460946398555420)
XLA Ops:
  7.3 0.7 all-gather.8.cloned.1.call-update
  8.0 0.7 all-gather.6.cloned.1.call-update
  8.8 0.7 all-gather.10.cloned.1.call-update
  9.5 0.5 all-gather.12.cloned.1.call-update
  11.2 0.2 dynamic-update-slice
  11.4 0.2 dynamic-update-slice.1
  11.6 0.2 dynamic-update-slice.2
  11.9 0.2 dynamic-update-slice.3
  12.1 0.2 dynamic-update-slice.4
  12.9 0.6 pad_bitcast_fusion.small
  13.5 78.5 %first.1 = (bf16[8,16,128]{2,1,0:T(8,128)(2,1)}, bf16[4,256,2048]{2,1,0:T(8,128)(2,1)}) custom-call(bf16[16,128]{1,0:T(8,128)(2,1)} %pad_bitcast_fusion.small, bf16[256,2048]{1,0:T(8,128)(2,1)} %tok_in.1), custom_call_target="tpu_custom_call" | custom-call | tf_op jit(solution)/shard_map/first/pallas_call | solution.py:449
  92.0 0.8 copy.81
  93.3 0.8 copy.60
  94.1 0.3 reshape.162
  94.5 0.6 pad_convert_fusion.vecs
  95.2 1.2 multiply_convert_fusion.cot.gm_in
  96.4 1.0 broadcast_in_dim.36.bar
  97.4 0.6 broadcast_in_dim.33.shift
  98.0 32.1 %front.1 = (bf16[1024,1536]{1,0:T(8,128)(2,1)}, bf16[1024,512]{1,0:T(8,128)(2,1)}, f32[4,8,1024]{2,1,0:T(8,128)}, bf16[1024,2048]{1,0:T(8,128)(2,1)}, bf16[2,256,2048]{2,1,0:T(8,128)(2,1)}) custom-call(bf16[1024,2048]{1,0:T(8,128)(2,1)} %bitcast.84, bf16[8,3,256,512]{3,2,1,0:T(8,128)(2,1)} %bitcast.81, f32[8,1536]{1,0:T(8,128)} %broadcast_in_dim.33.shift, ...), custom_call_target="tpu_custom_call" | custom-call | tf_op jit(solution)/shard_map/front/pallas_call | solution.py:996
  130.2 0.8 broadcast_in_dim.37.valid
  130.9 75.8 %middle.1 = (bf16[256,2048]{1,0:T(8,128)(2,1)}, bf16[4,256,2048]{2,1,0:T(8,128)(2,1)}, f32[256,2048]{1,0:T(8,128)}, f32[24,2048]{1,0:T(8,128)}) custom-call(bf16[4,256,2048]{2,1,0:T(8,128)(2,1)} %bitcast.93, bf16[256,2048]{1,0:T(8,128)(2,1)} %multiply_convert_fusion.cot.gm_in, bf16[2,256,2048]{2,1,0:T(8,128)(2,1)} %get-tuple-element.58.near, ...), custom_call_target="tpu_custom_call" | custom-call | tf_op jit(solution)/shard_map/middle/pallas_call | solution.py:531
  206.8 0.6 broadcast_in_dim.38.bias
  207.4 86.1 %hidden.1 = (bf16[4,256,2048]{2,1,0:T(8,128)(2,1)}, bf16[4,256,2048]{2,1,0:T(8,128)(2,1)}, bf16[4,256,2048]{2,1,0:T(8,128)(2,1)}, bf16[4,256,2048]{2,1,0:T(8,128...) custom-call(bf16[256,2048]{1,0:T(8,128)(2,1)} %get-tuple-element.59.c_own, ...), custom_call_target="tpu_custom_call" | custom-call | tf_op jit(solution)/shard_map/hidden/pallas_call | solution.py:1204
  293.6 25.9 %products.1 = (bf16[2048,2048]{1,0:T(8,128)(2,1)}, bf16[2048,2048]{1,0:T(8,128)(2,1)}, bf16[2,256,2048]{2,1,0:T(8,128)(2,1)}) custom-call(bf16[1024,2048]{1,0:T(8,128)(2,1)} %bitcast.91, bf16[1024,2048]{1,0:T(8,128)(2,1)} %bitcast.83, bf16[1024,2048]{1,0:T(8,128)(2,1)} %bitcast.90, bf16[1024,2048]{1,0:T(8,128)(2,1)} %bitcast.92, ...), custom_call_target="tpu_custom_call" | custom-call | tf_op jit(solution)/shard_map/products/pallas_call | solution.py:1272
  319.6 0.5 reduce-scatter.6.cloned.1.call-update
  320.1 114.4 %back_middle.1 = (bf16[4,256,2048]{2,1,0:T(8,128)(2,1)}, f32[256,2048]{1,0:T(8,128)}, bf16[2,256,2048]{2,1,0:T(8,128)(2,1)}, f32[32,2048]{1,0:T(8,128)}, bf16[4,256,512]{2,1,0:T(8,128)(2,1)}) custom-call(bf16[4,256,2048]{2,1,0:T(8,128)(2,1)} %get-tuple-element.61.terms, bf16[2,256,2048]{2,1,0:T(8,128)(2,1)} %get-tuple-element.65.landed, ...), custom_call_target="tpu_custom_call" | custom-call | tf_op jit(solution)/shard_map/back_middle/pallas_call | solution.py:634
  434.5 29.6 %attend_back.1 = (bf16[1024,1536]{1,0:T(8,128)(2,1)}, f32[4,16,128]{2,1,0:T(8,128)}, bf16[1024,2048]{1,0:T(8,128)(2,1)}, bf16[2,256,2048]{2,1,0:T(8,128)(2,1)}) custom-call(bf16[1024,1536]{1,0:T(8,128)(2,1)} %get-tuple-element.56.q.k.v, bf16[1024,1536]{1,0:T(8,128)(2,1)} %get-tuple-element.56.q.k.v, bf16[1024,1536]{1,0:T(8,128)(2,1)} %get-tuple-element.56.q.k.v, ...), custom_call_target="tpu_custom_call" | custom-call | tf_op jit(solution)/shard_map/attend_back/pallas_call | solution.py:1090
  464.2 22.9 %head_products.1 = (bf16[2048,2048]{1,0:T(8,128)(2,1)}, bf16[2,256,2048]{2,1,0:T(8,128)(2,1)}) custom-call(bf16[1024,2048]{1,0:T(8,128)(2,1)} %bitcast.94, bf16[1024,2048]{1,0:T(8,128)(2,1)} %bitcast.85, bf16[1024,512]{1,0:T(8,128)(2,1)} %get-tuple-element.73.o, bf16[1024,1536]{1,0:T(8,128)(2,1)} %get-tuple-element.74.gqkv, bf16[4,256,2048]{2,1,0:T(8,128)(2,1)} %bitcast.86), custom_call_target="tpu_custom_call" | custom-call | tf_op jit(solution)/shard_map/head_products/pallas_call | solution.py:1325
  487.1 0.8 copy-done.6
  488.0 0.5 reshape.156
  488.4 0.8 copy.61
  489.3 0.8 slice_reduce_fusion.2
  490.4 0.6 copy.80
  491.0 68.7 %finish.1 = (f32[256,2048]{1,0:T(8,128)}, bf16[256,2048]{1,0:T(8,128)(2,1)}, f32[32,128]{1,0:T(8,128)}, f32[8,128]{1,0:T(8,128)}) custom-call(bf16[4,256,2048]{2,1,0:T(8,128)(2,1)} %bitcast.87, bf16[2,256,2048]{2,1,0:T(8,128)(2,1)} %get-tuple-element.79.first_landed, bf16[256,2048]{1,0:T(8,128)(2,1)} %tok_in.1, f32[256,2048]{1,0:T(8,128)} %get-tuple-element.80.gmid_in, ...), custom_call_target="tpu_custom_call" | custom-call | tf_op jit(solution)/shard_map/finish/pallas_call | solution.py:864
  559.7 0.8 slice_reduce_fusion.3
  560.5 0.7 reshape.160
  561.2 1.4 slice_bitcast_fusion.6
  562.7 0.6 copy.67
  563.4 1.6 convert_element_type.82
  564.9 1.5 convert_element_type.83
  566.4 0.6 slice_reduce_fusion
  567.1 1.1 convert_bitcast_fusion
  568.2 1.0 copy.66
  569.3 0.5 copy.64
  569.8 1.6 copy.65
  571.4 1.0 copy.93
  572.4 1.0 copy-done
  573.4 1.3 copy.94
  (83 shorter events, 2.6 us)
Async XLA Ops:
  7.2 3.6 copy-start.8
  7.2 3.7 copy-start.9
  7.2 4.0 copy-start.10
  7.2 4.2 copy-start.11
  7.2 4.4 copy-start.12
  7.2 4.6 copy-start.13
  7.2 4.8 copy-start.14
  7.3 5.0 copy-start.15
  7.3 89.1 %all-gather.8.cloned.1.call-start = ((), (), s32[]{:S(2)}) async-start(), calls=%async_computation.4 | async-start | bytes 2359296 | tf_op jit(solution)/shard_map/all_gather | solution.py:1387
  8.0 88.4 %all-gather.6.cloned.1.call-start = ((), (), s32[]{:S(2)}) async-start(), calls=%async_computation.3 | async-start | bytes 7077888 | tf_op jit(solution)/shard_map/all_gather | solution.py:1384
  8.7 198.0 %all-gather.10.cloned.1.call-start = ((), (), s32[]{:S(2)}) async-start(), calls=%async_computation.5 | async-start | bytes 9437184 | tf_op jit(solution)/shard_map/all_gather | solution.py:1388
  9.5 85.7 %copy-start.5 = (bf16[256,2048]{1,0:T(8,128)(2,1)S(1)}, bf16[256,2048]{1,0:T(8,128)(2,1)}, u32[]{:S(2)}) copy-start(bf16[256,2048]{1,0:T(8,128)(2,1)} %param.29) | copy-start | bytes 3145732
  9.5 197.3 %all-gather.12.cloned.1.call-start = ((), (), s32[]{:S(2)}) async-start(), calls=%async_computation.9 | async-start | bytes 9437184 | tf_op jit(solution)/shard_map/all_gather | solution.py:1389
  10.1 477.0 %reduce-scatter.4.cloned.1.call-start = ((), (), s32[]{:S(2)}) async-start(), calls=%async_computation.6 | async-start | bytes 9437184 | tf_op jit(solution)/shard_map/reduce_scatter | solution.py:1411
  319.5 167.6 %reduce-scatter.6.cloned.1.call-start = ((), (), s32[]{:S(2)}) async-start(), calls=%async_computation.7 | async-start | bytes 9437184 | tf_op jit(solution)/shard_map/reduce_scatter | solution.py:1412
  320.1 247.0 %reduce-scatter.8.cloned.1.call-start = ((), (), s32[]{:S(2)}) async-start(), calls=%async_computation.8 | async-start | bytes 9437184 | tf_op jit(solution)/shard_map/reduce_scatter | solution.py:1426
  487.1 0.8 copy-start.6
  491.0 72.4 %copy-start.2 = (bf16[256,2048]{1,0:T(8,128)(2,1)S(1)}, bf16[256,2048]{1,0:T(8,128)(2,1)}, u32[]{:S(2)}) copy-start(bf16[256,2048]{1,0:T(8,128)(2,1)} %reduce-scatter.6.cloned.1.call-done) | copy-start | bytes 3145732
  559.7 5.2 copy-start.1
  564.9 1.5 copy-start.7
  567.1 2.1 copy-start.3
  569.8 1.6 copy-start.4
  571.4 2.0 copy-start
Sparse Core Ops, SparseCore 0:
  9.9 30.8 all-gather.7
  42.7 45.4 all-gather.5
  90.1 54.3 all-gather.9
  146.2 54.2 all-gather.11
  319.6 68.9 reduce-scatter.3
  391.9 71.4 reduce-scatter.5
  487.2 72.3 reduce-scatter.7
